TPU v7x, 32 devices: a whole 2x2x4 slice. The times are simulated.
32 devices in a mesh: groups: 2 (over y), seq: 16 (over z, x, core).
Axes of the slice: x: 2, y: 2, z: 4, core: 2. Of those that a mesh axis runs over, the one named last changes fastest.
Arguments:
- readings: bfloat16 [32, 2048, 1024], P('groups', 'seq'), parts along dimension 0, may hold values from -6 to 6
- block_graph: int32 [32, 16], P('groups'), parts along dimension 0, may hold values 0 or 1
- cluster_of: int32 [32], P('groups'), parts along dimension 0, may hold values from 0 to 15, each once
- mix_weight: float32 [16, 16], replicated, may hold values from -2.4 to 2.4
- boundaries: int32 [4096], P(('groups', 'seq')), parts along dimension 0, may hold values 0 or 1
- w_channels: bfloat16 [1024, 512], replicated, may hold values from -0.1875 to 0.1875
- w_state: bfloat16 [1024, 128], replicated, may hold values from -0.01953125 to 0.01953125
- w_step: bfloat16 [1024, 8], replicated, may hold values from -0.1875 to 0.1875
- step_bias: float32 [8], replicated, may hold values from -1 to 1
- channel_fading_exponent: float32 [8], replicated
- skip_gain: float32 [8], replicated, may hold values from 0.5 to 1.5
- norm_gain: float32 [512], replicated, may hold values from 0.5 to 1.5
- w_out: bfloat16 [512, 1024], replicated, may hold values from -0.25 to 0.25
- cotangent: bfloat16 [32, 2048, 1024], P('groups', 'seq'), parts along dimension 0, may hold values from -0.032958984 to 0.032958984
Outputs:
- grad_out: float32 [1024, 1024], P('groups'), parts along dimension 0
- grad_read: float32 [2048, 64], P('groups'), parts along dimension 0
- grad_gain: float32 [1024], P('groups'), parts along dimension 0
There are 2 independent parts, one for each index of `groups`. A program takes and returns all parts, laid end to end along the dimension named above; an argument that names none is the same for every part. Nothing has to cross between parts.
Inputs may be any that keep to these rules, and one draw needn't show every extreme that they name: `cluster_of`: each cluster holds exactly one sensor.
All inputs are finite; a program needn't handle non-finite values. No bound on the sum of `boundaries` on one device may be relied on, other than what follows from the above.
Results may differ from a plain program's by a relative error of at most 0.0079.
Values may be sent and summed in bfloat16 or wider, within the bound.
No kernel may reach another device: no remote copies, remote signals or barrier semaphores. Data moves between devices by JAX's collectives and lax.ppermute only.
A program may use at most 128 MiB of HBM per device.

v0:
```python
import math

import jax
import jax.numpy as jnp
from jax import lax
from jax.sharding import PartitionSpec as P

HIGHEST_PREC = lax.Precision.HIGHEST
surviving_pulse_multiplier = math.log(0.7)


def mix_block(block_data, coupling):
    sensors = block_data.shape[0]
    flat_data = block_data.reshape(sensors, -1)
    spread_factor = jnp.dot(coupling, flat_data, preferred_element_type=jnp.float32)
    mixed_data = (flat_data.astype(jnp.float32) + spread_factor).astype(jnp.bfloat16)
    return mixed_data.reshape(-1, block_data.shape[2])


def mapped_matrix_lines(mixed_rows, w_channels, w_state, w_step, step_bias):
    channels = jnp.dot(mixed_rows, w_channels, preferred_element_type=jnp.float32).astype(
        jnp.bfloat16
    )
    state_maps = jnp.dot(mixed_rows, w_state, preferred_element_type=jnp.float32).astype(
        jnp.bfloat16
    )
    step_raw = (jnp.dot(mixed_rows, w_step, preferred_element_type=jnp.float32) + step_bias).astype(
        jnp.bfloat16
    )
    return (channels, state_maps, step_raw)


def decay_terms(step_raw, interval_start_markers, channel_fading_exponent):
    increment_size_per_tick = jax.nn.softplus(step_raw.astype(jnp.float32))
    natural_fading_exponent = (
        -jnp.exp(channel_fading_exponent) * increment_size_per_tick
        + surviving_pulse_multiplier * interval_start_markers
    )
    return (increment_size_per_tick, natural_fading_exponent)


def block_decays(natural_fading_exponent):
    cumulative = jnp.cumsum(natural_fading_exponent, axis=1)
    span = natural_fading_exponent.shape[1]
    later = jnp.arange(span)[:, None] >= jnp.arange(span)[None, :]
    lower = later[None, :, :, None]
    gap = cumulative[:, :, None, :] - cumulative[:, None, :, :]
    decays = jnp.where(lower, jnp.exp(jnp.where(lower, gap, 0.0)), 0.0)
    return (cumulative, decays)


def block_summary(scaled_in, writes, cumulative):
    tail = jnp.exp(cumulative[:, -1:, :] - cumulative)
    local_state = jnp.einsum(
        "bsh,bshp,bsn->bhpn", tail, scaled_in, writes.astype(jnp.float32), precision=HIGHEST_PREC
    )
    return (jnp.exp(cumulative[:, -1, :]), local_state)


def block_output(channels, scaled_in, writes, reads, cumulative, decays, state_in, skip_gain):
    read_f = reads.astype(jnp.float32)
    write_f = writes.astype(jnp.float32)
    scores = jnp.einsum("btn,bsn->bts", read_f, write_f, precision=HIGHEST_PREC)
    within = jnp.einsum("bts,btsh,bshp->bthp", scores, decays, scaled_in, precision=HIGHEST_PREC)
    carried = (
        jnp.einsum("btn,bhpn->bthp", read_f, state_in, precision=HIGHEST_PREC)
        * jnp.exp(cumulative)[..., None]
    )
    return within + carried + skip_gain[:, None] * channels.astype(jnp.float32)


def readout_gradient_parts(ssd_grad, scaled_in, writes, cumulative, decays, state_in):
    carried = jnp.einsum(
        "bthp,bhpn->btn",
        ssd_grad * jnp.exp(cumulative)[..., None],
        state_in,
        precision=HIGHEST_PREC,
    )
    pair_sums = jnp.einsum(
        "bthp,bshp,btsh->bts", ssd_grad, scaled_in, decays, precision=HIGHEST_PREC
    )
    within = jnp.einsum(
        "bts,bsn->btn", pair_sums, writes.astype(jnp.float32), precision=HIGHEST_PREC
    )
    return carried + within


def combine_states(earlier, later):
    return (earlier[0] * later[0], later[0][..., None, None] * earlier[1] + later[1])


def norm_forward(ssd_out, gain_vec):
    inv_rms = lax.rsqrt(jnp.mean(ssd_out * ssd_out, axis=-1, keepdims=True) + 1e-05)
    normed = ssd_out * inv_rms
    return (normed, inv_rms, (normed * gain_vec).astype(jnp.bfloat16))


def norm_backward(normed_grad, normed, inv_rms, gain_vec):
    scaled_grad = normed_grad * gain_vec
    return inv_rms * (scaled_grad - normed * jnp.mean(scaled_grad * normed, axis=-1, keepdims=True))


def per_device(
    readings,
    block_graph,
    cluster_of,
    mix_weight,
    boundaries,
    w_channels,
    w_state,
    w_step,
    step_bias,
    channel_fading_exponent,
    skip_gain,
    norm_gain,
    w_out,
    cotangent,
):
    sensors = readings.shape[0]
    span = readings.shape[1]
    width = readings.shape[2]
    heads = channel_fading_exponent.shape[0]
    channel_count = w_channels.shape[1]
    head_size = channel_count // heads
    state_size = w_state.shape[1] // 2
    rows_now = sensors * span
    pairs = sensors * heads
    cluster_ids = jnp.arange(sensors, dtype=jnp.int32)
    onehot = (cluster_of[:, None] == cluster_ids[None, :]).astype(jnp.float32)
    linked = jnp.dot(
        jnp.dot(onehot, block_graph.astype(jnp.float32), precision=HIGHEST_PREC),
        onehot.T,
        precision=HIGHEST_PREC,
    )
    coupling = (linked * mix_weight).astype(jnp.bfloat16)
    mixed_rows = mix_block(readings, coupling)
    channels, state_maps, step_raw = mapped_matrix_lines(
        mixed_rows, w_channels, w_state, w_step, step_bias
    )
    chan_pairs = (
        channels.reshape(sensors, span, heads, head_size)
        .transpose(0, 2, 1, 3)
        .reshape(pairs, span, head_size)
    )
    maps_pairs = jnp.broadcast_to(
        state_maps.reshape(sensors, 1, span, 2 * state_size), (sensors, heads, span, 2 * state_size)
    ).reshape(pairs, span, 2 * state_size)
    step_pairs = step_raw.reshape(sensors, span, heads).transpose(0, 2, 1).reshape(pairs, span, 1)
    marks_pairs = jnp.broadcast_to(boundaries.astype(jnp.bfloat16)[None, :, None], (pairs, span, 1))
    arrived = (
        lax.all_to_all(chan_pairs, "seq", split_axis=0, concat_axis=1, tiled=True),
        lax.all_to_all(maps_pairs, "seq", split_axis=0, concat_axis=1, tiled=True),
        lax.all_to_all(step_pairs, "seq", split_axis=0, concat_axis=1, tiled=True),
        lax.all_to_all(marks_pairs, "seq", split_axis=0, concat_axis=1, tiled=True),
    )
    own_pairs = arrived[0].shape[0]
    entire_sequence_count = arrived[0].shape[1]
    per_pair = entire_sequence_count // span
    blocks = own_pairs * per_pair
    pair_ids = lax.axis_index("seq") * own_pairs + jnp.arange(own_pairs, dtype=jnp.int32)
    head_pick = ((pair_ids % heads)[:, None] == jnp.arange(heads, dtype=jnp.int32)[None, :]).astype(
        jnp.float32
    )
    decay_pair = jnp.dot(head_pick, channel_fading_exponent, precision=HIGHEST_PREC)
    skip_pair = jnp.dot(head_pick, skip_gain, precision=HIGHEST_PREC)
    decay_block = jnp.broadcast_to(decay_pair[:, None], (own_pairs, per_pair)).reshape(blocks, 1, 1)
    skip_block = jnp.broadcast_to(skip_pair[:, None], (own_pairs, per_pair)).reshape(blocks, 1, 1)
    chan_four = arrived[0].reshape(blocks, span, 1, head_size)
    maps_here = arrived[1].reshape(blocks, span, 2 * state_size)
    writes = maps_here[..., :state_size]
    reads = maps_here[..., state_size:]
    increment_size_per_tick, natural_fading_exponent = decay_terms(
        arrived[2].reshape(blocks, span, 1),
        arrived[3].reshape(blocks, span, 1).astype(jnp.float32),
        decay_block,
    )
    cumulative, decays = block_decays(natural_fading_exponent)
    scaled_in = chan_four.astype(jnp.float32) * increment_size_per_tick[..., None]
    running_sums, local_state = block_summary(scaled_in, writes, cumulative)
    inclusive = lax.associative_scan(
        combine_states,
        (
            running_sums.reshape(own_pairs, per_pair, 1),
            local_state.reshape(own_pairs, per_pair, 1, head_size, state_size),
        ),
        axis=1,
    )
    state_in = jnp.concatenate(
        [jnp.zeros_like(inclusive[1][:, :1]), inclusive[1][:, :-1]], axis=1
    ).reshape(blocks, 1, head_size, state_size)
    block_out = block_output(
        chan_four, scaled_in, writes, reads, cumulative, decays, state_in, skip_block
    ).reshape(own_pairs, entire_sequence_count, head_size)
    back_pairs = lax.all_to_all(block_out, "seq", split_axis=1, concat_axis=0, tiled=True)
    ssd_out = (
        back_pairs.reshape(sensors, heads, span, head_size)
        .transpose(0, 2, 1, 3)
        .reshape(rows_now, channel_count)
    )
    cot_rows = cotangent.reshape(rows_now, width)
    normed, inv_rms, normed_out = norm_forward(ssd_out, norm_gain)
    grad_out = lax.dot_general(
        normed_out, cot_rows, (((0,), (0,)), ((), ())), preferred_element_type=jnp.float32
    )
    normed_grad = lax.dot_general(
        cot_rows, w_out, (((1,), (1,)), ((), ())), preferred_element_type=jnp.float32
    )
    grad_gain = jnp.sum(normed * normed_grad, axis=0)
    ssd_grad = norm_backward(normed_grad, normed, inv_rms, norm_gain)
    grad_pairs = (
        ssd_grad.reshape(sensors, span, heads, head_size)
        .transpose(0, 2, 1, 3)
        .reshape(pairs, span, head_size)
    )
    grad_here = lax.all_to_all(grad_pairs, "seq", split_axis=0, concat_axis=1, tiled=True).reshape(
        blocks, span, 1, head_size
    )
    read_local = readout_gradient_parts(
        grad_here, scaled_in, writes, cumulative, decays, state_in
    ).reshape(own_pairs, entire_sequence_count, state_size)
    read_pairs = lax.all_to_all(read_local, "seq", split_axis=1, concat_axis=0, tiled=True)
    read_grad = (
        jnp.sum(read_pairs.reshape(sensors, heads, span, state_size), axis=1)
        .astype(jnp.bfloat16)
        .reshape(rows_now, state_size)
    )
    grad_read = lax.dot_general(
        mixed_rows, read_grad, (((0,), (0,)), ((), ())), preferred_element_type=jnp.float32
    )
    return lax.psum((grad_out, grad_read, grad_gain), "seq")


def solution(mesh):
    in_specs = (
        P("groups", "seq", None),
        P("groups", None),
        P("groups"),
        P(),
        P(("groups", "seq")),
        P(),
        P(),
        P(),
        P(),
        P(),
        P(),
        P(),
        P(),
        P("groups", "seq", None),
    )
    out_specs = (P("groups", None), P("groups", None), P("groups"))
    return jax.shard_map(
        per_device, mesh=mesh, in_specs=in_specs, out_specs=out_specs, check_vma=False
    )
```

profile of v0, /device:TPU:0, one launch (start us, length us, event | category | flops | bytes accessed | tf_op | source)
XLA Modules:
  0.0 953.8 jit_solution(7639864418636455563)
XLA Ops:
  7.2 4.6 copy.180
  15.5 4.8 reshape.402
  25.8 7.4 all-to-all-start.1
  34.7 5.1 all-to-all-done.1
  43.3 5.9 convolution_convert_fusion
  54.6 6.0 all-to-all-start.3
  60.6 4.3 convolution_convert_fusion.1
  64.8 36.8 %all-to-all-done.3 = bf16[128,128,64]{1,2,0:T(8,128)(2,1)S(1)} async-done(((bf16[128,128,64]{1,2,0:T(8,128)(2,1)}), bf16[128,128,64]{1,2,0:T(8,128)(2,1)S(1)}, u32[]{:S(2)}, u32[]{:S(2)}) %all-to-all-start.3) | async-done | bytes 2097184 | tf_op jit(solution)/shard_map/all_to_all | solution.py:151
  101.7 4.1 broadcast_in_dim.25
  105.8 11.6 %all-to-all-start = ((bf16[128,128,128]{2,1,0:T(8,128)(2,1)}), bf16[128,128,128]{2,1,0:T(8,128)(2,1)}, u32[]{:S(2)}, u32[]{:S(2)}) async-start(bf16[128,128,128]{2,1,0:T(8,128)(2,1)} %bitcast.189), calls=%async_computation | async-start | bytes 8388608 | tf_op jit(solution)/shard_map/all_to_all | solution.py:152
  130.5 64.5 %all-to-all-done = bf16[128,128,128]{2,1,0:T(8,128)(2,1)} async-done(((bf16[128,128,128]{2,1,0:T(8,128)(2,1)}), bf16[128,128,128]{2,1,0:T(8,128)(2,1)}, u32[]{:S(2)}, u32[]{:S(2)}) %all-to-all-start) | async-done | bytes 4194336 | tf_op jit(solution)/shard_map/all_to_all | solution.py:152
  195.0 6.4 copy.143
  201.5 7.0 fusion.31
  215.5 6.3 pad.29
  223.9 12.4 %pad.31 = f32[8,8,1,64,64]{4,3,1,0,2:T(8,128)S(1)} pad(f32[8,4,1,64,64]{4,3,1,0,2:T(8,128)} %add.157, f32[]{:T(128)} %constant.31.clone.1), padding=0_0_0x1_0_1x0_0_0x0_0_0x0_0_0 | pad | bytes 1572868 | tf_op jit(solution)/shard_map/pad | solution.py:180
  239.1 16.6 %pad.30 = f32[8,8,1,64,64]{4,3,1,0,2:T(8,128)} pad(f32[8,4,1,64,64]{4,3,1,0,2:T(8,128)} %pad_maximum_fusion.1, f32[]{:T(128)} %constant.31.clone.1), padding=0_0_0x0_1_1x0_0_0x0_0_0x0_0_0 | pad | bytes 1572868 | tf_op jit(solution)/shard_map/pad | solution.py:180
  262.6 31.8 %pad.41 = f32[8,15,1,64,64]{4,3,1,0,2:T(8,128)} pad(f32[8,8,1,64,64]{4,3,1,0,2:T(8,128)} %pad_maximum_fusion, f32[]{:T(128)} %constant.31.clone.1), padding=0_0_0x0_0_1x0_0_0x0_0_0x0_0_0 | pad | bytes 3014660 | tf_op jit(solution)/shard_map/slice | solution.py:189
  294.5 21.2 %pad.61 = f32[8,16,1,64,64]{4,3,1,0,2:T(8,128)} pad(f32[8,8,1,64,64]{4,3,1,0,2:T(8,128)S(1)} %copy-done.16, f32[]{:T(128)} %constant.31.clone.1), padding=0_0_0x1_0_1x0_0_0x0_0_0x0_0_0 | pad | bytes 3145732
  315.7 4.2 slice_add_fusion.4
  322.1 21.4 %fusion.3 = f32[128,128,64]{1,2,0:T(8,128)S(1)} fusion(f32[128,128,64]{1,2,0:T(8,128)S(1)} %copy-done.3, f32[128,128,128]{2,1,0:T(8,128)} %fusion.31, f32[128,128]{1,0:T(8,128)S(1)} %copy.150, pred[128,128]{1,0:T(8,128)(4,1)S(1)} %iota_compare_fusion), kind=kOutput, calls=%fused_computation.4 | convolution fusion | flops 1619001344 | bytes 16859136 | tf_op jit(solution)/shard_map/bts,btsh,bshp->bthp/dot_general | solution.py:64
  346.3 4.4 copy.164
  350.8 4.9 reshape.411
  355.6 7.6 copy.165
  363.3 13.3 %reshape.441 = f32[16,1,65536]{2,1,0:T(1,128)} reshape(f32[2048,8,64]{2,1,0:T(8,128)} %bitcast.183) | data formatting | bytes 8388608
  376.5 112.0 %all_to_all.78 = f32[16,1,65536]{2,1,0:T(1,128)} all-to-all(f32[16,1,65536]{2,1,0:T(1,128)} %reshape.441), channel_id=1, replica_groups=mesh['groups'=2,'seq'=16] {'seq'}, dimensions={0} | all-to-all | bytes 8388608 | tf_op jit(solution)/shard_map/all_to_all | solution.py:194
  489.0 13.7 %reduce.14 = f32[16,65536]{1,0:T(8,128)} reduce(f32[16,1,65536]{2,1,0:T(1,128)} %all_to_all.78, f32[]{:T(128)} %broadcast.219), dimensions={1}, to_apply=%all_to_all.30.reduce_sub_computation | reduce | bytes 8388612 | tf_op jit(solution)/shard_map/all_to_all | solution.py:194
  502.7 6.9 reshape.442
  509.6 6.0 copy.166
  519.1 3.9 copy.193
  523.0 5.4 copy.167
  528.4 6.7 multiply_reduce_fusion
  537.5 5.8 copy.168
  547.8 97.4 %all_to_all.79 = f32[128,128,64]{1,2,0:T(8,128)S(1)} all-to-all(f32[128,128,64]{1,2,0:T(8,128)S(1)} %bitcast.192), channel_id=1, replica_groups=mesh['groups'=2,'seq'=16] {'seq'}, dimensions={0} | all-to-all | bytes 8388608 | tf_op jit(solution)/shard_map/all_to_all | solution.py:215
  647.4 13.6 %fusion.71 = f32[128,128,128]{2,1,0:T(8,128)S(1)} fusion(f32[128,128,64]{1,2,0:T(8,128)S(1)} %bitcast.181, f32[128,128,64]{1,2,0:T(8,128)S(1)} %copy-done.4), kind=kOutput, calls=%fused_computation.124 | convolution fusion | flops 1610612736 | bytes 16777216 | tf_op jit(solution)/shard_map/bthp,bshp,btsh->bts/dot_general | solution.py:79
  661.0 9.4 fusion.1
  670.4 7.0 fusion.22
  677.4 4.4 copy.172
  681.8 4.9 reshape.417
  686.8 7.5 copy.173
  694.3 13.3 %reshape.443 = f32[16,1,65536]{2,1,0:T(1,128)} reshape(f32[2048,8,64]{2,1,0:T(8,128)} %bitcast.185) | data formatting | bytes 8388608
  707.5 5.4 all-to-all-start.6
  720.2 70.4 %all-to-all-done.6 = f32[16,1,65536]{2,1,0:T(1,128)} async-done(((f32[16,1,65536]{2,1,0:T(1,128)}), f32[16,1,65536]{2,1,0:T(1,128)}, u32[]{:S(2)}, u32[]{:S(2)}) %all-to-all-start.6) | async-done | bytes 4194336 | tf_op jit(solution)/shard_map/all_to_all | solution.py:221
  790.6 13.7 %reduce.15 = f32[16,65536]{1,0:T(8,128)} reduce(f32[16,1,65536]{2,1,0:T(1,128)} %all-to-all-done.6, f32[]{:T(128)} %broadcast.219), dimensions={1}, to_apply=%all_to_all.70.reduce_sub_computation | reduce | bytes 8388612 | tf_op jit(solution)/shard_map/all_to_all | solution.py:221
  804.3 6.9 reshape.444
  811.2 13.1 %bitcast_reduce_fusion = bf16[2048,64]{1,0:T(8,128)(2,1)S(1)} fusion(f32[2048,8,64]{2,1,0:T(8,128)} %reshape.444), kind=kLoop, calls=%fused_computation.120 | loop fusion | flops 917504 | bytes 4456448 | tf_op jit(solution)/shard_map/reduce_sum | solution.py:223
  824.4 3.7 fusion.72
  828.2 48.8 %psum.23 = f32[512]{0:T(512)} all-reduce(f32[512]{0:T(512)S(1)} %get-tuple-element.3), channel_id=1, replica_groups=mesh['groups'=2,'seq'=16] {'seq'}, use_global_device_ids=true, to_apply=%region_7.8 | all-reduce | flops 512 | bytes 4096 | tf_op jit(solution)/shard_map/psum | solution.py:230
  877.0 65.7 %all-reduce.12.cloned.1.call-done = (f32[512,1024]{1,0:T(8,128)}, f32[1024,64]{0,1:T(8,128)}) async-done(((f32[512,1024]{1,0:T(8,128)}, f32[1024,64]{0,1:T(8,128)}), (f32[512,1024]{1,0:T(8,128)}, f32[1024,64]{0,1:T(8,128)})) %all-reduce.12.cloned.1.call-update) | async-done | bytes 2359312 | tf_op jit(solution)/shard_map/psum | solution.py:230
  (173 shorter events, 80.7 us)
Async XLA Ops:
  7.2 521.2 %copy-start = (bf16[512,1024]{1,0:T(8,128)(2,1)S(1)}, bf16[512,1024]{1,0:T(8,128)(2,1)}, u32[]{:S(2)}) copy-start(bf16[512,1024]{1,0:T(8,128)(2,1)} %param.26) | copy-start | bytes 3145732
  7.2 4.6 copy-start.34
  7.2 4.6 copy-start.36
  7.2 4.8 copy-start.35
  15.4 4.8 copy-start.27
  15.4 4.8 copy-start.30
  20.3 12.9 %copy-start.37 = (s32[128]{0:T(128)S(1)}, s32[128]{0:T(128)}, u32[]{:S(2)}) copy-start(s32[128]{0:T(128)} %param.18) | copy-start | bytes 1540
  20.3 23.0 %copy-start.33 = (bf16[1024,512]{1,0:T(8,128)(2,1)S(1)}, bf16[1024,512]{1,0:T(8,128)(2,1)}, u32[]{:S(2)}) copy-start(bf16[1024,512]{1,0:T(8,128)(2,1)} %param.19) | copy-start | bytes 3145732
  25.8 14.0 %all-to-all-start.1 = ((bf16[16,2,512]{2,1,0:T(2,128)(2,1)}), bf16[16,2,512]{2,1,0:T(2,128)(2,1)S(1)}, u32[]{:S(2)}, u32[]{:S(2)}) async-start(bf16[16,2,512]{2,1,0:T(2,128)(2,1)} %reshape.437), calls=%async_computation.1 | async-start | bytes 65536 | tf_op jit(solution)/shard_map/all_to_all | solution.py:153
  39.8 14.8 %all-to-all-start.2 = ((bf16[16,2,512]{2,1,0:T(2,128)(2,1)}), bf16[16,2,512]{2,1,0:T(2,128)(2,1)S(1)}, u32[]{:S(2)}, u32[]{:S(2)}) async-start(bf16[16,2,512]{2,1,0:T(2,128)(2,1)} %reshape.439), calls=%async_computation.2 | async-start | bytes 65536 | tf_op jit(solution)/shard_map/all_to_all | solution.py:154
  54.6 47.1 %all-to-all-start.3 = ((bf16[128,128,64]{1,2,0:T(8,128)(2,1)}), bf16[128,128,64]{1,2,0:T(8,128)(2,1)S(1)}, u32[]{:S(2)}, u32[]{:S(2)}) async-start(bf16[128,128,64]{1,2,0:T(8,128)(2,1)} %bitcast.197), calls=%async_computation.3 | async-start | bytes 4194304 | tf_op jit(solution)/shard_map/all_to_all | solution.py:151
  105.8 11.7 %copy-start.38 = (f32[8]{0:T(128)S(1)}, f32[8]{0:T(128)}, u32[]{:S(2)}) copy-start(f32[8]{0:T(128)} %param.23) | copy-start | bytes 100
  105.8 12.0 %copy-start.39 = (f32[8]{0:T(128)S(1)}, f32[8]{0:T(128)}, u32[]{:S(2)}) copy-start(f32[8]{0:T(128)} %param.24) | copy-start | bytes 100
  105.8 89.3 %all-to-all-start = ((bf16[128,128,128]{2,1,0:T(8,128)(2,1)}), bf16[128,128,128]{2,1,0:T(8,128)(2,1)}, u32[]{:S(2)}, u32[]{:S(2)}) async-start(bf16[128,128,128]{2,1,0:T(8,128)(2,1)} %bitcast.189), calls=%async_computation | async-start | bytes 8388608 | tf_op jit(solution)/shard_map/all_to_all | solution.py:152
  119.3 0.6 copy-start.25
  120.0 2.8 copy-start.22
  120.0 2.8 copy-start.21
  125.9 1.9 copy-start.8
  201.5 7.0 copy-start.2
  201.5 7.0 copy-start.5
  208.5 4.3 copy-start.26
  212.0 2.0 copy-start.12
  212.0 1.1 copy-start.23
  212.8 1.2 copy-start.24
  213.1 2.1 copy-start.15
  215.5 6.3 copy-start.17
  221.8 1.0 copy-start.18
  222.7 15.3 %slice-start = ((f32[8,8,1,64,64]{4,3,1,0,2:T(8,128)}), f32[8,1,1,64,64]{4,3,1,0,2:T(8,128)S(1)}, s32[]{:S(2)}) async-start(f32[8,8,1,64,64]{4,3,1,0,2:T(8,128)} %copy-done.15), calls=%async_computation.8 | async-start | bytes 524288 | tf_op jit(solution)/shard_map/slice | solution.py:180
  239.1 20.1 %copy-start.28 = (f32[8,7,1]{1,0,2:T(8,128)S(1)}, f32[8,7,1]{1,0,2:T(8,128)}, u32[]{:S(2)}) copy-start(f32[8,7,1]{1,0,2:T(8,128)} %slice.104) | copy-start | bytes 676
  255.7 3.5 copy-start.13
  259.2 1.9 copy-start.19
  261.1 33.4 %copy-start.16 = (f32[8,8,1,64,64]{4,3,1,0,2:T(8,128)S(1)}, f32[8,8,1,64,64]{4,3,1,0,2:T(8,128)}, u32[]{:S(2)}) copy-start(f32[8,8,1,64,64]{4,3,1,0,2:T(8,128)} %add.159) | copy-start | bytes 3145732
  319.9 2.2 copy-start.3
  322.1 21.4 %copy-start.10 = (f32[8,16,1,64,64]{4,3,1,0,2:T(8,128)}, f32[8,16,1,64,64]{4,3,1,0,2:T(8,128)S(1)}, u32[]{:S(2)}) copy-start(f32[8,16,1,64,64]{4,3,1,0,2:T(8,128)S(1)} %concatenate.15) | copy-start | bytes 6291460
  322.1 21.4 %copy-start.6 = (bf16[8,16,128,128]{2,3,1,0:T(8,128)(2,1)S(1)}, bf16[8,16,128,128]{2,3,1,0:T(8,128)(2,1)}, u32[]{:S(2)}) copy-start(bf16[8,16,128,128]{2,3,1,0:T(8,128)(2,1)} %copy.143) | copy-start | bytes 12582916
  322.1 21.4 %copy-start.9 = (f32[8,16,128,64]{2,3,1,0:T(8,128)S(1)}, f32[8,16,128,64]{2,3,1,0:T(8,128)}, u32[]{:S(2)}) copy-start(f32[8,16,128,64]{2,3,1,0:T(8,128)} %copy-done.8) | copy-start | bytes 12582916
  322.1 21.4 %copy-start.31 = (f32[128]{0:T(128)S(1)}, f32[128]{0:T(128)}, u32[]{:S(2)}) copy-start(f32[128]{0:T(128)} %mul.259) | copy-start | bytes 1540
  515.6 3.4 copy-start.1
  523.0 5.4 copy-start.29
  528.4 6.7 copy-start.14
  645.2 2.2 copy-start.4
  647.4 13.6 %copy-start.7 = (bf16[8,16,128,128]{2,3,1,0:T(8,128)(2,1)S(1)}, bf16[8,16,128,128]{2,3,1,0:T(8,128)(2,1)}, u32[]{:S(2)}) copy-start(bf16[8,16,128,128]{2,3,1,0:T(8,128)(2,1)} %copy.143) | copy-start | bytes 12582916
  661.0 9.4 copy-start.11
  707.5 83.0 %all-to-all-start.6 = ((f32[16,1,65536]{2,1,0:T(1,128)}), f32[16,1,65536]{2,1,0:T(1,128)}, u32[]{:S(2)}, u32[]{:S(2)}) async-start(f32[16,1,65536]{2,1,0:T(1,128)} %reshape.443), calls=%async_computation.6 | async-start | bytes 8388608 | tf_op jit(solution)/shard_map/all_to_all | solution.py:221
  712.9 229.7 %all-reduce.12.cloned.1.call-start = ((), (), s32[]{:S(2)}) async-start(), calls=%async_computation.7 | async-start | bytes 4718592 | tf_op jit(solution)/shard_map/psum | solution.py:230
  713.0 3.4 copy-start.32
  942.7 3.2 copy-start.20
Sparse Core Ops, SparseCore 0:
  828.3 114.2 all-reduce.11
where the time goes:
time: 972 us; the launch traced here: 954 us
  blocking collectives  258 us (27%)
  waiting for transfers between devices  243 us (25%)
  local copies, waits for them, and re-layouts  236 us (24%)
  matrix products  96.4 us (10%)
  other arithmetic  71.3 us (7%)
  starting transfers between devices  33.8 us (3%)
  between operations  15.2 us (2%)
    all_to_all x1, blocking collectives, per_device(): lax.all_to_all(block_out, 'seq', split_axis=1, concat_axis=0, tiled=True)  112 us
    all_to_all x1, blocking collectives, per_device(): lax.all_to_all(grad_pairs, 'seq', split_axis=0, concat_axis=1, tiled=True)  97.4 us
    unnamed x98, local copies, waits for them, and re-layouts  88.6 us
    all_to_all x1, waiting for transfers between devices, per_device(): lax.all_to_all(read_local, 'seq', split_axis=1, concat_axis=0, tiled=True)  70.4 us
    psum x1, waiting for transfers between devices, per_device(): return lax.psum((grad_out, grad_read, grad_gain), 'seq')  65.7 us
    all_to_all x1, waiting for transfers between devices, per_device(): lax.all_to_all(maps_pairs, 'seq', split_axis=0, concat_axis=1, tiled=True)  64.5 us
    psum x1, blocking collectives, per_device(): return lax.psum((grad_out, grad_read, grad_gain), 'seq')  48.8 us
    all_to_all x1, waiting for transfers between devices, per_device(): lax.all_to_all(chan_pairs, 'seq', split_axis=0, concat_axis=1, tiled=True)  36.8 us
  transfers between devices with their start and end apart: 6, of which 5 were waited for; matrix products, arithmetic and copies ran while one was open for 4% of the time, Pallas kernels for 0%

commit v1 on v0

v1 whole, which is shorter than its diff:
```python
import functools
import math

import jax
import jax.numpy as jnp
from jax import lax
from jax.experimental import pallas as pl
from jax.experimental.pallas import tpu as pltpu
from jax.sharding import PartitionSpec as P

f32 = jnp.float32
bf16 = jnp.bfloat16
LOG2E = math.log2(math.e)
LOG_PULSE = math.log(0.7)
NT = (((1,), (1,)), ((), ()))
TN = (((0,), (0,)), ((), ()))


def dot(a, b, dims=(((1,), (0,)), ((), ()))):
    return lax.dot_general(a, b, dims, preferred_element_type=f32)


def split(x, terms):
    parts = []
    for _ in range(terms):
        part = x.astype(bf16)
        parts.append(part)
        x = x - part.astype(f32)
    return parts


def iota(shape, axis):
    return lax.broadcasted_iota(jnp.int32, shape, axis)


def spread_matrix(rows, heads, channels):
    size = channels // heads
    return (iota((rows, channels), 0) % heads == iota((rows, channels), 1) // size).astype(bf16)


def spread(values, sensor, heads, spread2):
    lane = iota(values.shape, 1)
    own = jnp.where(lane // heads == sensor, values, 0.0)
    return dot(jnp.concatenate(split(own, 2), axis=1), spread2)


def front_kernel(
    half_ref, readings, kmix, w_channels, w_state, w_step, bias, rate, marks,
    mixed_ref, channels_ref, maps_ref, step_ref, cum_ref, cum_t_ref, keep_ref, send_ref, tail_ref,
    wms, spread2, state_sc, log_sc, *, heads,
):
    i = pl.program_id(0)
    sensors, chunk, width = readings.shape
    rows = sensors * chunk
    maps = w_state.shape[1]
    nstate = maps // 2
    channels = w_channels.shape[1]
    lanes = sensors * heads

    @pl.when(i == 0)
    def _():
        wms[...] = jnp.zeros_like(wms)
        wms[:, 0:maps] = w_state[...]
        wms[:, maps : maps + heads] = w_step[...]
        spread2[...] = spread_matrix(spread2.shape[0], heads, channels)

    x = readings[...].reshape(rows, width)
    mixed = (x.astype(f32) + dot(kmix[...], x)).astype(bf16)
    mixed_ref[...] = mixed.reshape(sensors, chunk, width)
    here = pl.ds(pl.multiple_of(i * chunk, chunk), chunk)
    channels_ref[:, here, :] = dot(mixed, w_channels[...]).astype(bf16).reshape(sensors, chunk, channels)
    small = dot(mixed, wms[...])
    maps_ref[:, here, :] = small[:, 0:maps].astype(bf16).reshape(sensors, chunk, maps)
    steps = small[:, maps:].reshape(sensors, chunk, lanes)
    packed = steps[0]
    for s in range(1, sensors):
        packed = packed + pltpu.roll(steps[s], heads * s, 1)
    raw = (packed + bias[...]).astype(bf16).astype(f32)
    step = jnp.maximum(raw, 0.0) + jnp.log1p(jnp.exp(-jnp.abs(raw)))
    step_ref[here, :] = step
    log_sc[here, :] = (rate[...] * step + LOG_PULSE * marks[...]) * LOG2E

    @pl.when(i == pl.num_programs(0) - 1)
    def _():
        span = log_sc.shape[0]
        lower = (iota((span, span), 0) >= iota((span, span), 1)).astype(bf16)
        cum = sum(dot(lower, part) for part in split(log_sc[...], 3))
        cum_ref[...] = cum
        cum_t_ref[...] = cum.T
        last = cum[span - 1 : span, :]
        weight = jnp.exp2(last - cum) * step_ref[...]

        def one(s, carry):
            scale = spread(weight, s, heads, spread2[...])
            scaled = (channels_ref[s].astype(f32) * scale).astype(bf16)
            state = dot(maps_ref[s], scaled, TN)
            state_sc[s] = state[0:nstate]
            return carry

        lax.fori_loop(0, sensors, one, 0)
        own = jnp.where(iota((sensors, lanes), 1) // heads == iota((sensors, lanes), 0), last, 0.0)
        tail = sum(dot(part, spread2[0:lanes, :]) for part in split(own, 3))
        tail_ref[...] = tail
        half = sensors // 2
        mine = half_ref[0] * half
        other = half - mine
        keep_ref[...] = state_sc[pl.ds(mine, half)].reshape(half * nstate, channels)
        send_ref[0 : half * nstate, :] = state_sc[pl.ds(other, half)].reshape(half * nstate, channels)
        send_ref[half * nstate :, :] = tail


def pair_blocks(x, size):
    lane = iota(x.shape, 1)
    zero = jnp.zeros_like(x)
    return jnp.concatenate([jnp.where(lane < size, x, zero), jnp.where(lane >= size, x, zero)], axis=0)


def within_kernel(
    channels, maps, step, cum, cum_t, cot, w_out, skip,
    part_ref, scaled_ref, decay_ref, grad_ref, spread2, *, heads,
):
    i = pl.program_id(0)
    group, span, width = channels.shape
    nstate = maps.shape[2] // 2
    size = width // heads

    @pl.when(i == 0)
    def _():
        spread2[...] = spread_matrix(spread2.shape[0], heads, width)

    grad = dot(cot[...].reshape(group * span, cot.shape[2]), w_out[...], NT)
    grad_ref[...] = grad.reshape(group, span, width)
    causal = iota((span, span), 0) >= iota((span, span), 1)
    for k in range(group):
        s = i * group + k
        chan = channels[k].astype(f32)
        scaled = (chan * spread(step[...], s, heads, spread2[...])).astype(bf16)
        scaled_ref[k] = scaled
        both = maps[k]
        scores = dot(both[:, nstate:], both[:, 0:nstate], NT)
        row = cum_t[k * heads : (k + 1) * heads, :]
        col = row.T
        for pair in range(heads // 2):
            weighted = []
            for h in (2 * pair, 2 * pair + 1):
                gap = jnp.broadcast_to(col[:, h : h + 1], (span, span)) - row[h : h + 1, :]
                decay = jnp.exp2(jnp.where(causal, gap, -jnp.inf))
                decay_ref[k, h] = decay.astype(bf16)
                weighted.append((scores * decay).astype(bf16))
            lanes = slice(2 * pair * size, 2 * (pair + 1) * size)
            out = dot(jnp.concatenate(weighted, axis=1), pair_blocks(scaled[:, lanes], size))
            part_ref[k, :, lanes] = out + skip[:, lanes] * chan[:, lanes]


def back_kernel(
    half_ref, state, maps, scaled, decay, part, grad, cum, cot, mixed, gain,
    keep_ref, send_ref, spread2, total, gain_sc, *, heads,
):
    i = pl.program_id(0)
    group, span, width = part.shape
    nstate = maps.shape[2] // 2
    size = width // heads

    @pl.when(i == 0)
    def _():
        spread2[...] = spread_matrix(spread2.shape[0], heads, width)
        total[...] = jnp.zeros_like(total)
        gain_sc[...] = jnp.zeros_like(gain_sc)

    fade = jnp.exp2(cum[...])
    outs = []
    reads = []
    for k in range(group):
        s = i * group + k
        both = maps[k]
        fade_s = spread(fade, s, heads, spread2[...])
        out = part[k] + dot(both[:, nstate:], state[k]) * fade_s
        inv = lax.rsqrt(jnp.mean(out * out, axis=-1, keepdims=True) + 1e-05)
        normed = out * inv
        outs.append((normed * gain[...]).astype(bf16))
        g = grad[k]
        by_gain = normed * g
        gain_sc[...] += jnp.sum(by_gain.reshape(span // 8, 8, width), axis=0)
        mean = jnp.mean(by_gain * gain[...], axis=-1, keepdims=True)
        back = inv * (g * gain[...] - normed * mean)
        back16 = back.astype(bf16)
        carried = dot((back * fade_s).astype(bf16), state[k], NT)
        pairs = jnp.zeros((span, span), f32)
        for pair in range(heads // 2):
            lanes = slice(2 * pair * size, 2 * (pair + 1) * size)
            both_heads = dot(back16[:, lanes], pair_blocks(scaled[k][:, lanes], size), NT)
            pairs = pairs + both_heads[:, 0:span] * decay[k, 2 * pair].astype(f32)
            pairs = pairs + both_heads[:, span:] * decay[k, 2 * pair + 1].astype(f32)
        inner = dot(pairs.astype(bf16), both[:, 0:nstate])
        reads.append((carried + inner).astype(bf16))
    rows = group * span
    normed_out = jnp.concatenate(outs, axis=0)
    read_grad = jnp.concatenate(reads, axis=0)
    total[0:width, :] += dot(normed_out, cot[...].reshape(rows, cot.shape[2]), TN)
    total[width : width + nstate, :] += dot(read_grad, mixed[...].reshape(rows, mixed.shape[2]), TN)

    @pl.when(i == pl.num_programs(0) - 1)
    def _():
        total[width + nstate : width + nstate + 1, 0:width] = jnp.sum(gain_sc[...], axis=0, keepdims=True)
        half = keep_ref.shape[0]
        mine = pl.multiple_of(half_ref[0] * half, 8)
        other = pl.multiple_of(half - half_ref[0] * half, 8)
        keep_ref[...] = total[pl.ds(mine, half), :]
        send_ref[...] = total[pl.ds(other, half), :]


def whole(shape):
    return pl.BlockSpec(shape, lambda *_: (0,) * len(shape), pipeline_mode=pl.Buffered(1))


def swap(x, distance, count):
    return lax.ppermute(x, "seq", [(i, i ^ distance) for i in range(count)])


def narrow(x):
    return lax.reduce_precision(x, 8, 7)


def pick(bit, when_one, when_zero):
    return jnp.where(bit == 1, when_one, when_zero)


def fading(tail, start, states):
    sensors, nstate, width = states.shape
    own = lax.dynamic_slice_in_dim(tail, start, sensors, 0)
    return jnp.exp2(own)[:, None, :]


def exchange(keep, send, tail, me, count, shards):
    sensors, width = tail.shape
    levels = count.bit_length() - 1
    size = sensors // 2
    nstate = keep.shape[0] // size
    own = keep.reshape(size, nstate, width)
    start = (me & 1) * size
    saved = []
    for level in range(shards):
        bit = (me >> level) & 1
        came = swap(send, 1 << level, count)
        rows = size * nstate
        other = came[0:rows].astype(f32).reshape(size, nstate, width)
        if came.dtype == f32:
            other_tail = came[rows:]
        else:
            other_tail = came[rows : rows + sensors].astype(f32) + came[rows + sensors :].astype(f32)
        low, high = pick(bit, other, own), pick(bit, own, other)
        low_tail, high_tail = pick(bit, other_tail, tail), pick(bit, tail, other_tail)
        total = low * fading(high_tail, start, low) + high
        saved.append((low, low_tail, start, bit))
        tail = tail + other_tail
        if level + 1 < shards:
            next_bit = (me >> (level + 1)) & 1
            size //= 2
            own = lax.dynamic_slice_in_dim(total, next_bit * size, size, 0)
            gone = lax.dynamic_slice_in_dim(total, (1 - next_bit) * size, size, 0)
            start = start + next_bit * size
        else:
            own = gone = total
        first = tail.astype(bf16)
        second = (tail - narrow(tail)).astype(bf16)
        send = jnp.concatenate([gone.astype(bf16).reshape(size * nstate, width), first, second], axis=0)
    before = jnp.zeros_like(own)
    before_tail = jnp.zeros_like(tail)
    for level in range(shards, levels):
        bit = (me >> level) & 1
        came = swap(send, 1 << level, count)
        rows = size * nstate
        other = came[0:rows].astype(f32).reshape(size, nstate, width)
        other_tail = came[rows : rows + sensors].astype(f32) + came[rows + sensors :].astype(f32)
        before = pick(bit, other * fading(before_tail, start, other) + before, before)
        before_tail = pick(bit, before_tail + other_tail, before_tail)
        if level + 1 < levels:
            low, high = pick(bit, other, own), pick(bit, own, other)
            own = low * fading(pick(bit, tail, other_tail), start, low) + high
            tail = tail + other_tail
            first = tail.astype(bf16)
            second = (tail - narrow(tail)).astype(bf16)
            send = jnp.concatenate([own.astype(bf16).reshape(rows, width), first, second], axis=0)
    for level in reversed(range(shards)):
        low, low_tail, start, bit = saved[level]
        after = before * fading(low_tail, start, low) + low
        mine, gone = pick(bit, after, before), pick(bit, before, after)
        came = swap(gone.astype(bf16), 1 << level, count).astype(f32)
        before = pick(bit, jnp.concatenate([came, mine], axis=0), jnp.concatenate([mine, came], axis=0))
    return before.astype(bf16)


def all_sum(keep, send, me, count, shards):
    levels = count.bit_length() - 1
    own = keep
    for level in range(shards):
        came = swap(send, 1 << level, count)
        own = own + came.astype(f32)
        if level + 1 < shards:
            bit = (me >> (level + 1)) & 1
            size = own.shape[0] // 2
            send = lax.dynamic_slice_in_dim(own, (1 - bit) * size, size, 0).astype(bf16)
            own = lax.dynamic_slice_in_dim(own, bit * size, size, 0)
    for level in range(shards, levels):
        own = narrow(own)
        own = own + swap(own.astype(bf16), 1 << level, count).astype(f32)
    out = own.astype(bf16)
    for level in reversed(range(shards)):
        bit = (me >> level) & 1
        came = swap(out, 1 << level, count)
        out = pick(bit, jnp.concatenate([came, out], axis=0), jnp.concatenate([out, came], axis=0))
    return out.astype(f32)


def per_device(
    count, readings, block_graph, cluster_of, mix_weight, boundaries, w_channels, w_state, w_step,
    step_bias, channel_fading_exponent, skip_gain, norm_gain, w_out, cotangent,
):
    sensors, span, width = readings.shape
    heads = channel_fading_exponent.shape[0]
    channels = w_channels.shape[1]
    maps = w_state.shape[1]
    nstate = maps // 2
    size = channels // heads
    lanes = sensors * heads
    me = lax.axis_index("seq")
    shards = min(max(count.bit_length() - 2, 1), 3)
    chunk = 16
    rows = sensors * chunk

    onehot = (cluster_of[:, None] == jnp.arange(sensors, dtype=jnp.int32)[None, :]).astype(f32)
    linked = jnp.dot(jnp.dot(onehot, block_graph.astype(f32)), onehot.T)
    coupling = (linked * mix_weight).astype(bf16)
    same = (jnp.arange(rows)[:, None] % chunk == jnp.arange(rows)[None, :] % chunk)
    kmix = jnp.where(same, jnp.repeat(jnp.repeat(coupling, chunk, 0), chunk, 1), 0).astype(bf16)
    bias = jnp.tile(step_bias, sensors)[None, :]
    rate = jnp.tile(-jnp.exp(channel_fading_exponent), sensors)[None, :]
    skip = jnp.repeat(skip_gain, size)[None, :]
    marks = boundaries.astype(f32)[:, None]
    half = (me & 1).astype(jnp.int32)[None]
    half_rows = sensors // 2 * nstate

    mixed, chans, maps_all, step, cum, cum_t, keep, send, tail = pl.pallas_call(
        functools.partial(front_kernel, heads=heads),
        name="front",
        grid_spec=pltpu.PrefetchScalarGridSpec(
            num_scalar_prefetch=1,
            grid=(span // chunk,),
            in_specs=[
                pl.BlockSpec((sensors, chunk, width), lambda i, *_: (0, i, 0)),
                whole((rows, rows)),
                whole((width, channels)),
                whole((width, maps)),
                whole((width, heads)),
                whole((1, lanes)),
                whole((1, lanes)),
                pl.BlockSpec((chunk, 1), lambda i, *_: (i, 0)),
            ],
            out_specs=[
                pl.BlockSpec((sensors, chunk, width), lambda i, *_: (0, i, 0)),
                whole((sensors, span, channels)),
                whole((sensors, span, maps)),
                whole((span, lanes)),
                whole((span, lanes)),
                whole((lanes, span)),
                whole((half_rows, channels)),
                whole((half_rows + sensors, channels)),
                whole((sensors, channels)),
            ],
            scratch_shapes=[
                pltpu.VMEM((width, maps + lanes), bf16),
                pltpu.VMEM((2 * lanes, channels), bf16),
                pltpu.VMEM((sensors, nstate, channels), f32),
                pltpu.VMEM((span, lanes), f32),
            ],
        ),
        out_shape=[
            jax.ShapeDtypeStruct((sensors, span, width), bf16),
            jax.ShapeDtypeStruct((sensors, span, channels), bf16),
            jax.ShapeDtypeStruct((sensors, span, maps), bf16),
            jax.ShapeDtypeStruct((span, lanes), f32),
            jax.ShapeDtypeStruct((span, lanes), f32),
            jax.ShapeDtypeStruct((lanes, span), f32),
            jax.ShapeDtypeStruct((half_rows, channels), f32),
            jax.ShapeDtypeStruct((half_rows + sensors, channels), f32),
            jax.ShapeDtypeStruct((sensors, channels), f32),
        ],
        compiler_params=pltpu.CompilerParams(
            dimension_semantics=("arbitrary",), vmem_limit_bytes=48 << 20
        ),
        cost_estimate=pl.CostEstimate(flops=5 * 10**9, bytes_accessed=14 << 20, transcendentals=0),
    )(half, readings, kmix, w_channels, w_state, w_step, bias, rate, marks)

    group = 2

    def by_sensor(*shape):
        return pl.BlockSpec((group,) + shape, lambda i, *_: (i,) + (0,) * len(shape))

    part, scaled, decay, grad = pl.pallas_call(
        functools.partial(within_kernel, heads=heads),
        name="within",
        grid_spec=pltpu.PrefetchScalarGridSpec(
            num_scalar_prefetch=0,
            grid=(sensors // group,),
            in_specs=[
                by_sensor(span, channels),
                by_sensor(span, maps),
                whole((span, lanes)),
                whole((span, lanes)),
                pl.BlockSpec((group * heads, span), lambda i, *_: (i, 0)),
                by_sensor(span, width),
                whole((channels, width)),
                whole((1, channels)),
            ],
            out_specs=[
                by_sensor(span, channels),
                by_sensor(span, channels),
                by_sensor(heads, span, span),
                by_sensor(span, channels),
            ],
            scratch_shapes=[pltpu.VMEM((2 * lanes, channels), bf16)],
        ),
        out_shape=[
            jax.ShapeDtypeStruct((sensors, span, channels), f32),
            jax.ShapeDtypeStruct((sensors, span, channels), bf16),
            jax.ShapeDtypeStruct((sensors, heads, span, span), bf16),
            jax.ShapeDtypeStruct((sensors, span, channels), f32),
        ],
        compiler_params=pltpu.CompilerParams(
            dimension_semantics=("arbitrary",), vmem_limit_bytes=48 << 20
        ),
        cost_estimate=pl.CostEstimate(flops=5 * 10**9, bytes_accessed=22 << 20, transcendentals=2 << 20),
    )(chans, maps_all, step, cum, cum_t, cotangent, w_out, skip)

    state = exchange(keep, send, tail, me, count, shards)

    total_rows = -(-(channels + nstate + 1) // 64) * 64
    keep_sum, send_sum = pl.pallas_call(
        functools.partial(back_kernel, heads=heads),
        name="back",
        grid_spec=pltpu.PrefetchScalarGridSpec(
            num_scalar_prefetch=1,
            grid=(sensors // group,),
            in_specs=[
                by_sensor(nstate, channels),
                by_sensor(span, maps),
                by_sensor(span, channels),
                by_sensor(heads, span, span),
                by_sensor(span, channels),
                by_sensor(span, channels),
                whole((span, lanes)),
                by_sensor(span, width),
                by_sensor(span, width),
                whole((1, channels)),
            ],
            out_specs=[whole((total_rows // 2, width)), whole((total_rows // 2, width))],
            scratch_shapes=[
                pltpu.VMEM((2 * lanes, channels), bf16),
                pltpu.VMEM((total_rows, width), f32),
                pltpu.VMEM((8, channels), f32),
            ],
        ),
        out_shape=[jax.ShapeDtypeStruct((total_rows // 2, width), f32)] * 2,
        compiler_params=pltpu.CompilerParams(
            dimension_semantics=("arbitrary",), vmem_limit_bytes=48 << 20
        ),
        cost_estimate=pl.CostEstimate(flops=5 * 10**9, bytes_accessed=26 << 20, transcendentals=0),
    )(half, state, maps_all, scaled, decay, part, grad, cum, cotangent, mixed, norm_gain[None, :])

    sums = all_sum(keep_sum, send_sum, me, count, shards)
    return (
        sums[0:channels],
        sums[channels : channels + nstate].T,
        sums[channels + nstate, 0:channels],
    )


def solution(mesh):
    in_specs = (
        P("groups", "seq", None), P("groups", None), P("groups"), P(), P(("groups", "seq")),
        P(), P(), P(), P(), P(), P(), P(), P(), P("groups", "seq", None),
    )
    out_specs = (P("groups", None), P("groups", None), P("groups"))
    return jax.shard_map(
        functools.partial(per_device, mesh.shape["seq"]),
        mesh=mesh, in_specs=in_specs, out_specs=out_specs, check_vma=False,
    )
```

time: 972 us -> 157 us (0.16); the launches traced: 954 us -> 156 us
  blocking collectives: 258 us -> 0 us
  local copies, waits for them, and re-layouts: 236 us -> 11.2 us
  waiting for transfers between devices: 243 us -> 68.8 us
  matrix products: 96.4 us -> 1.05 us
  other arithmetic: 71.3 us -> 14.9 us
  Pallas kernels: 0 us -> 44.4 us
  starting transfers between devices: 33.8 us -> 14.4 us
  between operations: 15.2 us -> 0.97 us
    all_to_all x2 -> x0, blocking collectives: 209 us -> none  [the longest x1 112 us: per_device(): lax.all_to_all(block_out, 'seq', split_axis=1, concat_axis=0, tiled=True)]
    all_to_all x5 -> x0, waiting for transfers between devices: 177 us -> none  [the longest x1 70.4 us: per_device(): lax.all_to_all(read_local, 'seq', split_axis=1, concat_axis=0, tiled=True)]
    dot_general x18 -> x1, matrix products: 96.4 us -> 1.05 us  [per_device(): linked = jnp.dot(jnp.dot(onehot, block_graph.astype(f32)), onehot.T)]
    unnamed x98 -> x17, local copies, waits for them, and re-layouts: 88.6 us -> 3.99 us
    ppermute x0 -> x14, waiting for transfers between devices: none -> 68.8 us  [swap(): return lax.ppermute(x, 'seq', [(i, i ^ distance) for i in range(count)])]
    psum x1 -> x0, waiting for transfers between devices: 65.7 us -> none  [per_device(): return lax.psum((grad_out, grad_read, grad_gain), 'seq')]
    psum x1 -> x0, blocking collectives: 48.8 us -> none  [per_device(): return lax.psum((grad_out, grad_read, grad_gain), 'seq')]
    pallas_call x0 -> x3, Pallas kernels: none -> 44.4 us  [the longest x1 17.2 us: per_device(): pl.pallas_call(functools.partial(front_kernel, heads=heads), name='front'...]
  transfers between devices with their start and end apart: 6 -> 14, of which waited for: 5 -> 13; matrix products, arithmetic and copies ran while one was open for 4% -> 0% of each run, Pallas kernels for 0% -> 7%
where the time goes in v1:
time: 157 us; the launch traced here: 156 us
  waiting for transfers between devices  68.8 us (44%)
  Pallas kernels  44.4 us (28%)
  other arithmetic  14.9 us (9%)
  starting transfers between devices  14.4 us (9%)
  local copies, waits for them, and re-layouts  11.2 us (7%)
    ppermute x14, waiting for transfers between devices, swap(): return lax.ppermute(x, 'seq', [(i, i ^ distance) for i in range(count)])  68.8 us
    pallas_call x1, Pallas kernels, per_device(): pl.pallas_call(functools.partial(front_kernel, heads=heads), name='front'...  17.2 us
    pallas_call x1, Pallas kernels, per_device(): pl.pallas_call(functools.partial(back_kernel, heads=heads), name='back',...  15.8 us
    ppermute x14, starting transfers between devices, swap(): return lax.ppermute(x, 'seq', [(i, i ^ distance) for i in range(count)])  14.4 us
    pallas_call x1, Pallas kernels, per_device(): pl.pallas_call(functools.partial(within_kernel, heads=heads), name='withi...  11.4 us
    select_n x7, other arithmetic, pick(): return jnp.where(bit == 1, when_one, when_zero)  4.09 us
    unnamed x17, local copies, waits for them, and re-layouts  3.99 us
  transfers between devices with their start and end apart: 14, of which 13 were waited for; matrix products, arithmetic and copies ran while one was open for 0% of the time, Pallas kernels for 7%

profile of v1, /device:TPU:0, one launch (start us, length us, event | category | flops | bytes accessed | tf_op | source)
XLA Modules:
  0.0 155.7 jit_solution(4442048888872122925)
XLA Ops:
  0.7 0.7 convert_bitcast_fusion
  1.4 0.7 exponential_negate_fusion
  2.0 1.1 fusion.4
  3.2 0.7 tile.4
  4.5 0.9 copy.21.w_step
  5.5 1.2 copy-done.2
  6.7 17.2 %front.1 = (bf16[16,128,1024]{2,1,0:T(8,128)(2,1)}, bf16[16,128,512]{2,1,0:T(8,128)(2,1)}, bf16[16,128,128]{2,1,0:T(8,128)(2,1)S(1)}, f32[128,128]{1,0:T(8,128)S...) custom-call(s32[1]{0:T(128)} %bitcast.half_ref, ...), custom_call_target="tpu_custom_call" | custom-call | flops 5000000000 | bytes 14680064 | tf_op jit(solution)/shard_map/front/pallas_call | solution.py:343
  24.3 2.5 %collective-permute-done = f32[528,512]{1,0:T(8,128)} collective-permute-done((f32[528,512]{1,0:T(8,128)S(1)}, f32[528,512]{1,0:T(8,128)}, u32[]{:S(2)}, u32[]{:S(2)}) %collective-permute-start) | collective-permute-done | bytes 1081376 | tf_op jit(solution)/shard_map/ppermute | solution.py:217
  26.8 0.8 fusion.24
  27.6 1.5 slice_select_fusion
  29.4 2.9 %collective-permute-start.1 = (bf16[288,512]{1,0:T(8,128)(2,1)S(1)}, bf16[288,512]{1,0:T(8,128)(2,1)}, u32[]{:S(2)}, u32[]{:S(2)}) collective-permute-start(bf16[288,512]{1,0:T(8,128)(2,1)S(1)} %pad_maximum_fusion), channel_id=1, source_target_pairs={{0,2},{1,3},{2,0},{3,1},{4,6},{5,7},{6,4},{7,5},{8,10},{9,11},{10,... | collective-permute-start | bytes 884744 | tf_op jit(solution)/shard_map/ppermute | solution.py:217
  32.3 7.4 %collective-permute-done.1 = bf16[288,512]{1,0:T(8,128)(2,1)} collective-permute-done((bf16[288,512]{1,0:T(8,128)(2,1)S(1)}, bf16[288,512]{1,0:T(8,128)(2,1)}, u32[]{:S(2)}, u32[]{:S(2)}) %collective-permute-start.1) | collective-permute-done | bytes 294944 | tf_op jit(solution)/shard_map/ppermute | solution.py:217
  39.7 0.7 fusion.22
  40.5 1.0 slice.50
  41.5 0.9 fusion.8
  42.4 1.0 dynamic-slice_convert_fusion.3
  43.4 1.9 %collective-permute-start.2 = (bf16[160,512]{1,0:T(8,128)(2,1)S(1)}, bf16[160,512]{1,0:T(8,128)(2,1)}, u32[]{:S(2)}, u32[]{:S(2)}) collective-permute-start(bf16[160,512]{1,0:T(8,128)(2,1)S(1)} %pad_maximum_fusion.1), channel_id=1, source_target_pairs={{0,4},{1,5},{2,6},{3,7},{4,0},{5,1},{6,2},{7,3},{8,12},{9,13},{10,... | collective-permute-start | bytes 491528 | tf_op jit(solution)/shard_map/ppermute | solution.py:217
  45.3 4.0 %collective-permute-done.2 = bf16[160,512]{1,0:T(8,128)(2,1)} collective-permute-done((bf16[160,512]{1,0:T(8,128)(2,1)S(1)}, bf16[160,512]{1,0:T(8,128)(2,1)}, u32[]{:S(2)}, u32[]{:S(2)}) %collective-permute-start.2) | collective-permute-done | bytes 163872 | tf_op jit(solution)/shard_map/ppermute | solution.py:217
  49.3 0.7 add_convert_fusion.1
  50.1 0.9 slice.53
  51.0 1.0 fusion.11
  52.0 0.7 pad_maximum_fusion.2
  52.7 2.5 %collective-permute-start.3 = (bf16[160,512]{1,0:T(8,128)(2,1)}, bf16[160,512]{1,0:T(8,128)(2,1)S(1)}, u32[]{:S(2)}, u32[]{:S(2)}) collective-permute-start(bf16[160,512]{1,0:T(8,128)(2,1)} %pad_maximum_fusion.2), channel_id=1, source_target_pairs={{0,8},{1,9},{2,10},{3,11},{4,12},{5,13},{6,14},{7,15},{8,0},{9,1},... | collective-permute-start | bytes 491528 | tf_op jit(solution)/shard_map/ppermute | solution.py:217
  55.2 6.9 %collective-permute-done.3 = bf16[160,512]{1,0:T(8,128)(2,1)S(1)} collective-permute-done((bf16[160,512]{1,0:T(8,128)(2,1)}, bf16[160,512]{1,0:T(8,128)(2,1)S(1)}, u32[]{:S(2)}, u32[]{:S(2)}) %collective-permute-start.3) | collective-permute-done | bytes 163872 | tf_op jit(solution)/shard_map/ppermute | solution.py:217
  62.2 1.0 fusion.12
  63.7 4.6 %collective-permute-done.4 = bf16[2,64,512]{2,1,0:T(8,128)(2,1)S(1)} collective-permute-done((bf16[2,64,512]{2,1,0:T(8,128)(2,1)S(1)}, bf16[2,64,512]{2,1,0:T(8,128)(2,1)S(1)}, u32[]{:S(2)}, u32[]{:S(2)}) %collective-permute-start.4) | collective-permute-done | bytes 131104 | tf_op jit(solution)/shard_map/ppermute | solution.py:217
  68.3 1.0 fusion.9
  69.3 1.1 collective-permute-start.5
  70.6 5.4 %collective-permute-done.5 = bf16[4,64,512]{2,1,0:T(8,128)(2,1)S(1)} collective-permute-done((bf16[4,64,512]{2,1,0:T(8,128)(2,1)}, bf16[4,64,512]{2,1,0:T(8,128)(2,1)S(1)}, u32[]{:S(2)}, u32[]{:S(2)}) %collective-permute-start.5) | collective-permute-done | bytes 262176 | tf_op jit(solution)/shard_map/ppermute | solution.py:217
  76.0 1.7 %select_convert_fusion = bf16[8,64,512]{2,1,0:T(8,128)(2,1)S(1)} fusion(f32[8,64,512]{2,1,0:T(8,128)S(1)} %bitcast.22, f32[4,64,512]{2,1,0:T(8,128)S(1)} %convert_element_type.121, f32[4,64,512]{2,1,0:T(8,128)} %get-tuple-element.39, f32[8,512]{1,0:T(8,128)S(1)} %get-tuple-element.48, pred[]{:T(512)S(6)} %eq.25, pred[]{:T(512)S(6)} %eq.24), kind=kLoop, calls=%fused_computation.8 | loop fusion | flops 1835008 | bytes 2637826 | tf_op jit(solution)/shard_map/convert_element_type | solution.py:288
  78.1 11.4 %within.1 = (f32[16,128,512]{2,1,0:T(8,128)}, bf16[16,128,512]{2,1,0:T(8,128)(2,1)S(1)}, bf16[16,8,128,128]{3,2,1,0:T(8,128)(2,1)}, f32[16,128,512]{2,1,0:T(8,128)}) custom-call(bf16[16,128,512]{2,1,0:T(8,128)(2,1)S(1)} %copy-done.5, bf16[16,128,128]{2,1,0:T(8,128)(2,1)S(1)} %get-tuple-element.21.maps, f32[128,128]{1,0:T(8,128)S(1)} %get-tuple-element.23.step, ...), custom_call_target="tpu_custom_call" | custom-call | flops 5000000000 | bytes 23068672 | tf_op jit(solution)/shard_map/within/pallas_call | solution.py:399
  89.8 1.0 copy-done
  91.0 0.5 copy-done.1
  91.5 15.8 %back.1 = (f32[320,1024]{1,0:T(8,128)S(1)}, f32[320,1024]{1,0:T(8,128)S(1)}) custom-call(s32[1]{0:T(128)} %bitcast.half_ref, bf16[16,64,512]{2,1,0:T(8,128)(2,1)S(1)} %fusion.state, bf16[16,128,128]{2,1,0:T(8,128)(2,1)S(1)} %get-tuple-element.21.maps, bf16[16,128,512]{2,1,0:T(8,128)(2,1)} %copy-done, bf16[16,8,128,128]{3,2,1,0:T(8,128)(2,1)} %get-tuple-element.27.decay, ...), custom_call_target="tpu_custom_call" | custom-call | flops 5000000000 | bytes 27262976 | tf_op jit(solution)/shard_map/back/pallas_call | solution.py:438
  107.6 3.0 %collective-permute-done.7 = f32[320,1024]{1,0:T(8,128)} collective-permute-done((f32[320,1024]{1,0:T(8,128)S(1)}, f32[320,1024]{1,0:T(8,128)}, u32[]{:S(2)}, u32[]{:S(2)}) %collective-permute-start.7) | collective-permute-done | bytes 1310752 | tf_op jit(solution)/shard_map/ppermute | solution.py:217
  110.6 1.5 add.128
  112.1 1.1 collective-permute-start.8
  113.3 8.8 %collective-permute-done.8 = bf16[160,1024]{1,0:T(8,128)(2,1)S(1)} collective-permute-done((bf16[160,1024]{1,0:T(8,128)(2,1)S(1)}, bf16[160,1024]{1,0:T(8,128)(2,1)S(1)}, u32[]{:S(2)}, u32[]{:S(2)}) %collective-permute-start.8) | collective-permute-done | bytes 327712 | tf_op jit(solution)/shard_map/ppermute | solution.py:217
  122.6 5.1 %collective-permute-done.9 = bf16[80,1024]{1,0:T(8,128)(2,1)S(1)} collective-permute-done((bf16[80,1024]{1,0:T(8,128)(2,1)S(1)}, bf16[80,1024]{1,0:T(8,128)(2,1)S(1)}, u32[]{:S(2)}, u32[]{:S(2)}) %collective-permute-start.9) | collective-permute-done | bytes 163872 | tf_op jit(solution)/shard_map/ppermute | solution.py:217
  127.7 1.9 %collective-permute-start.10 = (bf16[80,1024]{1,0:T(8,128)(2,1)S(1)}, bf16[80,1024]{1,0:T(8,128)(2,1)S(1)}, u32[]{:S(2)}, u32[]{:S(2)}) collective-permute-start(bf16[80,1024]{1,0:T(8,128)(2,1)S(1)} %fusion.13), channel_id=1, source_target_pairs={{0,8},{1,9},{2,10},{3,11},{4,12},{5,13},{6,14},{7,15},{8,0},{9,1},... | collective-permute-start | bytes 491528 | tf_op jit(solution)/shard_map/ppermute | solution.py:217
  129.7 7.1 %collective-permute-done.10 = bf16[80,1024]{1,0:T(8,128)(2,1)S(1)} collective-permute-done((bf16[80,1024]{1,0:T(8,128)(2,1)S(1)}, bf16[80,1024]{1,0:T(8,128)(2,1)S(1)}, u32[]{:S(2)}, u32[]{:S(2)}) %collective-permute-start.10) | collective-permute-done | bytes 163872 | tf_op jit(solution)/shard_map/ppermute | solution.py:217
  137.0 5.2 %collective-permute-done.11 = bf16[80,1024]{1,0:T(8,128)(2,1)S(1)} collective-permute-done((bf16[80,1024]{1,0:T(8,128)(2,1)S(1)}, bf16[80,1024]{1,0:T(8,128)(2,1)S(1)}, u32[]{:S(2)}, u32[]{:S(2)}) %collective-permute-start.11) | collective-permute-done | bytes 163872 | tf_op jit(solution)/shard_map/ppermute | solution.py:217
  142.3 1.1 collective-permute-start.12
  143.4 6.7 %collective-permute-done.12 = bf16[160,1024]{1,0:T(8,128)(2,1)S(1)} collective-permute-done((bf16[160,1024]{1,0:T(8,128)(2,1)S(1)}, bf16[160,1024]{1,0:T(8,128)(2,1)S(1)}, u32[]{:S(2)}, u32[]{:S(2)}) %collective-permute-start.12) | collective-permute-done | bytes 327712 | tf_op jit(solution)/shard_map/ppermute | solution.py:217
  150.4 2.1 %collective-permute-done.13 = bf16[320,1024]{1,0:T(8,128)(2,1)S(1)} collective-permute-done((bf16[320,1024]{1,0:T(8,128)(2,1)S(1)}, bf16[320,1024]{1,0:T(8,128)(2,1)S(1)}, u32[]{:S(2)}, u32[]{:S(2)}) %collective-permute-start.13) | collective-permute-done | bytes 655392 | tf_op jit(solution)/shard_map/ppermute | solution.py:217
  153.0 0.6 slice.59
  153.5 0.7 slice_bitcast_fusion
  154.3 1.5 slice.57
  (56 shorter events, 5.2 us)
Async XLA Ops:
  0.6 4.8 %copy-start.4 = (bf16[1024,128]{1,0:T(8,128)(2,1)S(1)}, bf16[1024,128]{1,0:T(8,128)(2,1)}, u32[]{:S(2)}) copy-start(bf16[1024,128]{1,0:T(8,128)(2,1)} %w_state.1) | copy-start | bytes 786436
  5.5 1.2 copy-start.2
  23.9 2.9 %collective-permute-start = (f32[528,512]{1,0:T(8,128)S(1)}, f32[528,512]{1,0:T(8,128)}, u32[]{:S(2)}, u32[]{:S(2)}) collective-permute-start(f32[528,512]{1,0:T(8,128)S(1)} %get-tuple-element.18), channel_id=1, source_target_pairs={{0,1},{1,0},{2,3},{3,2},{4,5},{5,4},{6,7},{7,6},{8,9},{9,8},{10,11... | collective-permute-start | bytes 3244040 | tf_op jit(solution)/shard_map/ppermute | solution.py:217
  29.4 10.3 %collective-permute-start.1 = (bf16[288,512]{1,0:T(8,128)(2,1)S(1)}, bf16[288,512]{1,0:T(8,128)(2,1)}, u32[]{:S(2)}, u32[]{:S(2)}) collective-permute-start(bf16[288,512]{1,0:T(8,128)(2,1)S(1)} %pad_maximum_fusion), channel_id=1, source_target_pairs={{0,2},{1,3},{2,0},{3,1},{4,6},{5,7},{6,4},{7,5},{8,10},{9,11},{10,... | collective-permute-start | bytes 884744 | tf_op jit(solution)/shard_map/ppermute | solution.py:217
  43.4 5.9 %collective-permute-start.2 = (bf16[160,512]{1,0:T(8,128)(2,1)S(1)}, bf16[160,512]{1,0:T(8,128)(2,1)}, u32[]{:S(2)}, u32[]{:S(2)}) collective-permute-start(bf16[160,512]{1,0:T(8,128)(2,1)S(1)} %pad_maximum_fusion.1), channel_id=1, source_target_pairs={{0,4},{1,5},{2,6},{3,7},{4,0},{5,1},{6,2},{7,3},{8,12},{9,13},{10,... | collective-permute-start | bytes 491528 | tf_op jit(solution)/shard_map/ppermute | solution.py:217
  52.7 9.5 %collective-permute-start.3 = (bf16[160,512]{1,0:T(8,128)(2,1)}, bf16[160,512]{1,0:T(8,128)(2,1)S(1)}, u32[]{:S(2)}, u32[]{:S(2)}) collective-permute-start(bf16[160,512]{1,0:T(8,128)(2,1)} %pad_maximum_fusion.2), channel_id=1, source_target_pairs={{0,8},{1,9},{2,10},{3,11},{4,12},{5,13},{6,14},{7,15},{8,0},{9,1},... | collective-permute-start | bytes 491528 | tf_op jit(solution)/shard_map/ppermute | solution.py:217
  63.2 7.2 %copy-start.7 = (f32[8]{0:T(128)S(1)}, f32[8]{0:T(128)}, u32[]{:S(2)}) copy-start(f32[8]{0:T(128)} %param.24) | copy-start | bytes 100
  63.2 5.0 %collective-permute-start.4 = (bf16[2,64,512]{2,1,0:T(8,128)(2,1)S(1)}, bf16[2,64,512]{2,1,0:T(8,128)(2,1)S(1)}, u32[]{:S(2)}, u32[]{:S(2)}) collective-permute-start(bf16[2,64,512]{2,1,0:T(8,128)(2,1)S(1)} %get-tuple-element.43), channel_id=1, source_target_pairs={{0,4},{1,5},{2,6},{3,7},{4,0},{5,1},{6,2},{7,3},{8,12},{9,13},{10,... | collective-permute-start | bytes 393224 | tf_op jit(solution)/shard_map/ppermute | solution.py:217
  69.3 6.6 %collective-permute-start.5 = (bf16[4,64,512]{2,1,0:T(8,128)(2,1)}, bf16[4,64,512]{2,1,0:T(8,128)(2,1)S(1)}, u32[]{:S(2)}, u32[]{:S(2)}) collective-permute-start(bf16[4,64,512]{2,1,0:T(8,128)(2,1)} %get-tuple-element.40), channel_id=1, source_target_pairs={{0,2},{1,3},{2,0},{3,1},{4,6},{5,7},{6,4},{7,5},{8,10},{9,11},{10,... | collective-permute-start | bytes 786440 | tf_op jit(solution)/shard_map/ppermute | solution.py:217
  76.0 1.9 %copy-start.5 = (bf16[16,128,512]{2,1,0:T(8,128)(2,1)S(1)}, bf16[16,128,512]{2,1,0:T(8,128)(2,1)}, u32[]{:S(2)}) copy-start(bf16[16,128,512]{2,1,0:T(8,128)(2,1)} %get-tuple-element.22.channels) | copy-start | bytes 6291460
  76.0 2.1 %copy-start.3 = (bf16[512,1024]{1,0:T(8,128)(2,1)S(1)}, bf16[512,1024]{1,0:T(8,128)(2,1)}, u32[]{:S(2)}) copy-start(bf16[512,1024]{1,0:T(8,128)(2,1)} %w_out.1) | copy-start | bytes 3145732
  77.7 13.1 %collective-permute-start.6 = (bf16[8,64,512]{2,1,0:T(8,128)(2,1)S(1)}, bf16[8,64,512]{2,1,0:T(8,128)(2,1)S(1)}, u32[]{:S(2)}, u32[]{:S(2)}) collective-permute-start(bf16[8,64,512]{2,1,0:T(8,128)(2,1)S(1)} %select_convert_fusion), channel_id=1, source_target_pairs={{0,1},{1,0},{2,3},{3,2},{4,5},{5,4},{6,7},{7,6},{8,9},{9,8},{10,11... | collective-permute-start | bytes 1572872 | tf_op jit(solution)/shard_map/ppermute | solution.py:217
  78.1 11.4 %copy-start.6 = (f32[4,64,512]{2,1,0:T(8,128)S(1)}, f32[4,64,512]{2,1,0:T(8,128)}, u32[]{:S(2)}) copy-start(f32[4,64,512]{2,1,0:T(8,128)} %get-tuple-element.39) | copy-start | bytes 1572868
  89.5 1.3 copy-start
  90.8 0.7 copy-start.1
  107.3 3.2 %collective-permute-start.7 = (f32[320,1024]{1,0:T(8,128)S(1)}, f32[320,1024]{1,0:T(8,128)}, u32[]{:S(2)}, u32[]{:S(2)}) collective-permute-start(f32[320,1024]{1,0:T(8,128)S(1)} %get-tuple-element.32), channel_id=1, source_target_pairs={{0,1},{1,0},{2,3},{3,2},{4,5},{5,4},{6,7},{7,6},{8,9},{9,8},{10,11... | collective-permute-start | bytes 3932168 | tf_op jit(solution)/shard_map/ppermute | solution.py:217
  112.1 9.9 %collective-permute-start.8 = (bf16[160,1024]{1,0:T(8,128)(2,1)S(1)}, bf16[160,1024]{1,0:T(8,128)(2,1)S(1)}, u32[]{:S(2)}, u32[]{:S(2)}) collective-permute-start(bf16[160,1024]{1,0:T(8,128)(2,1)S(1)} %dynamic-slice_convert_fusion), channel_id=1, source_target_pairs={{0,2},{1,3},{2,0},{3,1},{4,6},{5,7},{6,4},{7,5},{8,10},{9,11},{10,... | collective-permute-start | bytes 983048 | tf_op jit(solution)/shard_map/ppermute | solution.py:217
  122.1 5.5 %collective-permute-start.9 = (bf16[80,1024]{1,0:T(8,128)(2,1)S(1)}, bf16[80,1024]{1,0:T(8,128)(2,1)S(1)}, u32[]{:S(2)}, u32[]{:S(2)}) collective-permute-start(bf16[80,1024]{1,0:T(8,128)(2,1)S(1)} %dynamic-slice_convert_fusion.2), channel_id=1, source_target_pairs={{0,4},{1,5},{2,6},{3,7},{4,0},{5,1},{6,2},{7,3},{8,12},{9,13},{10,... | collective-permute-start | bytes 491528 | tf_op jit(solution)/shard_map/ppermute | solution.py:217
  127.7 9.0 %collective-permute-start.10 = (bf16[80,1024]{1,0:T(8,128)(2,1)S(1)}, bf16[80,1024]{1,0:T(8,128)(2,1)S(1)}, u32[]{:S(2)}, u32[]{:S(2)}) collective-permute-start(bf16[80,1024]{1,0:T(8,128)(2,1)S(1)} %fusion.13), channel_id=1, source_target_pairs={{0,8},{1,9},{2,10},{3,11},{4,12},{5,13},{6,14},{7,15},{8,0},{9,1},... | collective-permute-start | bytes 491528 | tf_op jit(solution)/shard_map/ppermute | solution.py:217
  136.8 5.4 %collective-permute-start.11 = (bf16[80,1024]{1,0:T(8,128)(2,1)S(1)}, bf16[80,1024]{1,0:T(8,128)(2,1)S(1)}, u32[]{:S(2)}, u32[]{:S(2)}) collective-permute-start(bf16[80,1024]{1,0:T(8,128)(2,1)S(1)} %add_convert_fusion), channel_id=1, source_target_pairs={{0,4},{1,5},{2,6},{3,7},{4,0},{5,1},{6,2},{7,3},{8,12},{9,13},{10,... | collective-permute-start | bytes 491528 | tf_op jit(solution)/shard_map/ppermute | solution.py:217
  142.3 7.7 %collective-permute-start.12 = (bf16[160,1024]{1,0:T(8,128)(2,1)S(1)}, bf16[160,1024]{1,0:T(8,128)(2,1)S(1)}, u32[]{:S(2)}, u32[]{:S(2)}) collective-permute-start(bf16[160,1024]{1,0:T(8,128)(2,1)S(1)} %maximum_select_fusion.5), channel_id=1, source_target_pairs={{0,2},{1,3},{2,0},{3,1},{4,6},{5,7},{6,4},{7,5},{8,10},{9,11},{10,... | collective-permute-start | bytes 983048 | tf_op jit(solution)/shard_map/ppermute | solution.py:217
  150.3 2.2 %collective-permute-start.13 = (bf16[320,1024]{1,0:T(8,128)(2,1)S(1)}, bf16[320,1024]{1,0:T(8,128)(2,1)S(1)}, u32[]{:S(2)}, u32[]{:S(2)}) collective-permute-start(bf16[320,1024]{1,0:T(8,128)(2,1)S(1)} %maximum_select_fusion.3), channel_id=1, source_target_pairs={{0,1},{1,0},{2,3},{3,2},{4,5},{5,4},{6,7},{7,6},{8,9},{9,8},{10,11... | collective-permute-start | bytes 1966088 | tf_op jit(solution)/shard_map/ppermute | solution.py:217

commit v2 on v1

v2 whole, which is shorter than its diff:
```python
import functools
import math

import jax
import jax.numpy as jnp
from jax import lax
from jax.experimental import pallas as pl
from jax.experimental.pallas import tpu as pltpu
from jax.sharding import PartitionSpec as P

f32 = jnp.float32
bf16 = jnp.bfloat16
LOG2E = math.log2(math.e)
LOG_PULSE = math.log(0.7)
NT = (((1,), (1,)), ((), ()))
TN = (((0,), (0,)), ((), ()))


def dot(a, b, dims=(((1,), (0,)), ((), ()))):
    return lax.dot_general(a, b, dims, preferred_element_type=f32)


def split(x, terms):
    parts = []
    for _ in range(terms):
        part = x.astype(bf16)
        parts.append(part)
        x = x - part.astype(f32)
    return parts


def iota(shape, axis):
    return lax.broadcasted_iota(jnp.int32, shape, axis)


def spread_matrix(rows, heads, channels):
    size = channels // heads
    return (iota((rows, channels), 0) % heads == iota((rows, channels), 1) // size).astype(bf16)


def spread(values, sensor, heads, spread2):
    lane = iota(values.shape, 1)
    own = jnp.where(lane // heads == sensor, values, 0.0)
    return dot(jnp.concatenate(split(own, 2), axis=1), spread2)


def front_kernel(
    half_ref, readings, graph, cluster, mix, marks, w_channels, w_state, w_step_t, bias, fading_exponent,
    mixed_ref, channels_ref, maps_ref, step_ref, cum_ref, cum_t_ref, keep_ref, send_ref, tail_ref, token_ref,
    kmix, wms, spread2, rows_sc, state_sc, log_sc, *, heads,
):
    i = pl.program_id(0)
    sensors, chunk, width = readings.shape
    rows = sensors * chunk
    maps = w_state.shape[1]
    nstate = maps // 2
    channels = w_channels.shape[1]
    lanes = sensors * heads

    @pl.when(i == 0)
    def _():
        token_ref[...] = jnp.zeros_like(token_ref)
        wms[...] = jnp.zeros_like(wms)
        wms[:, 0:maps] = w_state[...]
        wms[:, maps : maps + heads] = w_step_t[...].astype(f32).T.astype(bf16)
        spread2[...] = spread_matrix(spread2.shape[0], heads, channels)
        picked = (iota((sensors, sensors), 0) == cluster[...]).astype(bf16)
        linked = dot(dot(picked, graph[...].astype(f32).astype(bf16), TN).astype(bf16), picked)
        coupling = (linked * mix[...]).astype(bf16)
        sensor_of = (iota((rows, sensors), 0) // chunk == iota((rows, sensors), 1)).astype(bf16)
        full = dot(dot(sensor_of, coupling).astype(bf16), sensor_of, NT)
        same = iota((rows, rows), 0) % chunk == iota((rows, rows), 1) % chunk
        kmix[...] = jnp.where(same, full, 0.0).astype(bf16)
        tiled = (iota((heads, lanes), 1) % heads == iota((heads, lanes), 0)).astype(bf16)
        both = jnp.concatenate([bias[...], -jnp.exp(fading_exponent[...]) * LOG2E], axis=0)
        rows_sc[0:2, :] = sum(dot(part, tiled) for part in split(both, 3))

    x = readings[...].reshape(rows, width)
    mixed = (x.astype(f32) + dot(kmix[...], x)).astype(bf16)
    mixed_ref[...] = mixed.reshape(sensors, chunk, width)
    here = pl.ds(pl.multiple_of(i * chunk, chunk), chunk)
    channels_ref[:, here, :] = dot(mixed, w_channels[...]).astype(bf16).reshape(sensors, chunk, channels)
    small = dot(mixed, wms[...])
    maps_ref[:, here, :] = small[:, 0:maps].astype(bf16).reshape(sensors, chunk, maps)
    steps = small[:, maps:].reshape(sensors, chunk, lanes)
    packed = steps[0]
    for s in range(1, sensors):
        packed = packed + pltpu.roll(steps[s], heads * s, 1)
    raw = (packed + rows_sc[0:1, :]).astype(bf16).astype(f32)
    step = jnp.maximum(raw, 0.0) + jnp.log1p(jnp.exp(-jnp.abs(raw)))
    step_ref[here, :] = step
    log_sc[here, :] = rows_sc[1:2, :] * step

    @pl.when(i == pl.num_programs(0) - 1)
    def _():
        span = log_sc.shape[0]
        at, to = iota((span, span), 0), iota((span, span), 1)
        marked = jnp.sum(jnp.where(at == to, marks[...].astype(f32), 0.0), axis=1, keepdims=True)
        log_decay = log_sc[...] + (LOG_PULSE * LOG2E) * marked
        lower = (at >= to).astype(bf16)
        cum = sum(dot(lower, part) for part in split(log_decay, 3))
        cum_ref[...] = cum
        cum_t_ref[...] = cum.T
        last = cum[span - 1 : span, :]
        weight = jnp.exp2(last - cum) * step_ref[...]

        def one(s, carry):
            scale = spread(weight, s, heads, spread2[...])
            scaled = (channels_ref[s].astype(f32) * scale).astype(bf16)
            state = dot(maps_ref[s], scaled, TN)
            state_sc[s] = state[0:nstate]
            return carry

        lax.fori_loop(0, sensors, one, 0)
        own = jnp.where(iota((sensors, lanes), 1) // heads == iota((sensors, lanes), 0), last, 0.0)
        tail = sum(dot(part, spread2[0:lanes, :]) for part in split(own, 3))
        tail_ref[...] = tail
        half = sensors // 2
        mine = half_ref[0] * half
        other = half - mine
        keep_ref[...] = state_sc[pl.ds(mine, half)].reshape(half * nstate, channels)
        send_ref[0 : half * nstate, :] = state_sc[pl.ds(other, half)].reshape(half * nstate, channels)
        send_ref[half * nstate :, :] = tail


def pair_blocks(x, size):
    lane = iota(x.shape, 1)
    zero = jnp.zeros_like(x)
    return jnp.concatenate([jnp.where(lane < size, x, zero), jnp.where(lane >= size, x, zero)], axis=0)


def within_kernel(
    channels, maps, step, cum_t, cot, w_out, skip_gain, *refs, heads, first, aliases,
):
    part_ref, scaled_ref, decay_ref, grad_ref, _, spread2, skip = refs[aliases:]
    i = pl.program_id(0)
    group, span, width = channels.shape
    nstate = maps.shape[2] // 2
    size = width // heads

    @pl.when(i == 0)
    def _():
        spread2[...] = spread_matrix(spread2.shape[0], heads, width)
        skip[0:1, :] = sum(dot(part, spread2[0:heads, :]) for part in split(skip_gain[...], 3))

    grad = dot(cot[...].reshape(group * span, cot.shape[2]), w_out[...], NT)
    grad_ref[...] = grad.reshape(group, span, width)
    causal = iota((span, span), 0) >= iota((span, span), 1)
    for k in range(group):
        s = (first + i) * group + k
        chan = channels[k].astype(f32)
        scaled = (chan * spread(step[...], s, heads, spread2[...])).astype(bf16)
        scaled_ref[k] = scaled
        both = maps[k]
        scores = dot(both[:, nstate:], both[:, 0:nstate], NT)
        row = cum_t[k * heads : (k + 1) * heads, :]
        col = row.T
        for pair in range(heads // 2):
            weighted = []
            for h in (2 * pair, 2 * pair + 1):
                gap = jnp.broadcast_to(col[:, h : h + 1], (span, span)) - row[h : h + 1, :]
                decay = jnp.exp2(jnp.where(causal, gap, -jnp.inf))
                decay_ref[k, h] = decay.astype(bf16)
                weighted.append((scores * decay).astype(bf16))
            lanes = slice(2 * pair * size, 2 * (pair + 1) * size)
            out = dot(jnp.concatenate(weighted, axis=1), pair_blocks(scaled[:, lanes], size))
            part_ref[k, :, lanes] = out + skip[0:1, lanes] * chan[:, lanes]


def back_kernel(
    first_ref, state, maps, scaled, decay, part, grad, cum, gain, *refs, heads, aliases,
):
    normed_ref, read_ref, gain_ref, _, spread2 = refs[aliases:]
    i = pl.program_id(0)
    group, span, width = part.shape
    nstate = maps.shape[2] // 2
    size = width // heads

    @pl.when(i == 0)
    def _():
        spread2[...] = spread_matrix(spread2.shape[0], heads, width)
        gain_ref[...] = jnp.zeros_like(gain_ref)

    fade = jnp.exp2(cum[...])
    for k in range(group):
        s = (first_ref[0] + i) * group + k
        both = maps[k]
        fade_s = spread(fade, s, heads, spread2[...])
        out = part[k] + dot(both[:, nstate:], state[k]) * fade_s
        inv = lax.rsqrt(jnp.mean(out * out, axis=-1, keepdims=True) + 1e-05)
        normed = out * inv
        normed_ref[k] = (normed * gain[...]).astype(bf16)
        g = grad[k]
        by_gain = normed * g
        gain_ref[...] += jnp.sum(by_gain.reshape(span // 8, 8, width), axis=0)
        mean = jnp.mean(by_gain * gain[...], axis=-1, keepdims=True)
        back = inv * (g * gain[...] - normed * mean)
        back16 = back.astype(bf16)
        carried = dot((back * fade_s).astype(bf16), state[k], NT)
        pairs = jnp.zeros((span, span), f32)
        for pair in range(heads // 2):
            lanes = slice(2 * pair * size, 2 * (pair + 1) * size)
            both_heads = dot(back16[:, lanes], pair_blocks(scaled[k][:, lanes], size), NT)
            pairs = pairs + both_heads[:, 0:span] * decay[k, 2 * pair].astype(f32)
            pairs = pairs + both_heads[:, span:] * decay[k, 2 * pair + 1].astype(f32)
        inner = dot(pairs.astype(bf16), both[:, 0:nstate])
        read_ref[k] = (carried + inner).astype(bf16)


def grads_kernel(half_ref, normed, cot, read, mixed, *refs):
    *gains, keep_ref, send_ref, total = refs
    i = pl.program_id(0)
    rows = normed.shape[0] * normed.shape[1]
    channels, width, nstate = normed.shape[2], cot.shape[2], read.shape[2]
    piece = total.shape[1]
    pieces = width // piece

    @pl.when(i == 0)
    def _():
        total[...] = jnp.zeros_like(total)
        gain = sum(jnp.sum(ref[...], axis=0, keepdims=True) for ref in gains)
        for j in range(channels // piece):
            at = pieces * (channels + nstate) + j
            total[at : at + 1, :] = gain[:, j * piece : (j + 1) * piece]

    out = dot(normed[...].reshape(rows, channels), cot[...].reshape(rows, width), TN)
    into = dot(read[...].reshape(rows, nstate), mixed[...].reshape(rows, width), TN)
    for j in range(pieces):
        lanes = slice(j * piece, (j + 1) * piece)
        total[j * channels : (j + 1) * channels, :] += out[:, lanes]
        at = pieces * channels + j * nstate
        total[at : at + nstate, :] += into[:, lanes]

    @pl.when(i == pl.num_programs(0) - 1)
    def _():
        half = keep_ref.shape[0]
        mine = pl.multiple_of(half_ref[0] * half, 8)
        other = pl.multiple_of(half - half_ref[0] * half, 8)
        keep_ref[...] = total[pl.ds(mine, half), :]
        send_ref[...] = total[pl.ds(other, half), :]


def finish_kernel(half_ref, mine, came, out_ref, read_ref, gain_ref):
    channels, width = out_ref.shape
    nstate = read_ref.shape[0]
    half, piece = mine.shape
    pieces = width // piece

    def write(low, high):
        def rows(start, size):
            parts = []
            if start < half:
                parts.append(low[start : min(start + size, half), :])
            if start + size > half:
                parts.append(high[max(start - half, 0) : start + size - half, :])
            return jnp.concatenate([part.astype(f32) for part in parts], axis=0)

        for j in range(pieces):
            lanes = slice(j * piece, (j + 1) * piece)
            out_ref[:, lanes] = rows(j * channels, channels)
            read_ref[:, lanes] = rows(pieces * channels + j * nstate, nstate)
        tail = rows(pieces * (channels + nstate), 8)
        for j in range(channels // piece):
            gain_ref[:, j * piece : (j + 1) * piece] = tail[j : j + 1, :]

    pl.when(half_ref[0] == 0)(lambda: write(mine, came))
    pl.when(half_ref[0] == 1)(lambda: write(came, mine))


def whole(shape):
    return pl.BlockSpec(shape, lambda *_: (0,) * len(shape), pipeline_mode=pl.Buffered(1))


BIG = 1 << 19
ANYWHERE = pl.BlockSpec(memory_space=pl.ANY)


def call(body, name, scalars, grid, in_specs, out_specs, out_shape, scratch, vmem, flops, moved, aliases=None):
    inner = pl.pallas_call(
        body,
        name=name,
        grid_spec=pltpu.PrefetchScalarGridSpec(
            num_scalar_prefetch=scalars, grid=grid, in_specs=in_specs, out_specs=out_specs, scratch_shapes=scratch
        ),
        out_shape=[
            (pltpu.HBM if math.prod(shape) >= BIG else jax.ShapeDtypeStruct)(shape, dtype) for shape, dtype in out_shape
        ],
        input_output_aliases=aliases or {},
        compiler_params=pltpu.CompilerParams(dimension_semantics=("arbitrary",), vmem_limit_bytes=vmem << 20),
        cost_estimate=pl.CostEstimate(flops=int(flops), bytes_accessed=int(moved), transcendentals=0),
    )

    def outer(*args):
        return inner(*[pltpu.with_memory_space_constraint(x, pltpu.HBM) if x.size >= BIG else x for x in args])

    return outer


def front(half, readings, graph, cluster, mix, boundaries, w_channels, w_state, w_step, bias, fading_exponent):
    sensors, span, width = readings.shape
    heads, channels, maps = w_step.shape[1], w_channels.shape[1], w_state.shape[1]
    nstate, lanes, chunk = maps // 2, sensors * heads, 16
    rows, half_rows = sensors * chunk, sensors // 2 * nstate
    return call(
        functools.partial(front_kernel, heads=heads), "front", 1, (span // chunk,),
        [
            pl.BlockSpec((sensors, chunk, width), lambda i, *_: (0, i, 0)),
            whole((sensors, sensors)), whole((1, sensors)), whole((sensors, sensors)), whole((1, span)),
            whole((width, channels)), whole((width, maps)), whole((heads, width)),
            whole((1, heads)), whole((1, heads)),
        ],
        [
            pl.BlockSpec((sensors, chunk, width), lambda i, *_: (0, i, 0)),
            whole((sensors, span, channels)), whole((sensors, span, maps)),
            whole((span, lanes)), whole((span, lanes)), whole((lanes, span)),
            whole((half_rows, channels)), whole((half_rows + sensors, channels)), whole((sensors, channels)),
            whole((8, 128)),
        ],
        [
            ((sensors, span, width), bf16), ((sensors, span, channels), bf16), ((sensors, span, maps), bf16),
            ((span, lanes), f32), ((span, lanes), f32), ((lanes, span), f32),
            ((half_rows, channels), f32), ((half_rows + sensors, channels), f32), ((sensors, channels), f32),
            ((8, 128), f32),
        ],
        [
            pltpu.VMEM((rows, rows), bf16), pltpu.VMEM((width, maps + lanes), bf16),
            pltpu.VMEM((2 * lanes, channels), bf16), pltpu.VMEM((8, lanes), f32),
            pltpu.VMEM((sensors, nstate, channels), f32), pltpu.VMEM((span, lanes), f32),
        ],
        28, 5e9, 14e6,
    )(
        half, readings, graph, cluster[None, :], mix, boundaries[None, :], w_channels, w_state, w_step.T,
        bias[None, :], fading_exponent[None, :],
    )


GROUP = 2


def within(first, count, channels, maps, step, cum_t, cot, w_out, skip_gain, done, token):
    sensors, span, width = channels.shape
    heads, nmaps = skip_gain.shape[0], maps.shape[2]
    lanes = sensors * heads

    def block(*shape):
        return pl.BlockSpec((GROUP,) + shape, lambda i, *_: (first + i,) + (0,) * len(shape))

    n_in = 7
    aliases = {n_in + k: k for k in range(len(done))}
    aliases[n_in + len(done)] = 4
    return call(
        functools.partial(within_kernel, heads=heads, first=first, aliases=len(done) + 1), "within", 0, (count,),
        [
            block(span, width), block(span, nmaps), whole((span, lanes)),
            pl.BlockSpec((GROUP * heads, span), lambda i, *_: (first + i, 0)),
            block(span, cot.shape[2]), whole(w_out.shape), whole((1, heads)),
        ] + [ANYWHERE] * (len(done) + 1),
        [block(span, width), block(span, width), block(heads, span, span), block(span, width), ANYWHERE],
        [
            ((sensors, span, width), f32), ((sensors, span, width), bf16),
            ((sensors, heads, span, span), bf16), ((sensors, span, width), f32), (token.shape, token.dtype),
        ],
        [pltpu.VMEM((2 * lanes, width), bf16), pltpu.VMEM((8, width), f32)],
        16, 6e8 * count, 3e6 * count, aliases,
    )(channels, maps, step, cum_t, cot, w_out, skip_gain[None, :], *done, token)


def back(first, state, maps, scaled, decay, part, grad, cum, gain, done, token):
    sensors, span, width = part.shape
    heads, nmaps = decay.shape[1], maps.shape[2]
    nstate, lanes = nmaps // 2, sensors * heads
    count = state.shape[0] // GROUP

    def block(*shape):
        return pl.BlockSpec((GROUP,) + shape, lambda i, at: (at[0] + i,) + (0,) * len(shape))

    n_in = 9
    aliases = {n_in + k: k for k in range(len(done))}
    aliases[n_in + len(done)] = 3
    return call(
        functools.partial(back_kernel, heads=heads, aliases=len(done) + 1), "back", 1, (count,),
        [
            pl.BlockSpec((GROUP, nstate, width), lambda i, at: (i, 0, 0)),
            block(span, nmaps), block(span, width), block(heads, span, span), block(span, width), block(span, width),
            whole((span, lanes)), whole((1, width)),
        ] + [ANYWHERE] * (len(done) + 1),
        [block(span, width), block(span, nstate), whole((8, width)), ANYWHERE],
        [
            ((sensors, span, width), bf16), ((sensors, span, nstate), bf16), ((8, width), f32),
            (token.shape, token.dtype),
        ],
        [pltpu.VMEM((2 * lanes, width), bf16)],
        16, 6e8 * count, 3e6 * count, aliases,
    )(first, state, maps, scaled, decay, part, grad, cum, gain[None, :], *done, token)


def grads(half, normed, cot, read, mixed, gains):
    sensors, span, channels = normed.shape
    width, nstate = cot.shape[2], read.shape[2]
    group, piece = 4, 256
    rows = -(-(width // piece * (channels + nstate) + channels // piece) // 64) * 64

    def block(*shape):
        return pl.BlockSpec((group,) + shape, lambda i, *_: (i,) + (0,) * len(shape))

    return call(
        grads_kernel, "grads", 1, (sensors // group,),
        [block(span, channels), block(span, width), block(span, nstate), block(span, width)]
        + [whole((8, channels))] * len(gains),
        [whole((rows // 2, piece))] * 2,
        [((rows // 2, piece), f32)] * 2,
        [pltpu.VMEM((rows, piece), f32)],
        28, 2.5e9, 14e6,
    )(half, normed, cot, read, mixed, *gains)


def finish(half, mine, came, channels, width, nstate):
    return call(
        finish_kernel, "finish", 1, (1,),
        [whole(mine.shape)] * 2,
        [whole((channels, width)), whole((nstate, width)), whole((1, channels))],
        [((channels, width), f32), ((nstate, width), f32), ((1, channels), f32)],
        [], 12, 1e6, 4e6,
    )(half, mine, came)


def swap(x, distance, count):
    return lax.ppermute(x, "seq", [(i, i ^ distance) for i in range(count)])


def narrow(x):
    return lax.reduce_precision(x, 8, 7)


def pick(bit, when_one, when_zero):
    return jnp.where(bit == 1, when_one, when_zero)


def fading(tail, start, states):
    own = lax.dynamic_slice_in_dim(tail, start, states.shape[0], 0)
    return jnp.exp2(own)[:, None, :]


def tied(x, token):
    return lax.optimization_barrier((x, token))


def exchange(keep, send, tail, me, count, shards, swap_beside, ready):
    sensors, width = tail.shape
    levels = count.bit_length() - 1
    size = sensors // 2
    nstate = keep.shape[0] // size
    own = keep.reshape(size, nstate, width)
    start = (me & 1) * size
    saved = []

    def pack(states, tails):
        return jnp.concatenate([states.astype(bf16).reshape(-1, width), tails.astype(bf16)], axis=0)

    def unpack(came):
        rows = size * nstate
        return came[0:rows].astype(f32).reshape(size, nstate, width), came[rows:].astype(f32)

    for level in range(shards):
        bit = (me >> level) & 1
        other, other_tail = unpack(swap_beside(send, level, True))
        low, high = pick(bit, other, own), pick(bit, own, other)
        low_tail, high_tail = pick(bit, other_tail, tail), pick(bit, tail, other_tail)
        total = low * fading(high_tail, start, low) + high
        saved.append((low, low_tail, start, bit))
        tail = tail + other_tail
        if level + 1 < shards:
            next_bit = (me >> (level + 1)) & 1
            size //= 2
            own = lax.dynamic_slice_in_dim(total, next_bit * size, size, 0)
            gone = lax.dynamic_slice_in_dim(total, (1 - next_bit) * size, size, 0)
            start = start + next_bit * size
        else:
            own = gone = total
        send = pack(gone, tail)
    before = jnp.zeros_like(own)
    before_tail = jnp.zeros_like(tail)
    for level in range(shards, levels):
        bit = (me >> level) & 1
        other, other_tail = unpack(swap_beside(send, level, True))
        before = pick(bit, other * fading(before_tail, start, other) + before, before)
        before_tail = pick(bit, before_tail + other_tail, before_tail)
        if level + 1 < levels:
            low, high = pick(bit, other, own), pick(bit, own, other)
            own = low * fading(pick(bit, tail, other_tail), start, low) + high
            tail = tail + other_tail
            send = pack(own, tail)

    def narrowed(states, start, level):
        for low, low_tail, low_start, bit in reversed(saved[:level]):
            here = lax.dynamic_slice_in_dim(low, start - low_start, states.shape[0], 0)
            states = pick(bit, states * fading(low_tail, start, states) + here, states)
        return states.astype(bf16)

    known, known_start, known_level = before, start, shards
    for level in reversed(range(shards)):
        low, low_tail, start, bit = saved[level]
        after = before * fading(low_tail, start, low) + low
        mine, gone = pick(bit, after, before), pick(bit, before, after)
        ready(narrowed(known, known_start, known_level), known_start, False)
        came = swap_beside(gone.astype(bf16), level, False).astype(f32)
        before = pick(bit, jnp.concatenate([came, mine], axis=0), jnp.concatenate([mine, came], axis=0))
        known, known_start, known_level = came, start + pick(bit, -low.shape[0], low.shape[0]), level
    ready(narrowed(known, known_start, known_level), known_start, True)


def all_sum(keep, send, me, count, shards):
    levels = count.bit_length() - 1
    own = keep
    for level in range(shards):
        came = swap(send, 1 << level, count)
        own = own + came.astype(f32)
        if level + 1 < shards:
            bit = (me >> (level + 1)) & 1
            size = own.shape[0] // 2
            send = lax.dynamic_slice_in_dim(own, (1 - bit) * size, size, 0).astype(bf16)
            own = lax.dynamic_slice_in_dim(own, bit * size, size, 0)
    for level in range(shards, levels):
        own = narrow(own)
        own = own + swap(own.astype(bf16), 1 << level, count).astype(f32)
    out = own.astype(bf16)
    for level in reversed(range(1, shards)):
        bit = (me >> level) & 1
        came = swap(out, 1 << level, count)
        out = pick(bit, jnp.concatenate([came, out], axis=0), jnp.concatenate([out, came], axis=0))
    return out, swap(out, 1, count)


def per_device(
    count, readings, block_graph, cluster_of, mix_weight, boundaries, w_channels, w_state, w_step,
    step_bias, channel_fading_exponent, skip_gain, norm_gain, w_out, cotangent,
):
    sensors, span, width = readings.shape
    channels = w_channels.shape[1]
    nstate = w_state.shape[1] // 2
    me = lax.axis_index("seq")
    half = (me & 1).astype(jnp.int32)[None]
    shards = min(max(count.bit_length() - 2, 1), 3)

    mixed, chans, maps, step, cum, cum_t, keep, send, tail, token = front(
        half, readings, block_graph, cluster_of, mix_weight, boundaries, w_channels, w_state, w_step,
        step_bias, channel_fading_exponent,
    )
    work = {"token": token, "within": (), "back": (), "gains": [], "next": None}
    plan = {1: (0, 3), 2: (3, 2), 3: (5, 3)}

    def inside(level):
        if level in plan:
            first, blocks = plan[level]
            *arrays, work["token"] = within(
                first, blocks, chans, maps, step, cum_t, cotangent, w_out, skip_gain, work["within"], work["token"]
            )
            work["within"] = tuple(arrays)

    def run_back():
        states, start = work["next"]
        part, scaled, decay, grad = work["within"]
        first = (start // GROUP).astype(jnp.int32)[None]
        normed, read, gain, work["token"] = back(
            first, states, maps, scaled, decay, part, grad, cum, norm_gain, work["back"], work["token"]
        )
        work["back"] = (normed, read)
        work["gains"].append(gain)

    def swap_beside(x, level, up):
        x, work["token"] = tied(x, work["token"])
        came = swap(x, 1 << level, count)
        if up:
            inside(level)
        else:
            run_back()
        return came

    def ready(states, start, last):
        work["next"] = (states, start)
        if last:
            run_back()

    exchange(keep, send, tail, me, count, shards, swap_beside, ready)
    keep_sum, send_sum = grads(half, work["back"][0], cotangent, work["back"][1], mixed, work["gains"])
    mine, came = all_sum(keep_sum, send_sum, me, count, shards)
    grad_out, grad_read, grad_gain = finish(half, mine, came, channels, width, nstate)
    return grad_out, grad_read.T, grad_gain[0]


def solution(mesh):
    in_specs = (
        P("groups", "seq", None), P("groups", None), P("groups"), P(), P(("groups", "seq")),
        P(), P(), P(), P(), P(), P(), P(), P(), P("groups", "seq", None),
    )
    out_specs = (P("groups", None), P("groups", None), P("groups"))
    return jax.shard_map(
        functools.partial(per_device, mesh.shape["seq"]),
        mesh=mesh, in_specs=in_specs, out_specs=out_specs, check_vma=False,
    )
```

time: 157 us -> 147 us (0.936)
  Pallas kernels: 44.4 us -> 62.5 us
  waiting for transfers between devices: 68.8 us -> 50.9 us
  local copies, waits for them, and re-layouts: 11.2 us -> 6.8 us
  starting transfers between devices: 14.4 us -> 11.9 us
  other arithmetic: 14.9 us -> 12.5 us
    pallas_call x3 -> x10, Pallas kernels: 44.4 us -> 62.5 us  [outer(): inner(*[pltpu.with_memory_space_constraint(x, pltpu.HBM) if x.size >= BIG...]
    ppermute x14, waiting for transfers between devices: 68.8 us -> 50.9 us  [swap(): return lax.ppermute(x, 'seq', [(i, i ^ distance) for i in range(count)])]
    slice x4 -> x2, local copies, waits for them, and re-layouts: 3.92 us -> 0.98 us  [unpack(): came[0:rows].astype(f32).reshape(size, nstate, width)]
    ppermute x14, starting transfers between devices: 14.4 us -> 11.9 us  [swap(): return lax.ppermute(x, 'seq', [(i, i ^ distance) for i in range(count)])]
    unnamed x17 -> x28, local copies, waits for them, and re-layouts: 3.99 us -> 5.7 us
    select_n x7 -> x5, other arithmetic: 4.09 us -> 2.85 us  [pick(): return jnp.where(bit == 1, when_one, when_zero)]
    convert_element_type x11 -> x12, other arithmetic: 5.69 us -> 4.84 us  [the longest x3 1.54 us: pack(): tails.astype(bf16)]
  transfers between devices with their start and end apart: 14 -> 14, of which waited for: 13 -> 11; matrix products, arithmetic and copies ran while one was open for 0% -> 0% of each run, Pallas kernels for 7% -> 18%
where the time goes in v2:
time: 147 us; the launch traced here: 146 us
  Pallas kernels  62.5 us (43%)
  waiting for transfers between devices  50.9 us (35%)
  other arithmetic  12.5 us (9%)
  starting transfers between devices  11.9 us (8%)
  local copies, waits for them, and re-layouts  6.8 us (5%)
    pallas_call x10, Pallas kernels, outer(): inner(*[pltpu.with_memory_space_constraint(x, pltpu.HBM) if x.size >= BIG...  62.5 us
    ppermute x14, waiting for transfers between devices, swap(): return lax.ppermute(x, 'seq', [(i, i ^ distance) for i in range(count)])  50.9 us
    ppermute x14, starting transfers between devices, swap(): return lax.ppermute(x, 'seq', [(i, i ^ distance) for i in range(count)])  11.9 us
    unnamed x28, local copies, waits for them, and re-layouts  5.7 us
  transfers between devices with their start and end apart: 14, of which 11 were waited for; matrix products, arithmetic and copies ran while one was open for 0% of the time, Pallas kernels for 18%

profile of v2, /device:TPU:0, one launch (start us, length us, event | category | flops | bytes accessed | tf_op | source)
XLA Modules:
  0.0 145.6 jit_solution(17217301408917087702)
XLA Ops:
  0.6 0.9 copy-done.2
  1.6 0.7 copy-done.3
  2.3 0.7 copy-done.4
  3.0 0.7 copy-done.5
  3.7 0.7 copy-done.6
  4.4 0.7 copy-done.7
  5.0 0.7 copy-done.8
  5.7 0.7 copy-done.9
  6.3 17.9 %front.1 = (bf16[16,128,1024]{2,1,0:T(8,128)(2,1)}, bf16[16,128,512]{2,1,0:T(8,128)(2,1)}, bf16[16,128,128]{2,1,0:T(8,128)(2,1)S(1)}, f32[128,128]{1,0:T(8,128)S...) custom-call(s32[1]{0:T(128)} %bitcast.half_ref, ...), custom_call_target="tpu_custom_call" | custom-call | flops 5000000000 | bytes 14000000 | tf_op jit(solution)/shard_map/front/pallas_call | solution.py:294
  24.3 0.5 collective-permute-start
  24.7 2.5 %collective-permute-done = f32[528,512]{1,0:T(8,128)} collective-permute-done((f32[528,512]{1,0:T(8,128)S(1)}, f32[528,512]{1,0:T(8,128)}, u32[]{:S(2)}, u32[]{:S(2)}) %collective-permute-start) | collective-permute-done | bytes 1081376 | tf_op jit(solution)/shard_map/ppermute | solution.py:428
  27.2 0.8 fusion.22
  28.0 1.5 slice_select_fusion
  29.7 0.8 pad_maximum_fusion
  30.6 2.9 %collective-permute-start.1 = (bf16[272,512]{1,0:T(8,128)(2,1)}, bf16[272,512]{1,0:T(8,128)(2,1)}, u32[]{:S(2)}, u32[]{:S(2)}) collective-permute-start(bf16[272,512]{1,0:T(8,128)(2,1)} %pad_maximum_fusion), channel_id=1, source_target_pairs={{0,2},{1,3},{2,0},{3,1},{4,6},{5,7},{6,4},{7,5},{8,10},{9,11},{10,... | collective-permute-start | bytes 835592 | tf_op jit(solution)/shard_map/ppermute | solution.py:428
  33.4 6.4 %within.3 = (f32[16,128,512]{2,1,0:T(8,128)}, bf16[16,128,512]{2,1,0:T(8,128)(2,1)}, bf16[16,8,128,128]{3,2,1,0:T(8,128)(2,1)}, f32[16,128,512]{2,1,0:T(8,128)}, f32[8,128]{1,0:T(8,128)S(1)}) custom-call(bf16[16,128,512]{2,1,0:T(8,128)(2,1)} %get-tuple-element.69.channels, ...), custom_call_target="tpu_custom_call", output_to_operand_aliasing={{4}: (7, {})} | custom-call | flops 1800000000 | bytes 9000000 | tf_op jit(solution)/shard_map/within/pallas_call | solution.py:294
  39.9 0.8 collective-permute-done.1
  40.7 0.7 slice_convert_fusion.1
  41.4 1.0 slice.30
  42.4 2.0 %fusion = (f32[4,64,512]{2,1,0:T(8,128)S(1)}, f32[4,64,512]{2,1,0:T(8,128)}) fusion(bf16[4,64,512]{2,1,0:T(8,128)(2,1)S(1)} %bitcast.46, f32[8,64,512]{2,1,0:T(8,128)} %copy-done.12, s32[]{:T(128)S(6)} %select_n.263, f32[4,512]{1,0:T(4,128)S(1)} %fusion.10, pred[]{:T(512)S(6)} %eq.8), kind=kLoop, calls=%fused_computation.10 | loop fusion | flops 655360 | bytes 1843205 | tf_op jit(solution)/shard_map/add | solution.py:469
  44.4 0.8 fusion.20
  45.2 1.9 %collective-permute-start.2 = (bf16[144,512]{1,0:T(8,128)(2,1)S(1)}, bf16[144,512]{1,0:T(8,128)(2,1)S(1)}, u32[]{:S(2)}, u32[]{:S(2)}) collective-permute-start(bf16[144,512]{1,0:T(8,128)(2,1)S(1)} %pad_maximum_fusion.1), channel_id=1, source_target_pairs={{0,4},{1,5},{2,6},{3,7},{4,0},{5,1},{6,2},{7,3},{8,12},{9,13},{10,... | collective-permute-start | bytes 442376 | tf_op jit(solution)/shard_map/ppermute | solution.py:428
  47.1 4.9 %within.4 = (f32[16,128,512]{2,1,0:T(8,128)}, bf16[16,128,512]{2,1,0:T(8,128)(2,1)}, bf16[16,8,128,128]{3,2,1,0:T(8,128)(2,1)}, f32[16,128,512]{2,1,0:T(8,128)}, f32[8,128]{1,0:T(8,128)S(1)}) custom-call(bf16[16,128,512]{2,1,0:T(8,128)(2,1)} %get-tuple-element.69.channels, ...), custom_call_target="tpu_custom_call", output_to_operand_aliasing={{0}: (7, {}), {1}: (8, {}), {2}: (9, {}), {3}: (10, {}), {4... | custom-call | flops 1200000000 | bytes 6000000 | tf_op jit(solution)/shard_map/within/pallas_call | solution.py:294
  52.1 2.7 %collective-permute-start.3 = (bf16[144,512]{1,0:T(8,128)(2,1)S(1)}, bf16[144,512]{1,0:T(8,128)(2,1)S(1)}, u32[]{:S(2)}, u32[]{:S(2)}) collective-permute-start(bf16[144,512]{1,0:T(8,128)(2,1)S(1)} %pad_maximum_fusion.2), channel_id=1, source_target_pairs={{0,8},{1,9},{2,10},{3,11},{4,12},{5,13},{6,14},{7,15},{8,0},{9,1},... | collective-permute-start | bytes 442376 | tf_op jit(solution)/shard_map/ppermute | solution.py:428
  54.8 6.5 %within.5 = (f32[16,128,512]{2,1,0:T(8,128)}, bf16[16,128,512]{2,1,0:T(8,128)(2,1)}, bf16[16,8,128,128]{3,2,1,0:T(8,128)(2,1)}, f32[16,128,512]{2,1,0:T(8,128)}, f32[8,128]{1,0:T(8,128)S(1)}) custom-call(bf16[16,128,512]{2,1,0:T(8,128)(2,1)} %get-tuple-element.69.channels, ...), custom_call_target="tpu_custom_call", output_to_operand_aliasing={{0}: (7, {}), {1}: (8, {}), {2}: (9, {}), {3}: (10, {}), {4... | custom-call | flops 1800000000 | bytes 9000000 | tf_op jit(solution)/shard_map/within/pallas_call | solution.py:294
  61.4 0.5 collective-permute-start.4
  62.0 4.6 %collective-permute-done.4 = bf16[2,64,512]{2,1,0:T(8,128)(2,1)S(1)} collective-permute-done((bf16[2,64,512]{2,1,0:T(8,128)(2,1)S(1)}, bf16[2,64,512]{2,1,0:T(8,128)(2,1)S(1)}, u32[]{:S(2)}, u32[]{:S(2)}) %collective-permute-start.4) | collective-permute-done | bytes 131104 | tf_op jit(solution)/shard_map/ppermute | solution.py:428
  66.6 1.2 select_convert_fusion.4
  67.8 1.0 fusion.1
  68.9 3.1 %back.4 = (bf16[16,128,512]{2,1,0:T(8,128)(2,1)}, bf16[16,128,64]{2,1,0:T(8,128)(2,1)S(1)}, f32[8,512]{1,0:T(8,128)S(1)}, f32[8,128]{1,0:T(8,128)S(1)}) custom-call(s32[1]{0:T(128)} %bitcast.18.first_ref, bf16[2,64,512]{2,1,0:T(8,128)(2,1)S(1)} %get-tuple-element.121.state, ...), custom_call_target="tpu_custom_call", output_to_operand_aliasing={{3}: (9, {})} | custom-call | flops 600000000 | bytes 3000000 | tf_op jit(solution)/shard_map/back/pallas_call | solution.py:294
  72.0 1.3 collective-permute-start.5
  73.3 3.2 %back.5 = (bf16[16,128,512]{2,1,0:T(8,128)(2,1)}, bf16[16,128,64]{2,1,0:T(8,128)(2,1)S(1)}, f32[8,512]{1,0:T(8,128)S(1)}, f32[8,128]{1,0:T(8,128)S(1)}) custom-call(s32[1]{0:T(128)} %bitcast.20.first_ref, bf16[2,64,512]{2,1,0:T(8,128)(2,1)S(1)} %get-tuple-element.131.state, ...), custom_call_target="tpu_custom_call", output_to_operand_aliasing={{0}: (9, {}), {1}: (10, {}), {3}: (11, {})} | custom-call | flops 600000000 | bytes 3000000 | tf_op jit(solution)/shard_map/back/pallas_call | solution.py:294
  76.5 2.7 %collective-permute-done.5 = bf16[4,64,512]{2,1,0:T(8,128)(2,1)S(1)} collective-permute-done((bf16[4,64,512]{2,1,0:T(8,128)(2,1)}, bf16[4,64,512]{2,1,0:T(8,128)(2,1)S(1)}, u32[]{:S(2)}, u32[]{:S(2)}) %collective-permute-start.5) | collective-permute-done | bytes 262176 | tf_op jit(solution)/shard_map/ppermute | solution.py:428
  79.3 1.1 select_convert_fusion
  80.5 4.8 %back.6 = (bf16[16,128,512]{2,1,0:T(8,128)(2,1)}, bf16[16,128,64]{2,1,0:T(8,128)(2,1)S(1)}, f32[8,512]{1,0:T(8,128)S(1)}, f32[8,128]{1,0:T(8,128)S(1)}) custom-call(s32[1]{0:T(128)} %bitcast.21.first_ref, bf16[4,64,512]{2,1,0:T(8,128)(2,1)S(1)} %select_convert_fusion.1.state, ...), custom_call_target="tpu_custom_call", output_to_operand_aliasing={{0}: (9, {}), {1}: (10, {}), {3}: (11, {})} | custom-call | flops 1200000000 | bytes 6000000 | tf_op jit(solution)/shard_map/back/pallas_call | solution.py:294
  85.3 7.6 %back.7 = (bf16[16,128,512]{2,1,0:T(8,128)(2,1)}, bf16[16,128,64]{2,1,0:T(8,128)(2,1)S(1)}, f32[8,512]{1,0:T(8,128)S(1)}, f32[8,128]{1,0:T(8,128)S(1)}) custom-call(s32[1]{0:T(128)} %bitcast.1.first_ref, bf16[8,64,512]{2,1,0:T(8,128)(2,1)S(1)} %collective-permute-done.6.state, ...), custom_call_target="tpu_custom_call", output_to_operand_aliasing={{0}: (9, {}), {1}: (10, {}), {3}: (11, {})} | custom-call | flops 2400000000 | bytes 12000000 | tf_op jit(solution)/shard_map/back/pallas_call | solution.py:294
  92.9 6.6 %grads.1 = (f32[1184,256]{1,0:T(8,128)S(1)}, f32[1184,256]{1,0:T(8,128)S(1)}) custom-call(s32[1]{0:T(128)} %bitcast.half_ref, bf16[16,128,512]{2,1,0:T(8,128)(2,1)} %get-tuple-element.109.normed, bf16[16,128,1024]{2,1,0:T(8,128)(2,1)} %cot.7, bf16[16,128,64]{2,1,0:T(8,128)(2,1)S(1)} %get-tuple-element.110.read, ...), custom_call_target="tpu_custom_call" | custom-call | flops 2500000000 | bytes 14000000 | tf_op jit(solution)/shard_map/grads/pallas_call | solution.py:294
  99.5 0.6 collective-permute-start.7
  100.1 2.7 %collective-permute-done.7 = f32[1184,256]{1,0:T(8,128)} collective-permute-done((f32[1184,256]{1,0:T(8,128)S(1)}, f32[1184,256]{1,0:T(8,128)}, u32[]{:S(2)}, u32[]{:S(2)}) %collective-permute-start.7) | collective-permute-done | bytes 1212448 | tf_op jit(solution)/shard_map/ppermute | solution.py:428
  102.7 1.4 add.165
  104.2 0.8 collective-permute-start.8
  105.0 8.8 %collective-permute-done.8 = bf16[592,256]{1,0:T(8,128)(2,1)S(1)} collective-permute-done((bf16[592,256]{1,0:T(8,128)(2,1)S(1)}, bf16[592,256]{1,0:T(8,128)(2,1)S(1)}, u32[]{:S(2)}, u32[]{:S(2)}) %collective-permute-start.8) | collective-permute-done | bytes 303136 | tf_op jit(solution)/shard_map/ppermute | solution.py:428
  113.9 5.4 %collective-permute-done.9 = bf16[296,256]{1,0:T(8,128)(2,1)S(1)} collective-permute-done((bf16[296,256]{1,0:T(8,128)(2,1)S(1)}, bf16[296,256]{1,0:T(8,128)(2,1)S(1)}, u32[]{:S(2)}, u32[]{:S(2)}) %collective-permute-start.9) | collective-permute-done | bytes 151584 | tf_op jit(solution)/shard_map/ppermute | solution.py:428
  119.7 8.4 %collective-permute-done.10 = bf16[296,256]{1,0:T(8,128)(2,1)S(1)} collective-permute-done((bf16[296,256]{1,0:T(8,128)(2,1)S(1)}, bf16[296,256]{1,0:T(8,128)(2,1)S(1)}, u32[]{:S(2)}, u32[]{:S(2)}) %collective-permute-start.10) | collective-permute-done | bytes 151584 | tf_op jit(solution)/shard_map/ppermute | solution.py:428
  128.2 5.4 %collective-permute-done.11 = bf16[296,256]{1,0:T(8,128)(2,1)S(1)} collective-permute-done((bf16[296,256]{1,0:T(8,128)(2,1)S(1)}, bf16[296,256]{1,0:T(8,128)(2,1)S(1)}, u32[]{:S(2)}, u32[]{:S(2)}) %collective-permute-start.11) | collective-permute-done | bytes 151584 | tf_op jit(solution)/shard_map/ppermute | solution.py:428
  134.1 7.5 %collective-permute-done.12 = bf16[592,256]{1,0:T(8,128)(2,1)S(1)} collective-permute-done((bf16[592,256]{1,0:T(8,128)(2,1)S(1)}, bf16[592,256]{1,0:T(8,128)(2,1)S(1)}, u32[]{:S(2)}, u32[]{:S(2)}) %collective-permute-start.12) | collective-permute-done | bytes 303136 | tf_op jit(solution)/shard_map/ppermute | solution.py:428
  142.0 2.0 %collective-permute-done.13.came = bf16[1184,256]{1,0:T(8,128)(2,1)S(1)} collective-permute-done((bf16[1184,256]{1,0:T(8,128)(2,1)S(1)}, bf16[1184,256]{1,0:T(8,128)(2,1)S(1)}, u32[]{:S(2)}, u32[]{:S(2)}) %collective-permute-start.13) | collective-permute-done | bytes 606240 | tf_op jit(solution)/shard_map/ppermute | solution.py:428
  144.0 1.6 %finish.1 = (f32[512,1024]{1,0:T(8,128)}, f32[64,1024]{1,0:T(8,128)}, f32[1,512]{1,0:T(1,128)}) custom-call(s32[1]{0:T(128)} %bitcast.half_ref, bf16[1184,256]{1,0:T(8,128)(2,1)S(1)} %maximum_select_fusion.1.mine, bf16[1184,256]{1,0:T(8,128)(2,1)S(1)} %collective-permute-done.13.came), custom_call_target="tpu_custom_call" | custom-call | flops 1000000 | bytes 4000000 | tf_op jit(solution)/shard_map/finish/pallas_call | solution.py:294
  (57 shorter events, 2.3 us)
Async XLA Ops:
  0.6 1.0 copy-start.2
  1.6 0.7 copy-start.3
  2.3 0.7 copy-start.4
  3.0 0.7 copy-start.5
  3.7 0.7 copy-start.6
  4.4 0.7 copy-start.7
  5.0 0.7 copy-start.8
  5.7 0.7 copy-start.9
  24.3 2.9 %collective-permute-start = (f32[528,512]{1,0:T(8,128)S(1)}, f32[528,512]{1,0:T(8,128)}, u32[]{:S(2)}, u32[]{:S(2)}) collective-permute-start(f32[528,512]{1,0:T(8,128)S(1)} %get-tuple-element.64), channel_id=1, source_target_pairs={{0,1},{1,0},{2,3},{3,2},{4,5},{5,4},{6,7},{7,6},{8,9},{9,8},{10,11... | collective-permute-start | bytes 3244040 | tf_op jit(solution)/shard_map/ppermute | solution.py:428
  29.4 4.0 %copy-start.1 = (f32[8]{0:T(128)S(1)}, f32[8]{0:T(128)}, u32[]{:S(2)}) copy-start(f32[8]{0:T(128)} %param.24) | copy-start | bytes 100
  29.7 12.7 %copy-start.12 = (f32[8,64,512]{2,1,0:T(8,128)}, f32[8,64,512]{2,1,0:T(8,128)S(1)}, u32[]{:S(2)}) copy-start(f32[8,64,512]{2,1,0:T(8,128)S(1)} %multiply_add_fusion) | copy-start | bytes 3145732
  30.6 10.1 %collective-permute-start.1 = (bf16[272,512]{1,0:T(8,128)(2,1)}, bf16[272,512]{1,0:T(8,128)(2,1)}, u32[]{:S(2)}, u32[]{:S(2)}) collective-permute-start(bf16[272,512]{1,0:T(8,128)(2,1)} %pad_maximum_fusion), channel_id=1, source_target_pairs={{0,2},{1,3},{2,0},{3,1},{4,6},{5,7},{6,4},{7,5},{8,10},{9,11},{10,... | collective-permute-start | bytes 835592 | tf_op jit(solution)/shard_map/ppermute | solution.py:428
  44.4 16.9 %copy-start.11 = (f32[4,64,512]{2,1,0:T(8,128)}, f32[4,64,512]{2,1,0:T(8,128)S(1)}, u32[]{:S(2)}) copy-start(f32[4,64,512]{2,1,0:T(8,128)S(1)} %get-tuple-element.123) | copy-start | bytes 1572868
  45.2 6.8 %collective-permute-start.2 = (bf16[144,512]{1,0:T(8,128)(2,1)S(1)}, bf16[144,512]{1,0:T(8,128)(2,1)S(1)}, u32[]{:S(2)}, u32[]{:S(2)}) collective-permute-start(bf16[144,512]{1,0:T(8,128)(2,1)S(1)} %pad_maximum_fusion.1), channel_id=1, source_target_pairs={{0,4},{1,5},{2,6},{3,7},{4,0},{5,1},{6,2},{7,3},{8,12},{9,13},{10,... | collective-permute-start | bytes 442376 | tf_op jit(solution)/shard_map/ppermute | solution.py:428
  52.1 9.1 %collective-permute-start.3 = (bf16[144,512]{1,0:T(8,128)(2,1)S(1)}, bf16[144,512]{1,0:T(8,128)(2,1)S(1)}, u32[]{:S(2)}, u32[]{:S(2)}) collective-permute-start(bf16[144,512]{1,0:T(8,128)(2,1)S(1)} %pad_maximum_fusion.2), channel_id=1, source_target_pairs={{0,8},{1,9},{2,10},{3,11},{4,12},{5,13},{6,14},{7,15},{8,0},{9,1},... | collective-permute-start | bytes 442376 | tf_op jit(solution)/shard_map/ppermute | solution.py:428
  54.8 11.8 %copy-start.10 = (f32[4,64,512]{2,1,0:T(8,128)S(1)}, f32[4,64,512]{2,1,0:T(8,128)}, u32[]{:S(2)}) copy-start(f32[4,64,512]{2,1,0:T(8,128)} %get-tuple-element.124) | copy-start | bytes 1572868
  61.4 5.2 %collective-permute-start.4 = (bf16[2,64,512]{2,1,0:T(8,128)(2,1)S(1)}, bf16[2,64,512]{2,1,0:T(8,128)(2,1)S(1)}, u32[]{:S(2)}, u32[]{:S(2)}) collective-permute-start(bf16[2,64,512]{2,1,0:T(8,128)(2,1)S(1)} %select_convert_fusion.5), channel_id=1, source_target_pairs={{0,4},{1,5},{2,6},{3,7},{4,0},{5,1},{6,2},{7,3},{8,12},{9,13},{10,... | collective-permute-start | bytes 393224 | tf_op jit(solution)/shard_map/ppermute | solution.py:428
  66.6 2.2 %copy-start = (f32[512]{0:T(512)S(1)}, f32[512]{0:T(512)}, u32[]{:S(2)}) copy-start(f32[512]{0:T(512)} %param.25) | copy-start | bytes 6148
  72.0 7.3 %collective-permute-start.5 = (bf16[4,64,512]{2,1,0:T(8,128)(2,1)}, bf16[4,64,512]{2,1,0:T(8,128)(2,1)S(1)}, u32[]{:S(2)}, u32[]{:S(2)}) collective-permute-start(bf16[4,64,512]{2,1,0:T(8,128)(2,1)} %get-tuple-element.97), channel_id=1, source_target_pairs={{0,2},{1,3},{2,0},{3,1},{4,6},{5,7},{6,4},{7,5},{8,10},{9,11},{10,... | collective-permute-start | bytes 786440 | tf_op jit(solution)/shard_map/ppermute | solution.py:428
  73.3 6.0 %copy-start.13 = (f32[4,64,512]{2,1,0:T(8,128)S(1)}, f32[4,64,512]{2,1,0:T(8,128)}, u32[]{:S(2)}) copy-start(f32[4,64,512]{2,1,0:T(8,128)} %get-tuple-element.134) | copy-start | bytes 1572868
  80.4 4.9 %collective-permute-start.6 = (bf16[8,64,512]{2,1,0:T(8,128)(2,1)}, bf16[8,64,512]{2,1,0:T(8,128)(2,1)S(1)}, u32[]{:S(2)}, u32[]{:S(2)}) collective-permute-start(bf16[8,64,512]{2,1,0:T(8,128)(2,1)} %select_convert_fusion), channel_id=1, source_target_pairs={{0,1},{1,0},{2,3},{3,2},{4,5},{5,4},{6,7},{7,6},{8,9},{9,8},{10,11... | collective-permute-start | bytes 1572872 | tf_op jit(solution)/shard_map/ppermute | solution.py:428
  99.5 3.2 %collective-permute-start.7 = (f32[1184,256]{1,0:T(8,128)S(1)}, f32[1184,256]{1,0:T(8,128)}, u32[]{:S(2)}, u32[]{:S(2)}) collective-permute-start(f32[1184,256]{1,0:T(8,128)S(1)} %get-tuple-element.117), channel_id=1, source_target_pairs={{0,1},{1,0},{2,3},{3,2},{4,5},{5,4},{6,7},{7,6},{8,9},{9,8},{10,11... | collective-permute-start | bytes 3637256 | tf_op jit(solution)/shard_map/ppermute | solution.py:428
  104.2 9.5 %collective-permute-start.8 = (bf16[592,256]{1,0:T(8,128)(2,1)S(1)}, bf16[592,256]{1,0:T(8,128)(2,1)S(1)}, u32[]{:S(2)}, u32[]{:S(2)}) collective-permute-start(bf16[592,256]{1,0:T(8,128)(2,1)S(1)} %dynamic-slice_convert_fusion), channel_id=1, source_target_pairs={{0,2},{1,3},{2,0},{3,1},{4,6},{5,7},{6,4},{7,5},{8,10},{9,11},{10,... | collective-permute-start | bytes 909320 | tf_op jit(solution)/shard_map/ppermute | solution.py:428
  113.9 5.5 %collective-permute-start.9 = (bf16[296,256]{1,0:T(8,128)(2,1)S(1)}, bf16[296,256]{1,0:T(8,128)(2,1)S(1)}, u32[]{:S(2)}, u32[]{:S(2)}) collective-permute-start(bf16[296,256]{1,0:T(8,128)(2,1)S(1)} %dynamic-slice_convert_fusion.2), channel_id=1, source_target_pairs={{0,4},{1,5},{2,6},{3,7},{4,0},{5,1},{6,2},{7,3},{8,12},{9,13},{10,... | collective-permute-start | bytes 454664 | tf_op jit(solution)/shard_map/ppermute | solution.py:428
  119.4 8.7 %collective-permute-start.10 = (bf16[296,256]{1,0:T(8,128)(2,1)S(1)}, bf16[296,256]{1,0:T(8,128)(2,1)S(1)}, u32[]{:S(2)}, u32[]{:S(2)}) collective-permute-start(bf16[296,256]{1,0:T(8,128)(2,1)S(1)} %fusion.5), channel_id=1, source_target_pairs={{0,8},{1,9},{2,10},{3,11},{4,12},{5,13},{6,14},{7,15},{8,0},{9,1},... | collective-permute-start | bytes 454664 | tf_op jit(solution)/shard_map/ppermute | solution.py:428
  128.1 5.5 %collective-permute-start.11 = (bf16[296,256]{1,0:T(8,128)(2,1)S(1)}, bf16[296,256]{1,0:T(8,128)(2,1)S(1)}, u32[]{:S(2)}, u32[]{:S(2)}) collective-permute-start(bf16[296,256]{1,0:T(8,128)(2,1)S(1)} %add_convert_fusion), channel_id=1, source_target_pairs={{0,4},{1,5},{2,6},{3,7},{4,0},{5,1},{6,2},{7,3},{8,12},{9,13},{10,... | collective-permute-start | bytes 454664 | tf_op jit(solution)/shard_map/ppermute | solution.py:428
  133.8 7.9 %collective-permute-start.12 = (bf16[592,256]{1,0:T(8,128)(2,1)S(1)}, bf16[592,256]{1,0:T(8,128)(2,1)S(1)}, u32[]{:S(2)}, u32[]{:S(2)}) collective-permute-start(bf16[592,256]{1,0:T(8,128)(2,1)S(1)} %maximum_select_fusion.3), channel_id=1, source_target_pairs={{0,2},{1,3},{2,0},{3,1},{4,6},{5,7},{6,4},{7,5},{8,10},{9,11},{10,... | collective-permute-start | bytes 909320 | tf_op jit(solution)/shard_map/ppermute | solution.py:428
  141.9 2.1 %collective-permute-start.13 = (bf16[1184,256]{1,0:T(8,128)(2,1)S(1)}, bf16[1184,256]{1,0:T(8,128)(2,1)S(1)}, u32[]{:S(2)}, u32[]{:S(2)}) collective-permute-start(bf16[1184,256]{1,0:T(8,128)(2,1)S(1)} %maximum_select_fusion.1.mine), channel_id=1, source_target_pairs={{0,1},{1,0},{2,3},{3,2},{4,5},{5,4},{6,7},{7,6},{8,9},{9,8},{10,11... | collective-permute-start | bytes 1818632 | tf_op jit(solution)/shard_map/ppermute | solution.py:428

commit v3 on v2

v3 whole, which is shorter than its diff:
```python
import functools
import math

import jax
import jax.numpy as jnp
from jax import lax
from jax.experimental import pallas as pl
from jax.experimental.pallas import tpu as pltpu
from jax.sharding import PartitionSpec as P

f32 = jnp.float32
bf16 = jnp.bfloat16
LOG2E = math.log2(math.e)
LOG_PULSE = math.log(0.7)
NT = (((1,), (1,)), ((), ()))
TN = (((0,), (0,)), ((), ()))


def dot(a, b, dims=(((1,), (0,)), ((), ()))):
    return lax.dot_general(a, b, dims, preferred_element_type=f32)


def split(x, terms):
    parts = []
    for _ in range(terms):
        part = x.astype(bf16)
        parts.append(part)
        x = x - part.astype(f32)
    return parts


def iota(shape, axis):
    return lax.broadcasted_iota(jnp.int32, shape, axis)


def spread_matrix(rows, heads, channels):
    size = channels // heads
    return (iota((rows, channels), 0) % heads == iota((rows, channels), 1) // size).astype(bf16)


def spread(values, sensor, heads, spread2):
    lane = iota(values.shape, 1)
    own = jnp.where(lane // heads == sensor, values, 0.0)
    return dot(jnp.concatenate(split(own, 2), axis=1), spread2)


def front_kernel(
    me_ref, readings, graph, cluster, mix, marks, w_channels, w_state, w_step_t, bias, fading_exponent, skip_gain, norm_gain, cot_hbm, w_out_hbm,
    mixed_ref, channels_ref, maps_ref, step_ref, cum_ref, cum_t_ref, keep_ref, send_ref, tail_ref, token_ref, consts_ref, cot_ref, w_out_ref,
    kmix, wms, spread2, rows_sc, state_sc, log_sc, sems, *, heads,
):
    i = pl.program_id(0)
    sensors, chunk, width = readings.shape
    rows = sensors * chunk
    maps = w_state.shape[1]
    nstate = maps // 2
    channels = w_channels.shape[1]
    lanes = sensors * heads
    last_step = pl.num_programs(0) - 1
    each = cot_ref.shape[0] // (cot_ref.shape[1] // chunk)

    def cot_copy(k):
        part = pl.ds(k * each, each)
        return pltpu.make_async_copy(cot_hbm.at[part], cot_ref.at[part], sems.at[k])

    w_out_copy = pltpu.make_async_copy(w_out_hbm, w_out_ref, sems.at[cot_ref.shape[1] // chunk])
    cot_copy(i).start()

    @pl.when(i == last_step)
    def _():
        w_out_copy.start()

    @pl.when(i == 0)
    def _():
        token_ref[...] = jnp.zeros_like(token_ref)
        wms[...] = jnp.zeros_like(wms)
        wms[:, 0:maps] = w_state[...]
        wms[:, maps : maps + heads] = w_step_t[...].astype(f32).T.astype(bf16)
        spread2[...] = spread_matrix(spread2.shape[0], heads, channels)
        picked = (iota((sensors, sensors), 0) == cluster[...]).astype(bf16)
        linked = dot(dot(picked, graph[...].astype(f32).astype(bf16), TN).astype(bf16), picked)
        coupling = (linked * mix[...]).astype(bf16)
        sensor_of = (iota((rows, sensors), 0) // chunk == iota((rows, sensors), 1)).astype(bf16)
        full = dot(dot(sensor_of, coupling).astype(bf16), sensor_of, NT)
        same = iota((rows, rows), 0) % chunk == iota((rows, rows), 1) % chunk
        kmix[...] = jnp.where(same, full, 0.0).astype(bf16)
        tiled = (iota((heads, lanes), 1) % heads == iota((heads, lanes), 0)).astype(bf16)
        both = jnp.concatenate([bias[...], -jnp.exp(fading_exponent[...]) * LOG2E], axis=0)
        rows_sc[0:2, :] = sum(dot(part, tiled) for part in split(both, 3))
        consts_ref[...] = jnp.zeros_like(consts_ref)
        consts_ref[0:1, :] = sum(dot(part, spread2[0:heads, :]) for part in split(skip_gain[...], 3))
        consts_ref[1:2, :] = norm_gain[...]

    x = readings[...].reshape(rows, width)
    mixed = (x.astype(f32) + dot(kmix[...], x)).astype(bf16)
    here = pl.ds(pl.multiple_of(i * chunk, chunk), chunk)
    mixed_ref[:, here, :] = mixed.reshape(sensors, chunk, width)
    channels_ref[:, here, :] = dot(mixed, w_channels[...]).astype(bf16).reshape(sensors, chunk, channels)
    small = dot(mixed, wms[...])
    maps_ref[:, here, :] = small[:, 0:maps].astype(bf16).reshape(sensors, chunk, maps)
    steps = small[:, maps:].reshape(sensors, chunk, lanes)
    packed = steps[0]
    for s in range(1, sensors):
        packed = packed + pltpu.roll(steps[s], heads * s, 1)
    raw = (packed + rows_sc[0:1, :]).astype(bf16).astype(f32)
    step = jnp.maximum(raw, 0.0) + jnp.log1p(jnp.exp(-jnp.abs(raw)))
    step_ref[here, :] = step
    log_sc[here, :] = rows_sc[1:2, :] * step

    @pl.when(i == pl.num_programs(0) - 1)
    def _():
        span = log_sc.shape[0]
        at, to = iota((span, span), 0), iota((span, span), 1)
        marked = jnp.sum(jnp.where(at == to, marks[...].astype(f32), 0.0), axis=1, keepdims=True)
        log_decay = log_sc[...] + (LOG_PULSE * LOG2E) * marked
        lower = (at >= to).astype(bf16)
        cum = sum(dot(lower, part) for part in split(log_decay, 3))
        cum_ref[...] = cum
        cum_t_ref[...] = cum.T
        last = cum[span - 1 : span, :]
        weight = jnp.exp2(last - cum) * step_ref[...]

        def one(s, carry):
            scale = spread(weight, s, heads, spread2[...])
            scaled = (channels_ref[s].astype(f32) * scale).astype(bf16)
            state = dot(maps_ref[s], scaled, TN)
            state_sc[s] = state[0:nstate]
            return carry

        lax.fori_loop(0, sensors, one, 0, unroll=4)
        own = jnp.where(iota((sensors, lanes), 1) // heads == iota((sensors, lanes), 0), last, 0.0)
        tail = sum(dot(part, spread2[0:lanes, :]) for part in split(own, 3))
        tail_ref[...] = tail
        half = sensors // 2
        mine = (me_ref[0] & 1) * half
        other = half - mine
        keep_ref[...] = state_sc[pl.ds(mine, half)]
        send_ref[0 : half * nstate, :] = state_sc[pl.ds(other, half)].reshape(half * nstate, channels).astype(bf16)
        send_ref[half * nstate :, :] = tail.astype(bf16)
        for k in range(cot_ref.shape[1] // chunk):
            cot_copy(k).wait()
        w_out_copy.wait()


def pair_blocks(x, size):
    lane = iota(x.shape, 1)
    zero = jnp.zeros_like(x)
    return jnp.concatenate([jnp.where(lane < size, x, zero), jnp.where(lane >= size, x, zero)], axis=0)


def within_kernel(channels, maps, step, cum_t, cot, w_out, consts, *refs, heads, first, count, aliases):
    part_ref, scaled_ref, decay_ref, grad_ref, _, spread2 = refs[aliases:]
    _, span, width = channels.shape
    nstate = maps.shape[2] // 2
    size = width // heads
    spread2[...] = spread_matrix(spread2.shape[0], heads, width)

    def block(i, carry):
        here = pl.ds((first + i) * GROUP, GROUP)
        grad = dot(cot[here].reshape(GROUP * span, cot.shape[2]), w_out[...], NT)
        grad_ref[here] = grad.reshape(GROUP, span, width)
        causal = iota((span, span), 0) >= iota((span, span), 1)
        for k in range(GROUP):
            s = (first + i) * GROUP + k
            chan = channels[s].astype(f32)
            scaled = (chan * spread(step[...], s, heads, spread2[...])).astype(bf16)
            scaled_ref[s] = scaled
            both = maps[s]
            scores = dot(both[:, nstate:], both[:, 0:nstate], NT)
            row = cum_t[pl.ds(pl.multiple_of(s * heads, heads), heads), :]
            col = row.T
            for pair in range(heads // 2):
                weighted = []
                for h in (2 * pair, 2 * pair + 1):
                    gap = jnp.broadcast_to(col[:, h : h + 1], (span, span)) - row[h : h + 1, :]
                    decay = jnp.exp2(jnp.where(causal, gap, -jnp.inf))
                    decay_ref[s, h] = decay.astype(bf16)
                    weighted.append((scores * decay).astype(bf16))
                lanes = slice(2 * pair * size, 2 * (pair + 1) * size)
                out = dot(jnp.concatenate(weighted, axis=1), pair_blocks(scaled[:, lanes], size))
                part_ref[s, :, lanes] = out + consts[0:1, lanes] * chan[:, lanes]
        return carry

    lax.fori_loop(0, count, block, 0)


def back_kernel(me_ref, state, maps, scaled, decay, part, grad, cum, consts, *refs, heads, aliases, first):
    normed_ref, read_ref, gain_ref, _, spread2 = refs[aliases:]
    _, span, width = part.shape
    nstate = maps.shape[2] // 2
    size = width // heads
    spread2[...] = spread_matrix(spread2.shape[0], heads, width)
    gain = consts[1:2, :]
    begin = first(me_ref[0])

    def sensor(k, gain_sum):
        s = begin + k
        both = maps[s]
        fade_s = spread(jnp.exp2(cum[...]), s, heads, spread2[...])
        out = part[s] + dot(both[:, nstate:], state[k]) * fade_s
        inv = lax.rsqrt(jnp.mean(out * out, axis=-1, keepdims=True) + 1e-05)
        normed = out * inv
        normed_ref[s] = (normed * gain).astype(bf16)
        g = grad[s]
        by_gain = normed * g
        gain_sum = gain_sum + jnp.sum(by_gain.reshape(span // 8, 8, width), axis=0)
        mean = jnp.mean(by_gain * gain, axis=-1, keepdims=True)
        back = inv * (g * gain - normed * mean)
        back16 = back.astype(bf16)
        carried = dot((back * fade_s).astype(bf16), state[k], NT)
        pairs = jnp.zeros((span, span), f32)
        for pair in range(heads // 2):
            lanes = slice(2 * pair * size, 2 * (pair + 1) * size)
            both_heads = dot(back16[:, lanes], pair_blocks(scaled[s, :, lanes], size), NT)
            pairs = pairs + both_heads[:, 0:span] * decay[s, 2 * pair].astype(f32)
            pairs = pairs + both_heads[:, span:] * decay[s, 2 * pair + 1].astype(f32)
        inner = dot(pairs.astype(bf16), both[:, 0:nstate])
        read_ref[s] = (carried + inner).astype(bf16)
        return gain_sum

    gain_ref[...] = lax.fori_loop(0, state.shape[0], sensor, jnp.zeros(gain_ref.shape, f32), unroll=2)


def grads_kernel(me_ref, normed, cot, read, mixed, *refs):
    *gains, keep_ref, send_ref, total = refs
    sensors, span, channels = normed.shape
    width, nstate = cot.shape[2], read.shape[2]
    piece = total.shape[1]
    pieces = width // piece
    rows = sensors * span

    total[pieces * (channels + nstate) :, :] = jnp.zeros((total.shape[0] - pieces * (channels + nstate), piece), f32)
    gain = sum(jnp.sum(ref[...], axis=0, keepdims=True) for ref in gains)
    for j in range(channels // piece):
        at = pieces * (channels + nstate) + j
        total[at : at + 1, :] = gain[:, j * piece : (j + 1) * piece]
    for j in range(pieces):
        lanes = slice(j * piece, (j + 1) * piece)
        right = cot[:, :, lanes].reshape(rows, piece)
        total[j * channels : (j + 1) * channels, :] = dot(normed[...].reshape(rows, channels), right, TN)
        at = pieces * channels + j * nstate
        total[at : at + nstate, :] = dot(read[...].reshape(rows, nstate), mixed[:, :, lanes].reshape(rows, piece), TN)
    half = keep_ref.shape[0]
    mine = pl.multiple_of((me_ref[0] & 1) * half, 8)
    other = pl.multiple_of(half - (me_ref[0] & 1) * half, 8)
    keep_ref[...] = total[pl.ds(mine, half), :]
    send_ref[...] = total[pl.ds(other, half), :].astype(bf16)


def finish_kernel(me_ref, mine, came, out_ref, read_ref, gain_ref):
    channels, width = out_ref.shape
    nstate = read_ref.shape[0]
    half, piece = mine.shape
    pieces = width // piece

    def write(low, high):
        def rows(start, size):
            parts = []
            if start < half:
                parts.append(low[start : min(start + size, half), :])
            if start + size > half:
                parts.append(high[max(start - half, 0) : start + size - half, :])
            return jnp.concatenate([part.astype(f32) for part in parts], axis=0)

        for j in range(pieces):
            lanes = slice(j * piece, (j + 1) * piece)
            out_ref[:, lanes] = rows(j * channels, channels)
            read_ref[:, lanes] = rows(pieces * channels + j * nstate, nstate)
        tail = rows(pieces * (channels + nstate), 8)
        for j in range(channels // piece):
            gain_ref[:, j * piece : (j + 1) * piece] = tail[j : j + 1, :]

    pl.when(me_ref[0] & 1 == 0)(lambda: write(mine, came))
    pl.when(me_ref[0] & 1 == 1)(lambda: write(came, mine))


def whole(shape):
    return pl.BlockSpec(shape, lambda *_: (0,) * len(shape), pipeline_mode=pl.Buffered(1))


ANYWHERE = pl.BlockSpec(memory_space=pl.ANY)
HELD = pl.BlockSpec(memory_space=pltpu.VMEM)
GROUP = 2


def held(x):
    return pltpu.with_memory_space_constraint(x, pltpu.VMEM)


def call(body, name, scalars, grid, in_specs, out_specs, out_shape, scratch, vmem, flops, moved, aliases=None):
    return pl.pallas_call(
        body,
        name=name,
        grid_spec=pltpu.PrefetchScalarGridSpec(
            num_scalar_prefetch=scalars, grid=grid, in_specs=in_specs, out_specs=out_specs, scratch_shapes=scratch
        ),
        out_shape=out_shape,
        input_output_aliases=aliases or {},
        compiler_params=pltpu.CompilerParams(vmem_limit_bytes=vmem << 20),
        cost_estimate=pl.CostEstimate(flops=int(flops), bytes_accessed=int(moved), transcendentals=0),
    )


def front(
    me, readings, graph, cluster, mix, boundaries, w_channels, w_state, w_step, bias, fading_exponent, skip_gain, gain,
    cot, w_out,
):
    sensors, span, width = readings.shape
    heads, channels, maps = w_step.shape[1], w_channels.shape[1], w_state.shape[1]
    nstate, lanes, chunk = maps // 2, sensors * heads, 16
    rows, half_rows = sensors * chunk, sensors // 2 * nstate
    small = [
        graph, cluster[None, :], mix, boundaries[None, :], w_channels, w_state, w_step.T,
        bias[None, :], fading_exponent[None, :], skip_gain[None, :], gain[None, :],
    ]
    outs = [
        ((sensors, span, width), bf16), ((sensors, span, channels), bf16), ((sensors, span, maps), bf16),
        ((span, lanes), f32), ((span, lanes), f32), ((lanes, span), f32),
        ((sensors // 2, nstate, channels), f32), ((half_rows + sensors, channels), bf16), ((sensors, channels), f32),
        ((8, 128), f32), ((8, channels), f32), (cot.shape, cot.dtype), (w_out.shape, w_out.dtype),
    ]
    return call(
        functools.partial(front_kernel, heads=heads), "front", 1, (span // chunk,),
        [pl.BlockSpec((sensors, chunk, width), lambda i, *_: (0, i, 0))] + [whole(x.shape) for x in small] + [ANYWHERE] * 2,
        [HELD] * len(outs),
        [pltpu.VMEM(shape, dtype) for shape, dtype in outs],
        [
            pltpu.VMEM((rows, rows), bf16), pltpu.VMEM((width, maps + lanes), bf16),
            pltpu.VMEM((2 * lanes, channels), bf16), pltpu.VMEM((8, lanes), f32),
            pltpu.VMEM((sensors, nstate, channels), f32), pltpu.VMEM((span, lanes), f32),
            pltpu.SemaphoreType.DMA((span // chunk + 1,)),
        ],
        14, 5e9, 14e6,
    )(me, *[pltpu.with_memory_space_constraint(x, pltpu.HBM) for x in [readings] + small + [cot, w_out]])


def within(first, count, channels, maps, step, cum_t, cot, w_out, consts, heads, done, token):
    sensors, span, width = channels.shape
    lanes = sensors * heads
    n_in = 7
    aliases = {n_in + k: k for k in range(len(done))}
    aliases[n_in + len(done)] = 4
    return call(
        functools.partial(within_kernel, heads=heads, first=first, count=count, aliases=len(done) + 1),
        "within", 0, (),
        [HELD] * (n_in + len(done)) + [ANYWHERE],
        [HELD] * 4 + [ANYWHERE],
        [
            pltpu.VMEM((sensors, span, width), f32), pltpu.VMEM((sensors, span, width), bf16),
            pltpu.VMEM((sensors, heads, span, span), bf16), pltpu.VMEM((sensors, span, width), f32),
            jax.ShapeDtypeStruct(token.shape, token.dtype),
        ],
        [pltpu.VMEM((2 * lanes, width), bf16)],
        6, 6e8 * count, 3e6 * count, aliases,
    )(*[held(x) for x in (channels, maps, step, cum_t, cot, w_out, consts) + done], token)


def back(me, first, state, maps, scaled, decay, part, grad, cum, consts, done, token):
    sensors, span, width = part.shape
    heads, nmaps = decay.shape[1], maps.shape[2]
    nstate, lanes = nmaps // 2, sensors * heads
    count = state.shape[0]
    n_in = 9
    aliases = {n_in + k: k for k in range(len(done))}
    aliases[n_in + len(done)] = 3
    return call(
        functools.partial(back_kernel, heads=heads, aliases=len(done) + 1, first=first), "back", 1, (),
        [HELD] * (n_in - 1 + len(done)) + [ANYWHERE],
        [HELD] * 3 + [ANYWHERE],
        [
            pltpu.VMEM((sensors, span, width), bf16), pltpu.VMEM((sensors, span, nstate), bf16),
            pltpu.VMEM((8, width), f32), jax.ShapeDtypeStruct(token.shape, token.dtype),
        ],
        [pltpu.VMEM((2 * lanes, width), bf16)],
        6, 3e8 * count, 1.5e6 * count, aliases,
    )(me, *[held(x) for x in (state, maps, scaled, decay, part, grad, cum, consts) + done], token)


def grads(me, normed, cot, read, mixed, gains):
    channels, width, nstate = normed.shape[2], cot.shape[2], read.shape[2]
    piece = 256
    rows = -(-(width // piece * (channels + nstate) + channels // piece) // 64) * 64
    return call(
        grads_kernel, "grads", 1, (),
        [HELD] * (4 + len(gains)),
        [HELD] * 2,
        [pltpu.VMEM((rows // 2, piece), f32), pltpu.VMEM((rows // 2, piece), bf16)],
        [pltpu.VMEM((rows, piece), f32)],
        14, 2.5e9, 14e6,
    )(me, *[held(x) for x in (normed, cot, read, mixed, *gains)])


def finish(me, mine, came, channels, width, nstate):
    return call(
        finish_kernel, "finish", 1, (1,),
        [whole(mine.shape)] * 2,
        [whole((channels, width)), whole((nstate, width)), whole((1, channels))],
        [
            jax.ShapeDtypeStruct((channels, width), f32), jax.ShapeDtypeStruct((nstate, width), f32),
            jax.ShapeDtypeStruct((1, channels), f32),
        ],
        [], 8, 1e6, 4e6,
    )(me, mine, came)


def swap(x, distance, count):
    return lax.ppermute(x, "seq", [(i, i ^ distance) for i in range(count)])


def narrow(x):
    return lax.reduce_precision(x, 8, 7)


def pick(bit, when_one, when_zero):
    return jnp.where(bit == 1, when_one, when_zero)


def tied(x, token):
    return lax.optimization_barrier((x, token))


def bit_of(me, level):
    return (me >> level) & 1


def shard_start(me, level, sensors):
    return sum(bit_of(me, k) * (sensors >> (k + 1)) for k in range(level + 1))


def row(ref, k):
    return ref[pl.ds(k, 1), :]


def rise_kernel(me_ref, own, tail, came, low_ref, low_tail_ref, tail_ref, next_ref, send_ref, other_tail, *, level, last):
    me = me_ref[0]
    bit = bit_of(me, level)
    size, nstate, width = own.shape
    sensors = tail.shape[0]
    start = shard_start(me, level, sensors)
    other_tail[...] = came[size * nstate :, :].astype(f32)
    low_tail_ref[...] = pick(bit, other_tail[...], tail[...])
    total_tail = tail[...] + other_tail[...]
    tail_ref[...] = total_tail

    def total(j):
        other = came[pl.ds(pl.multiple_of(j * nstate, nstate), nstate), :].astype(f32)
        low, high = pick(bit, other, own[j]), pick(bit, own[j], other)
        low_ref[j] = low
        fade = jnp.exp2(pick(bit, row(tail, start + j), row(other_tail, start + j)))
        return low * fade + high

    half = next_ref.shape[0]
    mine = 0 if last else bit_of(me, level + 1) * half
    for j in range(half):
        kept = total(mine + j)
        next_ref[j] = kept
        gone = kept if last else total(half - mine + j)
        send_ref[j * nstate : (j + 1) * nstate, :] = gone.astype(bf16)
    send_ref[half * nstate :, :] = total_tail.astype(bf16)


def rise(me, own, tail, came, level, last):
    size, nstate, width = own.shape
    half = size if last else size // 2
    return call(
        functools.partial(rise_kernel, level=level, last=last), "rise", 1, (),
        [HELD] * 3, [HELD] * 5,
        [
            pltpu.VMEM(own.shape, f32), pltpu.VMEM(tail.shape, f32), pltpu.VMEM(tail.shape, f32),
            pltpu.VMEM((half, nstate, width), f32), pltpu.VMEM((half * nstate + tail.shape[0], width), bf16),
        ],
        [pltpu.VMEM(tail.shape, f32)], 6, 1e6, 1e6,
    )(me, *[held(x) for x in (own, tail, came)])


def across_kernel(
    me_ref, own, tail, before, before_tail, came, next_ref, tail_ref, before_ref, before_tail_ref, send_ref, other_tail,
    *, level, shards,
):
    me = me_ref[0]
    bit = bit_of(me, level)
    size, nstate, width = own.shape
    start = shard_start(me, shards - 1, tail.shape[0])
    other_tail[...] = came[size * nstate :, :].astype(f32)
    before_tail_ref[...] = before_tail[...] + pick(bit, other_tail[...], jnp.zeros_like(other_tail))
    total_tail = tail[...] + other_tail[...]
    tail_ref[...] = total_tail
    for j in range(size):
        other = came[j * nstate : (j + 1) * nstate, :].astype(f32)
        passed = other * jnp.exp2(row(before_tail, start + j)) + before[j]
        before_ref[j] = pick(bit, passed, before[j])
        low, high = pick(bit, other, own[j]), pick(bit, own[j], other)
        total = low * jnp.exp2(pick(bit, row(tail, start + j), row(other_tail, start + j))) + high
        next_ref[j] = total
        send_ref[j * nstate : (j + 1) * nstate, :] = total.astype(bf16)
    send_ref[size * nstate :, :] = total_tail.astype(bf16)


def across(me, own, tail, before, before_tail, came, level, shards):
    return call(
        functools.partial(across_kernel, level=level, shards=shards), "across", 1, (),
        [HELD] * 5, [HELD] * 5,
        [
            pltpu.VMEM(own.shape, f32), pltpu.VMEM(tail.shape, f32), pltpu.VMEM(own.shape, f32),
            pltpu.VMEM(tail.shape, f32), pltpu.VMEM(came.shape, bf16),
        ],
        [pltpu.VMEM(tail.shape, f32)], 6, 1e6, 1e6,
    )(me, *[held(x) for x in (own, tail, before, before_tail, came)])


def fall_kernel(me_ref, *refs, level, first, last_across, ways):
    me = me_ref[0]
    lows, tails = refs[: level + 1], refs[level + 1 : 2 * (level + 1)]
    refs = refs[2 * (level + 1) :]
    sensors = tails[0].shape[0]
    low = lows[level]
    size, nstate, width = low.shape
    start = shard_start(me, level, sensors)

    def step(state, q, sensor):
        at = sensor - shard_start(me, q, sensors)
        return state * jnp.exp2(row(tails[q], sensor)) + lows[q][at]

    def split_at(j, before, state_ref, k):
        after = step(before, level, start + j)
        bit = bit_of(me, level)
        mine = pick(bit, after, before)
        mine_ref[j] = mine
        gone_ref[j] = pick(bit, before, after).astype(bf16)
        if state_ref is not None:
            for q in reversed(range(level)):
                mine = pick(bit_of(me, q), step(mine, q, start + j), mine)
            state_ref[k] = mine.astype(bf16)

    if first:
        came, mine_ref, gone_ref, state_ref = refs
        for j in range(size):
            if last_across is None:
                before = came[j]
            else:
                other = came[j * nstate : (j + 1) * nstate, :].astype(f32)
                before = pick(bit_of(me, last_across), other, jnp.zeros_like(other))
            split_at(j, before, state_ref, j)
    else:
        had, came, mine_ref, gone_ref, state_ref = refs
        half = size // 2
        at = bit_of(me, level + 1) * half
        for k in range(half):
            split_at(at + k, had[k], None, k)
            split_at(half - at + k, came[k].astype(f32), state_ref, k)


def fall(me, saved, level, had, came, last_across):
    lows = [low for low, _ in saved[: level + 1]]
    tails = [tail for _, tail in saved[: level + 1]]
    size, nstate, width = lows[level].shape
    first = had is None
    arrays = lows + tails + ([came] if first else [had, came])
    return call(
        functools.partial(fall_kernel, level=level, first=first, last_across=last_across, ways=len(saved)), "fall", 1, (),
        [HELD] * len(arrays), [HELD] * 3,
        [
            pltpu.VMEM((size, nstate, width), f32), pltpu.VMEM((size, nstate, width), bf16),
            pltpu.VMEM((size if first else size // 2, nstate, width), bf16),
        ],
        [], 6, 1e6, 1e6,
    )(me, *[held(x) for x in arrays])


def exchange(keep, send, tail, me, count, shards, swap_beside, ready):
    sensors = tail.shape[0]
    levels = count.bit_length() - 1
    own = keep
    saved = []
    for level in range(shards):
        came = swap_beside(send, level, True)
        low, low_tail, tail, own, send = rise(me, own, tail, came, level, level + 1 == shards)
        saved.append((low, low_tail))
    if levels == shards + 1:
        came = swap_beside(send, shards, True)
        parts = (None, came, shards)
    else:
        before, before_tail = jnp.zeros_like(own), jnp.zeros_like(tail)
        for level in range(shards, levels):
            came = swap_beside(send, level, True)
            own, tail, before, before_tail, send = across(me, own, tail, before, before_tail, came, level, shards)
        parts = (None, before, None)
    for level in reversed(range(shards)):
        mine, gone, states = fall(me, saved, level, *parts)

        def first(at, level=level):
            if level + 1 == shards:
                return shard_start(at, level, sensors)
            size = sensors >> (level + 2)
            return shard_start(at, level + 1, sensors) + pick(bit_of(at, level + 1), -size, size)

        ready(states, first, False)
        came = swap_beside(gone, level, False)
        parts = (mine, came, None)
    ready(came, lambda at: (1 - bit_of(at, 0)) * (sensors // 2), True)


def all_sum(keep, send, me, count, shards):
    levels = count.bit_length() - 1
    own = keep
    for level in range(shards):
        came = swap(send, 1 << level, count)
        own = own + came.astype(f32)
        if level + 1 < shards:
            bit = (me >> (level + 1)) & 1
            size = own.shape[0] // 2
            send = lax.dynamic_slice_in_dim(own, (1 - bit) * size, size, 0).astype(bf16)
            own = lax.dynamic_slice_in_dim(own, bit * size, size, 0)
    for level in range(shards, levels):
        own = narrow(own)
        own = own + swap(own.astype(bf16), 1 << level, count).astype(f32)
    out = own.astype(bf16)
    for level in reversed(range(1, shards)):
        bit = (me >> level) & 1
        came = swap(out, 1 << level, count)
        out = pick(bit, jnp.concatenate([came, out], axis=0), jnp.concatenate([out, came], axis=0))
    return out, swap(out, 1, count)


def per_device(
    count, readings, block_graph, cluster_of, mix_weight, boundaries, w_channels, w_state, w_step,
    step_bias, channel_fading_exponent, skip_gain, norm_gain, w_out, cotangent,
):
    sensors, span, width = readings.shape
    channels = w_channels.shape[1]
    nstate = w_state.shape[1] // 2
    me = lax.axis_index("seq").astype(jnp.int32)
    at = me[None]
    shards = min(max(count.bit_length() - 2, 1), 3)
    heads = skip_gain.shape[0]

    mixed, chans, maps, step, cum, cum_t, keep, send, tail, token, consts, cot, w_out = front(
        at, readings, block_graph, cluster_of, mix_weight, boundaries, w_channels, w_state, w_step,
        step_bias, channel_fading_exponent, skip_gain, norm_gain, cotangent, w_out,
    )
    work = {"token": token, "within": (), "back": (), "gains": [], "next": None}
    plan = {1: (0, 3), 2: (3, 2), 3: (5, 3)}

    def run_back():
        states, first = work["next"]
        part, scaled, decay, grad = work["within"]
        normed, read, gain, work["token"] = back(
            at, first, states, maps, scaled, decay, part, grad, cum, consts, work["back"], work["token"]
        )
        work["back"] = (normed, read)
        work["gains"].append(gain)

    def swap_beside(x, level, up):
        x, work["token"] = tied(x, work["token"])
        came = swap(x, 1 << level, count)
        if not up:
            run_back()
        elif level in plan:
            first, blocks = plan[level]
            *arrays, work["token"] = within(
                first, blocks, chans, maps, step, cum_t, cot, w_out, consts, heads, work["within"], work["token"]
            )
            work["within"] = tuple(arrays)
        return came

    def ready(states, first, last):
        work["next"] = (states, first)
        if last:
            run_back()

    exchange(keep, send, tail, at, count, shards, swap_beside, ready)
    keep_sum, send_sum = grads(at, work["back"][0], cot, work["back"][1], mixed, work["gains"])
    mine, came = all_sum(keep_sum, send_sum, me, count, shards)
    grad_out, grad_read, grad_gain = finish(at, mine, came, channels, width, nstate)
    return grad_out, grad_read.T, grad_gain[0]


def solution(mesh):
    in_specs = (
        P("groups", "seq", None), P("groups", None), P("groups"), P(), P(("groups", "seq")),
        P(), P(), P(), P(), P(), P(), P(), P(), P("groups", "seq", None),
    )
    out_specs = (P("groups", None), P("groups", None), P("groups"))
    return jax.shard_map(
        functools.partial(per_device, mesh.shape["seq"]),
        mesh=mesh, in_specs=in_specs, out_specs=out_specs, check_vma=False,
    )
```

time: 147 us -> 111 us (0.76)
  Pallas kernels: 62.5 us -> 42.5 us
  other arithmetic: 12.5 us -> 0.65 us
  local copies, waits for them, and re-layouts: 6.8 us -> 0.07 us
  waiting for transfers between devices: 50.9 us -> 52.9 us
  starting transfers between devices: 11.9 us -> 13.8 us
    pallas_call x10 -> x16, Pallas kernels: 62.5 us -> 42.5 us  [the longest x1 14.7 us: front(): call(functools.partial(front_kernel, heads=heads), 'front', 1, (span // c...]
    unnamed x28 -> x0, local copies, waits for them, and re-layouts: 5.7 us -> none
    convert_element_type x12 -> x0, other arithmetic: 4.84 us -> none  [the longest x3 1.54 us: pack(): tails.astype(bf16)]
    select_n x5 -> x2, other arithmetic: 2.85 us -> 0.36 us  [pick(): return jnp.where(bit == 1, when_one, when_zero)]
    add x2 -> x0, other arithmetic: 2.24 us -> none  [exchange(): total = low * fading(high_tail, start, low) + high]
    ppermute x14, waiting for transfers between devices: 50.9 us -> 52.9 us  [swap(): return lax.ppermute(x, 'seq', [(i, i ^ distance) for i in range(count)])]
    ppermute x14, starting transfers between devices: 11.9 us -> 13.8 us  [swap(): return lax.ppermute(x, 'seq', [(i, i ^ distance) for i in range(count)])]
  transfers between devices with their start and end apart: 14 -> 14, of which waited for: 11 -> 13; matrix products, arithmetic and copies ran while one was open for 0% -> 0% of each run, Pallas kernels for 18% -> 13%
where the time goes in v3:
time: 111 us
  waiting for transfers between devices  52.9 us (48%)
  Pallas kernels  42.5 us (38%)
  starting transfers between devices  13.8 us (12%)
    ppermute x14, waiting for transfers between devices, swap(): return lax.ppermute(x, 'seq', [(i, i ^ distance) for i in range(count)])  52.9 us
    pallas_call x1, Pallas kernels, front(): call(functools.partial(front_kernel, heads=heads), 'front', 1, (span // c...  14.7 us
    ppermute x14, starting transfers between devices, swap(): return lax.ppermute(x, 'seq', [(i, i ^ distance) for i in range(count)])  13.8 us
    pallas_call x4, Pallas kernels, back(): call(functools.partial(back_kernel, heads=heads, aliases=len(done) + 1, f...  11.2 us
    pallas_call x3, Pallas kernels, within(): call(functools.partial(within_kernel, heads=heads, first=first, count=cou...  8.75 us
    pallas_call x1, Pallas kernels, grads(): call(grads_kernel, 'grads', 1, (), [HELD] * (4 + len(gains)), [HELD] * 2,...  3.45 us
  transfers between devices with their start and end apart: 14, of which 13 were waited for; matrix products, arithmetic and copies ran while one was open for 0% of the time, Pallas kernels for 13%

profile of v3, /device:TPU:0, one launch (start us, length us, event | category | flops | bytes accessed | tf_op | source)
XLA Modules:
  0.0 110.7 jit_solution(7040229869129670638)
XLA Ops:
  0.6 14.7 %front.1 = (bf16[16,128,1024]{2,1,0:T(8,128)(2,1)S(1)}, bf16[16,128,512]{2,1,0:T(8,128)(2,1)S(1)}, bf16[16,128,128]{2,1,0:T(8,128)(2,1)S(1)}, f32[128,128]{1,0:T...) custom-call(s32[1]{0:T(128)} %bitcast.me_ref, ...), custom_call_target="tpu_custom_call" | custom-call | flops 5000000000 | bytes 14000000 | tf_op jit(solution)/shard_map/front/pallas_call | solution.py:322
  15.3 0.5 collective-permute-start
  15.9 1.6 %collective-permute-done.came = bf16[528,512]{1,0:T(8,128)(2,1)S(1)} collective-permute-done((bf16[528,512]{1,0:T(8,128)(2,1)S(1)}, bf16[528,512]{1,0:T(8,128)(2,1)S(1)}, u32[]{:S(2)}, u32[]{:S(2)}) %collective-permute-start) | collective-permute-done | bytes 540704 | tf_op jit(solution)/shard_map/ppermute | solution.py:407
  17.4 0.3 rise.3
  17.8 2.9 %collective-permute-start.1 = (bf16[272,512]{1,0:T(8,128)(2,1)S(1)}, bf16[272,512]{1,0:T(8,128)(2,1)S(1)}, u32[]{:S(2)}, u32[]{:S(2)}) collective-permute-start(bf16[272,512]{1,0:T(8,128)(2,1)S(1)} %get-tuple-element.97), channel_id=1, source_target_pairs={{0,2},{1,3},{2,0},{3,1},{4,6},{5,7},{6,4},{7,5},{8,10},{9,11},{10,... | collective-permute-start | bytes 835592 | tf_op jit(solution)/shard_map/ppermute | solution.py:407
  20.7 3.3 %within.3 = (f32[16,128,512]{2,1,0:T(8,128)S(1)}, bf16[16,128,512]{2,1,0:T(8,128)(2,1)S(1)}, bf16[16,8,128,128]{3,2,1,0:T(8,128)(2,1)S(1)}, f32[16,128,512]{2,1,0:T(8,128)S(1)}, f32[8,128]{1,0:T(8,128)S(1)}) custom-call(bf16[16,128,512]{2,1,0:T(8,128)(2,1)S(1)} %get-tuple-element.103.channels, ...), custom_call_target="tpu_custom_call", output_to_operand_aliasing={{4}: (7, {})} | custom-call | flops 1800000000 | bytes 9000000 | tf_op jit(solution)/shard_map/within/pallas_call | solution.py:343
  24.0 3.7 %collective-permute-done.1.came = bf16[272,512]{1,0:T(8,128)(2,1)S(1)} collective-permute-done((bf16[272,512]{1,0:T(8,128)(2,1)S(1)}, bf16[272,512]{1,0:T(8,128)(2,1)S(1)}, u32[]{:S(2)}, u32[]{:S(2)}) %collective-permute-start.1) | collective-permute-done | bytes 278560 | tf_op jit(solution)/shard_map/ppermute | solution.py:407
  27.6 0.2 rise.4
  27.8 1.9 %collective-permute-start.2 = (bf16[144,512]{1,0:T(8,128)(2,1)S(1)}, bf16[144,512]{1,0:T(8,128)(2,1)S(1)}, u32[]{:S(2)}, u32[]{:S(2)}) collective-permute-start(bf16[144,512]{1,0:T(8,128)(2,1)S(1)} %get-tuple-element.112), channel_id=1, source_target_pairs={{0,4},{1,5},{2,6},{3,7},{4,0},{5,1},{6,2},{7,3},{8,12},{9,13},{10,... | collective-permute-start | bytes 442376 | tf_op jit(solution)/shard_map/ppermute | solution.py:407
  29.7 2.2 %within.4 = (f32[16,128,512]{2,1,0:T(8,128)S(1)}, bf16[16,128,512]{2,1,0:T(8,128)(2,1)S(1)}, bf16[16,8,128,128]{3,2,1,0:T(8,128)(2,1)S(1)}, f32[16,128,512]{2,1,0:T(8,128)S(1)}, f32[8,128]{1,0:T(8,128)S(1)}) custom-call(bf16[16,128,512]{2,1,0:T(8,128)(2,1)S(1)} %get-tuple-element.103.c, ...), custom_call_target="tpu_custom_call", output_to_operand_aliasing={{0}: (7, {}), {1}: (8, {}), {2}: (9, {}), {3}: (10, {}), {4... | custom-call | flops 1200000000 | bytes 6000000 | tf_op jit(solution)/shard_map/within/pallas_call | solution.py:343
  31.9 1.3 %collective-permute-done.2.came = bf16[144,512]{1,0:T(8,128)(2,1)S(1)} collective-permute-done((bf16[144,512]{1,0:T(8,128)(2,1)S(1)}, bf16[144,512]{1,0:T(8,128)(2,1)S(1)}, u32[]{:S(2)}, u32[]{:S(2)}) %collective-permute-start.2) | collective-permute-done | bytes 147488 | tf_op jit(solution)/shard_map/ppermute | solution.py:407
  33.3 0.8 rise.5
  34.1 2.6 %collective-permute-start.3 = (bf16[144,512]{1,0:T(8,128)(2,1)S(1)}, bf16[144,512]{1,0:T(8,128)(2,1)S(1)}, u32[]{:S(2)}, u32[]{:S(2)}) collective-permute-start(bf16[144,512]{1,0:T(8,128)(2,1)S(1)} %get-tuple-element.122), channel_id=1, source_target_pairs={{0,8},{1,9},{2,10},{3,11},{4,12},{5,13},{6,14},{7,15},{8,0},{9,1},... | collective-permute-start | bytes 442376 | tf_op jit(solution)/shard_map/ppermute | solution.py:407
  36.7 3.3 %within.5 = (f32[16,128,512]{2,1,0:T(8,128)S(1)}, bf16[16,128,512]{2,1,0:T(8,128)(2,1)S(1)}, bf16[16,8,128,128]{3,2,1,0:T(8,128)(2,1)S(1)}, f32[16,128,512]{2,1,0:T(8,128)S(1)}, f32[8,128]{1,0:T(8,128)S(1)}) custom-call(bf16[16,128,512]{2,1,0:T(8,128)(2,1)S(1)} %get-tuple-element.103.c, ...), custom_call_target="tpu_custom_call", output_to_operand_aliasing={{0}: (7, {}), {1}: (8, {}), {2}: (9, {}), {3}: (10, {}), {4... | custom-call | flops 1800000000 | bytes 9000000 | tf_op jit(solution)/shard_map/within/pallas_call | solution.py:343
  39.9 2.7 %collective-permute-done.3.refs_6_ = bf16[144,512]{1,0:T(8,128)(2,1)S(1)} collective-permute-done((bf16[144,512]{1,0:T(8,128)(2,1)S(1)}, bf16[144,512]{1,0:T(8,128)(2,1)S(1)}, u32[]{:S(2)}, u32[]{:S(2)}) %collective-permute-start.3) | collective-permute-done | bytes 147488 | tf_op jit(solution)/shard_map/ppermute | solution.py:407
  42.6 0.2 fall.3
  42.8 0.2 collective-permute-start.4
  42.9 1.4 %back.4 = (bf16[16,128,512]{2,1,0:T(8,128)(2,1)S(1)}, bf16[16,128,64]{2,1,0:T(8,128)(2,1)S(1)}, f32[8,512]{1,0:T(8,128)S(1)}, f32[8,128]{1,0:T(8,128)S(1)}) custom-call(s32[1]{0:T(128)} %bitcast.me_ref, bf16[2,64,512]{2,1,0:T(8,128)(2,1)S(1)} %get-tuple-element.134.state, ...), custom_call_target="tpu_custom_call", output_to_operand_aliasing={{3}: (9, {})} | custom-call | flops 600000000 | bytes 3000000 | tf_op jit(solution)/shard_map/back/pallas_call | solution.py:366
  44.3 3.5 %collective-permute-done.4.refs_5_ = bf16[2,64,512]{2,1,0:T(8,128)(2,1)S(1)} collective-permute-done((bf16[2,64,512]{2,1,0:T(8,128)(2,1)S(1)}, bf16[2,64,512]{2,1,0:T(8,128)(2,1)S(1)}, u32[]{:S(2)}, u32[]{:S(2)}) %collective-permute-start.4) | collective-permute-done | bytes 131104 | tf_op jit(solution)/shard_map/ppermute | solution.py:407
  47.8 0.2 fall.4
  48.0 1.0 collective-permute-start.5
  49.0 1.4 %back.5 = (bf16[16,128,512]{2,1,0:T(8,128)(2,1)S(1)}, bf16[16,128,64]{2,1,0:T(8,128)(2,1)S(1)}, f32[8,512]{1,0:T(8,128)S(1)}, f32[8,128]{1,0:T(8,128)S(1)}) custom-call(s32[1]{0:T(128)} %bitcast.me_ref, bf16[2,64,512]{2,1,0:T(8,128)(2,1)S(1)} %get-tuple-element.144.state, ...), custom_call_target="tpu_custom_call", output_to_operand_aliasing={{0}: (9, {}), {1}: (10, {}), {3}: (11, {})} | custom-call | flops 600000000 | bytes 3000000 | tf_op jit(solution)/shard_map/back/pallas_call | solution.py:366
  50.3 4.1 %collective-permute-done.5.refs_3_ = bf16[4,64,512]{2,1,0:T(8,128)(2,1)S(1)} collective-permute-done((bf16[4,64,512]{2,1,0:T(8,128)(2,1)S(1)}, bf16[4,64,512]{2,1,0:T(8,128)(2,1)S(1)}, u32[]{:S(2)}, u32[]{:S(2)}) %collective-permute-start.5) | collective-permute-done | bytes 262176 | tf_op jit(solution)/shard_map/ppermute | solution.py:407
  54.5 1.2 %fall.5 = (f32[8,64,512]{2,1,0:T(8,128)}, bf16[8,64,512]{2,1,0:T(8,128)(2,1)S(1)}, bf16[4,64,512]{2,1,0:T(8,128)(2,1)S(1)}) custom-call(s32[1]{0:T(128)} %bitcast.me_ref, f32[8,64,512]{2,1,0:T(8,128)S(1)} %get-tuple-element.91.refs_0_, f32[16,512]{1,0:T(8,128)S(1)} %get-tuple-element.92.refs_3_.refs_2_.refs_1_, ...), custom_call_target="tpu_custom_call" | custom-call | flops 1000000 | bytes 1000000 | tf_op jit(solution)/shard_map/fall/pallas_call | solution.py:559
  55.7 0.0 collective-permute-start.6
  55.7 2.8 %back.6 = (bf16[16,128,512]{2,1,0:T(8,128)(2,1)S(1)}, bf16[16,128,64]{2,1,0:T(8,128)(2,1)S(1)}, f32[8,512]{1,0:T(8,128)S(1)}, f32[8,128]{1,0:T(8,128)S(1)}) custom-call(s32[1]{0:T(128)} %bitcast.me_ref, bf16[4,64,512]{2,1,0:T(8,128)(2,1)S(1)} %get-tuple-element.150.state, ...), custom_call_target="tpu_custom_call", output_to_operand_aliasing={{0}: (9, {}), {1}: (10, {}), {3}: (11, {})} | custom-call | flops 1200000000 | bytes 6000000 | tf_op jit(solution)/shard_map/back/pallas_call | solution.py:366
  58.5 5.7 %back.7 = (bf16[16,128,512]{2,1,0:T(8,128)(2,1)S(1)}, bf16[16,128,64]{2,1,0:T(8,128)(2,1)S(1)}, f32[8,512]{1,0:T(8,128)S(1)}, f32[8,128]{1,0:T(8,128)S(1)}) custom-call(s32[1]{0:T(128)} %bitcast.me_ref, bf16[8,64,512]{2,1,0:T(8,128)(2,1)S(1)} %collective-permute-done.6.state, ...), custom_call_target="tpu_custom_call", output_to_operand_aliasing={{0}: (9, {}), {1}: (10, {}), {3}: (11, {})} | custom-call | flops 2400000000 | bytes 12000000 | tf_op jit(solution)/shard_map/back/pallas_call | solution.py:366
  64.2 3.5 %grads.1 = (f32[1184,256]{1,0:T(8,128)S(1)}, bf16[1184,256]{1,0:T(8,128)(2,1)S(1)}) custom-call(s32[1]{0:T(128)} %bitcast.me_ref, bf16[16,128,512]{2,1,0:T(8,128)(2,1)S(1)} %get-tuple-element.157.normed, bf16[16,128,1024]{2,1,0:T(8,128)(2,1)S(1)} %get-tuple-element.107.cot, bf16[16,128,64]{2,1,0:T(8,128)(2,1)S(1)} %get-tuple-element.158.read, ...), custom_call_target="tpu_custom_call" | custom-call | flops 2500000000 | bytes 14000000 | tf_op jit(solution)/shard_map/grads/pallas_call | solution.py:383
  67.7 0.6 collective-permute-start.7
  68.3 1.7 %collective-permute-done.7 = bf16[1184,256]{1,0:T(8,128)(2,1)S(1)} collective-permute-done((bf16[1184,256]{1,0:T(8,128)(2,1)S(1)}, bf16[1184,256]{1,0:T(8,128)(2,1)S(1)}, u32[]{:S(2)}, u32[]{:S(2)}) %collective-permute-start.7) | collective-permute-done | bytes 606240 | tf_op jit(solution)/shard_map/ppermute | solution.py:407
  69.9 0.1 convert_add_fusion
  70.1 0.9 collective-permute-start.8
  71.0 8.6 %collective-permute-done.8 = bf16[592,256]{1,0:T(8,128)(2,1)S(1)} collective-permute-done((bf16[592,256]{1,0:T(8,128)(2,1)S(1)}, bf16[592,256]{1,0:T(8,128)(2,1)S(1)}, u32[]{:S(2)}, u32[]{:S(2)}) %collective-permute-start.8) | collective-permute-done | bytes 303136 | tf_op jit(solution)/shard_map/ppermute | solution.py:407
  79.6 0.1 convert_add_fusion.1
  79.7 0.4 collective-permute-start.9
  80.1 5.1 %collective-permute-done.9 = bf16[296,256]{1,0:T(8,128)(2,1)S(1)} collective-permute-done((bf16[296,256]{1,0:T(8,128)(2,1)S(1)}, bf16[296,256]{1,0:T(8,128)(2,1)S(1)}, u32[]{:S(2)}, u32[]{:S(2)}) %collective-permute-start.9) | collective-permute-done | bytes 151584 | tf_op jit(solution)/shard_map/ppermute | solution.py:407
  85.2 1.7 %collective-permute-start.10 = (bf16[296,256]{1,0:T(8,128)(2,1)S(1)}, bf16[296,256]{1,0:T(8,128)(2,1)S(1)}, u32[]{:S(2)}, u32[]{:S(2)}) collective-permute-start(bf16[296,256]{1,0:T(8,128)(2,1)S(1)} %fusion), channel_id=1, source_target_pairs={{0,8},{1,9},{2,10},{3,11},{4,12},{5,13},{6,14},{7,15},{8,0},{9,1},... | collective-permute-start | bytes 454664 | tf_op jit(solution)/shard_map/ppermute | solution.py:407
  87.0 7.0 %collective-permute-done.10 = bf16[296,256]{1,0:T(8,128)(2,1)S(1)} collective-permute-done((bf16[296,256]{1,0:T(8,128)(2,1)S(1)}, bf16[296,256]{1,0:T(8,128)(2,1)S(1)}, u32[]{:S(2)}, u32[]{:S(2)}) %collective-permute-start.10) | collective-permute-done | bytes 151584 | tf_op jit(solution)/shard_map/ppermute | solution.py:407
  93.9 0.1 add_convert_fusion
  94.0 0.1 collective-permute-start.11
  94.1 5.2 %collective-permute-done.11 = bf16[296,256]{1,0:T(8,128)(2,1)S(1)} collective-permute-done((bf16[296,256]{1,0:T(8,128)(2,1)S(1)}, bf16[296,256]{1,0:T(8,128)(2,1)S(1)}, u32[]{:S(2)}, u32[]{:S(2)}) %collective-permute-start.11) | collective-permute-done | bytes 151584 | tf_op jit(solution)/shard_map/ppermute | solution.py:407
  99.3 0.1 maximum_select_fusion.1
  99.4 0.9 collective-permute-start.12
  100.3 6.5 %collective-permute-done.12 = bf16[592,256]{1,0:T(8,128)(2,1)S(1)} collective-permute-done((bf16[592,256]{1,0:T(8,128)(2,1)S(1)}, bf16[592,256]{1,0:T(8,128)(2,1)S(1)}, u32[]{:S(2)}, u32[]{:S(2)}) %collective-permute-start.12) | collective-permute-done | bytes 303136 | tf_op jit(solution)/shard_map/ppermute | solution.py:407
  106.8 0.2 maximum_select_fusion.mine
  107.0 0.1 collective-permute-start.13
  107.1 2.0 %collective-permute-done.13.came = bf16[1184,256]{1,0:T(8,128)(2,1)S(1)} collective-permute-done((bf16[1184,256]{1,0:T(8,128)(2,1)S(1)}, bf16[1184,256]{1,0:T(8,128)(2,1)S(1)}, u32[]{:S(2)}, u32[]{:S(2)}) %collective-permute-start.13) | collective-permute-done | bytes 606240 | tf_op jit(solution)/shard_map/ppermute | solution.py:407
  109.1 1.6 %finish.1 = (f32[512,1024]{1,0:T(8,128)}, f32[64,1024]{1,0:T(8,128)}, f32[1,512]{1,0:T(1,128)}) custom-call(s32[1]{0:T(128)} %bitcast.me_ref, bf16[1184,256]{1,0:T(8,128)(2,1)S(1)} %maximum_select_fusion.mine, bf16[1184,256]{1,0:T(8,128)(2,1)S(1)} %collective-permute-done.13.came), custom_call_target="tpu_custom_call" | custom-call | flops 1000000 | bytes 4000000 | tf_op jit(solution)/shard_map/finish/pallas_call | solution.py:394
  (4 shorter events, 0.1 us)
Async XLA Ops:
  15.3 2.1 %collective-permute-start = (bf16[528,512]{1,0:T(8,128)(2,1)S(1)}, bf16[528,512]{1,0:T(8,128)(2,1)S(1)}, u32[]{:S(2)}, u32[]{:S(2)}) collective-permute-start(bf16[528,512]{1,0:T(8,128)(2,1)S(1)} %get-tuple-element.90), channel_id=1, source_target_pairs={{0,1},{1,0},{2,3},{3,2},{4,5},{5,4},{6,7},{7,6},{8,9},{9,8},{10,11... | collective-permute-start | bytes 1622024 | tf_op jit(solution)/shard_map/ppermute | solution.py:407
  17.8 9.9 %collective-permute-start.1 = (bf16[272,512]{1,0:T(8,128)(2,1)S(1)}, bf16[272,512]{1,0:T(8,128)(2,1)S(1)}, u32[]{:S(2)}, u32[]{:S(2)}) collective-permute-start(bf16[272,512]{1,0:T(8,128)(2,1)S(1)} %get-tuple-element.97), channel_id=1, source_target_pairs={{0,2},{1,3},{2,0},{3,1},{4,6},{5,7},{6,4},{7,5},{8,10},{9,11},{10,... | collective-permute-start | bytes 835592 | tf_op jit(solution)/shard_map/ppermute | solution.py:407
  27.8 5.4 %collective-permute-start.2 = (bf16[144,512]{1,0:T(8,128)(2,1)S(1)}, bf16[144,512]{1,0:T(8,128)(2,1)S(1)}, u32[]{:S(2)}, u32[]{:S(2)}) collective-permute-start(bf16[144,512]{1,0:T(8,128)(2,1)S(1)} %get-tuple-element.112), channel_id=1, source_target_pairs={{0,4},{1,5},{2,6},{3,7},{4,0},{5,1},{6,2},{7,3},{8,12},{9,13},{10,... | collective-permute-start | bytes 442376 | tf_op jit(solution)/shard_map/ppermute | solution.py:407
  34.1 8.5 %collective-permute-start.3 = (bf16[144,512]{1,0:T(8,128)(2,1)S(1)}, bf16[144,512]{1,0:T(8,128)(2,1)S(1)}, u32[]{:S(2)}, u32[]{:S(2)}) collective-permute-start(bf16[144,512]{1,0:T(8,128)(2,1)S(1)} %get-tuple-element.122), channel_id=1, source_target_pairs={{0,8},{1,9},{2,10},{3,11},{4,12},{5,13},{6,14},{7,15},{8,0},{9,1},... | collective-permute-start | bytes 442376 | tf_op jit(solution)/shard_map/ppermute | solution.py:407
  42.8 5.0 %collective-permute-start.4 = (bf16[2,64,512]{2,1,0:T(8,128)(2,1)S(1)}, bf16[2,64,512]{2,1,0:T(8,128)(2,1)S(1)}, u32[]{:S(2)}, u32[]{:S(2)}) collective-permute-start(bf16[2,64,512]{2,1,0:T(8,128)(2,1)S(1)} %get-tuple-element.131), channel_id=1, source_target_pairs={{0,4},{1,5},{2,6},{3,7},{4,0},{5,1},{6,2},{7,3},{8,12},{9,13},{10,... | collective-permute-start | bytes 393224 | tf_op jit(solution)/shard_map/ppermute | solution.py:407
  48.0 6.5 %collective-permute-start.5 = (bf16[4,64,512]{2,1,0:T(8,128)(2,1)S(1)}, bf16[4,64,512]{2,1,0:T(8,128)(2,1)S(1)}, u32[]{:S(2)}, u32[]{:S(2)}) collective-permute-start(bf16[4,64,512]{2,1,0:T(8,128)(2,1)S(1)} %get-tuple-element.142), channel_id=1, source_target_pairs={{0,2},{1,3},{2,0},{3,1},{4,6},{5,7},{6,4},{7,5},{8,10},{9,11},{10,... | collective-permute-start | bytes 786440 | tf_op jit(solution)/shard_map/ppermute | solution.py:407
  55.7 2.8 %collective-permute-start.6 = (bf16[8,64,512]{2,1,0:T(8,128)(2,1)S(1)}, bf16[8,64,512]{2,1,0:T(8,128)(2,1)S(1)}, u32[]{:S(2)}, u32[]{:S(2)}) collective-permute-start(bf16[8,64,512]{2,1,0:T(8,128)(2,1)S(1)} %get-tuple-element.149), channel_id=1, source_target_pairs={{0,1},{1,0},{2,3},{3,2},{4,5},{5,4},{6,7},{7,6},{8,9},{9,8},{10,11... | collective-permute-start | bytes 1572872 | tf_op jit(solution)/shard_map/ppermute | solution.py:407
  67.7 2.2 %collective-permute-start.7 = (bf16[1184,256]{1,0:T(8,128)(2,1)S(1)}, bf16[1184,256]{1,0:T(8,128)(2,1)S(1)}, u32[]{:S(2)}, u32[]{:S(2)}) collective-permute-start(bf16[1184,256]{1,0:T(8,128)(2,1)S(1)} %get-tuple-element.165), channel_id=1, source_target_pairs={{0,1},{1,0},{2,3},{3,2},{4,5},{5,4},{6,7},{7,6},{8,9},{9,8},{10,11... | collective-permute-start | bytes 1818632 | tf_op jit(solution)/shard_map/ppermute | solution.py:407
  70.1 9.5 %collective-permute-start.8 = (bf16[592,256]{1,0:T(8,128)(2,1)S(1)}, bf16[592,256]{1,0:T(8,128)(2,1)S(1)}, u32[]{:S(2)}, u32[]{:S(2)}) collective-permute-start(bf16[592,256]{1,0:T(8,128)(2,1)S(1)} %dynamic-slice_convert_fusion), channel_id=1, source_target_pairs={{0,2},{1,3},{2,0},{3,1},{4,6},{5,7},{6,4},{7,5},{8,10},{9,11},{10,... | collective-permute-start | bytes 909320 | tf_op jit(solution)/shard_map/ppermute | solution.py:407
  79.7 5.5 %collective-permute-start.9 = (bf16[296,256]{1,0:T(8,128)(2,1)S(1)}, bf16[296,256]{1,0:T(8,128)(2,1)S(1)}, u32[]{:S(2)}, u32[]{:S(2)}) collective-permute-start(bf16[296,256]{1,0:T(8,128)(2,1)S(1)} %dynamic-slice_convert_fusion.1), channel_id=1, source_target_pairs={{0,4},{1,5},{2,6},{3,7},{4,0},{5,1},{6,2},{7,3},{8,12},{9,13},{10,... | collective-permute-start | bytes 454664 | tf_op jit(solution)/shard_map/ppermute | solution.py:407
  85.2 8.7 %collective-permute-start.10 = (bf16[296,256]{1,0:T(8,128)(2,1)S(1)}, bf16[296,256]{1,0:T(8,128)(2,1)S(1)}, u32[]{:S(2)}, u32[]{:S(2)}) collective-permute-start(bf16[296,256]{1,0:T(8,128)(2,1)S(1)} %fusion), channel_id=1, source_target_pairs={{0,8},{1,9},{2,10},{3,11},{4,12},{5,13},{6,14},{7,15},{8,0},{9,1},... | collective-permute-start | bytes 454664 | tf_op jit(solution)/shard_map/ppermute | solution.py:407
  94.0 5.3 %collective-permute-start.11 = (bf16[296,256]{1,0:T(8,128)(2,1)S(1)}, bf16[296,256]{1,0:T(8,128)(2,1)S(1)}, u32[]{:S(2)}, u32[]{:S(2)}) collective-permute-start(bf16[296,256]{1,0:T(8,128)(2,1)S(1)} %add_convert_fusion), channel_id=1, source_target_pairs={{0,4},{1,5},{2,6},{3,7},{4,0},{5,1},{6,2},{7,3},{8,12},{9,13},{10,... | collective-permute-start | bytes 454664 | tf_op jit(solution)/shard_map/ppermute | solution.py:407
  99.4 7.4 %collective-permute-start.12 = (bf16[592,256]{1,0:T(8,128)(2,1)S(1)}, bf16[592,256]{1,0:T(8,128)(2,1)S(1)}, u32[]{:S(2)}, u32[]{:S(2)}) collective-permute-start(bf16[592,256]{1,0:T(8,128)(2,1)S(1)} %maximum_select_fusion.1), channel_id=1, source_target_pairs={{0,2},{1,3},{2,0},{3,1},{4,6},{5,7},{6,4},{7,5},{8,10},{9,11},{10,... | collective-permute-start | bytes 909320 | tf_op jit(solution)/shard_map/ppermute | solution.py:407
  107.0 2.1 %collective-permute-start.13 = (bf16[1184,256]{1,0:T(8,128)(2,1)S(1)}, bf16[1184,256]{1,0:T(8,128)(2,1)S(1)}, u32[]{:S(2)}, u32[]{:S(2)}) collective-permute-start(bf16[1184,256]{1,0:T(8,128)(2,1)S(1)} %maximum_select_fusion.mine), channel_id=1, source_target_pairs={{0,1},{1,0},{2,3},{3,2},{4,5},{5,4},{6,7},{7,6},{8,9},{9,8},{10,11... | collective-permute-start | bytes 1818632 | tf_op jit(solution)/shard_map/ppermute | solution.py:407

commit v4 on v3

v4 whole, which is shorter than its diff:
```python
import functools
import math

import jax
import jax.numpy as jnp
from jax import lax
from jax.experimental import pallas as pl
from jax.experimental.pallas import tpu as pltpu
from jax.sharding import PartitionSpec as P

f32 = jnp.float32
bf16 = jnp.bfloat16
LOG2E = math.log2(math.e)
LOG_PULSE = math.log(0.7)
NT = (((1,), (1,)), ((), ()))
TN = (((0,), (0,)), ((), ()))


def dot(a, b, dims=(((1,), (0,)), ((), ()))):
    return lax.dot_general(a, b, dims, preferred_element_type=f32)


def split(x, terms):
    parts = []
    for _ in range(terms):
        part = x.astype(bf16)
        parts.append(part)
        x = x - part.astype(f32)
    return parts


def iota(shape, axis):
    return lax.broadcasted_iota(jnp.int32, shape, axis)


def spread_matrix(rows, heads, channels):
    size = channels // heads
    return (iota((rows, channels), 0) % heads == iota((rows, channels), 1) // size).astype(bf16)


def spread(values, sensor, heads, spread2):
    lane = iota(values.shape, 1)
    own = jnp.where(lane // heads == sensor, values, 0.0)
    return dot(jnp.concatenate(split(own, 2), axis=1), spread2)


def front_kernel(
    me_ref, readings_hbm, *refs, heads, chunk, n_small,
):
    hbm, refs = refs[:n_small], refs[n_small:]
    (mixed_ref, channels_ref, maps_ref, step_ref, cum_ref, cum_t_ref, keep_ref, send_ref, tail_ref, token_ref,
     consts_ref), refs = refs[:11], refs[11:]
    vmem, refs = refs[:n_small], refs[n_small:]
    readings, kmix, wms, spread2, state_sc, log_sc, scaled_sc, sems = refs
    graph, cluster, mix, marks, w_step_t, bias, fading_exponent, skip_gain, norm_gain, w_state, w_channels = vmem
    sensors, span, width = readings.shape
    rows = sensors * chunk
    maps = w_state.shape[1]
    nstate = maps // 2
    channels = w_channels.shape[1]
    lanes = sensors * heads
    chunks = span // chunk

    def reading_copy(k):
        part = pl.ds(k * chunk, chunk)
        return pltpu.make_async_copy(readings_hbm.at[:, part], readings.at[:, part], sems.at[n_small + k])

    copies = [pltpu.make_async_copy(hbm[k], vmem[k], sems.at[k]) for k in range(n_small)]
    for copy in copies[:-2]:
        copy.start()
    reading_copy(0).start()
    copies[-2].start()
    copies[-1].start()
    for k in range(1, chunks):
        reading_copy(k).start()

    token_ref[...] = jnp.zeros_like(token_ref)
    wms[...] = jnp.zeros_like(wms)
    spread2[...] = spread_matrix(spread2.shape[0], heads, channels)
    for copy in copies[:-2]:
        copy.wait()
    wms[:, maps : maps + heads] = w_step_t[...].astype(f32).T.astype(bf16)
    picked = (iota((sensors, sensors), 0) == cluster[...]).astype(bf16)
    linked = dot(dot(picked, graph[...].astype(f32).astype(bf16), TN).astype(bf16), picked)
    coupling = (linked * mix[...]).astype(bf16)
    sensor_of = (iota((rows, sensors), 0) // chunk == iota((rows, sensors), 1)).astype(bf16)
    full = dot(dot(sensor_of, coupling).astype(bf16), sensor_of, NT)
    same = iota((rows, rows), 0) % chunk == iota((rows, rows), 1) % chunk
    kmix[...] = jnp.where(same, full, 0.0).astype(bf16)
    tiled = (iota((heads, lanes), 1) % heads == iota((heads, lanes), 0)).astype(bf16)
    both = jnp.concatenate([bias[...], -jnp.exp(fading_exponent[...]) * LOG2E], axis=0)
    wide = sum(dot(part, tiled) for part in split(both, 3))
    bias_row, rate_row = wide[0:1], wide[1:2]
    consts_ref[...] = jnp.zeros_like(consts_ref)
    consts_ref[0:1, :] = sum(dot(part, spread2[0:heads, :]) for part in split(skip_gain[...], 3))
    consts_ref[1:2, :] = norm_gain[...]

    def mix_chunk(i):
        here = slice(i * chunk, (i + 1) * chunk)
        reading_copy(i).wait()
        x = readings[:, here, :].reshape(rows, width)
        mixed_ref[:, here, :] = (x.astype(f32) + dot(kmix[...], x)).astype(bf16).reshape(sensors, chunk, width)

    mix_chunk(0)
    copies[-2].wait()
    wms[:, 0:maps] = w_state[...]
    copies[-1].wait()
    for i in range(chunks):
        here = slice(i * chunk, (i + 1) * chunk)
        if i + 1 < chunks:
            mix_chunk(i + 1)
        mixed = mixed_ref[:, here, :].reshape(rows, width)
        small = dot(mixed, wms[...])
        channels_ref[:, here, :] = dot(mixed, w_channels[...]).astype(bf16).reshape(sensors, chunk, channels)
        maps_ref[:, here, :] = small[:, 0:maps].astype(bf16).reshape(sensors, chunk, maps)
        steps = small[:, maps:].reshape(sensors, chunk, lanes)
        packed = steps[0]
        for s in range(1, sensors):
            packed = packed + pltpu.roll(steps[s], heads * s, 1)
        raw = (packed + bias_row).astype(bf16).astype(f32)
        step = jnp.maximum(raw, 0.0) + jnp.log1p(jnp.exp(-jnp.abs(raw)))
        step_ref[here, :] = step
        log_sc[here, :] = rate_row * step

    at, to = iota((span, span), 0), iota((span, span), 1)
    marked = jnp.sum(jnp.where(at == to, marks[...].astype(f32), 0.0), axis=1, keepdims=True)
    log_decay = log_sc[...] + (LOG_PULSE * LOG2E) * marked
    lower = (at >= to).astype(bf16)
    cum = sum(dot(lower, part) for part in split(log_decay, 3))
    cum_ref[...] = cum
    cum_t_ref[...] = cum.T
    last = cum[span - 1 : span, :]
    weight = jnp.exp2(last - cum) * step_ref[...]

    def scale(s):
        scaled_sc[s % 4] = (channels_ref[s].astype(f32) * spread(weight, s, heads, spread2[...])).astype(bf16)

    scale(0)
    scale(1)
    for s in range(sensors):
        if s + 2 < sensors:
            scale(s + 2)
        state_sc[s] = dot(maps_ref[s], scaled_sc[s % 4], TN)[0:nstate]
    own = jnp.where(iota((sensors, lanes), 1) // heads == iota((sensors, lanes), 0), last, 0.0)
    tail = sum(dot(part, spread2[0:lanes, :]) for part in split(own, 3))
    tail_ref[...] = tail
    half = sensors // 2
    mine = (me_ref[0] & 1) * half
    other = half - mine
    keep_ref[...] = state_sc[pl.ds(mine, half)]
    send_ref[0 : half * nstate, :] = state_sc[pl.ds(other, half)].reshape(half * nstate, channels).astype(bf16)
    send_ref[half * nstate :, :] = tail.astype(bf16)


def pair_blocks(x, size):
    lane = iota(x.shape, 1)
    zero = jnp.zeros_like(x)
    return jnp.concatenate([jnp.where(lane < size, x, zero), jnp.where(lane >= size, x, zero)], axis=0)


def within_kernel(channels, maps, step, cum_t, consts, cot_hbm, w_out_hbm, *refs, heads, first, count, aliases):
    part_ref, scaled_ref, decay_ref, grad_ref, cot_ref, w_out_ref, _, spread2, sems = refs[aliases:]
    _, span, width = channels.shape
    nstate = maps.shape[2] // 2
    size = width // heads
    own = slice(first, first + count)
    cot_copy = pltpu.make_async_copy(cot_hbm.at[own], cot_ref.at[own], sems.at[0])
    if first == 0:
        w_out_copy = pltpu.make_async_copy(w_out_hbm, w_out_ref, sems.at[1])
        w_out_copy.start()
    cot_copy.start()
    spread2[...] = spread_matrix(spread2.shape[0], heads, width)

    def sensor(k, carry):
        s = first + k
        causal = iota((span, span), 0) >= iota((span, span), 1)
        chan = channels[s].astype(f32)
        scaled = (chan * spread(step[...], s, heads, spread2[...])).astype(bf16)
        scaled_ref[s] = scaled
        both = maps[s]
        scores = dot(both[:, nstate:], both[:, 0:nstate], NT)
        row = cum_t[pl.ds(pl.multiple_of(s * heads, heads), heads), :]
        col = row.T
        for pair in range(heads // 2):
            weighted = []
            for h in (2 * pair, 2 * pair + 1):
                gap = jnp.broadcast_to(col[:, h : h + 1], (span, span)) - row[h : h + 1, :]
                decay = jnp.exp2(jnp.where(causal, gap, -jnp.inf))
                decay_ref[s, h] = decay.astype(bf16)
                weighted.append((scores * decay).astype(bf16))
            lanes = slice(2 * pair * size, 2 * (pair + 1) * size)
            out = dot(jnp.concatenate(weighted, axis=1), pair_blocks(scaled[:, lanes], size))
            part_ref[s, :, lanes] = out + consts[0:1, lanes] * chan[:, lanes]
        return carry

    lax.fori_loop(0, count, sensor, 0, unroll=2)
    if first == 0:
        w_out_copy.wait()
    cot_copy.wait()
    grad = dot(cot_ref[own].reshape(count * span, cot_ref.shape[2]), w_out_ref[...], NT)
    grad_ref[own] = grad.reshape(count, span, width)


def back_kernel(me_ref, state, maps, scaled, decay, part, grad, cum, consts, *refs, heads, aliases, first):
    normed_ref, read_ref, gain_ref, _, spread2, fade_sc, carried_sc, spread_sc, back_sc, faded_sc = refs[aliases:]
    _, span, width = part.shape
    nstate = maps.shape[2] // 2
    size = width // heads
    at_once = carried_sc.shape[0]
    spread2[...] = spread_matrix(spread2.shape[0], heads, width)
    fade_sc[...] = jnp.exp2(cum[...])
    begin = first(me_ref[0])
    chunk = 32

    def carry_in(k, slot):
        s = begin + k
        carried_sc[slot] = dot(maps[s][:, nstate:], state[k])
        spread_sc[slot] = spread(fade_sc[...], s, heads, spread2[...])

    def normalize(k, slot, gain_sum):
        s = begin + k
        gain = consts[1:2, :]
        for c in range(0, span, chunk):
            rows = slice(c, c + chunk)
            fade = spread_sc[slot, rows, :]
            out = part[s, rows, :] + carried_sc[slot, rows, :] * fade
            inv = lax.rsqrt(jnp.mean(out * out, axis=-1, keepdims=True) + 1e-05)
            normed = out * inv
            normed_ref[s, rows, :] = (normed * gain).astype(bf16)
            g = grad[s, rows, :]
            gain_sum = gain_sum + jnp.sum((normed * g).reshape(chunk // 8, 8, width), axis=0)
            by_gain = g * gain
            mean = jnp.mean(by_gain * normed, axis=-1, keepdims=True)
            back = inv * (by_gain - normed * mean)
            back_sc[slot, rows, :] = back.astype(bf16)
            faded_sc[slot, rows, :] = (back * fade).astype(bf16)
        return gain_sum

    def read_out(k, slot):
        s = begin + k
        read = dot(faded_sc[slot], state[k], NT)
        pairs = jnp.zeros((span, span), f32)
        for pair in range(heads // 2):
            lanes = slice(2 * pair * size, 2 * (pair + 1) * size)
            both_heads = dot(back_sc[slot, :, lanes], pair_blocks(scaled[s, :, lanes], size), NT)
            pairs = pairs + both_heads[:, 0:span] * decay[s, 2 * pair].astype(f32)
            pairs = pairs + both_heads[:, span:] * decay[s, 2 * pair + 1].astype(f32)
        read_ref[s] = (read + dot(pairs.astype(bf16), maps[s][:, 0:nstate])).astype(bf16)

    def block(i, gain_sum):
        for slot in range(at_once):
            carry_in(i * at_once + slot, slot)
        for slot in range(at_once):
            gain_sum = normalize(i * at_once + slot, slot, gain_sum)
        for slot in range(at_once):
            read_out(i * at_once + slot, slot)
        return gain_sum

    gain_ref[...] = lax.fori_loop(0, state.shape[0] // at_once, block, jnp.zeros(gain_ref.shape, f32))


def grads_kernel(me_ref, normed, cot, read, mixed, *refs, starts, more, n_gains):
    if more:
        before, gains, (keep_ref, send_ref, total) = refs[0], refs[1 : 1 + n_gains], refs[1 + n_gains :]
    else:
        total = refs[0]
    block = normed.shape[0] // 4
    span, channels = normed.shape[1:]
    width, nstate = cot.shape[2], read.shape[2]
    piece = total.shape[1]
    pieces = width // piece
    rows = block * span
    blocks = [pl.ds(start, block) for start in starts(me_ref[0])]

    def put(at, size, value):
        total[at : at + size, :] = value + before[at : at + size, :] if more else value

    for j in range(pieces):
        lanes = slice(j * piece, (j + 1) * piece)
        put(j * channels, channels, sum(
            dot(normed[here].reshape(rows, channels), cot[here, :, lanes].reshape(rows, piece), TN) for here in blocks
        ))
        put(pieces * channels + j * nstate, nstate, sum(
            dot(read[here].reshape(rows, nstate), mixed[here, :, lanes].reshape(rows, piece), TN) for here in blocks
        ))
    if not more:
        return
    used = pieces * (channels + nstate)
    total[used:, :] = jnp.zeros((total.shape[0] - used, piece), f32)
    gain = sum(jnp.sum(ref[...], axis=0, keepdims=True) for ref in gains)
    for j in range(channels // piece):
        total[used + j : used + j + 1, :] = gain[:, j * piece : (j + 1) * piece]
    half = keep_ref.shape[0]
    mine = pl.multiple_of((me_ref[0] & 1) * half, 8)
    other = pl.multiple_of(half - (me_ref[0] & 1) * half, 8)
    keep_ref[...] = total[pl.ds(mine, half), :]
    send_ref[...] = total[pl.ds(other, half), :].astype(bf16)


def finish_kernel(me_ref, mine, came, out_ref, read_ref, gain_ref):
    channels, width = out_ref.shape
    nstate = read_ref.shape[0]
    half, piece = mine.shape
    pieces = width // piece

    def write(low, high):
        def rows(start, size):
            parts = []
            if start < half:
                parts.append(low[start : min(start + size, half), :])
            if start + size > half:
                parts.append(high[max(start - half, 0) : start + size - half, :])
            return jnp.concatenate([part.astype(f32) for part in parts], axis=0)

        for j in range(pieces):
            lanes = slice(j * piece, (j + 1) * piece)
            out_ref[:, lanes] = rows(j * channels, channels)
            read_ref[:, lanes] = rows(pieces * channels + j * nstate, nstate)
        tail = rows(pieces * (channels + nstate), 8)
        for j in range(channels // piece):
            gain_ref[:, j * piece : (j + 1) * piece] = tail[j : j + 1, :]

    pl.when(me_ref[0] & 1 == 0)(lambda: write(mine, came))
    pl.when(me_ref[0] & 1 == 1)(lambda: write(came, mine))


def whole(shape):
    return pl.BlockSpec(shape, lambda *_: (0,) * len(shape), pipeline_mode=pl.Buffered(1))


ANYWHERE = pl.BlockSpec(memory_space=pl.ANY)
HELD = pl.BlockSpec(memory_space=pltpu.VMEM)


def held(x):
    return pltpu.with_memory_space_constraint(x, pltpu.VMEM)


def call(body, name, scalars, grid, in_specs, out_specs, out_shape, scratch, vmem, flops, moved, aliases=None):
    return pl.pallas_call(
        body,
        name=name,
        grid_spec=pltpu.PrefetchScalarGridSpec(
            num_scalar_prefetch=scalars, grid=grid, in_specs=in_specs, out_specs=out_specs, scratch_shapes=scratch
        ),
        out_shape=out_shape,
        input_output_aliases=aliases or {},
        compiler_params=pltpu.CompilerParams(vmem_limit_bytes=vmem << 20),
        cost_estimate=pl.CostEstimate(flops=int(flops), bytes_accessed=int(moved), transcendentals=0),
    )


def front(me, readings, graph, cluster, mix, boundaries, w_channels, w_state, w_step, bias, fading_exponent, skip_gain, gain):
    sensors, span, width = readings.shape
    heads, channels, maps = w_step.shape[1], w_channels.shape[1], w_state.shape[1]
    nstate, lanes, chunk = maps // 2, sensors * heads, 16
    rows, half_rows = sensors * chunk, sensors // 2 * nstate
    small = [
        graph, cluster[None, :], mix, boundaries[None, :], w_step.T, bias[None, :], fading_exponent[None, :],
        skip_gain[None, :], gain[None, :], w_state, w_channels,
    ]
    outs = [
        ((sensors, span, width), bf16), ((sensors, span, channels), bf16), ((sensors, span, maps), bf16),
        ((span, lanes), f32), ((span, lanes), f32), ((lanes, span), f32),
        ((sensors // 2, nstate, channels), f32), ((half_rows + sensors, channels), bf16), ((sensors, channels), f32),
        ((8, 128), f32), ((8, channels), f32),
    ]
    return call(
        functools.partial(front_kernel, heads=heads, chunk=chunk, n_small=len(small)), "front", 1, (),
        [ANYWHERE] * (1 + len(small)),
        [HELD] * len(outs),
        [pltpu.VMEM(shape, dtype) for shape, dtype in outs],
        [pltpu.VMEM(x.shape, x.dtype) for x in small] + [
            pltpu.VMEM(readings.shape, bf16), pltpu.VMEM((rows, rows), bf16), pltpu.VMEM((width, maps + lanes), bf16),
            pltpu.VMEM((2 * lanes, channels), bf16), pltpu.VMEM((sensors, nstate, channels), f32),
            pltpu.VMEM((span, lanes), f32), pltpu.VMEM((4, span, channels), bf16),
            pltpu.SemaphoreType.DMA((len(small) + span // chunk,)),
        ],
        20, 5e9, 14e6,
    )(me, *[pltpu.with_memory_space_constraint(x, pltpu.HBM) for x in [readings] + small])


def within(first, count, channels, maps, step, cum_t, consts, cot, w_out, heads, done, token):
    sensors, span, width = channels.shape
    lanes = sensors * heads
    n_in = 7
    aliases = {n_in + k: k for k in range(len(done))}
    aliases[n_in + len(done)] = 6
    return call(
        functools.partial(within_kernel, heads=heads, first=first, count=count, aliases=len(done) + 1),
        "within", 0, (),
        [HELD] * 5 + [ANYWHERE] * 2 + [HELD] * len(done) + [ANYWHERE],
        [HELD] * 6 + [ANYWHERE],
        [
            pltpu.VMEM((sensors, span, width), f32), pltpu.VMEM((sensors, span, width), bf16),
            pltpu.VMEM((sensors, heads, span, span), bf16), pltpu.VMEM((sensors, span, width), f32),
            pltpu.VMEM(cot.shape, bf16), pltpu.VMEM(w_out.shape, bf16),
            jax.ShapeDtypeStruct(token.shape, token.dtype),
        ],
        [pltpu.VMEM((2 * lanes, width), bf16), pltpu.SemaphoreType.DMA((2,))],
        8, 3e8 * count, 1.5e6 * count, aliases,
    )(
        *[held(x) for x in (channels, maps, step, cum_t, consts)],
        *[pltpu.with_memory_space_constraint(x, pltpu.HBM) for x in (cot, w_out)], *[held(x) for x in done], token,
    )


def back(me, first, state, maps, scaled, decay, part, grad, cum, consts, done, token):
    sensors, span, width = part.shape
    heads, nmaps = decay.shape[1], maps.shape[2]
    nstate, lanes = nmaps // 2, sensors * heads
    count = state.shape[0]
    at_once = min(count, 4)
    n_in = 9
    aliases = {n_in + k: k for k in range(len(done))}
    aliases[n_in + len(done)] = 3
    return call(
        functools.partial(back_kernel, heads=heads, aliases=len(done) + 1, first=first), "back", 1, (),
        [HELD] * (n_in - 1 + len(done)) + [ANYWHERE],
        [HELD] * 3 + [ANYWHERE],
        [
            pltpu.VMEM((sensors, span, width), bf16), pltpu.VMEM((sensors, span, nstate), bf16),
            pltpu.VMEM((8, width), f32), jax.ShapeDtypeStruct(token.shape, token.dtype),
        ],
        [
            pltpu.VMEM((2 * lanes, width), bf16), pltpu.VMEM((span, lanes), f32),
            pltpu.VMEM((at_once, span, width), f32), pltpu.VMEM((at_once, span, width), f32),
            pltpu.VMEM((at_once, span, width), bf16), pltpu.VMEM((at_once, span, width), bf16),
        ],
        8, 3e8 * count, 1.5e6 * count, aliases,
    )(me, *[held(x) for x in (state, maps, scaled, decay, part, grad, cum, consts) + done], token)


def grads(me, normed, cot, read, mixed, starts, before, gains, token):
    channels, width, nstate = normed.shape[2], cot.shape[2], read.shape[2]
    piece = 256
    rows = -(-(width // piece * (channels + nstate) + channels // piece) // 128) * 128
    more = before is not None
    body = functools.partial(grads_kernel, starts=starts, more=more, n_gains=len(gains))
    if not more:

        def first(me_ref, normed, cot, read, mixed, _, total, __):
            body(me_ref, normed, cot, read, mixed, total)

        return call(
            first, "grads", 1, (), [HELD] * 4 + [ANYWHERE], [HELD, ANYWHERE],
            [pltpu.VMEM((rows, piece), f32), jax.ShapeDtypeStruct(token.shape, token.dtype)],
            [], 8, 1.2e9, 7e6, {5: 1},
        )(me, *[held(x) for x in (normed, cot, read, mixed)], token)
    return call(
        body, "grads", 1, (), [HELD] * (5 + len(gains)), [HELD] * 2,
        [pltpu.VMEM((rows // 2, piece), f32), pltpu.VMEM((rows // 2, piece), bf16)],
        [pltpu.VMEM((rows, piece), f32)], 12, 1.2e9, 7e6,
    )(me, *[held(x) for x in (normed, cot, read, mixed, before, *gains)])


def finish(me, mine, came, channels, width, nstate):
    return call(
        finish_kernel, "finish", 1, (1,),
        [whole(mine.shape)] * 2,
        [whole((channels, width)), whole((nstate, width)), whole((1, channels))],
        [
            jax.ShapeDtypeStruct((channels, width), f32), jax.ShapeDtypeStruct((nstate, width), f32),
            jax.ShapeDtypeStruct((1, channels), f32),
        ],
        [], 8, 1e6, 4e6,
    )(me, mine, came)


def swap(x, distance, count):
    return lax.ppermute(x, "seq", [(i, i ^ distance) for i in range(count)])


def narrow(x):
    return lax.reduce_precision(x, 8, 7)


def pick(bit, when_one, when_zero):
    return jnp.where(bit == 1, when_one, when_zero)


def tied(x, token):
    return lax.optimization_barrier((x, token))


def bit_of(me, level):
    return (me >> level) & 1


def shard_start(me, level, sensors):
    return sum(bit_of(me, k) * (sensors >> (k + 1)) for k in range(level + 1))


def row(ref, k):
    return ref[pl.ds(k, 1), :]


def rise_kernel(me_ref, own, tail, came, low_ref, low_tail_ref, tail_ref, next_ref, send_ref, other_tail, *, level, last):
    me = me_ref[0]
    bit = bit_of(me, level)
    size, nstate, width = own.shape
    sensors = tail.shape[0]
    start = shard_start(me, level, sensors)
    other_tail[...] = came[size * nstate :, :].astype(f32)
    low_tail_ref[...] = pick(bit, other_tail[...], tail[...])
    total_tail = tail[...] + other_tail[...]
    tail_ref[...] = total_tail

    def total(j):
        other = came[pl.ds(pl.multiple_of(j * nstate, nstate), nstate), :].astype(f32)
        low, high = pick(bit, other, own[j]), pick(bit, own[j], other)
        low_ref[j] = low
        fade = jnp.exp2(pick(bit, row(tail, start + j), row(other_tail, start + j)))
        return low * fade + high

    half = next_ref.shape[0]
    mine = 0 if last else bit_of(me, level + 1) * half
    for j in range(half):
        kept = total(mine + j)
        next_ref[j] = kept
        gone = kept if last else total(half - mine + j)
        send_ref[j * nstate : (j + 1) * nstate, :] = gone.astype(bf16)
    send_ref[half * nstate :, :] = total_tail.astype(bf16)


def rise(me, own, tail, came, level, last):
    size, nstate, width = own.shape
    half = size if last else size // 2
    return call(
        functools.partial(rise_kernel, level=level, last=last), "rise", 1, (),
        [HELD] * 3, [HELD] * 5,
        [
            pltpu.VMEM(own.shape, f32), pltpu.VMEM(tail.shape, f32), pltpu.VMEM(tail.shape, f32),
            pltpu.VMEM((half, nstate, width), f32), pltpu.VMEM((half * nstate + tail.shape[0], width), bf16),
        ],
        [pltpu.VMEM(tail.shape, f32)], 6, 1e6, 1e6,
    )(me, *[held(x) for x in (own, tail, came)])


def across_kernel(
    me_ref, own, tail, before, before_tail, came, next_ref, tail_ref, before_ref, before_tail_ref, send_ref, other_tail,
    *, level, shards,
):
    me = me_ref[0]
    bit = bit_of(me, level)
    size, nstate, width = own.shape
    start = shard_start(me, shards - 1, tail.shape[0])
    other_tail[...] = came[size * nstate :, :].astype(f32)
    before_tail_ref[...] = before_tail[...] + pick(bit, other_tail[...], jnp.zeros_like(other_tail))
    total_tail = tail[...] + other_tail[...]
    tail_ref[...] = total_tail
    for j in range(size):
        other = came[j * nstate : (j + 1) * nstate, :].astype(f32)
        passed = other * jnp.exp2(row(before_tail, start + j)) + before[j]
        before_ref[j] = pick(bit, passed, before[j])
        low, high = pick(bit, other, own[j]), pick(bit, own[j], other)
        total = low * jnp.exp2(pick(bit, row(tail, start + j), row(other_tail, start + j))) + high
        next_ref[j] = total
        send_ref[j * nstate : (j + 1) * nstate, :] = total.astype(bf16)
    send_ref[size * nstate :, :] = total_tail.astype(bf16)


def across(me, own, tail, before, before_tail, came, level, shards):
    return call(
        functools.partial(across_kernel, level=level, shards=shards), "across", 1, (),
        [HELD] * 5, [HELD] * 5,
        [
            pltpu.VMEM(own.shape, f32), pltpu.VMEM(tail.shape, f32), pltpu.VMEM(own.shape, f32),
            pltpu.VMEM(tail.shape, f32), pltpu.VMEM(came.shape, bf16),
        ],
        [pltpu.VMEM(tail.shape, f32)], 6, 1e6, 1e6,
    )(me, *[held(x) for x in (own, tail, before, before_tail, came)])


def fall_kernel(me_ref, *refs, level, first, across_level):
    me = me_ref[0]
    lows, tails = refs[: level + 1], refs[level + 1 : 2 * (level + 1)]
    refs = refs[2 * (level + 1) :]
    sensors = tails[0].shape[0]
    size, nstate, width = lows[level].shape
    start = shard_start(me, level, sensors)

    def step(state, q, sensor):
        return state * jnp.exp2(row(tails[q], sensor)) + lows[q][sensor - shard_start(me, q, sensors)]

    def choose(before, q, sensor):
        after = step(before, q, sensor)
        bit = bit_of(me, q)
        return pick(bit, after, before), pick(bit, before, after)

    def land(state, top, sensor, k):
        for q in reversed(range(1, top)):
            state, _ = choose(state, q, sensor)
        state, other = choose(state, 0, sensor)
        state_ref[k] = state.astype(bf16)
        other_ref[k] = other.astype(bf16)

    if level == 0:
        came, state_ref, other_ref = refs
        came_size = came.shape[0]
        came_start = shard_start(me, 1, sensors) + pick(bit_of(me, 1), -came_size, came_size)
        for k in range(came_size):
            land(came[k].astype(f32), 1, came_start + k, k)
        return
    if first:
        came, mine_ref, gone_ref, state_ref, other_ref = refs
        for j in range(size):
            if across_level is None:
                before = came[j]
            else:
                before = came[j * nstate : (j + 1) * nstate, :].astype(f32)
                before = pick(bit_of(me, across_level), before, jnp.zeros_like(before))
            mine, gone = choose(before, level, start + j)
            mine_ref[j] = mine
            gone_ref[j] = gone.astype(bf16)
            land(mine, level, start + j, j)
    else:
        had, came, mine_ref, gone_ref, state_ref, other_ref = refs
        half = size // 2
        at = bit_of(me, level + 1) * half
        for k in range(half):
            mine, gone = choose(had[k], level, start + at + k)
            mine_ref[at + k] = mine
            gone_ref[at + k] = gone.astype(bf16)
            mine, gone = choose(came[k].astype(f32), level, start + half - at + k)
            mine_ref[half - at + k] = mine
            gone_ref[half - at + k] = gone.astype(bf16)
            land(mine, level, start + half - at + k, k)


def fall(me, saved, level, had, came, across_level):
    lows = [low for low, _ in saved[: level + 1]]
    tails = [tail for _, tail in saved[: level + 1]]
    size, nstate, width = lows[level].shape
    first = had is None
    arrays = lows + tails + ([came] if first else [had, came])
    known = size if first and level else size // 2
    outs = [pltpu.VMEM((size, nstate, width), f32), pltpu.VMEM((size, nstate, width), bf16)] if level else []
    outs += [pltpu.VMEM((known, nstate, width), bf16)] * 2
    return call(
        functools.partial(fall_kernel, level=level, first=first, across_level=across_level), "fall", 1, (),
        [HELD] * len(arrays), [HELD] * len(outs), outs, [], 6, 1e6, 1e6,
    )(me, *[held(x) for x in arrays])


def exchange(keep, send, tail, me, count, shards, swap_beside, ready):
    sensors = tail.shape[0]
    levels = count.bit_length() - 1
    own = keep
    saved = []
    for level in range(shards):
        came = swap_beside(send, level)
        low, low_tail, tail, own, send = rise(me, own, tail, came, level, level + 1 == shards)
        saved.append((low, low_tail))
    if levels == shards + 1:
        parts = (None, swap_beside(send, shards), shards)
    else:
        before, before_tail = jnp.zeros_like(own), jnp.zeros_like(tail)
        for level in range(shards, levels):
            came = swap_beside(send, level)
            own, tail, before, before_tail, send = across(me, own, tail, before, before_tail, came, level, shards)
        parts = (None, before, None)

    def first_of(at, level):
        if level + 1 == shards:
            return shard_start(at, level, sensors)
        size = sensors >> (level + 2)
        return shard_start(at, level + 1, sensors) + pick(bit_of(at, level + 1), -size, size)

    for level in reversed(range(1, shards)):
        mine, gone, states, other = fall(me, saved, level, *parts)
        came = ready(states, other, functools.partial(first_of, level=level), level, gone)
        parts = (mine, came, None)
    states, other = fall(me, saved, 0, None, came, None)
    ready(states, other, functools.partial(first_of, level=0), 0, None)


def all_sum(keep, send, me, count):
    levels = count.bit_length() - 1
    own = keep + swap(send, 1, count).astype(f32)
    half = own.shape[0] // 2
    parts = [own[:half], own[half:]]
    orders = [(1, 2), (2, 1)]
    for turn in range(2):
        sent = []
        for part, order in zip(parts, orders):
            size = part.shape[0] // 2
            bit = bit_of(me, order[turn])
            gone = lax.dynamic_slice_in_dim(part, (1 - bit) * size, size, 0).astype(bf16)
            sent.append(swap(gone, 1 << order[turn], count))
        for k, order in enumerate(orders):
            size = parts[k].shape[0] // 2
            kept = lax.dynamic_slice_in_dim(parts[k], bit_of(me, order[turn]) * size, size, 0)
            parts[k] = kept + sent[k].astype(f32)
    both = jnp.concatenate(parts, axis=0)
    for level in range(3, levels):
        both = narrow(both)
        both = both + swap(both.astype(bf16), 1 << level, count).astype(f32)
    size = both.shape[0] // 2
    both = both.astype(bf16)
    parts = [both[:size], both[size:]]
    for turn in (1, 0):
        came = [swap(part, 1 << order[turn], count) for part, order in zip(parts, orders)]
        for k, order in enumerate(orders):
            bit = bit_of(me, order[turn])
            parts[k] = pick(
                bit, jnp.concatenate([came[k], parts[k]], axis=0), jnp.concatenate([parts[k], came[k]], axis=0)
            )
    out = jnp.concatenate(parts, axis=0)
    return out, swap(out, 1, count)


def per_device(
    count, readings, block_graph, cluster_of, mix_weight, boundaries, w_channels, w_state, w_step,
    step_bias, channel_fading_exponent, skip_gain, norm_gain, w_out, cotangent,
):
    sensors, span, width = readings.shape
    channels = w_channels.shape[1]
    nstate = w_state.shape[1] // 2
    me = lax.axis_index("seq").astype(jnp.int32)
    at = me[None]
    shards = 3
    heads = skip_gain.shape[0]

    mixed, chans, maps, step, cum, cum_t, keep, send, tail, token, consts = front(
        at, readings, block_graph, cluster_of, mix_weight, boundaries, w_channels, w_state, w_step,
        step_bias, channel_fading_exponent, skip_gain, norm_gain,
    )
    work = {"token": token, "within": (), "back": (), "gains": []}
    plan = {1: (0, 6), 2: (6, 4), 3: (10, 6)}

    def run_back(states, first):
        part, scaled, decay, grad = work["within"][:4]
        normed, read, gain, work["token"] = back(
            at, first, states, maps, scaled, decay, part, grad, cum, consts, work["back"], work["token"]
        )
        work["back"] = (normed, read)
        work["gains"].append(gain)

    def swap_beside(x, level):
        x, work["token"] = tied(x, work["token"])
        came = swap(x, 1 << level, count)
        if level in plan:
            first, size = plan[level]
            *arrays, work["token"] = within(
                first, size, chans, maps, step, cum_t, consts, cotangent, w_out, heads, work["within"], work["token"]
            )
            work["within"] = tuple(arrays)
            came, work["token"] = tied(came, work["token"])
        return came

    def known(level):
        def starts(where):
            size = sensors // 4
            for device in (where, where ^ 1):
                begin = shard_start(device, 1, sensors)
                yield begin if level else begin + pick(bit_of(device, 1), -size, size)

        return starts

    def ready(states, other, first, level, gone):
        if level:
            gone, work["token"] = tied(gone, work["token"])
            gone = swap(gone, 1 << level, count)
        came = swap(other, 1, count)
        run_back(states, first)
        run_back(came, lambda where: first(where ^ 1))
        if level == 1:
            work["total"], work["token"] = grads(
                at, work["back"][0], work["within"][4], work["back"][1], mixed, known(1), None, [], work["token"]
            )
        if level:
            gone, work["token"] = tied(gone, work["token"])
        return gone

    exchange(keep, send, tail, at, count, shards, swap_beside, ready)
    keep_sum, send_sum = grads(
        at, work["back"][0], work["within"][4], work["back"][1], mixed, known(0), work["total"], work["gains"], None
    )
    mine, came = all_sum(keep_sum, send_sum, me, count)
    grad_out, grad_read, grad_gain = finish(at, mine, came, channels, width, nstate)
    return grad_out, grad_read.T, grad_gain[0]


def solution(mesh):
    in_specs = (
        P("groups", "seq", None), P("groups", None), P("groups"), P(), P(("groups", "seq")),
        P(), P(), P(), P(), P(), P(), P(), P(), P("groups", "seq", None),
    )
    out_specs = (P("groups", None), P("groups", None), P("groups"))
    return jax.shard_map(
        functools.partial(per_device, mesh.shape["seq"]),
        mesh=mesh, in_specs=in_specs, out_specs=out_specs, check_vma=False,
    )
```

time: 111 us -> 98 us (0.88)
  waiting for transfers between devices: 52.9 us -> 42.2 us
  Pallas kernels: 42.5 us -> 35.8 us
  starting transfers between devices: 13.8 us -> 18.2 us
    ppermute x14 -> x20, waiting for transfers between devices: 52.9 us -> 42.2 us  [swap(): return lax.ppermute(x, 'seq', [(i, i ^ distance) for i in range(count)])]
    pallas_call x5 -> x6, Pallas kernels: 19.7 us -> 14.3 us  [the longest x1 9.51 us: front(): call(functools.partial(front_kernel, heads=heads, chunk=chunk, n_small=le...]
    ppermute x14 -> x20, starting transfers between devices: 13.8 us -> 18.2 us  [swap(): return lax.ppermute(x, 'seq', [(i, i ^ distance) for i in range(count)])]
    pallas_call x4 -> x6, Pallas kernels: 11.2 us -> 8.52 us  [back(): call(functools.partial(back_kernel, heads=heads, aliases=len(done) + 1, f...]
    pallas_call x3, Pallas kernels: 8.75 us -> 10 us  [within(): call(functools.partial(within_kernel, heads=heads, first=first, count=cou...]
  transfers between devices with their start and end apart: 14 -> 20, of which waited for: 13 -> 16; matrix products, arithmetic and copies ran while one was open for 0% -> 0% of each run, Pallas kernels for 13% -> 19%
where the time goes in v4:
time: 98 us; the launch traced here: 97.8 us
  waiting for transfers between devices  42.2 us (43%)
  Pallas kernels  35.8 us (37%)
  starting transfers between devices  18.2 us (19%)
    ppermute x20, waiting for transfers between devices, swap(): return lax.ppermute(x, 'seq', [(i, i ^ distance) for i in range(count)])  42.2 us
    ppermute x20, starting transfers between devices, swap(): return lax.ppermute(x, 'seq', [(i, i ^ distance) for i in range(count)])  18.2 us
    pallas_call x3, Pallas kernels, within(): call(functools.partial(within_kernel, heads=heads, first=first, count=cou...  10 us
    pallas_call x1, Pallas kernels, front(): call(functools.partial(front_kernel, heads=heads, chunk=chunk, n_small=le...  9.51 us
    pallas_call x6, Pallas kernels, back(): call(functools.partial(back_kernel, heads=heads, aliases=len(done) + 1, f...  8.52 us
    pallas_call x1, Pallas kernels, grads(): call(body, 'grads', 1, (), [HELD] * (5 + len(gains)), [HELD] * 2, [pltpu....  2.02 us
  transfers between devices with their start and end apart: 20, of which 16 were waited for; matrix products, arithmetic and copies ran while one was open for 0% of the time, Pallas kernels for 19%

profile of v4, /device:TPU:0, one launch (start us, length us, event | category | flops | bytes accessed | tf_op | source)
XLA Modules:
  0.0 97.8 jit_solution(5180200533078891984)
XLA Ops:
  0.6 9.5 %front.1 = (bf16[16,128,1024]{2,1,0:T(8,128)(2,1)S(1)}, bf16[16,128,512]{2,1,0:T(8,128)(2,1)S(1)}, bf16[16,128,128]{2,1,0:T(8,128)(2,1)S(1)}, f32[128,128]{1,0:T...) custom-call(s32[1]{0:T(128)} %bitcast.me_ref, ...), custom_call_target="tpu_custom_call" | custom-call | flops 5000000000 | bytes 14000000 | tf_op jit(solution)/shard_map/front/pallas_call | solution.py:368
  10.2 0.5 collective-permute-start
  10.7 1.6 %collective-permute-done.came = bf16[528,512]{1,0:T(8,128)(2,1)S(1)} collective-permute-done((bf16[528,512]{1,0:T(8,128)(2,1)S(1)}, bf16[528,512]{1,0:T(8,128)(2,1)S(1)}, u32[]{:S(2)}, u32[]{:S(2)}) %collective-permute-start) | collective-permute-done | bytes 540704 | tf_op jit(solution)/shard_map/ppermute | solution.py:471
  12.2 0.3 rise.3
  12.6 2.9 %collective-permute-start.1 = (bf16[272,512]{1,0:T(8,128)(2,1)S(1)}, bf16[272,512]{1,0:T(8,128)(2,1)S(1)}, u32[]{:S(2)}, u32[]{:S(2)}) collective-permute-start(bf16[272,512]{1,0:T(8,128)(2,1)S(1)} %get-tuple-element.119), channel_id=1, source_target_pairs={{0,2},{1,3},{2,0},{3,1},{4,6},{5,7},{6,4},{7,5},{8,10},{9,11},{10,... | collective-permute-start | bytes 835592 | tf_op jit(solution)/shard_map/ppermute | solution.py:471
  15.5 3.6 %within.3 = (f32[16,128,512]{2,1,0:T(8,128)S(1)}, bf16[16,128,512]{2,1,0:T(8,128)(2,1)S(1)}, bf16[16,8,128,128]{3,2,1,0:T(8,128)(2,1)S(1)}, f32[16,128,512]{2,1,...) custom-call(bf16[16,128,512]{2,1,0:T(8,128)(2,1)S(1)} %get-tuple-ele, ...), custom_call_target="tpu_custom_call", output_to_operand_aliasing={{6}: (7, {})} | custom-call | flops 1800000000 | bytes 9000000 | tf_op jit(solution)/shard_map/within/pallas_call | solution.py:389
  19.2 3.3 %collective-permute-done.1.came = bf16[272,512]{1,0:T(8,128)(2,1)S(1)} collective-permute-done((bf16[272,512]{1,0:T(8,128)(2,1)S(1)}, bf16[272,512]{1,0:T(8,128)(2,1)S(1)}, u32[]{:S(2)}, u32[]{:S(2)}) %collective-permute-start.1) | collective-permute-done | bytes 278560 | tf_op jit(solution)/shard_map/ppermute | solution.py:471
  22.5 0.2 rise.4
  22.6 1.9 %collective-permute-start.2 = (bf16[144,512]{1,0:T(8,128)(2,1)S(1)}, bf16[144,512]{1,0:T(8,128)(2,1)S(1)}, u32[]{:S(2)}, u32[]{:S(2)}) collective-permute-start(bf16[144,512]{1,0:T(8,128)(2,1)S(1)} %get-tuple-element.134), channel_id=1, source_target_pairs={{0,4},{1,5},{2,6},{3,7},{4,0},{5,1},{6,2},{7,3},{8,12},{9,13},{10,... | collective-permute-start | bytes 442376 | tf_op jit(solution)/shard_map/ppermute | solution.py:471
  24.5 2.5 %within.4 = (f32[16,128,512]{2,1,0:T(8,128)S(1)}, bf16[16,128,512]{2,1,0:T(8,128)(2,1)S(1)}, bf16[16,8,128,128]{3,2,1,0:T(8,128)(2,1)S(1)}, f32[16,128,512]{2,1,...) custom-call(bf16[16,128,512]{2,1,0:T(8,128)(2,1)S(1)} %get-tuple-ele, ...), custom_call_target="tpu_custom_call", output_to_operand_aliasing={{0}: (7, {}), {1}: (8, {}), {2}: (9, {}), {3}: (10, {}), {4... | custom-call | flops 1200000000 | bytes 6000000 | tf_op jit(solution)/shard_map/within/pallas_call | solution.py:389
  27.1 1.0 %collective-permute-done.2.came = bf16[144,512]{1,0:T(8,128)(2,1)S(1)} collective-permute-done((bf16[144,512]{1,0:T(8,128)(2,1)S(1)}, bf16[144,512]{1,0:T(8,128)(2,1)S(1)}, u32[]{:S(2)}, u32[]{:S(2)}) %collective-permute-start.2) | collective-permute-done | bytes 147488 | tf_op jit(solution)/shard_map/ppermute | solution.py:471
  28.1 0.8 rise.5
  28.9 2.6 %collective-permute-start.3 = (bf16[144,512]{1,0:T(8,128)(2,1)S(1)}, bf16[144,512]{1,0:T(8,128)(2,1)S(1)}, u32[]{:S(2)}, u32[]{:S(2)}) collective-permute-start(bf16[144,512]{1,0:T(8,128)(2,1)S(1)} %get-tuple-element.148), channel_id=1, source_target_pairs={{0,8},{1,9},{2,10},{3,11},{4,12},{5,13},{6,14},{7,15},{8,0},{9,1},... | collective-permute-start | bytes 442376 | tf_op jit(solution)/shard_map/ppermute | solution.py:471
  31.5 3.8 %within.5 = (f32[16,128,512]{2,1,0:T(8,128)S(1)}, bf16[16,128,512]{2,1,0:T(8,128)(2,1)S(1)}, bf16[16,8,128,128]{3,2,1,0:T(8,128)(2,1)S(1)}, f32[16,128,512]{2,1,...) custom-call(bf16[16,128,512]{2,1,0:T(8,128)(2,1)S(1)} %get-tuple-ele, ...), custom_call_target="tpu_custom_call", output_to_operand_aliasing={{0}: (7, {}), {1}: (8, {}), {2}: (9, {}), {3}: (10, {}), {4... | custom-call | flops 1800000000 | bytes 9000000 | tf_op jit(solution)/shard_map/within/pallas_call | solution.py:389
  35.3 2.1 %collective-permute-done.3.refs_6_ = bf16[144,512]{1,0:T(8,128)(2,1)S(1)} collective-permute-done((bf16[144,512]{1,0:T(8,128)(2,1)S(1)}, bf16[144,512]{1,0:T(8,128)(2,1)S(1)}, u32[]{:S(2)}, u32[]{:S(2)}) %collective-permute-start.3) | collective-permute-done | bytes 147488 | tf_op jit(solution)/shard_map/ppermute | solution.py:471
  37.7 0.2 collective-permute-start.4
  37.9 1.2 %back.6 = (bf16[16,128,512]{2,1,0:T(8,128)(2,1)S(1)}, bf16[16,128,64]{2,1,0:T(8,128)(2,1)S(1)}, f32[8,512]{1,0:T(8,128)S(1)}, f32[8,128]{1,0:T(8,128)S(1)}) custom-call(s32[1]{0:T(128)} %bitcast.me_ref, bf16[2,64,512]{2,1,0:T(8,128)(2,1)S(1)} %get-tuple-element.168.state, ...), custom_call_target="tpu_custom_call", output_to_operand_aliasing={{3}: (9, {})} | custom-call | flops 600000000 | bytes 3000000 | tf_op jit(solution)/shard_map/back/pallas_call | solution.py:417
  39.0 1.2 %back.7 = (bf16[16,128,512]{2,1,0:T(8,128)(2,1)S(1)}, bf16[16,128,64]{2,1,0:T(8,128)(2,1)S(1)}, f32[8,512]{1,0:T(8,128)S(1)}, f32[8,128]{1,0:T(8,128)S(1)}) custom-call(s32[1]{0:T(128)} %bitcast.me_ref, bf16[2,64,512]{2,1,0:T(8,128)(2,1)S(1)} %collective-permute-done.5.state, ...), custom_call_target="tpu_custom_call", output_to_operand_aliasing={{0}: (9, {}), {1}: (10, {}), {3}: (11, {})} | custom-call | flops 600000000 | bytes 3000000 | tf_op jit(solution)/shard_map/back/pallas_call | solution.py:417
  40.2 3.4 %collective-permute-done.4.refs_5_ = bf16[2,64,512]{2,1,0:T(8,128)(2,1)S(1)} collective-permute-done((bf16[2,64,512]{2,1,0:T(8,128)(2,1)S(1)}, bf16[2,64,512]{2,1,0:T(8,128)(2,1)S(1)}, u32[]{:S(2)}, u32[]{:S(2)}) %collective-permute-start.4) | collective-permute-done | bytes 131104 | tf_op jit(solution)/shard_map/ppermute | solution.py:471
  43.6 0.9 fall.4
  44.5 0.9 collective-permute-start.6
  45.5 1.2 %back.8 = (bf16[16,128,512]{2,1,0:T(8,128)(2,1)S(1)}, bf16[16,128,64]{2,1,0:T(8,128)(2,1)S(1)}, f32[8,512]{1,0:T(8,128)S(1)}, f32[8,128]{1,0:T(8,128)S(1)}) custom-call(s32[1]{0:T(128)} %bitcast.me_ref, bf16[2,64,512]{2,1,0:T(8,128)(2,1)S(1)} %get-tuple-element.179.state, ...), custom_call_target="tpu_custom_call", output_to_operand_aliasing={{0}: (9, {}), {1}: (10, {}), {3}: (11, {})} | custom-call | flops 600000000 | bytes 3000000 | tf_op jit(solution)/shard_map/back/pallas_call | solution.py:417
  46.6 1.2 %back.9 = (bf16[16,128,512]{2,1,0:T(8,128)(2,1)S(1)}, bf16[16,128,64]{2,1,0:T(8,128)(2,1)S(1)}, f32[8,512]{1,0:T(8,128)S(1)}, f32[8,128]{1,0:T(8,128)S(1)}) custom-call(s32[1]{0:T(128)} %bitcast.me_ref, bf16[2,64,512]{2,1,0:T(8,128)(2,1)S(1)} %collective-permute-done.7.state, ...), custom_call_target="tpu_custom_call", output_to_operand_aliasing={{0}: (9, {}), {1}: (10, {}), {3}: (11, {})} | custom-call | flops 600000000 | bytes 3000000 | tf_op jit(solution)/shard_map/back/pallas_call | solution.py:417
  47.8 1.6 %grads.2 = (f32[2432,256]{1,0:T(8,128)S(1)}, f32[8,128]{1,0:T(8,128)S(1)}) custom-call(s32[1]{0:T(128)} %bitcast.me_ref, bf16[16,128,512]{2,1,0:T(8,128)(2,1)S(1)} %get-tuple-element.186.normed.refs_0_, bf16[16,128,1024]{2,1,0:T(8,128)(2,1)S(1)} %get-tuple-element.187.cot, ...), custom_call_target="tpu_custom_call", output_to_operand_aliasing={{1}: (5, {})} | custom-call | flops 1200000000 | bytes 7000000 | tf_op jit(solution)/shard_map/grads/pallas_call | solution.py:445
  49.4 3.8 %collective-permute-done.6.refs_2_ = bf16[4,64,512]{2,1,0:T(8,128)(2,1)S(1)} collective-permute-done((bf16[4,64,512]{2,1,0:T(8,128)(2,1)S(1)}, bf16[4,64,512]{2,1,0:T(8,128)(2,1)S(1)}, u32[]{:S(2)}, u32[]{:S(2)}) %collective-permute-start.6) | collective-permute-done | bytes 262176 | tf_op jit(solution)/shard_map/ppermute | solution.py:471
  53.4 1.9 %back.10 = (bf16[16,128,512]{2,1,0:T(8,128)(2,1)S(1)}, bf16[16,128,64]{2,1,0:T(8,128)(2,1)S(1)}, f32[8,512]{1,0:T(8,128)S(1)}, f32[8,128]{1,0:T(8,128)S(1)}) custom-call(s32[1]{0:T(128)} %bitcast.me_ref, bf16[4,64,512]{2,1,0:T(8,128)(2,1)S(1)} %get-tuple-element.194.state, ...), custom_call_target="tpu_custom_call", output_to_operand_aliasing={{0}: (9, {}), {1}: (10, {}), {3}: (11, {})} | custom-call | flops 1200000000 | bytes 6000000 | tf_op jit(solution)/shard_map/back/pallas_call | solution.py:417
  55.4 1.9 %back.11 = (bf16[16,128,512]{2,1,0:T(8,128)(2,1)S(1)}, bf16[16,128,64]{2,1,0:T(8,128)(2,1)S(1)}, f32[8,512]{1,0:T(8,128)S(1)}, f32[8,128]{1,0:T(8,128)S(1)}) custom-call(s32[1]{0:T(128)} %bitcast.me_ref, bf16[4,64,512]{2,1,0:T(8,128)(2,1)S(1)} %collective-permute-done.8.state, ...), custom_call_target="tpu_custom_call", output_to_operand_aliasing={{0}: (9, {}), {1}: (10, {}), {3}: (11, {})} | custom-call | flops 1200000000 | bytes 6000000 | tf_op jit(solution)/shard_map/back/pallas_call | solution.py:417
  57.3 2.0 %grads.3 = (f32[1216,256]{1,0:T(8,128)S(1)}, bf16[1216,256]{1,0:T(8,128)(2,1)S(1)}) custom-call(s32[1]{0:T(128)} %bitcast.me_ref, bf16[16,128,512]{2,1,0:T(8,128)(2,1)S(1)} %get-tuple-element.199.normed, bf16[16,128,1024]{2,1,0:T(8,128)(2,1)S(1)} %get-tuple-element.187.cot, bf16[16,128,64]{2,1,0:T(8,128)(2,1)S(1)} %get-tuple-element.200.read, ...), custom_call_target="tpu_custom_call" | custom-call | flops 1200000000 | bytes 7000000 | tf_op jit(solution)/shard_map/grads/pallas_call | solution.py:450
  59.3 0.6 collective-permute-start.9
  59.9 1.7 %collective-permute-done.9 = bf16[1216,256]{1,0:T(8,128)(2,1)S(1)} collective-permute-done((bf16[1216,256]{1,0:T(8,128)(2,1)S(1)}, bf16[1216,256]{1,0:T(8,128)(2,1)S(1)}, u32[]{:S(2)}, u32[]{:S(2)}) %collective-permute-start.9) | collective-permute-done | bytes 622624 | tf_op jit(solution)/shard_map/ppermute | solution.py:471
  61.8 0.3 collective-permute-start.12
  62.2 1.4 %collective-permute-start.10 = (bf16[304,256]{1,0:T(8,128)(2,1)S(1)}, bf16[304,256]{1,0:T(8,128)(2,1)S(1)}, u32[]{:S(2)}, u32[]{:S(2)}) collective-permute-start(bf16[304,256]{1,0:T(8,128)(2,1)S(1)} %dynamic-slice_convert_fusion.1), channel_id=1, source_target_pairs={{0,2},{1,3},{2,0},{3,1},{4,6},{5,7},{6,4},{7,5},{8,10},{9,11},{10,... | collective-permute-start | bytes 466952 | tf_op jit(solution)/shard_map/ppermute | solution.py:471
  63.6 4.6 %collective-permute-done.12 = bf16[304,256]{1,0:T(8,128)(2,1)S(1)} collective-permute-done((bf16[304,256]{1,0:T(8,128)(2,1)S(1)}, bf16[304,256]{1,0:T(8,128)(2,1)S(1)}, u32[]{:S(2)}, u32[]{:S(2)}) %collective-permute-start.12) | collective-permute-done | bytes 155680 | tf_op jit(solution)/shard_map/ppermute | solution.py:471
  68.3 1.0 %collective-permute-start.13 = (bf16[152,256]{1,0:T(8,128)(2,1)S(1)}, bf16[152,256]{1,0:T(8,128)(2,1)S(1)}, u32[]{:S(2)}, u32[]{:S(2)}) collective-permute-start(bf16[152,256]{1,0:T(8,128)(2,1)S(1)} %dynamic-slice_convert_fusion.2), channel_id=1, source_target_pairs={{0,2},{1,3},{2,0},{3,1},{4,6},{5,7},{6,4},{7,5},{8,10},{9,11},{10,... | collective-permute-start | bytes 233480 | tf_op jit(solution)/shard_map/ppermute | solution.py:471
  69.3 0.8 collective-permute-start.11
  70.2 2.6 %collective-permute-done.13 = bf16[152,256]{1,0:T(8,128)(2,1)S(1)} collective-permute-done((bf16[152,256]{1,0:T(8,128)(2,1)S(1)}, bf16[152,256]{1,0:T(8,128)(2,1)S(1)}, u32[]{:S(2)}, u32[]{:S(2)}) %collective-permute-start.13) | collective-permute-done | bytes 77856 | tf_op jit(solution)/shard_map/ppermute | solution.py:471
  72.8 1.0 %collective-permute-done.11 = bf16[152,256]{1,0:T(8,128)(2,1)S(1)} collective-permute-done((bf16[152,256]{1,0:T(8,128)(2,1)S(1)}, bf16[152,256]{1,0:T(8,128)(2,1)S(1)}, u32[]{:S(2)}, u32[]{:S(2)}) %collective-permute-start.11) | collective-permute-done | bytes 77856 | tf_op jit(solution)/shard_map/ppermute | solution.py:471
  73.9 2.4 %collective-permute-start.14 = (bf16[304,256]{1,0:T(8,128)(2,1)S(1)}, bf16[304,256]{1,0:T(8,128)(2,1)S(1)}, u32[]{:S(2)}, u32[]{:S(2)}) collective-permute-start(bf16[304,256]{1,0:T(8,128)(2,1)S(1)} %fusion), channel_id=1, source_target_pairs={{0,8},{1,9},{2,10},{3,11},{4,12},{5,13},{6,14},{7,15},{8,0},{9,1},... | collective-permute-start | bytes 466952 | tf_op jit(solution)/shard_map/ppermute | solution.py:471
  76.2 6.3 %collective-permute-done.14 = bf16[304,256]{1,0:T(8,128)(2,1)S(1)} collective-permute-done((bf16[304,256]{1,0:T(8,128)(2,1)S(1)}, bf16[304,256]{1,0:T(8,128)(2,1)S(1)}, u32[]{:S(2)}, u32[]{:S(2)}) %collective-permute-start.14) | collective-permute-done | bytes 155680 | tf_op jit(solution)/shard_map/ppermute | solution.py:471
  82.6 1.1 %collective-permute-start.17 = (bf16[152,256]{1,0:T(8,128)(2,1)S(1)}, bf16[152,256]{1,0:T(8,128)(2,1)S(1)}, u32[]{:S(2)}, u32[]{:S(2)}) collective-permute-start(bf16[152,256]{1,0:T(8,128)(2,1)S(1)} %get-tuple-element.216), channel_id=1, source_target_pairs={{0,2},{1,3},{2,0},{3,1},{4,6},{5,7},{6,4},{7,5},{8,10},{9,11},{10,... | collective-permute-start | bytes 233480 | tf_op jit(solution)/shard_map/ppermute | solution.py:471
  83.7 3.3 %collective-permute-done.17 = bf16[152,256]{1,0:T(8,128)(2,1)S(1)} collective-permute-done((bf16[152,256]{1,0:T(8,128)(2,1)S(1)}, bf16[152,256]{1,0:T(8,128)(2,1)S(1)}, u32[]{:S(2)}, u32[]{:S(2)}) %collective-permute-start.17) | collective-permute-done | bytes 77856 | tf_op jit(solution)/shard_map/ppermute | solution.py:471
  87.1 0.5 collective-permute-start.18
  87.5 1.1 %collective-permute-done.15 = bf16[152,256]{1,0:T(8,128)(2,1)S(1)} collective-permute-done((bf16[152,256]{1,0:T(8,128)(2,1)S(1)}, bf16[152,256]{1,0:T(8,128)(2,1)S(1)}, u32[]{:S(2)}, u32[]{:S(2)}) %collective-permute-start.15) | collective-permute-done | bytes 77856 | tf_op jit(solution)/shard_map/ppermute | solution.py:471
  88.7 0.8 collective-permute-start.16
  89.4 2.9 %collective-permute-done.18 = bf16[304,256]{1,0:T(8,128)(2,1)S(1)} collective-permute-done((bf16[304,256]{1,0:T(8,128)(2,1)S(1)}, bf16[304,256]{1,0:T(8,128)(2,1)S(1)}, u32[]{:S(2)}, u32[]{:S(2)}) %collective-permute-start.18) | collective-permute-done | bytes 155680 | tf_op jit(solution)/shard_map/ppermute | solution.py:471
  92.5 1.5 %collective-permute-done.16 = bf16[304,256]{1,0:T(8,128)(2,1)S(1)} collective-permute-done((bf16[304,256]{1,0:T(8,128)(2,1)S(1)}, bf16[304,256]{1,0:T(8,128)(2,1)S(1)}, u32[]{:S(2)}, u32[]{:S(2)}) %collective-permute-start.16) | collective-permute-done | bytes 155680 | tf_op jit(solution)/shard_map/ppermute | solution.py:471
  94.2 2.0 %collective-permute-done.19.came = bf16[1216,256]{1,0:T(8,128)(2,1)S(1)} collective-permute-done((bf16[1216,256]{1,0:T(8,128)(2,1)S(1)}, bf16[1216,256]{1,0:T(8,128)(2,1)S(1)}, u32[]{:S(2)}, u32[]{:S(2)}) %collective-permute-start.19) | collective-permute-done | bytes 622624 | tf_op jit(solution)/shard_map/ppermute | solution.py:471
  96.3 1.6 %finish.1 = (f32[512,1024]{1,0:T(8,128)}, f32[64,1024]{1,0:T(8,128)}, f32[1,512]{1,0:T(1,128)}) custom-call(s32[1]{0:T(128)} %bitcast.me_ref, bf16[1216,256]{1,0:T(8,128)(2,1)S(1)} %pad_maximum_fusion.mine, bf16[1216,256]{1,0:T(8,128)(2,1)S(1)} %collective-permute-done.19.came), custom_call_target="tpu_custom_call" | custom-call | flops 1000000 | bytes 4000000 | tf_op jit(solution)/shard_map/finish/pallas_call | solution.py:458
  (29 shorter events, 1.4 us)
Async XLA Ops:
  10.2 2.1 %collective-permute-start = (bf16[528,512]{1,0:T(8,128)(2,1)S(1)}, bf16[528,512]{1,0:T(8,128)(2,1)S(1)}, u32[]{:S(2)}, u32[]{:S(2)}) collective-permute-start(bf16[528,512]{1,0:T(8,128)(2,1)S(1)} %get-tuple-element.112), channel_id=1, source_target_pairs={{0,1},{1,0},{2,3},{3,2},{4,5},{5,4},{6,7},{7,6},{8,9},{9,8},{10,11... | collective-permute-start | bytes 1622024 | tf_op jit(solution)/shard_map/ppermute | solution.py:471
  12.6 9.9 %collective-permute-start.1 = (bf16[272,512]{1,0:T(8,128)(2,1)S(1)}, bf16[272,512]{1,0:T(8,128)(2,1)S(1)}, u32[]{:S(2)}, u32[]{:S(2)}) collective-permute-start(bf16[272,512]{1,0:T(8,128)(2,1)S(1)} %get-tuple-element.119), channel_id=1, source_target_pairs={{0,2},{1,3},{2,0},{3,1},{4,6},{5,7},{6,4},{7,5},{8,10},{9,11},{10,... | collective-permute-start | bytes 835592 | tf_op jit(solution)/shard_map/ppermute | solution.py:471
  22.6 5.4 %collective-permute-start.2 = (bf16[144,512]{1,0:T(8,128)(2,1)S(1)}, bf16[144,512]{1,0:T(8,128)(2,1)S(1)}, u32[]{:S(2)}, u32[]{:S(2)}) collective-permute-start(bf16[144,512]{1,0:T(8,128)(2,1)S(1)} %get-tuple-element.134), channel_id=1, source_target_pairs={{0,4},{1,5},{2,6},{3,7},{4,0},{5,1},{6,2},{7,3},{8,12},{9,13},{10,... | collective-permute-start | bytes 442376 | tf_op jit(solution)/shard_map/ppermute | solution.py:471
  28.9 8.5 %collective-permute-start.3 = (bf16[144,512]{1,0:T(8,128)(2,1)S(1)}, bf16[144,512]{1,0:T(8,128)(2,1)S(1)}, u32[]{:S(2)}, u32[]{:S(2)}) collective-permute-start(bf16[144,512]{1,0:T(8,128)(2,1)S(1)} %get-tuple-element.148), channel_id=1, source_target_pairs={{0,8},{1,9},{2,10},{3,11},{4,12},{5,13},{6,14},{7,15},{8,0},{9,1},... | collective-permute-start | bytes 442376 | tf_op jit(solution)/shard_map/ppermute | solution.py:471
  37.6 1.4 %collective-permute-start.5 = (bf16[2,64,512]{2,1,0:T(8,128)(2,1)S(1)}, bf16[2,64,512]{2,1,0:T(8,128)(2,1)S(1)}, u32[]{:S(2)}, u32[]{:S(2)}) collective-permute-start(bf16[2,64,512]{2,1,0:T(8,128)(2,1)S(1)} %get-tuple-element.162), channel_id=1, source_target_pairs={{0,1},{1,0},{2,3},{3,2},{4,5},{5,4},{6,7},{7,6},{8,9},{9,8},{10,11... | collective-permute-start | bytes 393224 | tf_op jit(solution)/shard_map/ppermute | solution.py:471
  37.7 5.9 %collective-permute-start.4 = (bf16[2,64,512]{2,1,0:T(8,128)(2,1)S(1)}, bf16[2,64,512]{2,1,0:T(8,128)(2,1)S(1)}, u32[]{:S(2)}, u32[]{:S(2)}) collective-permute-start(bf16[2,64,512]{2,1,0:T(8,128)(2,1)S(1)} %get-tuple-element.161), channel_id=1, source_target_pairs={{0,4},{1,5},{2,6},{3,7},{4,0},{5,1},{6,2},{7,3},{8,12},{9,13},{10,... | collective-permute-start | bytes 393224 | tf_op jit(solution)/shard_map/ppermute | solution.py:471
  44.5 2.1 %collective-permute-start.7 = (bf16[2,64,512]{2,1,0:T(8,128)(2,1)S(1)}, bf16[2,64,512]{2,1,0:T(8,128)(2,1)S(1)}, u32[]{:S(2)}, u32[]{:S(2)}) collective-permute-start(bf16[2,64,512]{2,1,0:T(8,128)(2,1)S(1)} %get-tuple-element.178), channel_id=1, source_target_pairs={{0,1},{1,0},{2,3},{3,2},{4,5},{5,4},{6,7},{7,6},{8,9},{9,8},{10,11... | collective-permute-start | bytes 393224 | tf_op jit(solution)/shard_map/ppermute | solution.py:471
  44.5 8.7 %collective-permute-start.6 = (bf16[4,64,512]{2,1,0:T(8,128)(2,1)S(1)}, bf16[4,64,512]{2,1,0:T(8,128)(2,1)S(1)}, u32[]{:S(2)}, u32[]{:S(2)}) collective-permute-start(bf16[4,64,512]{2,1,0:T(8,128)(2,1)S(1)} %get-tuple-element.177), channel_id=1, source_target_pairs={{0,2},{1,3},{2,0},{3,1},{4,6},{5,7},{6,4},{7,5},{8,10},{9,11},{10,... | collective-permute-start | bytes 786440 | tf_op jit(solution)/shard_map/ppermute | solution.py:471
  53.4 2.0 %collective-permute-start.8 = (bf16[4,64,512]{2,1,0:T(8,128)(2,1)S(1)}, bf16[4,64,512]{2,1,0:T(8,128)(2,1)S(1)}, u32[]{:S(2)}, u32[]{:S(2)}) collective-permute-start(bf16[4,64,512]{2,1,0:T(8,128)(2,1)S(1)} %get-tuple-element.193), channel_id=1, source_target_pairs={{0,1},{1,0},{2,3},{3,2},{4,5},{5,4},{6,7},{7,6},{8,9},{9,8},{10,11... | collective-permute-start | bytes 786440 | tf_op jit(solution)/shard_map/ppermute | solution.py:471
  59.3 2.3 %collective-permute-start.9 = (bf16[1216,256]{1,0:T(8,128)(2,1)S(1)}, bf16[1216,256]{1,0:T(8,128)(2,1)S(1)}, u32[]{:S(2)}, u32[]{:S(2)}) collective-permute-start(bf16[1216,256]{1,0:T(8,128)(2,1)S(1)} %get-tuple-element.209), channel_id=1, source_target_pairs={{0,1},{1,0},{2,3},{3,2},{4,5},{5,4},{6,7},{7,6},{8,9},{9,8},{10,11... | collective-permute-start | bytes 1867784 | tf_op jit(solution)/shard_map/ppermute | solution.py:471
  61.8 6.4 %collective-permute-start.12 = (bf16[304,256]{1,0:T(8,128)(2,1)S(1)}, bf16[304,256]{1,0:T(8,128)(2,1)S(1)}, u32[]{:S(2)}, u32[]{:S(2)}) collective-permute-start(bf16[304,256]{1,0:T(8,128)(2,1)S(1)} %dynamic-slice_convert_fusion), channel_id=1, source_target_pairs={{0,4},{1,5},{2,6},{3,7},{4,0},{5,1},{6,2},{7,3},{8,12},{9,13},{10,... | collective-permute-start | bytes 466952 | tf_op jit(solution)/shard_map/ppermute | solution.py:471
  62.2 7.1 %collective-permute-start.10 = (bf16[304,256]{1,0:T(8,128)(2,1)S(1)}, bf16[304,256]{1,0:T(8,128)(2,1)S(1)}, u32[]{:S(2)}, u32[]{:S(2)}) collective-permute-start(bf16[304,256]{1,0:T(8,128)(2,1)S(1)} %dynamic-slice_convert_fusion.1), channel_id=1, source_target_pairs={{0,2},{1,3},{2,0},{3,1},{4,6},{5,7},{6,4},{7,5},{8,10},{9,11},{10,... | collective-permute-start | bytes 466952 | tf_op jit(solution)/shard_map/ppermute | solution.py:471
  68.3 4.5 %collective-permute-start.13 = (bf16[152,256]{1,0:T(8,128)(2,1)S(1)}, bf16[152,256]{1,0:T(8,128)(2,1)S(1)}, u32[]{:S(2)}, u32[]{:S(2)}) collective-permute-start(bf16[152,256]{1,0:T(8,128)(2,1)S(1)} %dynamic-slice_convert_fusion.2), channel_id=1, source_target_pairs={{0,2},{1,3},{2,0},{3,1},{4,6},{5,7},{6,4},{7,5},{8,10},{9,11},{10,... | collective-permute-start | bytes 233480 | tf_op jit(solution)/shard_map/ppermute | solution.py:471
  69.3 4.5 %collective-permute-start.11 = (bf16[152,256]{1,0:T(8,128)(2,1)S(1)}, bf16[152,256]{1,0:T(8,128)(2,1)S(1)}, u32[]{:S(2)}, u32[]{:S(2)}) collective-permute-start(bf16[152,256]{1,0:T(8,128)(2,1)S(1)} %dynamic-slice_convert_fusion.3), channel_id=1, source_target_pairs={{0,4},{1,5},{2,6},{3,7},{4,0},{5,1},{6,2},{7,3},{8,12},{9,13},{10,... | collective-permute-start | bytes 233480 | tf_op jit(solution)/shard_map/ppermute | solution.py:471
  73.9 8.6 %collective-permute-start.14 = (bf16[304,256]{1,0:T(8,128)(2,1)S(1)}, bf16[304,256]{1,0:T(8,128)(2,1)S(1)}, u32[]{:S(2)}, u32[]{:S(2)}) collective-permute-start(bf16[304,256]{1,0:T(8,128)(2,1)S(1)} %fusion), channel_id=1, source_target_pairs={{0,8},{1,9},{2,10},{3,11},{4,12},{5,13},{6,14},{7,15},{8,0},{9,1},... | collective-permute-start | bytes 466952 | tf_op jit(solution)/shard_map/ppermute | solution.py:471
  82.6 4.5 %collective-permute-start.17 = (bf16[152,256]{1,0:T(8,128)(2,1)S(1)}, bf16[152,256]{1,0:T(8,128)(2,1)S(1)}, u32[]{:S(2)}, u32[]{:S(2)}) collective-permute-start(bf16[152,256]{1,0:T(8,128)(2,1)S(1)} %get-tuple-element.216), channel_id=1, source_target_pairs={{0,2},{1,3},{2,0},{3,1},{4,6},{5,7},{6,4},{7,5},{8,10},{9,11},{10,... | collective-permute-start | bytes 233480 | tf_op jit(solution)/shard_map/ppermute | solution.py:471
  83.7 4.9 %collective-permute-start.15 = (bf16[152,256]{1,0:T(8,128)(2,1)S(1)}, bf16[152,256]{1,0:T(8,128)(2,1)S(1)}, u32[]{:S(2)}, u32[]{:S(2)}) collective-permute-start(bf16[152,256]{1,0:T(8,128)(2,1)S(1)} %get-tuple-element.215), channel_id=1, source_target_pairs={{0,4},{1,5},{2,6},{3,7},{4,0},{5,1},{6,2},{7,3},{8,12},{9,13},{10,... | collective-permute-start | bytes 233480 | tf_op jit(solution)/shard_map/ppermute | solution.py:471
  87.1 5.3 %collective-permute-start.18 = (bf16[304,256]{1,0:T(8,128)(2,1)S(1)}, bf16[304,256]{1,0:T(8,128)(2,1)S(1)}, u32[]{:S(2)}, u32[]{:S(2)}) collective-permute-start(bf16[304,256]{1,0:T(8,128)(2,1)S(1)} %maximum_select_fusion.3), channel_id=1, source_target_pairs={{0,4},{1,5},{2,6},{3,7},{4,0},{5,1},{6,2},{7,3},{8,12},{9,13},{10,... | collective-permute-start | bytes 466952 | tf_op jit(solution)/shard_map/ppermute | solution.py:471
  88.7 5.3 %collective-permute-start.16 = (bf16[304,256]{1,0:T(8,128)(2,1)S(1)}, bf16[304,256]{1,0:T(8,128)(2,1)S(1)}, u32[]{:S(2)}, u32[]{:S(2)}) collective-permute-start(bf16[304,256]{1,0:T(8,128)(2,1)S(1)} %maximum_select_fusion.2), channel_id=1, source_target_pairs={{0,2},{1,3},{2,0},{3,1},{4,6},{5,7},{6,4},{7,5},{8,10},{9,11},{10,... | collective-permute-start | bytes 466952 | tf_op jit(solution)/shard_map/ppermute | solution.py:471
  94.1 2.1 %collective-permute-start.19 = (bf16[1216,256]{1,0:T(8,128)(2,1)S(1)}, bf16[1216,256]{1,0:T(8,128)(2,1)S(1)}, u32[]{:S(2)}, u32[]{:S(2)}) collective-permute-start(bf16[1216,256]{1,0:T(8,128)(2,1)S(1)} %pad_maximum_fusion.mine), channel_id=1, source_target_pairs={{0,1},{1,0},{2,3},{3,2},{4,5},{5,4},{6,7},{7,6},{8,9},{9,8},{10,11... | collective-permute-start | bytes 1867784 | tf_op jit(solution)/shard_map/ppermute | solution.py:471

commit v5 on v4

--- a/solution.py
+++ b/solution.py
@@ -201,24 +201,34 @@
     grad_ref[own] = grad.reshape(count, span, width)
 
 
-def back_kernel(me_ref, state, maps, scaled, decay, part, grad, cum, consts, *refs, heads, aliases, first):
-    normed_ref, read_ref, gain_ref, _, spread2, fade_sc, carried_sc, spread_sc, back_sc, faded_sc = refs[aliases:]
-    _, span, width = part.shape
+def block_start(me, flips, sensors):
+    return shard_start(me ^ flips, 2, sensors)
+
+
+def back_kernel(me_ref, *refs, heads, blocks, aliases):
+    states, refs = refs[0], refs[1:]
+    maps, scaled, decay, part, grad, cum, consts = refs[:7]
+    normed_ref, read_ref, gain_ref, _, spread2, fade_sc, carried_sc, spread_sc, back_sc, faded_sc = refs[7 + aliases :]
+    sensors, span, width = part.shape
     nstate = maps.shape[2] // 2
     size = width // heads
-    at_once = carried_sc.shape[0]
+    each = states.shape[0] // len(blocks)
     spread2[...] = spread_matrix(spread2.shape[0], heads, width)
     fade_sc[...] = jnp.exp2(cum[...])
-    begin = first(me_ref[0])
     chunk = 32
-
-    def carry_in(k, slot):
-        s = begin + k
+    todo = [
+        (block_start(me_ref[0], flips, sensors) + k, states, n * each + k)
+        for n, flips in enumerate(blocks)
+        for k in range(each)
+    ]
+
+    def carry_in(slot):
+        s, state, k = todo[slot]
         carried_sc[slot] = dot(maps[s][:, nstate:], state[k])
         spread_sc[slot] = spread(fade_sc[...], s, heads, spread2[...])
 
-    def normalize(k, slot, gain_sum):
-        s = begin + k
+    def normalize(slot, gain_sum):
+        s = todo[slot][0]
         gain = consts[1:2, :]
         for c in range(0, span, chunk):
             rows = slice(c, c + chunk)
@@ -236,8 +246,8 @@
             faded_sc[slot, rows, :] = (back * fade).astype(bf16)
         return gain_sum
 
-    def read_out(k, slot):
-        s = begin + k
+    def read_out(slot):
+        s, state, k = todo[slot]
         read = dot(faded_sc[slot], state[k], NT)
         pairs = jnp.zeros((span, span), f32)
         for pair in range(heads // 2):
@@ -247,81 +257,99 @@
             pairs = pairs + both_heads[:, span:] * decay[s, 2 * pair + 1].astype(f32)
         read_ref[s] = (read + dot(pairs.astype(bf16), maps[s][:, 0:nstate])).astype(bf16)
 
-    def block(i, gain_sum):
-        for slot in range(at_once):
-            carry_in(i * at_once + slot, slot)
-        for slot in range(at_once):
-            gain_sum = normalize(i * at_once + slot, slot, gain_sum)
-        for slot in range(at_once):
-            read_out(i * at_once + slot, slot)
-        return gain_sum
-
-    gain_ref[...] = lax.fori_loop(0, state.shape[0] // at_once, block, jnp.zeros(gain_ref.shape, f32))
-
-
-def grads_kernel(me_ref, normed, cot, read, mixed, *refs, starts, more, n_gains):
-    if more:
-        before, gains, (keep_ref, send_ref, total) = refs[0], refs[1 : 1 + n_gains], refs[1 + n_gains :]
-    else:
-        total = refs[0]
-    block = normed.shape[0] // 4
+    gain_sum = jnp.zeros(gain_ref.shape, f32)
+    for slot in range(len(todo)):
+        carry_in(slot)
+    for slot in range(len(todo)):
+        gain_sum = normalize(slot, gain_sum)
+    for slot in range(len(todo)):
+        read_out(slot)
+    gain_ref[...] = gain_sum
+
+
+PIECE = 256
+
+
+def grad_piece(normed, cot, read, mixed, blocks, piece):
     span, channels = normed.shape[1:]
-    width, nstate = cot.shape[2], read.shape[2]
-    piece = total.shape[1]
-    pieces = width // piece
-    rows = block * span
-    blocks = [pl.ds(start, block) for start in starts(me_ref[0])]
-
-    def put(at, size, value):
-        total[at : at + size, :] = value + before[at : at + size, :] if more else value
-
-    for j in range(pieces):
-        lanes = slice(j * piece, (j + 1) * piece)
-        put(j * channels, channels, sum(
-            dot(normed[here].reshape(rows, channels), cot[here, :, lanes].reshape(rows, piece), TN) for here in blocks
-        ))
-        put(pieces * channels + j * nstate, nstate, sum(
-            dot(read[here].reshape(rows, nstate), mixed[here, :, lanes].reshape(rows, piece), TN) for here in blocks
-        ))
-    if not more:
-        return
-    used = pieces * (channels + nstate)
-    total[used:, :] = jnp.zeros((total.shape[0] - used, piece), f32)
+    lanes = slice(piece * PIECE, (piece + 1) * PIECE)
+
+    def product(left, right, start, size):
+        here = pl.ds(start, size)
+        rows = size * span
+        return dot(left[here].reshape(rows, left.shape[2]), right[here, :, lanes].reshape(rows, PIECE), TN)
+
+    return (
+        sum(product(normed, cot, *block) for block in blocks),
+        sum(product(read, mixed, *block) for block in blocks),
+    )
+
+
+def early_blocks(me, sensors):
+    return [(block_start(me, flips, sensors), 2) for flips in (0, 1)]
+
+
+def late_blocks(me, sensors):
+    size = sensors // 4
+    for other in (0, 1):
+        yield block_start(me, 4 ^ other, sensors), 2
+        yield shard_start(me ^ 2 ^ other, 1, sensors), size
+
+
+def early_kernel(me_ref, normed, cot, read, mixed, _, total, __):
+    channels, nstate = normed.shape[2], read.shape[2]
+    for piece in range(total.shape[0]):
+        out, into = grad_piece(normed, cot, read, mixed, early_blocks(me_ref[0], normed.shape[0]), piece)
+        total[piece, 0:channels, :] = out
+        total[piece, channels : channels + nstate, :] = into
+
+
+def late_kernel(me_ref, normed, cot, read, mixed, before, *refs, part):
+    *gains, keep_ref, send_ref, total = refs
+    channels, nstate = normed.shape[2], read.shape[2]
+    pieces = before.shape[0]
+    own = channels // pieces
+    bit = me_ref[0] & 1
     gain = sum(jnp.sum(ref[...], axis=0, keepdims=True) for ref in gains)
-    for j in range(channels // piece):
-        total[used + j : used + j + 1, :] = gain[:, j * piece : (j + 1) * piece]
-    half = keep_ref.shape[0]
-    mine = pl.multiple_of((me_ref[0] & 1) * half, 8)
-    other = pl.multiple_of(half - (me_ref[0] & 1) * half, 8)
-    keep_ref[...] = total[pl.ds(mine, half), :]
-    send_ref[...] = total[pl.ds(other, half), :].astype(bf16)
-
-
-def finish_kernel(me_ref, mine, came, out_ref, read_ref, gain_ref):
-    channels, width = out_ref.shape
-    nstate = read_ref.shape[0]
-    half, piece = mine.shape
-    pieces = width // piece
-
-    def write(low, high):
-        def rows(start, size):
-            parts = []
-            if start < half:
-                parts.append(low[start : min(start + size, half), :])
-            if start + size > half:
-                parts.append(high[max(start - half, 0) : start + size - half, :])
-            return jnp.concatenate([part.astype(f32) for part in parts], axis=0)
-
-        for j in range(pieces):
-            lanes = slice(j * piece, (j + 1) * piece)
-            out_ref[:, lanes] = rows(j * channels, channels)
-            read_ref[:, lanes] = rows(pieces * channels + j * nstate, nstate)
-        tail = rows(pieces * (channels + nstate), 8)
-        for j in range(channels // piece):
-            gain_ref[:, j * piece : (j + 1) * piece] = tail[j : j + 1, :]
-
-    pl.when(me_ref[0] & 1 == 0)(lambda: write(mine, came))
-    pl.when(me_ref[0] & 1 == 1)(lambda: write(came, mine))
+    for half in range(2):
+        piece = half * (pieces // 2) + part
+        out, into = grad_piece(normed, cot, read, mixed, list(late_blocks(me_ref[0], normed.shape[0])), piece)
+        total[half, 0:channels, :] = out + before[piece, 0:channels, :]
+        total[half, channels : channels + nstate, :] = into + before[piece, channels : channels + nstate, :]
+        rest = total.shape[1] - channels - nstate
+        total[half, channels + nstate :, :] = jnp.zeros((rest, PIECE), f32)
+        total[half, channels + nstate : channels + nstate + 1, 0:own] = gain[:, piece * own : (piece + 1) * own]
+    keep_ref[...] = total[bit]
+    send_ref[...] = total[1 - bit].astype(bf16)
+
+
+def finish_kernel(me_ref, mine, came, *refs, part, aliases):
+    out_hbm, read_hbm, gain_hbm, out_sc, read_sc, gain_sc, sems = refs[aliases:]
+    nstate = read_hbm.shape[0]
+    channels, width = out_hbm.shape
+    pieces = width // PIECE
+    own = channels // pieces
+
+    def write(halves):
+        copies = []
+        for half, rows in enumerate(halves):
+            piece = half * (pieces // 2) + part
+            out_sc[half] = rows[0:channels, :].astype(f32)
+            read_sc[half] = rows[channels : channels + nstate, :].astype(f32)
+            gain_sc[half] = rows[channels + nstate : channels + nstate + 1, 0:own].astype(f32)
+            lanes = pl.ds(piece * PIECE, PIECE)
+            copies += [
+                pltpu.make_async_copy(out_sc.at[half], out_hbm.at[:, lanes], sems.at[half, 0]),
+                pltpu.make_async_copy(read_sc.at[half], read_hbm.at[:, lanes], sems.at[half, 1]),
+                pltpu.make_async_copy(gain_sc.at[half], gain_hbm.at[:, pl.ds(piece * own, own)], sems.at[half, 2]),
+            ]
+            for copy in copies[-3:]:
+                copy.start()
+        for copy in copies:
+            copy.wait()
+
+    pl.when(me_ref[0] & 1 == 0)(lambda: write((mine, came)))
+    pl.when(me_ref[0] & 1 == 1)(lambda: write((came, mine)))
 
 
 def whole(shape):
@@ -405,21 +433,19 @@
     )
 
 
-def back(me, first, state, maps, scaled, decay, part, grad, cum, consts, done, token):
+def back(me, blocks, states, maps, scaled, decay, part, grad, cum, consts, done, token):
     sensors, span, width = part.shape
-    heads, nmaps = decay.shape[1], maps.shape[2]
-    nstate, lanes = nmaps // 2, sensors * heads
-    count = state.shape[0]
-    at_once = min(count, 4)
-    n_in = 9
+    heads, lanes = decay.shape[1], cum.shape[1]
+    at_once = sum(state.shape[0] for state in states)
+    n_in = 8 + len(states)
     aliases = {n_in + k: k for k in range(len(done))}
     aliases[n_in + len(done)] = 3
     return call(
-        functools.partial(back_kernel, heads=heads, aliases=len(done) + 1, first=first), "back", 1, (),
+        functools.partial(back_kernel, heads=heads, blocks=blocks, aliases=len(done) + 1), "back", 1, (),
         [HELD] * (n_in - 1 + len(done)) + [ANYWHERE],
         [HELD] * 3 + [ANYWHERE],
         [
-            pltpu.VMEM((sensors, span, width), bf16), pltpu.VMEM((sensors, span, nstate), bf16),
+            pltpu.VMEM((sensors, span, width), bf16), pltpu.VMEM((sensors, span, maps.shape[2] // 2), bf16),
             pltpu.VMEM((8, width), f32), jax.ShapeDtypeStruct(token.shape, token.dtype),
         ],
         [
@@ -427,44 +453,46 @@
             pltpu.VMEM((at_once, span, width), f32), pltpu.VMEM((at_once, span, width), f32),
             pltpu.VMEM((at_once, span, width), bf16), pltpu.VMEM((at_once, span, width), bf16),
         ],
-        8, 3e8 * count, 1.5e6 * count, aliases,
-    )(me, *[held(x) for x in (state, maps, scaled, decay, part, grad, cum, consts) + done], token)
-
-
-def grads(me, normed, cot, read, mixed, starts, before, gains, token):
-    channels, width, nstate = normed.shape[2], cot.shape[2], read.shape[2]
-    piece = 256
-    rows = -(-(width // piece * (channels + nstate) + channels // piece) // 128) * 128
-    more = before is not None
-    body = functools.partial(grads_kernel, starts=starts, more=more, n_gains=len(gains))
-    if not more:
-
-        def first(me_ref, normed, cot, read, mixed, _, total, __):
-            body(me_ref, normed, cot, read, mixed, total)
-
-        return call(
-            first, "grads", 1, (), [HELD] * 4 + [ANYWHERE], [HELD, ANYWHERE],
-            [pltpu.VMEM((rows, piece), f32), jax.ShapeDtypeStruct(token.shape, token.dtype)],
-            [], 8, 1.2e9, 7e6, {5: 1},
-        )(me, *[held(x) for x in (normed, cot, read, mixed)], token)
-    return call(
-        body, "grads", 1, (), [HELD] * (5 + len(gains)), [HELD] * 2,
-        [pltpu.VMEM((rows // 2, piece), f32), pltpu.VMEM((rows // 2, piece), bf16)],
-        [pltpu.VMEM((rows, piece), f32)], 12, 1.2e9, 7e6,
+        8, 3e8 * at_once, 1.5e6 * at_once, aliases,
+    )(me, *[held(x) for x in (*states, maps, scaled, decay, part, grad, cum, consts) + done], token)
+
+
+def grad_rows(channels, nstate):
+    return -(-(channels + nstate + 1) // 32) * 32
+
+
+def early_grads(me, normed, cot, read, mixed, token):
+    rows = grad_rows(normed.shape[2], read.shape[2])
+    return call(
+        early_kernel, "early", 1, (), [HELD] * 4 + [ANYWHERE], [HELD, ANYWHERE],
+        [pltpu.VMEM((cot.shape[2] // PIECE, rows, PIECE), f32), jax.ShapeDtypeStruct(token.shape, token.dtype)],
+        [], 8, 6e8, 4e6, {5: 1},
+    )(me, *[held(x) for x in (normed, cot, read, mixed)], token)
+
+
+def late_grads(me, normed, cot, read, mixed, before, gains, part):
+    rows = before.shape[1]
+    return call(
+        functools.partial(late_kernel, part=part), "late", 1, (), [HELD] * (5 + len(gains)), [HELD] * 2,
+        [pltpu.VMEM((rows, PIECE), f32), pltpu.VMEM((rows, PIECE), bf16)],
+        [pltpu.VMEM((2, rows, PIECE), f32)], 10, 8e8, 5e6,
     )(me, *[held(x) for x in (normed, cot, read, mixed, before, *gains)])
 
 
-def finish(me, mine, came, channels, width, nstate):
-    return call(
-        finish_kernel, "finish", 1, (1,),
-        [whole(mine.shape)] * 2,
-        [whole((channels, width)), whole((nstate, width)), whole((1, channels))],
+def finish(me, mine, came, part, channels, width, nstate, done):
+    pieces = width // PIECE
+    return call(
+        functools.partial(finish_kernel, part=part, aliases=len(done)), "finish", 1, (),
+        [HELD] * 2 + [ANYWHERE] * len(done), [ANYWHERE] * 3,
         [
-            jax.ShapeDtypeStruct((channels, width), f32), jax.ShapeDtypeStruct((nstate, width), f32),
-            jax.ShapeDtypeStruct((1, channels), f32),
+            pltpu.HBM((channels, width), f32), pltpu.HBM((nstate, width), f32), pltpu.HBM((1, channels), f32),
         ],
-        [], 8, 1e6, 4e6,
-    )(me, mine, came)
+        [
+            pltpu.VMEM((2, channels, PIECE), f32), pltpu.VMEM((2, nstate, PIECE), f32),
+            pltpu.VMEM((2, 1, channels // pieces), f32), pltpu.SemaphoreType.DMA((2, 3)),
+        ],
+        8, 1e6, 2e6, {3 + k: k for k in range(len(done))},
+    )(me, held(mine), held(came), *[pltpu.with_memory_space_constraint(x, pltpu.HBM) for x in done])
 
 
 def swap(x, distance, count):
@@ -572,142 +600,114 @@
     )(me, *[held(x) for x in (own, tail, before, before_tail, came)])
 
 
-def fall_kernel(me_ref, *refs, level, first, across_level):
+def fall_kernel(me_ref, *refs, levels, sources, across_level, n_outs):
     me = me_ref[0]
-    lows, tails = refs[: level + 1], refs[level + 1 : 2 * (level + 1)]
-    refs = refs[2 * (level + 1) :]
+    lows, tails = refs[:levels], refs[levels : 2 * levels]
+    cames, outs = refs[2 * levels : 2 * levels + len(sources)], refs[2 * levels + len(sources) :]
     sensors = tails[0].shape[0]
-    size, nstate, width = lows[level].shape
-    start = shard_start(me, level, sensors)
-
-    def step(state, q, sensor):
-        return state * jnp.exp2(row(tails[q], sensor)) + lows[q][sensor - shard_start(me, q, sensors)]
-
-    def choose(before, q, sensor):
-        after = step(before, q, sensor)
-        bit = bit_of(me, q)
-        return pick(bit, after, before), pick(bit, before, after)
-
-    def land(state, top, sensor, k):
-        for q in reversed(range(1, top)):
-            state, _ = choose(state, q, sensor)
-        state, other = choose(state, 0, sensor)
-        state_ref[k] = state.astype(bf16)
-        other_ref[k] = other.astype(bf16)
-
-    if level == 0:
-        came, state_ref, other_ref = refs
-        came_size = came.shape[0]
-        came_start = shard_start(me, 1, sensors) + pick(bit_of(me, 1), -came_size, came_size)
-        for k in range(came_size):
-            land(came[k].astype(f32), 1, came_start + k, k)
-        return
-    if first:
-        came, mine_ref, gone_ref, state_ref, other_ref = refs
-        for j in range(size):
-            if across_level is None:
-                before = came[j]
+    nstate = lows[0].shape[1]
+    each = 2
+
+    for n, ((flips, top), came) in enumerate(zip(sources, cames)):
+        for k in range(each):
+            sensor = block_start(me, flips, sensors) + k
+            if len(came.shape) == 3:
+                state = came[k].astype(f32)
             else:
-                before = came[j * nstate : (j + 1) * nstate, :].astype(f32)
-                before = pick(bit_of(me, across_level), before, jnp.zeros_like(before))
-            mine, gone = choose(before, level, start + j)
-            mine_ref[j] = mine
-            gone_ref[j] = gone.astype(bf16)
-            land(mine, level, start + j, j)
-    else:
-        had, came, mine_ref, gone_ref, state_ref, other_ref = refs
-        half = size // 2
-        at = bit_of(me, level + 1) * half
-        for k in range(half):
-            mine, gone = choose(had[k], level, start + at + k)
-            mine_ref[at + k] = mine
-            gone_ref[at + k] = gone.astype(bf16)
-            mine, gone = choose(came[k].astype(f32), level, start + half - at + k)
-            mine_ref[half - at + k] = mine
-            gone_ref[half - at + k] = gone.astype(bf16)
-            land(mine, level, start + half - at + k, k)
-
-
-def fall(me, saved, level, had, came, across_level):
-    lows = [low for low, _ in saved[: level + 1]]
-    tails = [tail for _, tail in saved[: level + 1]]
-    size, nstate, width = lows[level].shape
-    first = had is None
-    arrays = lows + tails + ([came] if first else [had, came])
-    known = size if first and level else size // 2
-    outs = [pltpu.VMEM((size, nstate, width), f32), pltpu.VMEM((size, nstate, width), bf16)] if level else []
-    outs += [pltpu.VMEM((known, nstate, width), bf16)] * 2
-    return call(
-        functools.partial(fall_kernel, level=level, first=first, across_level=across_level), "fall", 1, (),
-        [HELD] * len(arrays), [HELD] * len(outs), outs, [], 6, 1e6, 1e6,
+                state = came[k * nstate : (k + 1) * nstate, :].astype(f32)
+                state = pick(bit_of(me, across_level), state, jnp.zeros_like(state))
+            for q in reversed(range(top)):
+                after = state * jnp.exp2(row(tails[q], sensor)) + lows[q][sensor - shard_start(me, q, sensors)]
+                bit = bit_of(me, q)
+                other = pick(bit, state, after)
+                state = pick(bit, after, state)
+                if q == 0:
+                    outs[1][n * each + k] = other.astype(bf16)
+                else:
+                    outs[1 + q][k] = other.astype(bf16)
+            outs[0][n * each + k] = state.astype(bf16)
+
+
+def fall(me, saved, sources, cames, across_level):
+    levels = max(top for _, top in sources)
+    lows = [low for low, _ in saved[:levels]]
+    tails = [tail for _, tail in saved[:levels]]
+    nstate, width = lows[0].shape[1:]
+    arrays = lows + tails + cames
+    outs = [pltpu.VMEM((2 * len(sources), nstate, width), bf16)] * 2 + [pltpu.VMEM((2, nstate, width), bf16)] * (levels - 1)
+    return call(
+        functools.partial(
+            fall_kernel, levels=levels, sources=sources, across_level=across_level, n_outs=len(outs)
+        ), "fall", 1, (), [HELD] * len(arrays), [HELD] * len(outs), outs, [], 6, 1e6, 1e6,
     )(me, *[held(x) for x in arrays])
 
 
-def exchange(keep, send, tail, me, count, shards, swap_beside, ready):
-    sensors = tail.shape[0]
+SHARDED = 3
+
+
+def rise_all(keep, send, tail, me, count, swap_beside):
     levels = count.bit_length() - 1
     own = keep
     saved = []
-    for level in range(shards):
+    for level in range(SHARDED):
         came = swap_beside(send, level)
-        low, low_tail, tail, own, send = rise(me, own, tail, came, level, level + 1 == shards)
+        low, low_tail, tail, own, send = rise(me, own, tail, came, level, level + 1 == SHARDED)
         saved.append((low, low_tail))
-    if levels == shards + 1:
-        parts = (None, swap_beside(send, shards), shards)
-    else:
-        before, before_tail = jnp.zeros_like(own), jnp.zeros_like(tail)
-        for level in range(shards, levels):
-            came = swap_beside(send, level)
-            own, tail, before, before_tail, send = across(me, own, tail, before, before_tail, came, level, shards)
-        parts = (None, before, None)
-
-    def first_of(at, level):
-        if level + 1 == shards:
-            return shard_start(at, level, sensors)
-        size = sensors >> (level + 2)
-        return shard_start(at, level + 1, sensors) + pick(bit_of(at, level + 1), -size, size)
-
-    for level in reversed(range(1, shards)):
-        mine, gone, states, other = fall(me, saved, level, *parts)
-        came = ready(states, other, functools.partial(first_of, level=level), level, gone)
-        parts = (mine, came, None)
-    states, other = fall(me, saved, 0, None, came, None)
-    ready(states, other, functools.partial(first_of, level=0), 0, None)
-
-
-def all_sum(keep, send, me, count):
+    if levels == SHARDED + 1:
+        return swap_beside(send, SHARDED), SHARDED, saved
+    before, before_tail = jnp.zeros_like(own), jnp.zeros_like(tail)
+    for level in range(SHARDED, levels):
+        came = swap_beside(send, level)
+        own, tail, before, before_tail, send = across(me, own, tail, before, before_tail, came, level, SHARDED)
+    return before, None, saved
+
+
+def halve_kernel(me_ref, part, came, kept_ref, gone_ref, *, level):
+    size = kept_ref.shape[0]
+    total = part[...] + came[...].astype(f32)
+    bit = bit_of(me_ref[0], level)
+    low, high = total[0:size], total[size:]
+    kept_ref[...] = pick(bit, high, low)
+    gone_ref[...] = pick(bit, low, high).astype(bf16)
+
+
+def halve(me, part, came, level):
+    shape = (part.shape[0] // 2, part.shape[1])
+    return call(
+        functools.partial(halve_kernel, level=level), "halve", 1, (), [HELD] * 2, [HELD] * 2,
+        [pltpu.VMEM(shape, f32), pltpu.VMEM(shape, bf16)], [], 6, 1e6, 1e6,
+    )(me, held(part), held(came))
+
+
+def join_kernel(me_ref, part, came, out_ref, *, level):
+    size = part.shape[0]
+    bit = bit_of(me_ref[0], level)
+    own, other = part[...].astype(f32), came[...].astype(f32)
+    out_ref[0:size, :] = pick(bit, other, own).astype(bf16)
+    out_ref[size:, :] = pick(bit, own, other).astype(bf16)
+
+
+def join(me, part, came, level):
+    return call(
+        functools.partial(join_kernel, level=level), "join", 1, (), [HELD] * 2, [HELD],
+        [pltpu.VMEM((2 * part.shape[0], part.shape[1]), bf16)], [], 6, 1e6, 1e6,
+    )(me, held(part), held(came))[0]
+
+
+def all_sum(keep, send, me, count, order):
     levels = count.bit_length() - 1
-    own = keep + swap(send, 1, count).astype(f32)
-    half = own.shape[0] // 2
-    parts = [own[:half], own[half:]]
-    orders = [(1, 2), (2, 1)]
-    for turn in range(2):
-        sent = []
-        for part, order in zip(parts, orders):
-            size = part.shape[0] // 2
-            bit = bit_of(me, order[turn])
-            gone = lax.dynamic_slice_in_dim(part, (1 - bit) * size, size, 0).astype(bf16)
-            sent.append(swap(gone, 1 << order[turn], count))
-        for k, order in enumerate(orders):
-            size = parts[k].shape[0] // 2
-            kept = lax.dynamic_slice_in_dim(parts[k], bit_of(me, order[turn]) * size, size, 0)
-            parts[k] = kept + sent[k].astype(f32)
-    both = jnp.concatenate(parts, axis=0)
-    for level in range(3, levels):
-        both = narrow(both)
-        both = both + swap(both.astype(bf16), 1 << level, count).astype(f32)
-    size = both.shape[0] // 2
-    both = both.astype(bf16)
-    parts = [both[:size], both[size:]]
-    for turn in (1, 0):
-        came = [swap(part, 1 << order[turn], count) for part, order in zip(parts, orders)]
-        for k, order in enumerate(orders):
-            bit = bit_of(me, order[turn])
-            parts[k] = pick(
-                bit, jnp.concatenate([came[k], parts[k]], axis=0), jnp.concatenate([parts[k], came[k]], axis=0)
-            )
-    out = jnp.concatenate(parts, axis=0)
-    return out, swap(out, 1, count)
+    part, came = keep, swap(send, 1, count)
+    for level in order:
+        part, gone = halve(me, part, came, level)
+        came = swap(gone, 1 << level, count)
+    part = part + came.astype(f32)
+    for level in range(SHARDED, levels):
+        part = narrow(part)
+        part = part + swap(part.astype(bf16), 1 << level, count).astype(f32)
+    part = part.astype(bf16)
+    for level in reversed(order):
+        part = join(me, part, swap(part, 1 << level, count), level)
+    return part, swap(part, 1, count)
 
 
 def per_device(
@@ -719,7 +719,6 @@
     nstate = w_state.shape[1] // 2
     me = lax.axis_index("seq").astype(jnp.int32)
     at = me[None]
-    shards = 3
     heads = skip_gain.shape[0]
 
     mixed, chans, maps, step, cum, cum_t, keep, send, tail, token, consts = front(
@@ -729,56 +728,58 @@
     work = {"token": token, "within": (), "back": (), "gains": []}
     plan = {1: (0, 6), 2: (6, 4), 3: (10, 6)}
 
-    def run_back(states, first):
+    def run_back(blocks, *states):
         part, scaled, decay, grad = work["within"][:4]
         normed, read, gain, work["token"] = back(
-            at, first, states, maps, scaled, decay, part, grad, cum, consts, work["back"], work["token"]
+            at, blocks, states, maps, scaled, decay, part, grad, cum, consts, work["back"], work["token"]
         )
         work["back"] = (normed, read)
         work["gains"].append(gain)
 
+    def tie(x):
+        x, work["token"] = tied(x, work["token"])
+        return x
+
     def swap_beside(x, level):
-        x, work["token"] = tied(x, work["token"])
-        came = swap(x, 1 << level, count)
+        came = swap(tie(x), 1 << level, count)
         if level in plan:
             first, size = plan[level]
             *arrays, work["token"] = within(
                 first, size, chans, maps, step, cum_t, consts, cotangent, w_out, heads, work["within"], work["token"]
             )
             work["within"] = tuple(arrays)
-            came, work["token"] = tied(came, work["token"])
+            came = tie(came)
         return came
 
-    def known(level):
-        def starts(where):
-            size = sensors // 4
-            for device in (where, where ^ 1):
-                begin = shard_start(device, 1, sensors)
-                yield begin if level else begin + pick(bit_of(device, 1), -size, size)
-
-        return starts
-
-    def ready(states, other, first, level, gone):
-        if level:
-            gone, work["token"] = tied(gone, work["token"])
-            gone = swap(gone, 1 << level, count)
-        came = swap(other, 1, count)
-        run_back(states, first)
-        run_back(came, lambda where: first(where ^ 1))
-        if level == 1:
-            work["total"], work["token"] = grads(
-                at, work["back"][0], work["within"][4], work["back"][1], mixed, known(1), None, [], work["token"]
-            )
-        if level:
-            gone, work["token"] = tied(gone, work["token"])
-        return gone
-
-    exchange(keep, send, tail, at, count, shards, swap_beside, ready)
-    keep_sum, send_sum = grads(
-        at, work["back"][0], work["within"][4], work["back"][1], mixed, known(0), work["total"], work["gains"], None
-    )
-    mine, came = all_sum(keep_sum, send_sum, me, count)
-    grad_out, grad_read, grad_gain = finish(at, mine, came, channels, width, nstate)
+    came, across_level, saved = rise_all(keep, send, tail, at, count, swap_beside)
+    states, to_core, to_one, to_two = fall(at, saved, [(0, 3)], [came], across_level)
+    to_core, to_one, to_two = tie((to_core, to_one, to_two))
+    from_two, from_one, core = swap(to_two, 4, count), swap(to_one, 2, count), swap(to_core, 1, count)
+    run_back((0,), states)
+    run_back((1,), core)
+    cot = work["within"][4]
+    early, work["token"] = early_grads(at, work["back"][0], cot, work["back"][1], mixed, work["token"])
+    from_two, from_one = tie((from_two, from_one))
+    states, to_core, to_one = fall(at, saved, [(4, 2), (2, 1)], [from_two, from_one], None)
+    to_core, to_one = tie((to_core, to_one))
+    from_one, core = swap(to_one, 2, count), swap(to_core, 1, count)
+    run_back((4, 2), states)
+    run_back((5, 3), core)
+    from_one = tie(from_one)
+    states, to_core = fall(at, saved, [(6, 1)], [from_one], None)
+    core = swap(tie(to_core), 1, count)
+    run_back((6,), states)
+    run_back((7,), core)
+    results = ()
+    sums = []
+    for part, order in ((0, (1, 2)), (1, (2, 1))):
+        keep_part, send_part = late_grads(
+            at, work["back"][0], cot, work["back"][1], mixed, early, work["gains"], part
+        )
+        sums.append(all_sum(keep_part, send_part, at, count, order))
+    for part in (0, 1):
+        results = finish(at, *sums[part], part, channels, width, nstate, tuple(results))
+    grad_out, grad_read, grad_gain = results
     return grad_out, grad_read.T, grad_gain[0]
 
 

time: 98 us -> 90.6 us (0.924)
  waiting for transfers between devices: 42.2 us -> 26.5 us
  starting transfers between devices: 18.2 us -> 26.4 us
    ppermute x20 -> x24, waiting for transfers between devices: 42.2 us -> 26.5 us  [swap(): return lax.ppermute(x, 'seq', [(i, i ^ distance) for i in range(count)])]
    ppermute x20 -> x24, starting transfers between devices: 18.2 us -> 26.4 us  [swap(): return lax.ppermute(x, 'seq', [(i, i ^ distance) for i in range(count)])]
    pallas_call x12 -> x22, Pallas kernels: 14.9 us -> 15.5 us  [the longest x6 8.55 us: back(): call(functools.partial(back_kernel, heads=heads, blocks=blocks, aliases=l...]
  transfers between devices with their start and end apart: 20 -> 24, of which waited for: 16 -> 15; matrix products, arithmetic and copies ran while one was open for 0% -> 0% of each run, Pallas kernels for 19% -> 24%
where the time goes in v5:
time: 90.6 us; the launch traced here: 90.3 us
  Pallas kernels  36.3 us (40%)
  waiting for transfers between devices  26.5 us (29%)
  starting transfers between devices  26.4 us (29%)
  between operations  1.06 us (1%)
    ppermute x24, waiting for transfers between devices, swap(): return lax.ppermute(x, 'seq', [(i, i ^ distance) for i in range(count)])  26.5 us
    ppermute x24, starting transfers between devices, swap(): return lax.ppermute(x, 'seq', [(i, i ^ distance) for i in range(count)])  26.4 us
    pallas_call x3, Pallas kernels, within(): call(functools.partial(within_kernel, heads=heads, first=first, count=cou...  9.98 us
    pallas_call x1, Pallas kernels, front(): call(functools.partial(front_kernel, heads=heads, chunk=chunk, n_small=le...  9.51 us
    pallas_call x6, Pallas kernels, back(): call(functools.partial(back_kernel, heads=heads, blocks=blocks, aliases=l...  8.55 us
    pallas_call x2, Pallas kernels, late_grads(): call(functools.partial(late_kernel, part=part), 'late', 1, (), [HELD] * (...  2.99 us
    pallas_call x2, Pallas kernels, finish(): call(functools.partial(finish_kernel, part=part, aliases=len(done)), 'fin...  2.18 us
  transfers between devices with their start and end apart: 24, of which 15 were waited for; matrix products, arithmetic and copies ran while one was open for 0% of the time, Pallas kernels for 24%

profile of v5, /device:TPU:0, one launch (start us, length us, event | category | flops | bytes accessed | tf_op | source)
XLA Modules:
  0.0 90.3 jit_solution(11020554385726610399)
XLA Ops:
  0.6 9.5 %front.1 = (bf16[16,128,1024]{2,1,0:T(8,128)(2,1)S(1)}, bf16[16,128,512]{2,1,0:T(8,128)(2,1)S(1)}, bf16[16,128,128]{2,1,0:T(8,128)(2,1)S(1)}, f32[128,128]{1,0:T...) custom-call(s32[1]{0:T(128)} %bitcast.me_ref, ...), custom_call_target="tpu_custom_call" | custom-call | flops 5000000000 | bytes 14000000 | tf_op jit(solution)/shard_map/front/pallas_call | solution.py:396
  10.2 0.5 collective-permute-start
  10.7 1.6 %collective-permute-done.came = bf16[528,512]{1,0:T(8,128)(2,1)S(1)} collective-permute-done((bf16[528,512]{1,0:T(8,128)(2,1)S(1)}, bf16[528,512]{1,0:T(8,128)(2,1)S(1)}, u32[]{:S(2)}, u32[]{:S(2)}) %collective-permute-start) | collective-permute-done | bytes 540704 | tf_op jit(solution)/shard_map/ppermute | solution.py:499
  12.2 0.3 rise.3
  12.6 2.9 %collective-permute-start.1 = (bf16[272,512]{1,0:T(8,128)(2,1)S(1)}, bf16[272,512]{1,0:T(8,128)(2,1)S(1)}, u32[]{:S(2)}, u32[]{:S(2)}) collective-permute-start(bf16[272,512]{1,0:T(8,128)(2,1)S(1)} %get-tuple-element.138), channel_id=1, source_target_pairs={{0,2},{1,3},{2,0},{3,1},{4,6},{5,7},{6,4},{7,5},{8,10},{9,11},{10,... | collective-permute-start | bytes 835592 | tf_op jit(solution)/shard_map/ppermute | solution.py:499
  15.5 3.6 %within.3 = (f32[16,128,512]{2,1,0:T(8,128)S(1)}, bf16[16,128,512]{2,1,0:T(8,128)(2,1)S(1)}, bf16[16,8,128,128]{3,2,1,0:T(8,128)(2,1)S(1)}, f32[16,128,512]{2,1,...) custom-call(bf16[16,128,512]{2,1,0:T(8,128)(2,1)S(1)} %get-tuple-ele, ...), custom_call_target="tpu_custom_call", output_to_operand_aliasing={{6}: (7, {})} | custom-call | flops 1800000000 | bytes 9000000 | tf_op jit(solution)/shard_map/within/pallas_call | solution.py:417
  19.2 3.3 %collective-permute-done.1.came = bf16[272,512]{1,0:T(8,128)(2,1)S(1)} collective-permute-done((bf16[272,512]{1,0:T(8,128)(2,1)S(1)}, bf16[272,512]{1,0:T(8,128)(2,1)S(1)}, u32[]{:S(2)}, u32[]{:S(2)}) %collective-permute-start.1) | collective-permute-done | bytes 278560 | tf_op jit(solution)/shard_map/ppermute | solution.py:499
  22.6 1.9 %collective-permute-start.2 = (bf16[144,512]{1,0:T(8,128)(2,1)S(1)}, bf16[144,512]{1,0:T(8,128)(2,1)S(1)}, u32[]{:S(2)}, u32[]{:S(2)}) collective-permute-start(bf16[144,512]{1,0:T(8,128)(2,1)S(1)} %get-tuple-element.153), channel_id=1, source_target_pairs={{0,4},{1,5},{2,6},{3,7},{4,0},{5,1},{6,2},{7,3},{8,12},{9,13},{10,... | collective-permute-start | bytes 442376 | tf_op jit(solution)/shard_map/ppermute | solution.py:499
  24.5 2.5 %within.4 = (f32[16,128,512]{2,1,0:T(8,128)S(1)}, bf16[16,128,512]{2,1,0:T(8,128)(2,1)S(1)}, bf16[16,8,128,128]{3,2,1,0:T(8,128)(2,1)S(1)}, f32[16,128,512]{2,1,...) custom-call(bf16[16,128,512]{2,1,0:T(8,128)(2,1)S(1)} %get-tuple-ele, ...), custom_call_target="tpu_custom_call", output_to_operand_aliasing={{0}: (7, {}), {1}: (8, {}), {2}: (9, {}), {3}: (10, {}), {4... | custom-call | flops 1200000000 | bytes 6000000 | tf_op jit(solution)/shard_map/within/pallas_call | solution.py:417
  27.1 1.0 %collective-permute-done.2.came = bf16[144,512]{1,0:T(8,128)(2,1)S(1)} collective-permute-done((bf16[144,512]{1,0:T(8,128)(2,1)S(1)}, bf16[144,512]{1,0:T(8,128)(2,1)S(1)}, u32[]{:S(2)}, u32[]{:S(2)}) %collective-permute-start.2) | collective-permute-done | bytes 147488 | tf_op jit(solution)/shard_map/ppermute | solution.py:499
  28.1 0.8 rise.5
  28.9 2.6 %collective-permute-start.3 = (bf16[144,512]{1,0:T(8,128)(2,1)S(1)}, bf16[144,512]{1,0:T(8,128)(2,1)S(1)}, u32[]{:S(2)}, u32[]{:S(2)}) collective-permute-start(bf16[144,512]{1,0:T(8,128)(2,1)S(1)} %get-tuple-element.167), channel_id=1, source_target_pairs={{0,8},{1,9},{2,10},{3,11},{4,12},{5,13},{6,14},{7,15},{8,0},{9,1},... | collective-permute-start | bytes 442376 | tf_op jit(solution)/shard_map/ppermute | solution.py:499
  31.5 3.8 %within.5 = (f32[16,128,512]{2,1,0:T(8,128)S(1)}, bf16[16,128,512]{2,1,0:T(8,128)(2,1)S(1)}, bf16[16,8,128,128]{3,2,1,0:T(8,128)(2,1)S(1)}, f32[16,128,512]{2,1,...) custom-call(bf16[16,128,512]{2,1,0:T(8,128)(2,1)S(1)} %get-tuple-ele, ...), custom_call_target="tpu_custom_call", output_to_operand_aliasing={{0}: (7, {}), {1}: (8, {}), {2}: (9, {}), {3}: (10, {}), {4... | custom-call | flops 1800000000 | bytes 9000000 | tf_op jit(solution)/shard_map/within/pallas_call | solution.py:417
  35.3 2.1 %collective-permute-done.3.refs_6_ = bf16[144,512]{1,0:T(8,128)(2,1)S(1)} collective-permute-done((bf16[144,512]{1,0:T(8,128)(2,1)S(1)}, bf16[144,512]{1,0:T(8,128)(2,1)S(1)}, u32[]{:S(2)}, u32[]{:S(2)}) %collective-permute-start.3) | collective-permute-done | bytes 147488 | tf_op jit(solution)/shard_map/ppermute | solution.py:499
  37.8 1.5 %collective-permute-start.5 = (bf16[2,64,512]{2,1,0:T(8,128)(2,1)S(1)}, bf16[2,64,512]{2,1,0:T(8,128)(2,1)S(1)}, u32[]{:S(2)}, u32[]{:S(2)}) collective-permute-start(bf16[2,64,512]{2,1,0:T(8,128)(2,1)S(1)} %get-tuple-element.182), channel_id=1, source_target_pairs={{0,2},{1,3},{2,0},{3,1},{4,6},{5,7},{6,4},{7,5},{8,10},{9,11},{10,... | collective-permute-start | bytes 393224 | tf_op jit(solution)/shard_map/ppermute | solution.py:499
  39.3 1.2 %back.6 = (bf16[16,128,512]{2,1,0:T(8,128)(2,1)S(1)}, bf16[16,128,64]{2,1,0:T(8,128)(2,1)S(1)}, f32[8,512]{1,0:T(8,128)S(1)}, f32[8,128]{1,0:T(8,128)S(1)}) custom-call(s32[1]{0:T(128)} %bitcast.me_ref, bf16[2,64,512]{2,1,0:T(8,128)(2,1)S(1)} %get-tuple-element.189.refs_0_, ...), custom_call_target="tpu_custom_call", output_to_operand_aliasing={{3}: (9, {})} | custom-call | flops 600000000 | bytes 3000000 | tf_op jit(solution)/shard_map/back/pallas_call | solution.py:443
  40.5 1.2 %back.7 = (bf16[16,128,512]{2,1,0:T(8,128)(2,1)S(1)}, bf16[16,128,64]{2,1,0:T(8,128)(2,1)S(1)}, f32[8,512]{1,0:T(8,128)S(1)}, f32[8,128]{1,0:T(8,128)S(1)}) custom-call(s32[1]{0:T(128)} %bitcast.me_ref, bf16[2,64,512]{2,1,0:T(8,128)(2,1)S(1)} %collective-permute-done.6.refs_0_, ...), custom_call_target="tpu_custom_call", output_to_operand_aliasing={{0}: (9, {}), {1}: (10, {}), {3}: (11, {})} | custom-call | flops 600000000 | bytes 3000000 | tf_op jit(solution)/shard_map/back/pallas_call | solution.py:443
  41.7 0.9 %early.1 = (f32[4,608,256]{2,1,0:T(8,128)S(1)}, f32[8,128]{1,0:T(8,128)S(1)}) custom-call(s32[1]{0:T(128)} %bitcast.me_ref, bf16[16,128,512]{2,1,0:T(8,128)(2,1)S(1)} %get-tuple-element.194.normed.refs_8_, bf16[16,128,1024]{2,1,0:T(8,128)(2,1)S(1)} %get-tuple-element.195.cot, ...), custom_call_target="tpu_custom_call", output_to_operand_aliasing={{1}: (5, {})} | custom-call | flops 600000000 | bytes 4000000 | tf_op jit(solution)/shard_map/early/pallas_call | solution.py:466
  42.6 0.9 %collective-permute-done.4.refs_4_ = bf16[2,64,512]{2,1,0:T(8,128)(2,1)S(1)} collective-permute-done((bf16[2,64,512]{2,1,0:T(8,128)(2,1)S(1)}, bf16[2,64,512]{2,1,0:T(8,128)(2,1)S(1)}, u32[]{:S(2)}, u32[]{:S(2)}) %collective-permute-start.4) | collective-permute-done | bytes 131104 | tf_op jit(solution)/shard_map/ppermute | solution.py:499
  43.8 1.4 %collective-permute-start.7 = (bf16[2,64,512]{2,1,0:T(8,128)(2,1)S(1)}, bf16[2,64,512]{2,1,0:T(8,128)(2,1)S(1)}, u32[]{:S(2)}, u32[]{:S(2)}) collective-permute-start(bf16[2,64,512]{2,1,0:T(8,128)(2,1)S(1)} %get-tuple-element.205), channel_id=1, source_target_pairs={{0,2},{1,3},{2,0},{3,1},{4,6},{5,7},{6,4},{7,5},{8,10},{9,11},{10,... | collective-permute-start | bytes 393224 | tf_op jit(solution)/shard_map/ppermute | solution.py:499
  45.2 1.9 %back.8 = (bf16[16,128,512]{2,1,0:T(8,128)(2,1)S(1)}, bf16[16,128,64]{2,1,0:T(8,128)(2,1)S(1)}, f32[8,512]{1,0:T(8,128)S(1)}, f32[8,128]{1,0:T(8,128)S(1)}) custom-call(s32[1]{0:T(128)} %bitcast.me_ref, bf16[4,64,512]{2,1,0:T(8,128)(2,1)S(1)} %get-tuple-element.207.refs_0_, ...), custom_call_target="tpu_custom_call", output_to_operand_aliasing={{0}: (9, {}), {1}: (10, {}), {3}: (11, {})} | custom-call | flops 1200000000 | bytes 6000000 | tf_op jit(solution)/shard_map/back/pallas_call | solution.py:443
  47.2 1.9 %back.9 = (bf16[16,128,512]{2,1,0:T(8,128)(2,1)S(1)}, bf16[16,128,64]{2,1,0:T(8,128)(2,1)S(1)}, f32[8,512]{1,0:T(8,128)S(1)}, f32[8,128]{1,0:T(8,128)S(1)}) custom-call(s32[1]{0:T(128)} %bitcast.me_ref, bf16[4,64,512]{2,1,0:T(8,128)(2,1)S(1)} %collective-permute-done.8.refs_0_, ...), custom_call_target="tpu_custom_call", output_to_operand_aliasing={{0}: (9, {}), {1}: (10, {}), {3}: (11, {})} | custom-call | flops 1200000000 | bytes 6000000 | tf_op jit(solution)/shard_map/back/pallas_call | solution.py:443
  49.1 0.7 collective-permute-done.7.refs_2_
  49.9 1.2 %back.10 = (bf16[16,128,512]{2,1,0:T(8,128)(2,1)S(1)}, bf16[16,128,64]{2,1,0:T(8,128)(2,1)S(1)}, f32[8,512]{1,0:T(8,128)S(1)}, f32[8,128]{1,0:T(8,128)S(1)}) custom-call(s32[1]{0:T(128)} %bitcast.me_ref, bf16[2,64,512]{2,1,0:T(8,128)(2,1)S(1)} %get-tuple-element.217.refs_0_, ...), custom_call_target="tpu_custom_call", output_to_operand_aliasing={{0}: (9, {}), {1}: (10, {}), {3}: (11, {})} | custom-call | flops 600000000 | bytes 3000000 | tf_op jit(solution)/shard_map/back/pallas_call | solution.py:443
  51.2 1.2 %back.11 = (bf16[16,128,512]{2,1,0:T(8,128)(2,1)S(1)}, bf16[16,128,64]{2,1,0:T(8,128)(2,1)S(1)}, f32[8,512]{1,0:T(8,128)S(1)}, f32[8,128]{1,0:T(8,128)S(1)}) custom-call(s32[1]{0:T(128)} %bitcast.me_ref, bf16[2,64,512]{2,1,0:T(8,128)(2,1)S(1)} %collective-permute-done.9.refs_0_, ...), custom_call_target="tpu_custom_call", output_to_operand_aliasing={{0}: (9, {}), {1}: (10, {}), {3}: (11, {})} | custom-call | flops 600000000 | bytes 3000000 | tf_op jit(solution)/shard_map/back/pallas_call | solution.py:443
  52.4 1.5 %late.3 = (f32[608,256]{1,0:T(8,128)S(1)}, bf16[608,256]{1,0:T(8,128)(2,1)S(1)}) custom-call(s32[1]{0:T(128)} %bitcast.me_ref, bf16[16,128,512]{2,1,0:T(8,128)(2,1)S(1)} %get-tuple-element.224.normed, bf16[16,128,1024]{2,1,0:T(8,128)(2,1)S(1)} %get-tuple-element.195.cot, bf16[16,128,64]{2,1,0:T(8,128)(2,1)S(1)} %get-tuple-element.225.read, ...), custom_call_target="tpu_custom_call" | custom-call | flops 800000000 | bytes 5000000 | tf_op jit(solution)/shard_map/late/pallas_call | solution.py:475
  53.9 0.4 collective-permute-start.17
  54.4 1.5 %late.2 = (f32[608,256]{1,0:T(8,128)S(1)}, bf16[608,256]{1,0:T(8,128)(2,1)S(1)}) custom-call(s32[1]{0:T(128)} %bitcast.me_ref, bf16[16,128,512]{2,1,0:T(8,128)(2,1)S(1)} %get-tuple-element.224.normed, bf16[16,128,1024]{2,1,0:T(8,128)(2,1)S(1)} %get-tuple-element.195.cot, bf16[16,128,64]{2,1,0:T(8,128)(2,1)S(1)} %get-tuple-element.225.read, ...), custom_call_target="tpu_custom_call" | custom-call | flops 800000000 | bytes 5000000 | tf_op jit(solution)/shard_map/late/pallas_call | solution.py:475
  55.9 0.2 collective-permute-start.10
  56.2 1.4 %collective-permute-start.18 = (bf16[304,256]{1,0:T(8,128)(2,1)S(1)}, bf16[304,256]{1,0:T(8,128)(2,1)S(1)}, u32[]{:S(2)}, u32[]{:S(2)}) collective-permute-start(bf16[304,256]{1,0:T(8,128)(2,1)S(1)} %get-tuple-element.242), channel_id=1, source_target_pairs={{0,2},{1,3},{2,0},{3,1},{4,6},{5,7},{6,4},{7,5},{8,10},{9,11},{10,... | collective-permute-start | bytes 466952 | tf_op jit(solution)/shard_map/ppermute | solution.py:499
  57.7 1.8 %collective-permute-start.11 = (bf16[304,256]{1,0:T(8,128)(2,1)S(1)}, bf16[304,256]{1,0:T(8,128)(2,1)S(1)}, u32[]{:S(2)}, u32[]{:S(2)}) collective-permute-start(bf16[304,256]{1,0:T(8,128)(2,1)S(1)} %get-tuple-element.236), channel_id=1, source_target_pairs={{0,4},{1,5},{2,6},{3,7},{4,0},{5,1},{6,2},{7,3},{8,12},{9,13},{10,... | collective-permute-start | bytes 466952 | tf_op jit(solution)/shard_map/ppermute | solution.py:499
  59.4 3.1 %collective-permute-done.18.came = bf16[304,256]{1,0:T(8,128)(2,1)S(1)} collective-permute-done((bf16[304,256]{1,0:T(8,128)(2,1)S(1)}, bf16[304,256]{1,0:T(8,128)(2,1)S(1)}, u32[]{:S(2)}, u32[]{:S(2)}) %collective-permute-start.18) | collective-permute-done | bytes 155680 | tf_op jit(solution)/shard_map/ppermute | solution.py:499
  62.6 1.8 %collective-permute-start.19 = (bf16[152,256]{1,0:T(8,128)(2,1)S(1)}, bf16[152,256]{1,0:T(8,128)(2,1)S(1)}, u32[]{:S(2)}, u32[]{:S(2)}) collective-permute-start(bf16[152,256]{1,0:T(8,128)(2,1)S(1)} %get-tuple-element.244), channel_id=1, source_target_pairs={{0,4},{1,5},{2,6},{3,7},{4,0},{5,1},{6,2},{7,3},{8,12},{9,13},{10,... | collective-permute-start | bytes 233480 | tf_op jit(solution)/shard_map/ppermute | solution.py:499
  64.4 1.0 %collective-permute-start.12 = (bf16[152,256]{1,0:T(8,128)(2,1)S(1)}, bf16[152,256]{1,0:T(8,128)(2,1)S(1)}, u32[]{:S(2)}, u32[]{:S(2)}) collective-permute-start(bf16[152,256]{1,0:T(8,128)(2,1)S(1)} %get-tuple-element.238), channel_id=1, source_target_pairs={{0,2},{1,3},{2,0},{3,1},{4,6},{5,7},{6,4},{7,5},{8,10},{9,11},{10,... | collective-permute-start | bytes 233480 | tf_op jit(solution)/shard_map/ppermute | solution.py:499
  65.4 1.6 %collective-permute-done.19 = bf16[152,256]{1,0:T(8,128)(2,1)S(1)} collective-permute-done((bf16[152,256]{1,0:T(8,128)(2,1)S(1)}, bf16[152,256]{1,0:T(8,128)(2,1)S(1)}, u32[]{:S(2)}, u32[]{:S(2)}) %collective-permute-start.19) | collective-permute-done | bytes 77856 | tf_op jit(solution)/shard_map/ppermute | solution.py:499
  67.1 3.3 %collective-permute-start.20 = (bf16[152,256]{1,0:T(8,128)(2,1)S(1)}, bf16[152,256]{1,0:T(8,128)(2,1)S(1)}, u32[]{:S(2)}, u32[]{:S(2)}) collective-permute-start(bf16[152,256]{1,0:T(8,128)(2,1)S(1)} %fusion.1), channel_id=1, source_target_pairs={{0,8},{1,9},{2,10},{3,11},{4,12},{5,13},{6,14},{7,15},{8,0},{9,1},... | collective-permute-start | bytes 233480 | tf_op jit(solution)/shard_map/ppermute | solution.py:499
  70.4 1.3 %collective-permute-start.13 = (bf16[152,256]{1,0:T(8,128)(2,1)S(1)}, bf16[152,256]{1,0:T(8,128)(2,1)S(1)}, u32[]{:S(2)}, u32[]{:S(2)}) collective-permute-start(bf16[152,256]{1,0:T(8,128)(2,1)S(1)} %fusion), channel_id=1, source_target_pairs={{0,8},{1,9},{2,10},{3,11},{4,12},{5,13},{6,14},{7,15},{8,0},{9,1},... | collective-permute-start | bytes 233480 | tf_op jit(solution)/shard_map/ppermute | solution.py:499
  71.7 4.2 %collective-permute-done.20 = bf16[152,256]{1,0:T(8,128)(2,1)S(1)} collective-permute-done((bf16[152,256]{1,0:T(8,128)(2,1)S(1)}, bf16[152,256]{1,0:T(8,128)(2,1)S(1)}, u32[]{:S(2)}, u32[]{:S(2)}) %collective-permute-start.20) | collective-permute-done | bytes 77856 | tf_op jit(solution)/shard_map/ppermute | solution.py:499
  76.0 0.7 collective-permute-done.13
  76.8 1.6 %collective-permute-start.14 = (bf16[152,256]{1,0:T(8,128)(2,1)S(1)}, bf16[152,256]{1,0:T(8,128)(2,1)S(1)}, u32[]{:S(2)}, u32[]{:S(2)}) collective-permute-start(bf16[152,256]{1,0:T(8,128)(2,1)S(1)} %add_convert_fusion.1.part), channel_id=1, source_target_pairs={{0,2},{1,3},{2,0},{3,1},{4,6},{5,7},{6,4},{7,5},{8,10},{9,11},{10,... | collective-permute-start | bytes 233480 | tf_op jit(solution)/shard_map/ppermute | solution.py:499
  78.4 2.1 %collective-permute-done.21.came = bf16[152,256]{1,0:T(8,128)(2,1)S(1)} collective-permute-done((bf16[152,256]{1,0:T(8,128)(2,1)S(1)}, bf16[152,256]{1,0:T(8,128)(2,1)S(1)}, u32[]{:S(2)}, u32[]{:S(2)}) %collective-permute-start.21) | collective-permute-done | bytes 77856 | tf_op jit(solution)/shard_map/ppermute | solution.py:499
  80.5 1.6 %collective-permute-start.22 = (bf16[304,256]{1,0:T(8,128)(2,1)S(1)}, bf16[304,256]{1,0:T(8,128)(2,1)S(1)}, u32[]{:S(2)}, u32[]{:S(2)}) collective-permute-start(bf16[304,256]{1,0:T(8,128)(2,1)S(1)} %join.6.part), channel_id=1, source_target_pairs={{0,2},{1,3},{2,0},{3,1},{4,6},{5,7},{6,4},{7,5},{8,10},{9,11},{10,... | collective-permute-start | bytes 466952 | tf_op jit(solution)/shard_map/ppermute | solution.py:499
  82.0 0.6 collective-permute-start.15
  82.7 3.1 %collective-permute-done.22.came = bf16[304,256]{1,0:T(8,128)(2,1)S(1)} collective-permute-done((bf16[304,256]{1,0:T(8,128)(2,1)S(1)}, bf16[304,256]{1,0:T(8,128)(2,1)S(1)}, u32[]{:S(2)}, u32[]{:S(2)}) %collective-permute-start.22) | collective-permute-done | bytes 155680 | tf_op jit(solution)/shard_map/ppermute | solution.py:499
  85.9 1.4 %collective-permute-done.15.came = bf16[304,256]{1,0:T(8,128)(2,1)S(1)} collective-permute-done((bf16[304,256]{1,0:T(8,128)(2,1)S(1)}, bf16[304,256]{1,0:T(8,128)(2,1)S(1)}, u32[]{:S(2)}, u32[]{:S(2)}) %collective-permute-start.15) | collective-permute-done | bytes 155680 | tf_op jit(solution)/shard_map/ppermute | solution.py:499
  87.5 1.1 %finish.2 = (f32[512,1024]{1,0:T(8,128)}, f32[64,1024]{1,0:T(8,128)}, f32[1,512]{1,0:T(1,128)}) custom-call(s32[1]{0:T(128)} %bitcast.me_ref, bf16[608,256]{1,0:T(8,128)(2,1)S(1)} %join.7.mine, bf16[608,256]{1,0:T(8,128)(2,1)S(1)} %collective-permute-done.23.came), custom_call_target="tpu_custom_call" | custom-call | flops 1000000 | bytes 2000000 | tf_op jit(solution)/shard_map/finish/pallas_call | solution.py:484
  88.6 0.5 collective-permute-done.16.came
  89.1 1.1 %finish.3 = (f32[512,1024]{1,0:T(8,128)}, f32[64,1024]{1,0:T(8,128)}, f32[1,512]{1,0:T(1,128)}) custom-call(s32[1]{0:T(128)} %bitcast.me_ref, bf16[608,256]{1,0:T(8,128)(2,1)S(1)} %join.5.mine, bf16[608,256]{1,0:T(8,128)(2,1)S(1)} %collective-permute-done.16.came, ...), custom_call_target="tpu_custom_call", output_to_operand_aliasing={{0}: (3, {}), {1}: (4, {}), {2}: (5, {})} | custom-call | flops 1000000 | bytes 2000000 | tf_op jit(solution)/shard_map/finish/pallas_call | solution.py:484
  (33 shorter events, 1.9 us)
Async XLA Ops:
  10.2 2.1 %collective-permute-start = (bf16[528,512]{1,0:T(8,128)(2,1)S(1)}, bf16[528,512]{1,0:T(8,128)(2,1)S(1)}, u32[]{:S(2)}, u32[]{:S(2)}) collective-permute-start(bf16[528,512]{1,0:T(8,128)(2,1)S(1)} %get-tuple-element.131), channel_id=1, source_target_pairs={{0,1},{1,0},{2,3},{3,2},{4,5},{5,4},{6,7},{7,6},{8,9},{9,8},{10,11... | collective-permute-start | bytes 1622024 | tf_op jit(solution)/shard_map/ppermute | solution.py:499
  12.6 9.9 %collective-permute-start.1 = (bf16[272,512]{1,0:T(8,128)(2,1)S(1)}, bf16[272,512]{1,0:T(8,128)(2,1)S(1)}, u32[]{:S(2)}, u32[]{:S(2)}) collective-permute-start(bf16[272,512]{1,0:T(8,128)(2,1)S(1)} %get-tuple-element.138), channel_id=1, source_target_pairs={{0,2},{1,3},{2,0},{3,1},{4,6},{5,7},{6,4},{7,5},{8,10},{9,11},{10,... | collective-permute-start | bytes 835592 | tf_op jit(solution)/shard_map/ppermute | solution.py:499
  22.6 5.4 %collective-permute-start.2 = (bf16[144,512]{1,0:T(8,128)(2,1)S(1)}, bf16[144,512]{1,0:T(8,128)(2,1)S(1)}, u32[]{:S(2)}, u32[]{:S(2)}) collective-permute-start(bf16[144,512]{1,0:T(8,128)(2,1)S(1)} %get-tuple-element.153), channel_id=1, source_target_pairs={{0,4},{1,5},{2,6},{3,7},{4,0},{5,1},{6,2},{7,3},{8,12},{9,13},{10,... | collective-permute-start | bytes 442376 | tf_op jit(solution)/shard_map/ppermute | solution.py:499
  28.9 8.5 %collective-permute-start.3 = (bf16[144,512]{1,0:T(8,128)(2,1)S(1)}, bf16[144,512]{1,0:T(8,128)(2,1)S(1)}, u32[]{:S(2)}, u32[]{:S(2)}) collective-permute-start(bf16[144,512]{1,0:T(8,128)(2,1)S(1)} %get-tuple-element.167), channel_id=1, source_target_pairs={{0,8},{1,9},{2,10},{3,11},{4,12},{5,13},{6,14},{7,15},{8,0},{9,1},... | collective-permute-start | bytes 442376 | tf_op jit(solution)/shard_map/ppermute | solution.py:499
  37.6 2.9 %collective-permute-start.6 = (bf16[2,64,512]{2,1,0:T(8,128)(2,1)S(1)}, bf16[2,64,512]{2,1,0:T(8,128)(2,1)S(1)}, u32[]{:S(2)}, u32[]{:S(2)}) collective-permute-start(bf16[2,64,512]{2,1,0:T(8,128)(2,1)S(1)} %get-tuple-element.183), channel_id=1, source_target_pairs={{0,1},{1,0},{2,3},{3,2},{4,5},{5,4},{6,7},{7,6},{8,9},{9,8},{10,11... | collective-permute-start | bytes 393224 | tf_op jit(solution)/shard_map/ppermute | solution.py:499
  37.7 5.9 %collective-permute-start.4 = (bf16[2,64,512]{2,1,0:T(8,128)(2,1)S(1)}, bf16[2,64,512]{2,1,0:T(8,128)(2,1)S(1)}, u32[]{:S(2)}, u32[]{:S(2)}) collective-permute-start(bf16[2,64,512]{2,1,0:T(8,128)(2,1)S(1)} %get-tuple-element.181), channel_id=1, source_target_pairs={{0,4},{1,5},{2,6},{3,7},{4,0},{5,1},{6,2},{7,3},{8,12},{9,13},{10,... | collective-permute-start | bytes 393224 | tf_op jit(solution)/shard_map/ppermute | solution.py:499
  37.8 5.7 %collective-permute-start.5 = (bf16[2,64,512]{2,1,0:T(8,128)(2,1)S(1)}, bf16[2,64,512]{2,1,0:T(8,128)(2,1)S(1)}, u32[]{:S(2)}, u32[]{:S(2)}) collective-permute-start(bf16[2,64,512]{2,1,0:T(8,128)(2,1)S(1)} %get-tuple-element.182), channel_id=1, source_target_pairs={{0,2},{1,3},{2,0},{3,1},{4,6},{5,7},{6,4},{7,5},{8,10},{9,11},{10,... | collective-permute-start | bytes 393224 | tf_op jit(solution)/shard_map/ppermute | solution.py:499
  43.8 3.4 %collective-permute-start.8 = (bf16[4,64,512]{2,1,0:T(8,128)(2,1)S(1)}, bf16[4,64,512]{2,1,0:T(8,128)(2,1)S(1)}, u32[]{:S(2)}, u32[]{:S(2)}) collective-permute-start(bf16[4,64,512]{2,1,0:T(8,128)(2,1)S(1)} %get-tuple-element.206), channel_id=1, source_target_pairs={{0,1},{1,0},{2,3},{3,2},{4,5},{5,4},{6,7},{7,6},{8,9},{9,8},{10,11... | collective-permute-start | bytes 786440 | tf_op jit(solution)/shard_map/ppermute | solution.py:499
  43.8 5.9 %collective-permute-start.7 = (bf16[2,64,512]{2,1,0:T(8,128)(2,1)S(1)}, bf16[2,64,512]{2,1,0:T(8,128)(2,1)S(1)}, u32[]{:S(2)}, u32[]{:S(2)}) collective-permute-start(bf16[2,64,512]{2,1,0:T(8,128)(2,1)S(1)} %get-tuple-element.205), channel_id=1, source_target_pairs={{0,2},{1,3},{2,0},{3,1},{4,6},{5,7},{6,4},{7,5},{8,10},{9,11},{10,... | collective-permute-start | bytes 393224 | tf_op jit(solution)/shard_map/ppermute | solution.py:499
  49.8 1.4 %collective-permute-start.9 = (bf16[2,64,512]{2,1,0:T(8,128)(2,1)S(1)}, bf16[2,64,512]{2,1,0:T(8,128)(2,1)S(1)}, u32[]{:S(2)}, u32[]{:S(2)}) collective-permute-start(bf16[2,64,512]{2,1,0:T(8,128)(2,1)S(1)} %get-tuple-element.216), channel_id=1, source_target_pairs={{0,1},{1,0},{2,3},{3,2},{4,5},{5,4},{6,7},{7,6},{8,9},{9,8},{10,11... | collective-permute-start | bytes 393224 | tf_op jit(solution)/shard_map/ppermute | solution.py:499
  53.9 2.1 %collective-permute-start.17 = (bf16[608,256]{1,0:T(8,128)(2,1)S(1)}, bf16[608,256]{1,0:T(8,128)(2,1)S(1)}, u32[]{:S(2)}, u32[]{:S(2)}) collective-permute-start(bf16[608,256]{1,0:T(8,128)(2,1)S(1)} %get-tuple-element.240), channel_id=1, source_target_pairs={{0,1},{1,0},{2,3},{3,2},{4,5},{5,4},{6,7},{7,6},{8,9},{9,8},{10,11... | collective-permute-start | bytes 933896 | tf_op jit(solution)/shard_map/ppermute | solution.py:499
  55.9 1.7 %collective-permute-start.10 = (bf16[608,256]{1,0:T(8,128)(2,1)S(1)}, bf16[608,256]{1,0:T(8,128)(2,1)S(1)}, u32[]{:S(2)}, u32[]{:S(2)}) collective-permute-start(bf16[608,256]{1,0:T(8,128)(2,1)S(1)} %get-tuple-element.234), channel_id=1, source_target_pairs={{0,1},{1,0},{2,3},{3,2},{4,5},{5,4},{6,7},{7,6},{8,9},{9,8},{10,11... | collective-permute-start | bytes 933896 | tf_op jit(solution)/shard_map/ppermute | solution.py:499
  56.2 6.4 %collective-permute-start.18 = (bf16[304,256]{1,0:T(8,128)(2,1)S(1)}, bf16[304,256]{1,0:T(8,128)(2,1)S(1)}, u32[]{:S(2)}, u32[]{:S(2)}) collective-permute-start(bf16[304,256]{1,0:T(8,128)(2,1)S(1)} %get-tuple-element.242), channel_id=1, source_target_pairs={{0,2},{1,3},{2,0},{3,1},{4,6},{5,7},{6,4},{7,5},{8,10},{9,11},{10,... | collective-permute-start | bytes 466952 | tf_op jit(solution)/shard_map/ppermute | solution.py:499
  57.7 6.7 %collective-permute-start.11 = (bf16[304,256]{1,0:T(8,128)(2,1)S(1)}, bf16[304,256]{1,0:T(8,128)(2,1)S(1)}, u32[]{:S(2)}, u32[]{:S(2)}) collective-permute-start(bf16[304,256]{1,0:T(8,128)(2,1)S(1)} %get-tuple-element.236), channel_id=1, source_target_pairs={{0,4},{1,5},{2,6},{3,7},{4,0},{5,1},{6,2},{7,3},{8,12},{9,13},{10,... | collective-permute-start | bytes 466952 | tf_op jit(solution)/shard_map/ppermute | solution.py:499
  62.6 4.5 %collective-permute-start.19 = (bf16[152,256]{1,0:T(8,128)(2,1)S(1)}, bf16[152,256]{1,0:T(8,128)(2,1)S(1)}, u32[]{:S(2)}, u32[]{:S(2)}) collective-permute-start(bf16[152,256]{1,0:T(8,128)(2,1)S(1)} %get-tuple-element.244), channel_id=1, source_target_pairs={{0,4},{1,5},{2,6},{3,7},{4,0},{5,1},{6,2},{7,3},{8,12},{9,13},{10,... | collective-permute-start | bytes 233480 | tf_op jit(solution)/shard_map/ppermute | solution.py:499
  64.4 5.9 %collective-permute-start.12 = (bf16[152,256]{1,0:T(8,128)(2,1)S(1)}, bf16[152,256]{1,0:T(8,128)(2,1)S(1)}, u32[]{:S(2)}, u32[]{:S(2)}) collective-permute-start(bf16[152,256]{1,0:T(8,128)(2,1)S(1)} %get-tuple-element.238), channel_id=1, source_target_pairs={{0,2},{1,3},{2,0},{3,1},{4,6},{5,7},{6,4},{7,5},{8,10},{9,11},{10,... | collective-permute-start | bytes 233480 | tf_op jit(solution)/shard_map/ppermute | solution.py:499
  67.1 8.9 %collective-permute-start.20 = (bf16[152,256]{1,0:T(8,128)(2,1)S(1)}, bf16[152,256]{1,0:T(8,128)(2,1)S(1)}, u32[]{:S(2)}, u32[]{:S(2)}) collective-permute-start(bf16[152,256]{1,0:T(8,128)(2,1)S(1)} %fusion.1), channel_id=1, source_target_pairs={{0,8},{1,9},{2,10},{3,11},{4,12},{5,13},{6,14},{7,15},{8,0},{9,1},... | collective-permute-start | bytes 233480 | tf_op jit(solution)/shard_map/ppermute | solution.py:499
  70.4 6.4 %collective-permute-start.13 = (bf16[152,256]{1,0:T(8,128)(2,1)S(1)}, bf16[152,256]{1,0:T(8,128)(2,1)S(1)}, u32[]{:S(2)}, u32[]{:S(2)}) collective-permute-start(bf16[152,256]{1,0:T(8,128)(2,1)S(1)} %fusion), channel_id=1, source_target_pairs={{0,8},{1,9},{2,10},{3,11},{4,12},{5,13},{6,14},{7,15},{8,0},{9,1},... | collective-permute-start | bytes 233480 | tf_op jit(solution)/shard_map/ppermute | solution.py:499
  76.0 4.5 %collective-permute-start.21 = (bf16[152,256]{1,0:T(8,128)(2,1)S(1)}, bf16[152,256]{1,0:T(8,128)(2,1)S(1)}, u32[]{:S(2)}, u32[]{:S(2)}) collective-permute-start(bf16[152,256]{1,0:T(8,128)(2,1)S(1)} %add_convert_fusion.part), channel_id=1, source_target_pairs={{0,4},{1,5},{2,6},{3,7},{4,0},{5,1},{6,2},{7,3},{8,12},{9,13},{10,... | collective-permute-start | bytes 233480 | tf_op jit(solution)/shard_map/ppermute | solution.py:499
  76.8 5.2 %collective-permute-start.14 = (bf16[152,256]{1,0:T(8,128)(2,1)S(1)}, bf16[152,256]{1,0:T(8,128)(2,1)S(1)}, u32[]{:S(2)}, u32[]{:S(2)}) collective-permute-start(bf16[152,256]{1,0:T(8,128)(2,1)S(1)} %add_convert_fusion.1.part), channel_id=1, source_target_pairs={{0,2},{1,3},{2,0},{3,1},{4,6},{5,7},{6,4},{7,5},{8,10},{9,11},{10,... | collective-permute-start | bytes 233480 | tf_op jit(solution)/shard_map/ppermute | solution.py:499
  80.5 5.3 %collective-permute-start.22 = (bf16[304,256]{1,0:T(8,128)(2,1)S(1)}, bf16[304,256]{1,0:T(8,128)(2,1)S(1)}, u32[]{:S(2)}, u32[]{:S(2)}) collective-permute-start(bf16[304,256]{1,0:T(8,128)(2,1)S(1)} %join.6.part), channel_id=1, source_target_pairs={{0,2},{1,3},{2,0},{3,1},{4,6},{5,7},{6,4},{7,5},{8,10},{9,11},{10,... | collective-permute-start | bytes 466952 | tf_op jit(solution)/shard_map/ppermute | solution.py:499
  82.0 5.3 %collective-permute-start.15 = (bf16[304,256]{1,0:T(8,128)(2,1)S(1)}, bf16[304,256]{1,0:T(8,128)(2,1)S(1)}, u32[]{:S(2)}, u32[]{:S(2)}) collective-permute-start(bf16[304,256]{1,0:T(8,128)(2,1)S(1)} %join.4.part), channel_id=1, source_target_pairs={{0,4},{1,5},{2,6},{3,7},{4,0},{5,1},{6,2},{7,3},{8,12},{9,13},{10,... | collective-permute-start | bytes 466952 | tf_op jit(solution)/shard_map/ppermute | solution.py:499
  85.8 1.7 %collective-permute-start.23 = (bf16[608,256]{1,0:T(8,128)(2,1)S(1)}, bf16[608,256]{1,0:T(8,128)(2,1)S(1)}, u32[]{:S(2)}, u32[]{:S(2)}) collective-permute-start(bf16[608,256]{1,0:T(8,128)(2,1)S(1)} %join.7.mine), channel_id=1, source_target_pairs={{0,1},{1,0},{2,3},{3,2},{4,5},{5,4},{6,7},{7,6},{8,9},{9,8},{10,11... | collective-permute-start | bytes 933896 | tf_op jit(solution)/shard_map/ppermute | solution.py:499
  87.4 1.7 %collective-permute-start.16 = (bf16[608,256]{1,0:T(8,128)(2,1)S(1)}, bf16[608,256]{1,0:T(8,128)(2,1)S(1)}, u32[]{:S(2)}, u32[]{:S(2)}) collective-permute-start(bf16[608,256]{1,0:T(8,128)(2,1)S(1)} %join.5.mine), channel_id=1, source_target_pairs={{0,1},{1,0},{2,3},{3,2},{4,5},{5,4},{6,7},{7,6},{8,9},{9,8},{10,11... | collective-permute-start | bytes 933896 | tf_op jit(solution)/shard_map/ppermute | solution.py:499

commit v6 on v5

--- a/solution.py
+++ b/solution.py
@@ -51,7 +51,7 @@
     (mixed_ref, channels_ref, maps_ref, step_ref, cum_ref, cum_t_ref, keep_ref, send_ref, tail_ref, token_ref,
      consts_ref), refs = refs[:11], refs[11:]
     vmem, refs = refs[:n_small], refs[n_small:]
-    readings, kmix, wms, spread2, state_sc, log_sc, scaled_sc, sems = refs
+    readings, kmix, wms, spread2, log_sc, scaled_sc, sems = refs
     graph, cluster, mix, marks, w_step_t, bias, fading_exponent, skip_gain, norm_gain, w_state, w_channels = vmem
     sensors, span, width = readings.shape
     rows = sensors * chunk
@@ -81,10 +81,10 @@
         copy.wait()
     wms[:, maps : maps + heads] = w_step_t[...].astype(f32).T.astype(bf16)
     picked = (iota((sensors, sensors), 0) == cluster[...]).astype(bf16)
-    linked = dot(dot(picked, graph[...].astype(f32).astype(bf16), TN).astype(bf16), picked)
-    coupling = (linked * mix[...]).astype(bf16)
-    sensor_of = (iota((rows, sensors), 0) // chunk == iota((rows, sensors), 1)).astype(bf16)
-    full = dot(dot(sensor_of, coupling).astype(bf16), sensor_of, NT)
+    sensor_of = (iota((sensors, rows), 1) // chunk == iota((sensors, rows), 0)).astype(bf16)
+    linked = dot(dot(picked, graph[...].astype(f32).astype(bf16), TN).astype(bf16), dot(picked, sensor_of).astype(bf16))
+    coupling = (linked * sum(dot(part, sensor_of) for part in split(mix[...], 3))).astype(bf16).astype(f32)
+    full = jnp.broadcast_to(coupling[:, None, :], (sensors, chunk, rows)).reshape(rows, rows)
     same = iota((rows, rows), 0) % chunk == iota((rows, rows), 1) % chunk
     kmix[...] = jnp.where(same, full, 0.0).astype(bf16)
     tiled = (iota((heads, lanes), 1) % heads == iota((heads, lanes), 0)).astype(bf16)
@@ -132,24 +132,30 @@
     last = cum[span - 1 : span, :]
     weight = jnp.exp2(last - cum) * step_ref[...]
 
-    def scale(s):
-        scaled_sc[s % 4] = (channels_ref[s].astype(f32) * spread(weight, s, heads, spread2[...])).astype(bf16)
-
-    scale(0)
-    scale(1)
-    for s in range(sensors):
-        if s + 2 < sensors:
-            scale(s + 2)
-        state_sc[s] = dot(maps_ref[s], scaled_sc[s % 4], TN)[0:nstate]
+    half = sensors // 2
+    mine = (me_ref[0] & 1) * half
+
+    def sensor_at(n):
+        return (half - mine if n < half else mine - half) + n
+
+    def scale(n):
+        s = sensor_at(n)
+        scaled_sc[n % 4] = (channels_ref[s].astype(f32) * spread(weight, s, heads, spread2[...])).astype(bf16)
+
     own = jnp.where(iota((sensors, lanes), 1) // heads == iota((sensors, lanes), 0), last, 0.0)
     tail = sum(dot(part, spread2[0:lanes, :]) for part in split(own, 3))
     tail_ref[...] = tail
-    half = sensors // 2
-    mine = (me_ref[0] & 1) * half
-    other = half - mine
-    keep_ref[...] = state_sc[pl.ds(mine, half)]
-    send_ref[0 : half * nstate, :] = state_sc[pl.ds(other, half)].reshape(half * nstate, channels).astype(bf16)
     send_ref[half * nstate :, :] = tail.astype(bf16)
+    scale(0)
+    scale(1)
+    for n in range(sensors):
+        if n + 2 < sensors:
+            scale(n + 2)
+        state = dot(maps_ref[sensor_at(n)], scaled_sc[n % 4], TN)[0:nstate]
+        if n < half:
+            send_ref[n * nstate : (n + 1) * nstate, :] = state.astype(bf16)
+        else:
+            keep_ref[n - half] = state
 
 
 def pair_blocks(x, size):
@@ -400,7 +406,7 @@
         [pltpu.VMEM(shape, dtype) for shape, dtype in outs],
         [pltpu.VMEM(x.shape, x.dtype) for x in small] + [
             pltpu.VMEM(readings.shape, bf16), pltpu.VMEM((rows, rows), bf16), pltpu.VMEM((width, maps + lanes), bf16),
-            pltpu.VMEM((2 * lanes, channels), bf16), pltpu.VMEM((sensors, nstate, channels), f32),
+            pltpu.VMEM((2 * lanes, channels), bf16),
             pltpu.VMEM((span, lanes), f32), pltpu.VMEM((4, span, channels), bf16),
             pltpu.SemaphoreType.DMA((len(small) + span // chunk,)),
         ],
@@ -523,143 +529,198 @@
     return ref[pl.ds(k, 1), :]
 
 
-def rise_kernel(me_ref, own, tail, came, low_ref, low_tail_ref, tail_ref, next_ref, send_ref, other_tail, *, level, last):
+EACH = 2
+
+
+def widened(came, k, nstate):
+    return came[k * nstate : (k + 1) * nstate, :].astype(f32)
+
+
+def tails_of(came, nstate):
+    return came[EACH * nstate :, :].astype(f32)
+
+
+def core_kernel(me_ref, own, tail, came, low_ref, low_tail_ref, tail_ref, kept_ref, *refs):
+    send_refs, other_tail = refs[:-1], refs[-1]
     me = me_ref[0]
-    bit = bit_of(me, level)
+    bit = bit_of(me, 0)
     size, nstate, width = own.shape
     sensors = tail.shape[0]
-    start = shard_start(me, level, sensors)
+    start = shard_start(me, 0, sensors)
     other_tail[...] = came[size * nstate :, :].astype(f32)
     low_tail_ref[...] = pick(bit, other_tail[...], tail[...])
     total_tail = tail[...] + other_tail[...]
     tail_ref[...] = total_tail
-
-    def total(j):
-        other = came[pl.ds(pl.multiple_of(j * nstate, nstate), nstate), :].astype(f32)
-        low, high = pick(bit, other, own[j]), pick(bit, own[j], other)
-        low_ref[j] = low
-        fade = jnp.exp2(pick(bit, row(tail, start + j), row(other_tail, start + j)))
-        return low * fade + high
-
-    half = next_ref.shape[0]
-    mine = 0 if last else bit_of(me, level + 1) * half
-    for j in range(half):
-        kept = total(mine + j)
-        next_ref[j] = kept
-        gone = kept if last else total(half - mine + j)
-        send_ref[j * nstate : (j + 1) * nstate, :] = gone.astype(bf16)
-    send_ref[half * nstate :, :] = total_tail.astype(bf16)
-
-
-def rise(me, own, tail, came, level, last):
+    for n in range(1 + len(send_refs)):
+        for k in range(EACH):
+            sensor = block_start(me, 2 * n, sensors) + k
+            j = sensor - start
+            other = came[pl.ds(pl.multiple_of(j * nstate, nstate), nstate), :].astype(f32)
+            low, high = pick(bit, other, own[j]), pick(bit, own[j], other)
+            low_ref[j] = low
+            total = low * jnp.exp2(pick(bit, row(tail, sensor), row(other_tail, sensor))) + high
+            if n == 0:
+                kept_ref[k] = total
+            else:
+                send_refs[n - 1][k * nstate : (k + 1) * nstate, :] = total.astype(bf16)
+    for ref in send_refs:
+        ref[EACH * nstate :, :] = total_tail.astype(bf16)
+
+
+def join_cores(me, own, tail, came):
     size, nstate, width = own.shape
-    half = size if last else size // 2
-    return call(
-        functools.partial(rise_kernel, level=level, last=last), "rise", 1, (),
-        [HELD] * 3, [HELD] * 5,
+    sent = pltpu.VMEM((EACH * nstate + tail.shape[0], width), bf16)
+    return call(
+        core_kernel, "cores", 1, (), [HELD] * 3, [HELD] * 7,
         [
             pltpu.VMEM(own.shape, f32), pltpu.VMEM(tail.shape, f32), pltpu.VMEM(tail.shape, f32),
-            pltpu.VMEM((half, nstate, width), f32), pltpu.VMEM((half * nstate + tail.shape[0], width), bf16),
+            pltpu.VMEM((EACH, nstate, width), f32), sent, sent, sent,
         ],
         [pltpu.VMEM(tail.shape, f32)], 6, 1e6, 1e6,
     )(me, *[held(x) for x in (own, tail, came)])
 
 
-def across_kernel(
-    me_ref, own, tail, before, before_tail, came, next_ref, tail_ref, before_ref, before_tail_ref, send_ref, other_tail,
-    *, level, shards,
+def chip_of(me):
+    return (me >> 1) & 3
+
+
+def group_kernel(me_ref, own, tail, *refs):
+    cames, (first_ref, pair_ref, third_ref, first_tail, pair_tail, third_tail, send_ref, tail_sc) = refs[:3], refs[3:]
+    me = me_ref[0]
+    nstate = own.shape[1]
+    sensors = tail.shape[0]
+    chip = chip_of(me)
+
+    def at(position, values):
+        flip = chip ^ position
+        return jnp.where(flip == 0, values[0], jnp.where(flip == 1, values[1], jnp.where(flip == 2, values[2], values[3])))
+
+    tails = [tail[...]] + [tails_of(came, nstate) for came in cames]
+    for position in range(4):
+        tail_sc[position] = at(position, tails)
+    first_tail[...] = tail_sc[0]
+    pair_tail[...] = tail_sc[0] + tail_sc[1]
+    third_tail[...] = tail_sc[2]
+    if send_ref.shape[0] > EACH * nstate:
+        send_ref[EACH * nstate :, :] = (tail_sc[0] + tail_sc[1] + tail_sc[2] + tail_sc[3]).astype(bf16)
+    for k in range(EACH):
+        sensor = pl.ds(block_start(me, 0, sensors) + k, 1)
+        values = [own[k]] + [widened(came, k, nstate) for came in cames]
+        first, second, third, fourth = [at(position, values) for position in range(4)]
+        pair = first * jnp.exp2(tail_sc[1, sensor, :]) + second
+        first_ref[k] = first
+        pair_ref[k] = pair
+        third_ref[k] = third
+        both = tail_sc[2, sensor, :] + tail_sc[3, sensor, :]
+        total = pair * jnp.exp2(both) + (third * jnp.exp2(tail_sc[3, sensor, :]) + fourth)
+        send_ref[k * nstate : (k + 1) * nstate, :] = total.astype(bf16)
+
+
+def join_group(me, own, tail, cames, with_tail):
+    state, tails = pltpu.VMEM(own.shape, f32), pltpu.VMEM(tail.shape, f32)
+    rows = cames[0].shape[0] - (0 if with_tail else tail.shape[0])
+    return call(
+        group_kernel, "group", 1, (), [HELD] * 5, [HELD] * 7,
+        [state] * 3 + [tails] * 3 + [pltpu.VMEM((rows, own.shape[2]), bf16)],
+        [pltpu.VMEM((4,) + tail.shape, f32)], 6, 1e6, 1e6,
+    )(me, *[held(x) for x in (own, tail, *cames)])
+
+
+def across_kernel(me_ref, own, before, came, next_ref, before_ref, *, level):
+    me = me_ref[0]
+    bit = bit_of(me, level)
+    nstate = (own.shape[0] - own.shape[0] // 9) // EACH
+    sensors = own.shape[0] - EACH * nstate
+    rows = EACH * nstate
+    for k in range(EACH):
+        sensor = block_start(me, 0, sensors) + k
+        here = slice(k * nstate, (k + 1) * nstate)
+        other, mine, ahead = came[here, :].astype(f32), own[here, :], before[here, :]
+        other_tail = came[rows:, :].astype(f32)
+        mask = (iota(other_tail.shape, 0) == sensor).astype(f32)
+
+        def of_sensor(tails):
+            return jnp.sum(tails * mask, axis=0, keepdims=True)
+
+        before_ref[here, :] = pick(bit, other * jnp.exp2(of_sensor(before[rows:, :])) + ahead, ahead)
+        low, high = pick(bit, other, mine), pick(bit, mine, other)
+        next_ref[here, :] = low * jnp.exp2(of_sensor(pick(bit, own[rows:, :], other_tail))) + high
+    other_tail = came[rows:, :].astype(f32)
+    next_ref[rows:, :] = own[rows:, :] + other_tail
+    before_ref[rows:, :] = before[rows:, :] + pick(bit, other_tail, jnp.zeros_like(other_tail))
+
+
+def across(me, own, before, came, level):
+    out = pltpu.VMEM(own.shape, f32)
+    return call(
+        functools.partial(across_kernel, level=level), "across", 1, (), [HELD] * 3, [HELD] * 2, [out, out],
+        [], 6, 1e6, 1e6,
+    )(me, *[held(x) for x in (own, before, came)])
+
+
+def landed(me, state, sensor, low, low_tail):
+    start = shard_start(me, 0, low_tail.shape[0])
+    after = state * jnp.exp2(row(low_tail, sensor)) + low[sensor - start]
+    bit = bit_of(me, 0)
+    return pick(bit, after, state).astype(bf16), pick(bit, state, after).astype(bf16)
+
+
+def fall_kernel(
+    me_ref, came, first, pair, third, first_tail, pair_tail, third_tail, low, low_tail,
+    state_ref, core_ref, *send_refs, level,
 ):
     me = me_ref[0]
-    bit = bit_of(me, level)
-    size, nstate, width = own.shape
-    start = shard_start(me, shards - 1, tail.shape[0])
-    other_tail[...] = came[size * nstate :, :].astype(f32)
-    before_tail_ref[...] = before_tail[...] + pick(bit, other_tail[...], jnp.zeros_like(other_tail))
-    total_tail = tail[...] + other_tail[...]
-    tail_ref[...] = total_tail
-    for j in range(size):
-        other = came[j * nstate : (j + 1) * nstate, :].astype(f32)
-        passed = other * jnp.exp2(row(before_tail, start + j)) + before[j]
-        before_ref[j] = pick(bit, passed, before[j])
-        low, high = pick(bit, other, own[j]), pick(bit, own[j], other)
-        total = low * jnp.exp2(pick(bit, row(tail, start + j), row(other_tail, start + j))) + high
-        next_ref[j] = total
-        send_ref[j * nstate : (j + 1) * nstate, :] = total.astype(bf16)
-    send_ref[size * nstate :, :] = total_tail.astype(bf16)
-
-
-def across(me, own, tail, before, before_tail, came, level, shards):
-    return call(
-        functools.partial(across_kernel, level=level, shards=shards), "across", 1, (),
-        [HELD] * 5, [HELD] * 5,
-        [
-            pltpu.VMEM(own.shape, f32), pltpu.VMEM(tail.shape, f32), pltpu.VMEM(own.shape, f32),
-            pltpu.VMEM(tail.shape, f32), pltpu.VMEM(came.shape, bf16),
-        ],
-        [pltpu.VMEM(tail.shape, f32)], 6, 1e6, 1e6,
-    )(me, *[held(x) for x in (own, tail, before, before_tail, came)])
-
-
-def fall_kernel(me_ref, *refs, levels, sources, across_level, n_outs):
+    nstate = first.shape[1]
+    sensors = low_tail.shape[0]
+    for k in range(EACH):
+        sensor = block_start(me, 0, sensors) + k
+        before = widened(came, k, nstate)
+        if level is not None:
+            before = pick(bit_of(me, level), before, jnp.zeros_like(before))
+        third_start = before * jnp.exp2(row(pair_tail, sensor)) + pair[k]
+        starts = [
+            before,
+            before * jnp.exp2(row(first_tail, sensor)) + first[k],
+            third_start,
+            third_start * jnp.exp2(row(third_tail, sensor)) + third[k],
+        ]
+        for n in range(4):
+            chip = chip_of(me) ^ n
+            state = jnp.where(
+                chip == 0, starts[0], jnp.where(chip == 1, starts[1], jnp.where(chip == 2, starts[2], starts[3]))
+            )
+            if n == 0:
+                state_ref[k], core_ref[k] = landed(me, state, sensor, low, low_tail)
+            else:
+                send_refs[n - 1][k] = state.astype(bf16)
+
+
+def fall(me, came, level, group, low, low_tail):
+    nstate, width = low.shape[1:]
+    return call(
+        functools.partial(fall_kernel, level=level), "fall", 1, (), [HELD] * 9, [HELD] * 5,
+        [pltpu.VMEM((EACH, nstate, width), bf16)] * 5, [], 6, 1e6, 1e6,
+    )(me, *[held(x) for x in (came, *group, low, low_tail)])
+
+
+def land_kernel(me_ref, low, low_tail, *refs, blocks):
+    cames, (state_ref, core_ref) = refs[: len(blocks)], refs[len(blocks) :]
     me = me_ref[0]
-    lows, tails = refs[:levels], refs[levels : 2 * levels]
-    cames, outs = refs[2 * levels : 2 * levels + len(sources)], refs[2 * levels + len(sources) :]
-    sensors = tails[0].shape[0]
-    nstate = lows[0].shape[1]
-    each = 2
-
-    for n, ((flips, top), came) in enumerate(zip(sources, cames)):
-        for k in range(each):
-            sensor = block_start(me, flips, sensors) + k
-            if len(came.shape) == 3:
-                state = came[k].astype(f32)
-            else:
-                state = came[k * nstate : (k + 1) * nstate, :].astype(f32)
-                state = pick(bit_of(me, across_level), state, jnp.zeros_like(state))
-            for q in reversed(range(top)):
-                after = state * jnp.exp2(row(tails[q], sensor)) + lows[q][sensor - shard_start(me, q, sensors)]
-                bit = bit_of(me, q)
-                other = pick(bit, state, after)
-                state = pick(bit, after, state)
-                if q == 0:
-                    outs[1][n * each + k] = other.astype(bf16)
-                else:
-                    outs[1 + q][k] = other.astype(bf16)
-            outs[0][n * each + k] = state.astype(bf16)
-
-
-def fall(me, saved, sources, cames, across_level):
-    levels = max(top for _, top in sources)
-    lows = [low for low, _ in saved[:levels]]
-    tails = [tail for _, tail in saved[:levels]]
-    nstate, width = lows[0].shape[1:]
-    arrays = lows + tails + cames
-    outs = [pltpu.VMEM((2 * len(sources), nstate, width), bf16)] * 2 + [pltpu.VMEM((2, nstate, width), bf16)] * (levels - 1)
-    return call(
-        functools.partial(
-            fall_kernel, levels=levels, sources=sources, across_level=across_level, n_outs=len(outs)
-        ), "fall", 1, (), [HELD] * len(arrays), [HELD] * len(outs), outs, [], 6, 1e6, 1e6,
-    )(me, *[held(x) for x in arrays])
+    for n, (flips, came) in enumerate(zip(blocks, cames)):
+        for k in range(EACH):
+            sensor = block_start(me, flips, low_tail.shape[0]) + k
+            state_ref[n * EACH + k], core_ref[n * EACH + k] = landed(me, came[k].astype(f32), sensor, low, low_tail)
+
+
+def land(me, low, low_tail, blocks, cames):
+    out = pltpu.VMEM((EACH * len(blocks),) + low.shape[1:], bf16)
+    return call(
+        functools.partial(land_kernel, blocks=blocks), "land", 1, (), [HELD] * (2 + len(blocks)), [HELD] * 2,
+        [out, out], [], 6, 1e6, 1e6,
+    )(me, *[held(x) for x in (low, low_tail, *cames)])
 
 
 SHARDED = 3
-
-
-def rise_all(keep, send, tail, me, count, swap_beside):
-    levels = count.bit_length() - 1
-    own = keep
-    saved = []
-    for level in range(SHARDED):
-        came = swap_beside(send, level)
-        low, low_tail, tail, own, send = rise(me, own, tail, came, level, level + 1 == SHARDED)
-        saved.append((low, low_tail))
-    if levels == SHARDED + 1:
-        return swap_beside(send, SHARDED), SHARDED, saved
-    before, before_tail = jnp.zeros_like(own), jnp.zeros_like(tail)
-    for level in range(SHARDED, levels):
-        came = swap_beside(send, level)
-        own, tail, before, before_tail, send = across(me, own, tail, before, before_tail, came, level, SHARDED)
-    return before, None, saved
 
 
 def halve_kernel(me_ref, part, came, kept_ref, gone_ref, *, level):
@@ -726,7 +787,6 @@
         step_bias, channel_fading_exponent, skip_gain, norm_gain,
     )
     work = {"token": token, "within": (), "back": (), "gains": []}
-    plan = {1: (0, 6), 2: (6, 4), 3: (10, 6)}
 
     def run_back(blocks, *states):
         part, scaled, decay, grad = work["within"][:4]
@@ -740,36 +800,43 @@
         x, work["token"] = tied(x, work["token"])
         return x
 
-    def swap_beside(x, level):
-        came = swap(tie(x), 1 << level, count)
-        if level in plan:
-            first, size = plan[level]
-            *arrays, work["token"] = within(
-                first, size, chans, maps, step, cum_t, consts, cotangent, w_out, heads, work["within"], work["token"]
-            )
-            work["within"] = tuple(arrays)
-            came = tie(came)
-        return came
-
-    came, across_level, saved = rise_all(keep, send, tail, at, count, swap_beside)
-    states, to_core, to_one, to_two = fall(at, saved, [(0, 3)], [came], across_level)
-    to_core, to_one, to_two = tie((to_core, to_one, to_two))
-    from_two, from_one, core = swap(to_two, 4, count), swap(to_one, 2, count), swap(to_core, 1, count)
+    def run_within(first, size):
+        *arrays, work["token"] = within(
+            first, size, chans, maps, step, cum_t, consts, cotangent, w_out, heads, work["within"], work["token"]
+        )
+        work["within"] = tuple(arrays)
+
+    came = swap(send, 1, count)
+    low, low_tail, tail, kept, *sends = join_cores(at, keep, tail, came)
+    sends = tie(sends)
+    cames = [swap(x, 2 * (n + 1), count) for n, x in enumerate(sends)]
+    run_within(0, 10)
+    cames = tie(cames)
+    levels = count.bit_length() - 1
+    *group, send = join_group(at, kept, tail, cames, levels > SHARDED + 1)
+    if levels == SHARDED + 1:
+        came, level = swap(tie(send), 1 << SHARDED, count), SHARDED
+        run_within(10, sensors - 10)
+        came = tie(came)
+    else:
+        run_within(10, sensors - 10)
+        own, before, level = send.astype(f32), jnp.zeros(send.shape, f32), None
+        for k in range(SHARDED, levels):
+            own, before = across(at, own, before, swap(own.astype(bf16), 1 << k, count), k)
+        came = before
+    states, to_core, *sends = fall(at, came, level, group, low, low_tail)
+    to_core, sends = tie((to_core, sends))
+    core = swap(to_core, 1, count)
+    from_one, from_two, from_three = [swap(x, 2 * (n + 1), count) for n, x in enumerate(sends)]
     run_back((0,), states)
     run_back((1,), core)
     cot = work["within"][4]
     early, work["token"] = early_grads(at, work["back"][0], cot, work["back"][1], mixed, work["token"])
-    from_two, from_one = tie((from_two, from_one))
-    states, to_core, to_one = fall(at, saved, [(4, 2), (2, 1)], [from_two, from_one], None)
-    to_core, to_one = tie((to_core, to_one))
-    from_one, core = swap(to_one, 2, count), swap(to_core, 1, count)
-    run_back((4, 2), states)
-    run_back((5, 3), core)
-    from_one = tie(from_one)
-    states, to_core = fall(at, saved, [(6, 1)], [from_one], None)
+    arrived = tie((from_two, from_one, from_three))
+    states, to_core = land(at, low, low_tail, (4, 2, 6), arrived)
     core = swap(tie(to_core), 1, count)
-    run_back((6,), states)
-    run_back((7,), core)
+    run_back((4, 2, 6), states)
+    run_back((5, 3, 7), core)
     results = ()
     sums = []
     for part, order in ((0, (1, 2)), (1, (2, 1))):

time: 90.6 us -> 86.3 us (0.953)
  Pallas kernels: 36.3 us -> 34.3 us
  waiting for transfers between devices: 26.5 us -> 25 us
    ppermute x24, waiting for transfers between devices: 26.5 us -> 25 us  [swap(): return lax.ppermute(x, 'seq', [(i, i ^ distance) for i in range(count)])]
    pallas_call x6 -> x4, Pallas kernels: 8.55 us -> 7.72 us  [back(): call(functools.partial(back_kernel, heads=heads, blocks=blocks, aliases=l...]
    pallas_call x3 -> x2, Pallas kernels: 9.98 us -> 9.7 us  [within(): call(functools.partial(within_kernel, heads=heads, first=first, count=cou...]
  transfers between devices with their start and end apart: 24 -> 24, of which waited for: 15 -> 14; matrix products, arithmetic and copies ran while one was open for 0% -> 0% of each run, Pallas kernels for 24% -> 22%
where the time goes in v6:
time: 86.3 us; the launch traced here: 86.1 us
  Pallas kernels  34.3 us (40%)
  starting transfers between devices  25.7 us (30%)
  waiting for transfers between devices  25 us (29%)
  between operations  1.05 us (1%)
    ppermute x24, starting transfers between devices, swap(): return lax.ppermute(x, 'seq', [(i, i ^ distance) for i in range(count)])  25.7 us
    ppermute x24, waiting for transfers between devices, swap(): return lax.ppermute(x, 'seq', [(i, i ^ distance) for i in range(count)])  25 us
    pallas_call x2, Pallas kernels, within(): call(functools.partial(within_kernel, heads=heads, first=first, count=cou...  9.7 us
    pallas_call x1, Pallas kernels, front(): call(functools.partial(front_kernel, heads=heads, chunk=chunk, n_small=le...  9.14 us
    pallas_call x4, Pallas kernels, back(): call(functools.partial(back_kernel, heads=heads, blocks=blocks, aliases=l...  7.72 us
    pallas_call x2, Pallas kernels, late_grads(): call(functools.partial(late_kernel, part=part), 'late', 1, (), [HELD] * (...  2.99 us
    pallas_call x2, Pallas kernels, finish(): call(functools.partial(finish_kernel, part=part, aliases=len(done)), 'fin...  2.18 us
  transfers between devices with their start and end apart: 24, of which 14 were waited for; matrix products, arithmetic and copies ran while one was open for 0% of the time, Pallas kernels for 22%

profile of v6, /device:TPU:0, one launch (start us, length us, event | category | flops | bytes accessed | tf_op | source)
XLA Modules:
  0.0 86.1 jit_solution(311573604244741672)
XLA Ops:
  0.6 9.1 %front.1 = (bf16[16,128,1024]{2,1,0:T(8,128)(2,1)S(1)}, bf16[16,128,512]{2,1,0:T(8,128)(2,1)S(1)}, bf16[16,128,128]{2,1,0:T(8,128)(2,1)S(1)}, f32[128,128]{1,0:T...) custom-call(s32[1]{0:T(128)} %bitcast.me_ref, ...), custom_call_target="tpu_custom_call" | custom-call | flops 5000000000 | bytes 14000000 | tf_op jit(solution)/shard_map/front/pallas_call | solution.py:402
  9.8 0.5 collective-permute-start
  10.3 1.6 %collective-permute-done.came = bf16[528,512]{1,0:T(8,128)(2,1)S(1)} collective-permute-done((bf16[528,512]{1,0:T(8,128)(2,1)S(1)}, bf16[528,512]{1,0:T(8,128)(2,1)S(1)}, u32[]{:S(2)}, u32[]{:S(2)}) %collective-permute-start) | collective-permute-done | bytes 540704 | tf_op jit(solution)/shard_map/ppermute | solution.py:505
  11.9 0.3 cores.1
  12.2 2.9 %collective-permute-start.1 = (bf16[144,512]{1,0:T(8,128)(2,1)S(1)}, bf16[144,512]{1,0:T(8,128)(2,1)S(1)}, u32[]{:S(2)}, u32[]{:S(2)}) collective-permute-start(bf16[144,512]{1,0:T(8,128)(2,1)S(1)} %get-tuple-element.117), channel_id=1, source_target_pairs={{0,2},{1,3},{2,0},{3,1},{4,6},{5,7},{6,4},{7,5},{8,10},{9,11},{10,... | collective-permute-start | bytes 442376 | tf_op jit(solution)/shard_map/ppermute | solution.py:505
  15.1 1.6 %collective-permute-start.2 = (bf16[144,512]{1,0:T(8,128)(2,1)S(1)}, bf16[144,512]{1,0:T(8,128)(2,1)S(1)}, u32[]{:S(2)}, u32[]{:S(2)}) collective-permute-start(bf16[144,512]{1,0:T(8,128)(2,1)S(1)} %get-tuple-element.118), channel_id=1, source_target_pairs={{0,4},{1,5},{2,6},{3,7},{4,0},{5,1},{6,2},{7,3},{8,12},{9,13},{10,... | collective-permute-start | bytes 442376 | tf_op jit(solution)/shard_map/ppermute | solution.py:505
  16.7 5.9 %within.2 = (f32[16,128,512]{2,1,0:T(8,128)S(1)}, bf16[16,128,512]{2,1,0:T(8,128)(2,1)S(1)}, bf16[16,8,128,128]{3,2,1,0:T(8,128)(2,1)S(1)}, f32[16,128,512]{2,1,...) custom-call(bf16[16,128,512]{2,1,0:T(8,128)(2,1)S(1)} %get-tuple-ele, ...), custom_call_target="tpu_custom_call", output_to_operand_aliasing={{6}: (7, {})} | custom-call | flops 3000000000 | bytes 15000000 | tf_op jit(solution)/shard_map/within/pallas_call | solution.py:423
  22.6 1.1 %collective-permute-done.3.refs_2_ = bf16[144,512]{1,0:T(8,128)(2,1)S(1)} collective-permute-done((bf16[144,512]{1,0:T(8,128)(2,1)S(1)}, bf16[144,512]{1,0:T(8,128)(2,1)S(1)}, u32[]{:S(2)}, u32[]{:S(2)}) %collective-permute-start.3) | collective-permute-done | bytes 147488 | tf_op jit(solution)/shard_map/ppermute | solution.py:505
  23.7 0.3 group.1
  24.1 2.8 %collective-permute-start.4 = (bf16[128,512]{1,0:T(8,128)(2,1)S(1)}, bf16[128,512]{1,0:T(8,128)(2,1)S(1)}, u32[]{:S(2)}, u32[]{:S(2)}) collective-permute-start(bf16[128,512]{1,0:T(8,128)(2,1)S(1)} %get-tuple-element.132), channel_id=1, source_target_pairs={{0,8},{1,9},{2,10},{3,11},{4,12},{5,13},{6,14},{7,15},{8,0},{9,1},... | collective-permute-start | bytes 393224 | tf_op jit(solution)/shard_map/ppermute | solution.py:505
  26.9 3.8 %within.3 = (f32[16,128,512]{2,1,0:T(8,128)S(1)}, bf16[16,128,512]{2,1,0:T(8,128)(2,1)S(1)}, bf16[16,8,128,128]{3,2,1,0:T(8,128)(2,1)S(1)}, f32[16,128,512]{2,1,...) custom-call(bf16[16,128,512]{2,1,0:T(8,128)(2,1)S(1)} %get-tuple-ele, ...), custom_call_target="tpu_custom_call", output_to_operand_aliasing={{0}: (7, {}), {1}: (8, {}), {2}: (9, {}), {3}: (10, {}), {4... | custom-call | flops 1800000000 | bytes 9000000 | tf_op jit(solution)/shard_map/within/pallas_call | solution.py:423
  30.7 2.0 %collective-permute-done.4.came = bf16[128,512]{1,0:T(8,128)(2,1)S(1)} collective-permute-done((bf16[128,512]{1,0:T(8,128)(2,1)S(1)}, bf16[128,512]{1,0:T(8,128)(2,1)S(1)}, u32[]{:S(2)}, u32[]{:S(2)}) %collective-permute-start.4) | collective-permute-done | bytes 131104 | tf_op jit(solution)/shard_map/ppermute | solution.py:505
  32.6 0.3 fall.1
  33.0 0.6 collective-permute-start.5
  33.6 1.4 %collective-permute-start.6 = (bf16[2,64,512]{2,1,0:T(8,128)(2,1)S(1)}, bf16[2,64,512]{2,1,0:T(8,128)(2,1)S(1)}, u32[]{:S(2)}, u32[]{:S(2)}) collective-permute-start(bf16[2,64,512]{2,1,0:T(8,128)(2,1)S(1)} %get-tuple-element.154), channel_id=1, source_target_pairs={{0,2},{1,3},{2,0},{3,1},{4,6},{5,7},{6,4},{7,5},{8,10},{9,11},{10,... | collective-permute-start | bytes 393224 | tf_op jit(solution)/shard_map/ppermute | solution.py:505
  35.0 1.6 %collective-permute-start.7 = (bf16[2,64,512]{2,1,0:T(8,128)(2,1)S(1)}, bf16[2,64,512]{2,1,0:T(8,128)(2,1)S(1)}, u32[]{:S(2)}, u32[]{:S(2)}) collective-permute-start(bf16[2,64,512]{2,1,0:T(8,128)(2,1)S(1)} %get-tuple-element.155), channel_id=1, source_target_pairs={{0,6},{1,7},{2,4},{3,5},{4,2},{5,3},{6,0},{7,1},{8,14},{9,15},{10,... | collective-permute-start | bytes 393224 | tf_op jit(solution)/shard_map/ppermute | solution.py:505
  36.6 1.2 %back.4 = (bf16[16,128,512]{2,1,0:T(8,128)(2,1)S(1)}, bf16[16,128,64]{2,1,0:T(8,128)(2,1)S(1)}, f32[8,512]{1,0:T(8,128)S(1)}, f32[8,128]{1,0:T(8,128)S(1)}) custom-call(s32[1]{0:T(128)} %bitcast.me_ref, bf16[2,64,512]{2,1,0:T(8,128)(2,1)S(1)} %get-tuple-element.162.refs_0_, ...), custom_call_target="tpu_custom_call", output_to_operand_aliasing={{3}: (9, {})} | custom-call | flops 600000000 | bytes 3000000 | tf_op jit(solution)/shard_map/back/pallas_call | solution.py:449
  37.8 1.2 %back.5 = (bf16[16,128,512]{2,1,0:T(8,128)(2,1)S(1)}, bf16[16,128,64]{2,1,0:T(8,128)(2,1)S(1)}, f32[8,512]{1,0:T(8,128)S(1)}, f32[8,128]{1,0:T(8,128)S(1)}) custom-call(s32[1]{0:T(128)} %bitcast.me_ref, bf16[2,64,512]{2,1,0:T(8,128)(2,1)S(1)} %collective-permute-done.8.refs_0_, ...), custom_call_target="tpu_custom_call", output_to_operand_aliasing={{0}: (9, {}), {1}: (10, {}), {3}: (11, {})} | custom-call | flops 600000000 | bytes 3000000 | tf_op jit(solution)/shard_map/back/pallas_call | solution.py:449
  39.0 0.9 %early.1 = (f32[4,608,256]{2,1,0:T(8,128)S(1)}, f32[8,128]{1,0:T(8,128)S(1)}) custom-call(s32[1]{0:T(128)} %bitcast.me_ref, bf16[16,128,512]{2,1,0:T(8,128)(2,1)S(1)} %get-tuple-element.167.normed.refs_8_, bf16[16,128,1024]{2,1,0:T(8,128)(2,1)S(1)} %get-tuple-element.168.cot, ...), custom_call_target="tpu_custom_call", output_to_operand_aliasing={{1}: (5, {})} | custom-call | flops 600000000 | bytes 4000000 | tf_op jit(solution)/shard_map/early/pallas_call | solution.py:472
  39.9 2.5 %collective-permute-done.7.refs_2_ = bf16[2,64,512]{2,1,0:T(8,128)(2,1)S(1)} collective-permute-done((bf16[2,64,512]{2,1,0:T(8,128)(2,1)S(1)}, bf16[2,64,512]{2,1,0:T(8,128)(2,1)S(1)}, u32[]{:S(2)}, u32[]{:S(2)}) %collective-permute-start.7) | collective-permute-done | bytes 131104 | tf_op jit(solution)/shard_map/ppermute | solution.py:505
  42.4 0.2 land.1
  42.7 2.7 %back.6 = (bf16[16,128,512]{2,1,0:T(8,128)(2,1)S(1)}, bf16[16,128,64]{2,1,0:T(8,128)(2,1)S(1)}, f32[8,512]{1,0:T(8,128)S(1)}, f32[8,128]{1,0:T(8,128)S(1)}) custom-call(s32[1]{0:T(128)} %bitcast.me_ref, bf16[6,64,512]{2,1,0:T(8,128)(2,1)S(1)} %get-tuple-element.179.refs_0_, ...), custom_call_target="tpu_custom_call", output_to_operand_aliasing={{0}: (9, {}), {1}: (10, {}), {3}: (11, {})} | custom-call | flops 1800000000 | bytes 9000000 | tf_op jit(solution)/shard_map/back/pallas_call | solution.py:449
  45.3 2.7 %back.7 = (bf16[16,128,512]{2,1,0:T(8,128)(2,1)S(1)}, bf16[16,128,64]{2,1,0:T(8,128)(2,1)S(1)}, f32[8,512]{1,0:T(8,128)S(1)}, f32[8,128]{1,0:T(8,128)S(1)}) custom-call(s32[1]{0:T(128)} %bitcast.me_ref, bf16[6,64,512]{2,1,0:T(8,128)(2,1)S(1)} %collective-permute-done.9.refs_0_, ...), custom_call_target="tpu_custom_call", output_to_operand_aliasing={{0}: (9, {}), {1}: (10, {}), {3}: (11, {})} | custom-call | flops 1800000000 | bytes 9000000 | tf_op jit(solution)/shard_map/back/pallas_call | solution.py:449
  48.0 1.5 %late.3 = (f32[608,256]{1,0:T(8,128)S(1)}, bf16[608,256]{1,0:T(8,128)(2,1)S(1)}) custom-call(s32[1]{0:T(128)} %bitcast.me_ref, bf16[16,128,512]{2,1,0:T(8,128)(2,1)S(1)} %get-tuple-element.184.normed, bf16[16,128,1024]{2,1,0:T(8,128)(2,1)S(1)} %get-tuple-element.168.cot, bf16[16,128,64]{2,1,0:T(8,128)(2,1)S(1)} %get-tuple-element.185.read, ...), custom_call_target="tpu_custom_call" | custom-call | flops 800000000 | bytes 5000000 | tf_op jit(solution)/shard_map/late/pallas_call | solution.py:481
  49.6 0.6 collective-permute-start.17
  50.1 1.5 %late.2 = (f32[608,256]{1,0:T(8,128)S(1)}, bf16[608,256]{1,0:T(8,128)(2,1)S(1)}) custom-call(s32[1]{0:T(128)} %bitcast.me_ref, bf16[16,128,512]{2,1,0:T(8,128)(2,1)S(1)} %get-tuple-element.184.normed, bf16[16,128,1024]{2,1,0:T(8,128)(2,1)S(1)} %get-tuple-element.168.cot, bf16[16,128,64]{2,1,0:T(8,128)(2,1)S(1)} %get-tuple-element.185.read, ...), custom_call_target="tpu_custom_call" | custom-call | flops 800000000 | bytes 5000000 | tf_op jit(solution)/shard_map/late/pallas_call | solution.py:481
  51.6 0.1 collective-permute-start.10
  51.8 1.0 %collective-permute-start.18 = (bf16[304,256]{1,0:T(8,128)(2,1)S(1)}, bf16[304,256]{1,0:T(8,128)(2,1)S(1)}, u32[]{:S(2)}, u32[]{:S(2)}) collective-permute-start(bf16[304,256]{1,0:T(8,128)(2,1)S(1)} %get-tuple-element.200), channel_id=1, source_target_pairs={{0,2},{1,3},{2,0},{3,1},{4,6},{5,7},{6,4},{7,5},{8,10},{9,11},{10,... | collective-permute-start | bytes 466952 | tf_op jit(solution)/shard_map/ppermute | solution.py:505
  52.8 0.4 collective-permute-done.10.came
  53.4 1.2 %collective-permute-start.11 = (bf16[304,256]{1,0:T(8,128)(2,1)S(1)}, bf16[304,256]{1,0:T(8,128)(2,1)S(1)}, u32[]{:S(2)}, u32[]{:S(2)}) collective-permute-start(bf16[304,256]{1,0:T(8,128)(2,1)S(1)} %get-tuple-element.194), channel_id=1, source_target_pairs={{0,4},{1,5},{2,6},{3,7},{4,0},{5,1},{6,2},{7,3},{8,12},{9,13},{10,... | collective-permute-start | bytes 466952 | tf_op jit(solution)/shard_map/ppermute | solution.py:505
  54.5 3.7 %collective-permute-done.18.came = bf16[304,256]{1,0:T(8,128)(2,1)S(1)} collective-permute-done((bf16[304,256]{1,0:T(8,128)(2,1)S(1)}, bf16[304,256]{1,0:T(8,128)(2,1)S(1)}, u32[]{:S(2)}, u32[]{:S(2)}) %collective-permute-start.18) | collective-permute-done | bytes 155680 | tf_op jit(solution)/shard_map/ppermute | solution.py:505
  58.3 1.2 %collective-permute-start.19 = (bf16[152,256]{1,0:T(8,128)(2,1)S(1)}, bf16[152,256]{1,0:T(8,128)(2,1)S(1)}, u32[]{:S(2)}, u32[]{:S(2)}) collective-permute-start(bf16[152,256]{1,0:T(8,128)(2,1)S(1)} %get-tuple-element.202), channel_id=1, source_target_pairs={{0,4},{1,5},{2,6},{3,7},{4,0},{5,1},{6,2},{7,3},{8,12},{9,13},{10,... | collective-permute-start | bytes 233480 | tf_op jit(solution)/shard_map/ppermute | solution.py:505
  59.5 1.3 %collective-permute-start.12 = (bf16[152,256]{1,0:T(8,128)(2,1)S(1)}, bf16[152,256]{1,0:T(8,128)(2,1)S(1)}, u32[]{:S(2)}, u32[]{:S(2)}) collective-permute-start(bf16[152,256]{1,0:T(8,128)(2,1)S(1)} %get-tuple-element.196), channel_id=1, source_target_pairs={{0,2},{1,3},{2,0},{3,1},{4,6},{5,7},{6,4},{7,5},{8,10},{9,11},{10,... | collective-permute-start | bytes 233480 | tf_op jit(solution)/shard_map/ppermute | solution.py:505
  60.8 2.0 %collective-permute-done.19 = bf16[152,256]{1,0:T(8,128)(2,1)S(1)} collective-permute-done((bf16[152,256]{1,0:T(8,128)(2,1)S(1)}, bf16[152,256]{1,0:T(8,128)(2,1)S(1)}, u32[]{:S(2)}, u32[]{:S(2)}) %collective-permute-start.19) | collective-permute-done | bytes 77856 | tf_op jit(solution)/shard_map/ppermute | solution.py:505
  62.8 3.1 %collective-permute-start.20 = (bf16[152,256]{1,0:T(8,128)(2,1)S(1)}, bf16[152,256]{1,0:T(8,128)(2,1)S(1)}, u32[]{:S(2)}, u32[]{:S(2)}) collective-permute-start(bf16[152,256]{1,0:T(8,128)(2,1)S(1)} %fusion.1), channel_id=1, source_target_pairs={{0,8},{1,9},{2,10},{3,11},{4,12},{5,13},{6,14},{7,15},{8,0},{9,1},... | collective-permute-start | bytes 233480 | tf_op jit(solution)/shard_map/ppermute | solution.py:505
  65.9 1.2 %collective-permute-start.13 = (bf16[152,256]{1,0:T(8,128)(2,1)S(1)}, bf16[152,256]{1,0:T(8,128)(2,1)S(1)}, u32[]{:S(2)}, u32[]{:S(2)}) collective-permute-start(bf16[152,256]{1,0:T(8,128)(2,1)S(1)} %fusion), channel_id=1, source_target_pairs={{0,8},{1,9},{2,10},{3,11},{4,12},{5,13},{6,14},{7,15},{8,0},{9,1},... | collective-permute-start | bytes 233480 | tf_op jit(solution)/shard_map/ppermute | solution.py:505
  67.1 3.5 %collective-permute-done.20 = bf16[152,256]{1,0:T(8,128)(2,1)S(1)} collective-permute-done((bf16[152,256]{1,0:T(8,128)(2,1)S(1)}, bf16[152,256]{1,0:T(8,128)(2,1)S(1)}, u32[]{:S(2)}, u32[]{:S(2)}) %collective-permute-start.20) | collective-permute-done | bytes 77856 | tf_op jit(solution)/shard_map/ppermute | solution.py:505
  70.6 0.8 collective-permute-start.21
  71.4 1.1 %collective-permute-done.13 = bf16[152,256]{1,0:T(8,128)(2,1)S(1)} collective-permute-done((bf16[152,256]{1,0:T(8,128)(2,1)S(1)}, bf16[152,256]{1,0:T(8,128)(2,1)S(1)}, u32[]{:S(2)}, u32[]{:S(2)}) %collective-permute-start.13) | collective-permute-done | bytes 77856 | tf_op jit(solution)/shard_map/ppermute | solution.py:505
  72.5 1.4 %collective-permute-start.14 = (bf16[152,256]{1,0:T(8,128)(2,1)S(1)}, bf16[152,256]{1,0:T(8,128)(2,1)S(1)}, u32[]{:S(2)}, u32[]{:S(2)}) collective-permute-start(bf16[152,256]{1,0:T(8,128)(2,1)S(1)} %add_convert_fusion.1.part), channel_id=1, source_target_pairs={{0,2},{1,3},{2,0},{3,1},{4,6},{5,7},{6,4},{7,5},{8,10},{9,11},{10,... | collective-permute-start | bytes 233480 | tf_op jit(solution)/shard_map/ppermute | solution.py:505
  73.9 1.2 %collective-permute-done.21.came = bf16[152,256]{1,0:T(8,128)(2,1)S(1)} collective-permute-done((bf16[152,256]{1,0:T(8,128)(2,1)S(1)}, bf16[152,256]{1,0:T(8,128)(2,1)S(1)}, u32[]{:S(2)}, u32[]{:S(2)}) %collective-permute-start.21) | collective-permute-done | bytes 77856 | tf_op jit(solution)/shard_map/ppermute | solution.py:505
  75.1 2.2 %collective-permute-start.22 = (bf16[304,256]{1,0:T(8,128)(2,1)S(1)}, bf16[304,256]{1,0:T(8,128)(2,1)S(1)}, u32[]{:S(2)}, u32[]{:S(2)}) collective-permute-start(bf16[304,256]{1,0:T(8,128)(2,1)S(1)} %join.6.part), channel_id=1, source_target_pairs={{0,2},{1,3},{2,0},{3,1},{4,6},{5,7},{6,4},{7,5},{8,10},{9,11},{10,... | collective-permute-start | bytes 466952 | tf_op jit(solution)/shard_map/ppermute | solution.py:505
  77.3 0.5 collective-permute-done.14.came
  77.9 2.6 %collective-permute-done.22.came = bf16[304,256]{1,0:T(8,128)(2,1)S(1)} collective-permute-done((bf16[304,256]{1,0:T(8,128)(2,1)S(1)}, bf16[304,256]{1,0:T(8,128)(2,1)S(1)}, u32[]{:S(2)}, u32[]{:S(2)}) %collective-permute-start.22) | collective-permute-done | bytes 155680 | tf_op jit(solution)/shard_map/ppermute | solution.py:505
  80.6 2.5 %collective-permute-done.15.came = bf16[304,256]{1,0:T(8,128)(2,1)S(1)} collective-permute-done((bf16[304,256]{1,0:T(8,128)(2,1)S(1)}, bf16[304,256]{1,0:T(8,128)(2,1)S(1)}, u32[]{:S(2)}, u32[]{:S(2)}) %collective-permute-start.15) | collective-permute-done | bytes 155680 | tf_op jit(solution)/shard_map/ppermute | solution.py:505
  83.3 1.1 %finish.2 = (f32[512,1024]{1,0:T(8,128)}, f32[64,1024]{1,0:T(8,128)}, f32[1,512]{1,0:T(1,128)}) custom-call(s32[1]{0:T(128)} %bitcast.me_ref, bf16[608,256]{1,0:T(8,128)(2,1)S(1)} %join.7.mine, bf16[608,256]{1,0:T(8,128)(2,1)S(1)} %collective-permute-done.23.came), custom_call_target="tpu_custom_call" | custom-call | flops 1000000 | bytes 2000000 | tf_op jit(solution)/shard_map/finish/pallas_call | solution.py:490
  84.4 0.5 collective-permute-done.16.came
  84.9 1.1 %finish.3 = (f32[512,1024]{1,0:T(8,128)}, f32[64,1024]{1,0:T(8,128)}, f32[1,512]{1,0:T(1,128)}) custom-call(s32[1]{0:T(128)} %bitcast.me_ref, bf16[608,256]{1,0:T(8,128)(2,1)S(1)} %join.5.mine, bf16[608,256]{1,0:T(8,128)(2,1)S(1)} %collective-permute-done.16.came, ...), custom_call_target="tpu_custom_call", output_to_operand_aliasing={{0}: (3, {}), {1}: (4, {}), {2}: (5, {})} | custom-call | flops 1000000 | bytes 2000000 | tf_op jit(solution)/shard_map/finish/pallas_call | solution.py:490
  (28 shorter events, 1.0 us)
Async XLA Ops:
  9.8 2.1 %collective-permute-start = (bf16[528,512]{1,0:T(8,128)(2,1)S(1)}, bf16[528,512]{1,0:T(8,128)(2,1)S(1)}, u32[]{:S(2)}, u32[]{:S(2)}) collective-permute-start(bf16[528,512]{1,0:T(8,128)(2,1)S(1)} %get-tuple-element.108), channel_id=1, source_target_pairs={{0,1},{1,0},{2,3},{3,2},{4,5},{5,4},{6,7},{7,6},{8,9},{9,8},{10,11... | collective-permute-start | bytes 1622024 | tf_op jit(solution)/shard_map/ppermute | solution.py:505
  12.2 10.4 %collective-permute-start.1 = (bf16[144,512]{1,0:T(8,128)(2,1)S(1)}, bf16[144,512]{1,0:T(8,128)(2,1)S(1)}, u32[]{:S(2)}, u32[]{:S(2)}) collective-permute-start(bf16[144,512]{1,0:T(8,128)(2,1)S(1)} %get-tuple-element.117), channel_id=1, source_target_pairs={{0,2},{1,3},{2,0},{3,1},{4,6},{5,7},{6,4},{7,5},{8,10},{9,11},{10,... | collective-permute-start | bytes 442376 | tf_op jit(solution)/shard_map/ppermute | solution.py:505
  15.1 7.5 %collective-permute-start.2 = (bf16[144,512]{1,0:T(8,128)(2,1)S(1)}, bf16[144,512]{1,0:T(8,128)(2,1)S(1)}, u32[]{:S(2)}, u32[]{:S(2)}) collective-permute-start(bf16[144,512]{1,0:T(8,128)(2,1)S(1)} %get-tuple-element.118), channel_id=1, source_target_pairs={{0,4},{1,5},{2,6},{3,7},{4,0},{5,1},{6,2},{7,3},{8,12},{9,13},{10,... | collective-permute-start | bytes 442376 | tf_op jit(solution)/shard_map/ppermute | solution.py:505
  16.7 7.0 %collective-permute-start.3 = (bf16[144,512]{1,0:T(8,128)(2,1)S(1)}, bf16[144,512]{1,0:T(8,128)(2,1)S(1)}, u32[]{:S(2)}, u32[]{:S(2)}) collective-permute-start(bf16[144,512]{1,0:T(8,128)(2,1)S(1)} %get-tuple-element.119), channel_id=1, source_target_pairs={{0,6},{1,7},{2,4},{3,5},{4,2},{5,3},{6,0},{7,1},{8,14},{9,15},{10,... | collective-permute-start | bytes 442376 | tf_op jit(solution)/shard_map/ppermute | solution.py:505
  24.1 8.6 %collective-permute-start.4 = (bf16[128,512]{1,0:T(8,128)(2,1)S(1)}, bf16[128,512]{1,0:T(8,128)(2,1)S(1)}, u32[]{:S(2)}, u32[]{:S(2)}) collective-permute-start(bf16[128,512]{1,0:T(8,128)(2,1)S(1)} %get-tuple-element.132), channel_id=1, source_target_pairs={{0,8},{1,9},{2,10},{3,11},{4,12},{5,13},{6,14},{7,15},{8,0},{9,1},... | collective-permute-start | bytes 393224 | tf_op jit(solution)/shard_map/ppermute | solution.py:505
  32.9 4.8 %collective-permute-start.8 = (bf16[2,64,512]{2,1,0:T(8,128)(2,1)S(1)}, bf16[2,64,512]{2,1,0:T(8,128)(2,1)S(1)}, u32[]{:S(2)}, u32[]{:S(2)}) collective-permute-start(bf16[2,64,512]{2,1,0:T(8,128)(2,1)S(1)} %get-tuple-element.156), channel_id=1, source_target_pairs={{0,1},{1,0},{2,3},{3,2},{4,5},{5,4},{6,7},{7,6},{8,9},{9,8},{10,11... | collective-permute-start | bytes 393224 | tf_op jit(solution)/shard_map/ppermute | solution.py:505
  33.0 6.9 %collective-permute-start.5 = (bf16[2,64,512]{2,1,0:T(8,128)(2,1)S(1)}, bf16[2,64,512]{2,1,0:T(8,128)(2,1)S(1)}, u32[]{:S(2)}, u32[]{:S(2)}) collective-permute-start(bf16[2,64,512]{2,1,0:T(8,128)(2,1)S(1)} %get-tuple-element.153), channel_id=1, source_target_pairs={{0,4},{1,5},{2,6},{3,7},{4,0},{5,1},{6,2},{7,3},{8,12},{9,13},{10,... | collective-permute-start | bytes 393224 | tf_op jit(solution)/shard_map/ppermute | solution.py:505
  33.6 6.3 %collective-permute-start.6 = (bf16[2,64,512]{2,1,0:T(8,128)(2,1)S(1)}, bf16[2,64,512]{2,1,0:T(8,128)(2,1)S(1)}, u32[]{:S(2)}, u32[]{:S(2)}) collective-permute-start(bf16[2,64,512]{2,1,0:T(8,128)(2,1)S(1)} %get-tuple-element.154), channel_id=1, source_target_pairs={{0,2},{1,3},{2,0},{3,1},{4,6},{5,7},{6,4},{7,5},{8,10},{9,11},{10,... | collective-permute-start | bytes 393224 | tf_op jit(solution)/shard_map/ppermute | solution.py:505
  35.0 7.4 %collective-permute-start.7 = (bf16[2,64,512]{2,1,0:T(8,128)(2,1)S(1)}, bf16[2,64,512]{2,1,0:T(8,128)(2,1)S(1)}, u32[]{:S(2)}, u32[]{:S(2)}) collective-permute-start(bf16[2,64,512]{2,1,0:T(8,128)(2,1)S(1)} %get-tuple-element.155), channel_id=1, source_target_pairs={{0,6},{1,7},{2,4},{3,5},{4,2},{5,3},{6,0},{7,1},{8,14},{9,15},{10,... | collective-permute-start | bytes 393224 | tf_op jit(solution)/shard_map/ppermute | solution.py:505
  42.6 2.8 %collective-permute-start.9 = (bf16[6,64,512]{2,1,0:T(8,128)(2,1)S(1)}, bf16[6,64,512]{2,1,0:T(8,128)(2,1)S(1)}, u32[]{:S(2)}, u32[]{:S(2)}) collective-permute-start(bf16[6,64,512]{2,1,0:T(8,128)(2,1)S(1)} %get-tuple-element.178), channel_id=1, source_target_pairs={{0,1},{1,0},{2,3},{3,2},{4,5},{5,4},{6,7},{7,6},{8,9},{9,8},{10,11... | collective-permute-start | bytes 1179656 | tf_op jit(solution)/shard_map/ppermute | solution.py:505
  49.6 2.2 %collective-permute-start.17 = (bf16[608,256]{1,0:T(8,128)(2,1)S(1)}, bf16[608,256]{1,0:T(8,128)(2,1)S(1)}, u32[]{:S(2)}, u32[]{:S(2)}) collective-permute-start(bf16[608,256]{1,0:T(8,128)(2,1)S(1)} %get-tuple-element.198), channel_id=1, source_target_pairs={{0,1},{1,0},{2,3},{3,2},{4,5},{5,4},{6,7},{7,6},{8,9},{9,8},{10,11... | collective-permute-start | bytes 933896 | tf_op jit(solution)/shard_map/ppermute | solution.py:505
  51.6 1.7 %collective-permute-start.10 = (bf16[608,256]{1,0:T(8,128)(2,1)S(1)}, bf16[608,256]{1,0:T(8,128)(2,1)S(1)}, u32[]{:S(2)}, u32[]{:S(2)}) collective-permute-start(bf16[608,256]{1,0:T(8,128)(2,1)S(1)} %get-tuple-element.192), channel_id=1, source_target_pairs={{0,1},{1,0},{2,3},{3,2},{4,5},{5,4},{6,7},{7,6},{8,9},{9,8},{10,11... | collective-permute-start | bytes 933896 | tf_op jit(solution)/shard_map/ppermute | solution.py:505
  51.8 6.5 %collective-permute-start.18 = (bf16[304,256]{1,0:T(8,128)(2,1)S(1)}, bf16[304,256]{1,0:T(8,128)(2,1)S(1)}, u32[]{:S(2)}, u32[]{:S(2)}) collective-permute-start(bf16[304,256]{1,0:T(8,128)(2,1)S(1)} %get-tuple-element.200), channel_id=1, source_target_pairs={{0,2},{1,3},{2,0},{3,1},{4,6},{5,7},{6,4},{7,5},{8,10},{9,11},{10,... | collective-permute-start | bytes 466952 | tf_op jit(solution)/shard_map/ppermute | solution.py:505
  53.4 6.1 %collective-permute-start.11 = (bf16[304,256]{1,0:T(8,128)(2,1)S(1)}, bf16[304,256]{1,0:T(8,128)(2,1)S(1)}, u32[]{:S(2)}, u32[]{:S(2)}) collective-permute-start(bf16[304,256]{1,0:T(8,128)(2,1)S(1)} %get-tuple-element.194), channel_id=1, source_target_pairs={{0,4},{1,5},{2,6},{3,7},{4,0},{5,1},{6,2},{7,3},{8,12},{9,13},{10,... | collective-permute-start | bytes 466952 | tf_op jit(solution)/shard_map/ppermute | solution.py:505
  58.3 4.5 %collective-permute-start.19 = (bf16[152,256]{1,0:T(8,128)(2,1)S(1)}, bf16[152,256]{1,0:T(8,128)(2,1)S(1)}, u32[]{:S(2)}, u32[]{:S(2)}) collective-permute-start(bf16[152,256]{1,0:T(8,128)(2,1)S(1)} %get-tuple-element.202), channel_id=1, source_target_pairs={{0,4},{1,5},{2,6},{3,7},{4,0},{5,1},{6,2},{7,3},{8,12},{9,13},{10,... | collective-permute-start | bytes 233480 | tf_op jit(solution)/shard_map/ppermute | solution.py:505
  59.5 6.3 %collective-permute-start.12 = (bf16[152,256]{1,0:T(8,128)(2,1)S(1)}, bf16[152,256]{1,0:T(8,128)(2,1)S(1)}, u32[]{:S(2)}, u32[]{:S(2)}) collective-permute-start(bf16[152,256]{1,0:T(8,128)(2,1)S(1)} %get-tuple-element.196), channel_id=1, source_target_pairs={{0,2},{1,3},{2,0},{3,1},{4,6},{5,7},{6,4},{7,5},{8,10},{9,11},{10,... | collective-permute-start | bytes 233480 | tf_op jit(solution)/shard_map/ppermute | solution.py:505
  62.8 7.7 %collective-permute-start.20 = (bf16[152,256]{1,0:T(8,128)(2,1)S(1)}, bf16[152,256]{1,0:T(8,128)(2,1)S(1)}, u32[]{:S(2)}, u32[]{:S(2)}) collective-permute-start(bf16[152,256]{1,0:T(8,128)(2,1)S(1)} %fusion.1), channel_id=1, source_target_pairs={{0,8},{1,9},{2,10},{3,11},{4,12},{5,13},{6,14},{7,15},{8,0},{9,1},... | collective-permute-start | bytes 233480 | tf_op jit(solution)/shard_map/ppermute | solution.py:505
  65.9 6.6 %collective-permute-start.13 = (bf16[152,256]{1,0:T(8,128)(2,1)S(1)}, bf16[152,256]{1,0:T(8,128)(2,1)S(1)}, u32[]{:S(2)}, u32[]{:S(2)}) collective-permute-start(bf16[152,256]{1,0:T(8,128)(2,1)S(1)} %fusion), channel_id=1, source_target_pairs={{0,8},{1,9},{2,10},{3,11},{4,12},{5,13},{6,14},{7,15},{8,0},{9,1},... | collective-permute-start | bytes 233480 | tf_op jit(solution)/shard_map/ppermute | solution.py:505
  70.6 4.5 %collective-permute-start.21 = (bf16[152,256]{1,0:T(8,128)(2,1)S(1)}, bf16[152,256]{1,0:T(8,128)(2,1)S(1)}, u32[]{:S(2)}, u32[]{:S(2)}) collective-permute-start(bf16[152,256]{1,0:T(8,128)(2,1)S(1)} %add_convert_fusion.part), channel_id=1, source_target_pairs={{0,4},{1,5},{2,6},{3,7},{4,0},{5,1},{6,2},{7,3},{8,12},{9,13},{10,... | collective-permute-start | bytes 233480 | tf_op jit(solution)/shard_map/ppermute | solution.py:505
  72.5 5.3 %collective-permute-start.14 = (bf16[152,256]{1,0:T(8,128)(2,1)S(1)}, bf16[152,256]{1,0:T(8,128)(2,1)S(1)}, u32[]{:S(2)}, u32[]{:S(2)}) collective-permute-start(bf16[152,256]{1,0:T(8,128)(2,1)S(1)} %add_convert_fusion.1.part), channel_id=1, source_target_pairs={{0,2},{1,3},{2,0},{3,1},{4,6},{5,7},{6,4},{7,5},{8,10},{9,11},{10,... | collective-permute-start | bytes 233480 | tf_op jit(solution)/shard_map/ppermute | solution.py:505
  75.1 5.4 %collective-permute-start.22 = (bf16[304,256]{1,0:T(8,128)(2,1)S(1)}, bf16[304,256]{1,0:T(8,128)(2,1)S(1)}, u32[]{:S(2)}, u32[]{:S(2)}) collective-permute-start(bf16[304,256]{1,0:T(8,128)(2,1)S(1)} %join.6.part), channel_id=1, source_target_pairs={{0,2},{1,3},{2,0},{3,1},{4,6},{5,7},{6,4},{7,5},{8,10},{9,11},{10,... | collective-permute-start | bytes 466952 | tf_op jit(solution)/shard_map/ppermute | solution.py:505
  77.8 5.3 %collective-permute-start.15 = (bf16[304,256]{1,0:T(8,128)(2,1)S(1)}, bf16[304,256]{1,0:T(8,128)(2,1)S(1)}, u32[]{:S(2)}, u32[]{:S(2)}) collective-permute-start(bf16[304,256]{1,0:T(8,128)(2,1)S(1)} %join.4.part), channel_id=1, source_target_pairs={{0,4},{1,5},{2,6},{3,7},{4,0},{5,1},{6,2},{7,3},{8,12},{9,13},{10,... | collective-permute-start | bytes 466952 | tf_op jit(solution)/shard_map/ppermute | solution.py:505
  80.6 2.7 %collective-permute-start.23 = (bf16[608,256]{1,0:T(8,128)(2,1)S(1)}, bf16[608,256]{1,0:T(8,128)(2,1)S(1)}, u32[]{:S(2)}, u32[]{:S(2)}) collective-permute-start(bf16[608,256]{1,0:T(8,128)(2,1)S(1)} %join.7.mine), channel_id=1, source_target_pairs={{0,1},{1,0},{2,3},{3,2},{4,5},{5,4},{6,7},{7,6},{8,9},{9,8},{10,11... | collective-permute-start | bytes 933896 | tf_op jit(solution)/shard_map/ppermute | solution.py:505
  83.2 1.7 %collective-permute-start.16 = (bf16[608,256]{1,0:T(8,128)(2,1)S(1)}, bf16[608,256]{1,0:T(8,128)(2,1)S(1)}, u32[]{:S(2)}, u32[]{:S(2)}) collective-permute-start(bf16[608,256]{1,0:T(8,128)(2,1)S(1)} %join.5.mine), channel_id=1, source_target_pairs={{0,1},{1,0},{2,3},{3,2},{4,5},{5,4},{6,7},{7,6},{8,9},{9,8},{10,11... | collective-permute-start | bytes 933896 | tf_op jit(solution)/shard_map/ppermute | solution.py:505

commit v7 on v6

--- a/solution.py
+++ b/solution.py
@@ -48,7 +48,7 @@
     me_ref, readings_hbm, *refs, heads, chunk, n_small,
 ):
     hbm, refs = refs[:n_small], refs[n_small:]
-    (mixed_ref, channels_ref, maps_ref, step_ref, cum_ref, cum_t_ref, keep_ref, send_ref, tail_ref, token_ref,
+    (mixed_ref, channels_ref, maps_ref, step_ref, cum_ref, cum_t_ref, weight_ref, send_ref, tail_ref, token_ref,
      consts_ref), refs = refs[:11], refs[11:]
     vmem, refs = refs[:n_small], refs[n_small:]
     readings, kmix, wms, spread2, log_sc, scaled_sc, sems = refs
@@ -131,15 +131,13 @@
     cum_t_ref[...] = cum.T
     last = cum[span - 1 : span, :]
     weight = jnp.exp2(last - cum) * step_ref[...]
+    weight_ref[...] = weight
 
     half = sensors // 2
     mine = (me_ref[0] & 1) * half
 
-    def sensor_at(n):
-        return (half - mine if n < half else mine - half) + n
-
     def scale(n):
-        s = sensor_at(n)
+        s = half - mine + n
         scaled_sc[n % 4] = (channels_ref[s].astype(f32) * spread(weight, s, heads, spread2[...])).astype(bf16)
 
     own = jnp.where(iota((sensors, lanes), 1) // heads == iota((sensors, lanes), 0), last, 0.0)
@@ -148,14 +146,29 @@
     send_ref[half * nstate :, :] = tail.astype(bf16)
     scale(0)
     scale(1)
-    for n in range(sensors):
-        if n + 2 < sensors:
+    for n in range(half):
+        if n + 2 < half:
             scale(n + 2)
-        state = dot(maps_ref[sensor_at(n)], scaled_sc[n % 4], TN)[0:nstate]
-        if n < half:
-            send_ref[n * nstate : (n + 1) * nstate, :] = state.astype(bf16)
-        else:
-            keep_ref[n - half] = state
+        state = dot(maps_ref[half - mine + n], scaled_sc[n % 4], TN)[0:nstate]
+        send_ref[n * nstate : (n + 1) * nstate, :] = state.astype(bf16)
+
+
+def own_kernel(me_ref, channels, maps, weight, keep_ref, spread2, scaled_sc, *, heads):
+    half, nstate, width = keep_ref.shape
+    mine = (me_ref[0] & 1) * half
+    spread2[...] = spread_matrix(spread2.shape[0], heads, width)
+
+    def scale(n):
+        scaled_sc[n % 4] = (
+            channels[mine + n].astype(f32) * spread(weight[...], mine + n, heads, spread2[...])
+        ).astype(bf16)
+
+    scale(0)
+    scale(1)
+    for n in range(half):
+        if n + 2 < half:
+            scale(n + 2)
+        keep_ref[n] = dot(maps[mine + n], scaled_sc[n % 4], TN)[0:nstate]
 
 
 def pair_blocks(x, size):
@@ -164,8 +177,8 @@
     return jnp.concatenate([jnp.where(lane < size, x, zero), jnp.where(lane >= size, x, zero)], axis=0)
 
 
-def within_kernel(channels, maps, step, cum_t, consts, cot_hbm, w_out_hbm, *refs, heads, first, count, aliases):
-    part_ref, scaled_ref, decay_ref, grad_ref, cot_ref, w_out_ref, _, spread2, sems = refs[aliases:]
+def within_kernel(channels, maps, step, cum, cum_t, consts, cot_hbm, w_out_hbm, *refs, heads, first, count, aliases):
+    part_ref, scaled_ref, decay_ref, grad_ref, cot_ref, w_out_ref, fade_ref, _, spread2, fade_sc, sems = refs[aliases:]
     _, span, width = channels.shape
     nstate = maps.shape[2] // 2
     size = width // heads
@@ -176,6 +189,7 @@
         w_out_copy.start()
     cot_copy.start()
     spread2[...] = spread_matrix(spread2.shape[0], heads, width)
+    fade_sc[...] = jnp.exp2(cum[...])
 
     def sensor(k, carry):
         s = first + k
@@ -183,6 +197,7 @@
         chan = channels[s].astype(f32)
         scaled = (chan * spread(step[...], s, heads, spread2[...])).astype(bf16)
         scaled_ref[s] = scaled
+        fade_ref[s] = spread(fade_sc[...], s, heads, spread2[...])
         both = maps[s]
         scores = dot(both[:, nstate:], both[:, 0:nstate], NT)
         row = cum_t[pl.ds(pl.multiple_of(s * heads, heads), heads), :]
@@ -213,14 +228,12 @@
 
 def back_kernel(me_ref, *refs, heads, blocks, aliases):
     states, refs = refs[0], refs[1:]
-    maps, scaled, decay, part, grad, cum, consts = refs[:7]
-    normed_ref, read_ref, gain_ref, _, spread2, fade_sc, carried_sc, spread_sc, back_sc, faded_sc = refs[7 + aliases :]
+    maps, scaled, decay, part, grad, fades, consts = refs[:7]
+    normed_ref, read_ref, gain_ref, _, carried_sc, back_sc, faded_sc = refs[7 + aliases :]
     sensors, span, width = part.shape
     nstate = maps.shape[2] // 2
     size = width // heads
     each = states.shape[0] // len(blocks)
-    spread2[...] = spread_matrix(spread2.shape[0], heads, width)
-    fade_sc[...] = jnp.exp2(cum[...])
     chunk = 32
     todo = [
         (block_start(me_ref[0], flips, sensors) + k, states, n * each + k)
@@ -231,14 +244,13 @@
     def carry_in(slot):
         s, state, k = todo[slot]
         carried_sc[slot] = dot(maps[s][:, nstate:], state[k])
-        spread_sc[slot] = spread(fade_sc[...], s, heads, spread2[...])
 
     def normalize(slot, gain_sum):
         s = todo[slot][0]
         gain = consts[1:2, :]
         for c in range(0, span, chunk):
             rows = slice(c, c + chunk)
-            fade = spread_sc[slot, rows, :]
+            fade = fades[s, rows, :]
             out = part[s, rows, :] + carried_sc[slot, rows, :] * fade
             inv = lax.rsqrt(jnp.mean(out * out, axis=-1, keepdims=True) + 1e-05)
             normed = out * inv
@@ -396,7 +408,7 @@
     outs = [
         ((sensors, span, width), bf16), ((sensors, span, channels), bf16), ((sensors, span, maps), bf16),
         ((span, lanes), f32), ((span, lanes), f32), ((lanes, span), f32),
-        ((sensors // 2, nstate, channels), f32), ((half_rows + sensors, channels), bf16), ((sensors, channels), f32),
+        ((span, lanes), f32), ((half_rows + sensors, channels), bf16), ((sensors, channels), f32),
         ((8, 128), f32), ((8, channels), f32),
     ]
     return call(
@@ -414,34 +426,44 @@
     )(me, *[pltpu.with_memory_space_constraint(x, pltpu.HBM) for x in [readings] + small])
 
 
-def within(first, count, channels, maps, step, cum_t, consts, cot, w_out, heads, done, token):
+def own_states(me, channels, maps, weight, nstate):
+    sensors, span, width = channels.shape
+    lanes = weight.shape[1]
+    return call(
+        functools.partial(own_kernel, heads=lanes // sensors), "own", 1, (), [HELD] * 3, [HELD],
+        [pltpu.VMEM((sensors // 2, nstate, width), f32)],
+        [pltpu.VMEM((2 * lanes, width), bf16), pltpu.VMEM((4, span, width), bf16)], 8, 3e8, 2e6,
+    )(me, *[held(x) for x in (channels, maps, weight)])[0]
+
+
+def within(first, count, channels, maps, step, cum, cum_t, consts, cot, w_out, heads, done, token):
     sensors, span, width = channels.shape
     lanes = sensors * heads
-    n_in = 7
+    n_in = 8
     aliases = {n_in + k: k for k in range(len(done))}
-    aliases[n_in + len(done)] = 6
+    aliases[n_in + len(done)] = 7
     return call(
         functools.partial(within_kernel, heads=heads, first=first, count=count, aliases=len(done) + 1),
         "within", 0, (),
-        [HELD] * 5 + [ANYWHERE] * 2 + [HELD] * len(done) + [ANYWHERE],
-        [HELD] * 6 + [ANYWHERE],
+        [HELD] * 6 + [ANYWHERE] * 2 + [HELD] * len(done) + [ANYWHERE],
+        [HELD] * 7 + [ANYWHERE],
         [
             pltpu.VMEM((sensors, span, width), f32), pltpu.VMEM((sensors, span, width), bf16),
             pltpu.VMEM((sensors, heads, span, span), bf16), pltpu.VMEM((sensors, span, width), f32),
-            pltpu.VMEM(cot.shape, bf16), pltpu.VMEM(w_out.shape, bf16),
+            pltpu.VMEM(cot.shape, bf16), pltpu.VMEM(w_out.shape, bf16), pltpu.VMEM((sensors, span, width), f32),
             jax.ShapeDtypeStruct(token.shape, token.dtype),
         ],
-        [pltpu.VMEM((2 * lanes, width), bf16), pltpu.SemaphoreType.DMA((2,))],
+        [pltpu.VMEM((2 * lanes, width), bf16), pltpu.VMEM((span, lanes), f32), pltpu.SemaphoreType.DMA((2,))],
         8, 3e8 * count, 1.5e6 * count, aliases,
     )(
-        *[held(x) for x in (channels, maps, step, cum_t, consts)],
+        *[held(x) for x in (channels, maps, step, cum, cum_t, consts)],
         *[pltpu.with_memory_space_constraint(x, pltpu.HBM) for x in (cot, w_out)], *[held(x) for x in done], token,
     )
 
 
-def back(me, blocks, states, maps, scaled, decay, part, grad, cum, consts, done, token):
+def back(me, blocks, states, maps, scaled, decay, part, grad, fades, consts, done, token):
     sensors, span, width = part.shape
-    heads, lanes = decay.shape[1], cum.shape[1]
+    heads = decay.shape[1]
     at_once = sum(state.shape[0] for state in states)
     n_in = 8 + len(states)
     aliases = {n_in + k: k for k in range(len(done))}
@@ -455,12 +477,11 @@
             pltpu.VMEM((8, width), f32), jax.ShapeDtypeStruct(token.shape, token.dtype),
         ],
         [
-            pltpu.VMEM((2 * lanes, width), bf16), pltpu.VMEM((span, lanes), f32),
-            pltpu.VMEM((at_once, span, width), f32), pltpu.VMEM((at_once, span, width), f32),
+            pltpu.VMEM((at_once, span, width), f32),
             pltpu.VMEM((at_once, span, width), bf16), pltpu.VMEM((at_once, span, width), bf16),
         ],
         8, 3e8 * at_once, 1.5e6 * at_once, aliases,
-    )(me, *[held(x) for x in (*states, maps, scaled, decay, part, grad, cum, consts) + done], token)
+    )(me, *[held(x) for x in (*states, maps, scaled, decay, part, grad, fades, consts) + done], token)
 
 
 def grad_rows(channels, nstate):
@@ -782,16 +803,16 @@
     at = me[None]
     heads = skip_gain.shape[0]
 
-    mixed, chans, maps, step, cum, cum_t, keep, send, tail, token, consts = front(
+    mixed, chans, maps, step, cum, cum_t, weight, send, tail, token, consts = front(
         at, readings, block_graph, cluster_of, mix_weight, boundaries, w_channels, w_state, w_step,
         step_bias, channel_fading_exponent, skip_gain, norm_gain,
     )
     work = {"token": token, "within": (), "back": (), "gains": []}
 
     def run_back(blocks, *states):
-        part, scaled, decay, grad = work["within"][:4]
+        part, scaled, decay, grad, _, _, fades = work["within"]
         normed, read, gain, work["token"] = back(
-            at, blocks, states, maps, scaled, decay, part, grad, cum, consts, work["back"], work["token"]
+            at, blocks, states, maps, scaled, decay, part, grad, fades, consts, work["back"], work["token"]
         )
         work["back"] = (normed, read)
         work["gains"].append(gain)
@@ -802,11 +823,13 @@
 
     def run_within(first, size):
         *arrays, work["token"] = within(
-            first, size, chans, maps, step, cum_t, consts, cotangent, w_out, heads, work["within"], work["token"]
+            first, size, chans, maps, step, cum, cum_t, consts, cotangent, w_out, heads, work["within"], work["token"]
         )
         work["within"] = tuple(arrays)
 
     came = swap(send, 1, count)
+    keep = own_states(at, chans, maps, weight, nstate)
+    came, keep = tied(came, keep)
     low, low_tail, tail, kept, *sends = join_cores(at, keep, tail, came)
     sends = tie(sends)
     cames = [swap(x, 2 * (n + 1), count) for n, x in enumerate(sends)]

time: 86.3 us -> 85.4 us (0.990)
  waiting for transfers between devices: 25 us -> 24 us
    ppermute x24, waiting for transfers between devices: 25 us -> 24 us  [swap(): return lax.ppermute(x, 'seq', [(i, i ^ distance) for i in range(count)])]
    pallas_call x0 -> x1, Pallas kernels: none -> 0.87 us  [own_states(): call(functools.partial(own_kernel, heads=lanes // sensors), 'own', 1, (),...]
  transfers between devices with their start and end apart: 24 -> 24, of which waited for: 14 -> 14; matrix products, arithmetic and copies ran while one was open for 0% -> 0% of each run, Pallas kernels for 22% -> 23%
where the time goes in v7:
time: 85.4 us; the launch traced here: 85.2 us
  Pallas kernels  34.3 us (40%)
  starting transfers between devices  25.7 us (30%)
  waiting for transfers between devices  24 us (28%)
  between operations  1.06 us (1%)
    ppermute x24, starting transfers between devices, swap(): return lax.ppermute(x, 'seq', [(i, i ^ distance) for i in range(count)])  25.7 us
    ppermute x24, waiting for transfers between devices, swap(): return lax.ppermute(x, 'seq', [(i, i ^ distance) for i in range(count)])  24 us
    pallas_call x2, Pallas kernels, within(): call(functools.partial(within_kernel, heads=heads, first=first, count=cou...  9.77 us
    pallas_call x1, Pallas kernels, front(): call(functools.partial(front_kernel, heads=heads, chunk=chunk, n_small=le...  8.56 us
    pallas_call x4, Pallas kernels, back(): call(functools.partial(back_kernel, heads=heads, blocks=blocks, aliases=l...  7.53 us
    pallas_call x2, Pallas kernels, late_grads(): call(functools.partial(late_kernel, part=part), 'late', 1, (), [HELD] * (...  2.86 us
    pallas_call x2, Pallas kernels, finish(): call(functools.partial(finish_kernel, part=part, aliases=len(done)), 'fin...  2.18 us
  transfers between devices with their start and end apart: 24, of which 14 were waited for; matrix products, arithmetic and copies ran while one was open for 0% of the time, Pallas kernels for 23%

profile of v7, /device:TPU:0, one launch (start us, length us, event | category | flops | bytes accessed | tf_op | source)
XLA Modules:
  0.0 85.2 jit_solution(12166011744102624497)
XLA Ops:
  0.6 8.6 %front.1 = (bf16[16,128,1024]{2,1,0:T(8,128)(2,1)S(1)}, bf16[16,128,512]{2,1,0:T(8,128)(2,1)S(1)}, bf16[16,128,128]{2,1,0:T(8,128)(2,1)S(1)}, f32[128,128]{1,0:T...) custom-call(s32[1]{0:T(128)} %bitcast.me_ref, ...), custom_call_target="tpu_custom_call" | custom-call | flops 5000000000 | bytes 14000000 | tf_op jit(solution)/shard_map/front/pallas_call | solution.py:414
  9.2 0.5 collective-permute-start
  9.7 0.9 %own.1 = f32[8,64,512]{2,1,0:T(8,128)S(1)} custom-call(s32[1]{0:T(128)} %bitcast.me_ref, bf16[16,128,512]{2,1,0:T(8,128)(2,1)S(1)} %get-tuple-element.111.channels, bf16[16,128,128]{2,1,0:T(8,128)(2,1)S(1)} %get-tuple-element.112.maps.refs_1_, f32[128,128]{1,0:T(8,128)S(1)} %get-tuple-element.113.weight), custom_call_target="tpu_custom_call" | custom-call | flops 300000000 | bytes 2000000 | tf_op jit(solution)/shard_map/own/pallas_call | solution.py:432
  10.6 0.7 collective-permute-done.came
  11.3 0.3 cores.1
  11.6 2.9 %collective-permute-start.1 = (bf16[144,512]{1,0:T(8,128)(2,1)S(1)}, bf16[144,512]{1,0:T(8,128)(2,1)S(1)}, u32[]{:S(2)}, u32[]{:S(2)}) collective-permute-start(bf16[144,512]{1,0:T(8,128)(2,1)S(1)} %get-tuple-element.125), channel_id=1, source_target_pairs={{0,2},{1,3},{2,0},{3,1},{4,6},{5,7},{6,4},{7,5},{8,10},{9,11},{10,... | collective-permute-start | bytes 442376 | tf_op jit(solution)/shard_map/ppermute | solution.py:526
  14.6 1.6 %collective-permute-start.2 = (bf16[144,512]{1,0:T(8,128)(2,1)S(1)}, bf16[144,512]{1,0:T(8,128)(2,1)S(1)}, u32[]{:S(2)}, u32[]{:S(2)}) collective-permute-start(bf16[144,512]{1,0:T(8,128)(2,1)S(1)} %get-tuple-element.126), channel_id=1, source_target_pairs={{0,4},{1,5},{2,6},{3,7},{4,0},{5,1},{6,2},{7,3},{8,12},{9,13},{10,... | collective-permute-start | bytes 442376 | tf_op jit(solution)/shard_map/ppermute | solution.py:526
  16.1 5.9 %within.2 = (f32[16,128,512]{2,1,0:T(8,128)S(1)}, bf16[16,128,512]{2,1,0:T(8,128)(2,1)S(1)}, bf16[16,8,128,128]{3,2,1,0:T(8,128)(2,1)S(1)}, f32[16,128,512]{2,1,...) custom-call(bf16[16,128,512]{2,1,0:T(8,128)(2,1)S(1)} %get-tuple-ele, ...), custom_call_target="tpu_custom_call", output_to_operand_aliasing={{7}: (8, {})} | custom-call | flops 3000000000 | bytes 15000000 | tf_op jit(solution)/shard_map/within/pallas_call | solution.py:445
  22.1 1.0 %collective-permute-done.3.refs_2_ = bf16[144,512]{1,0:T(8,128)(2,1)S(1)} collective-permute-done((bf16[144,512]{1,0:T(8,128)(2,1)S(1)}, bf16[144,512]{1,0:T(8,128)(2,1)S(1)}, u32[]{:S(2)}, u32[]{:S(2)}) %collective-permute-start.3) | collective-permute-done | bytes 147488 | tf_op jit(solution)/shard_map/ppermute | solution.py:526
  23.1 0.3 group.1
  23.5 2.8 %collective-permute-start.4 = (bf16[128,512]{1,0:T(8,128)(2,1)S(1)}, bf16[128,512]{1,0:T(8,128)(2,1)S(1)}, u32[]{:S(2)}, u32[]{:S(2)}) collective-permute-start(bf16[128,512]{1,0:T(8,128)(2,1)S(1)} %get-tuple-element.139), channel_id=1, source_target_pairs={{0,8},{1,9},{2,10},{3,11},{4,12},{5,13},{6,14},{7,15},{8,0},{9,1},... | collective-permute-start | bytes 393224 | tf_op jit(solution)/shard_map/ppermute | solution.py:526
  26.3 3.8 %within.3 = (f32[16,128,512]{2,1,0:T(8,128)S(1)}, bf16[16,128,512]{2,1,0:T(8,128)(2,1)S(1)}, bf16[16,8,128,128]{3,2,1,0:T(8,128)(2,1)S(1)}, f32[16,128,512]{2,1,...) custom-call(bf16[16,128,512]{2,1,0:T(8,128)(2,1)S(1)} %get-tuple-ele, ...), custom_call_target="tpu_custom_call", output_to_operand_aliasing={{0}: (8, {}), {1}: (9, {}), {2}: (10, {}), {3}: (11, {}), {... | custom-call | flops 1800000000 | bytes 9000000 | tf_op jit(solution)/shard_map/within/pallas_call | solution.py:445
  30.1 1.9 %collective-permute-done.4.came = bf16[128,512]{1,0:T(8,128)(2,1)S(1)} collective-permute-done((bf16[128,512]{1,0:T(8,128)(2,1)S(1)}, bf16[128,512]{1,0:T(8,128)(2,1)S(1)}, u32[]{:S(2)}, u32[]{:S(2)}) %collective-permute-start.4) | collective-permute-done | bytes 131104 | tf_op jit(solution)/shard_map/ppermute | solution.py:526
  32.1 0.3 fall.1
  32.4 0.6 collective-permute-start.5
  33.0 1.4 %collective-permute-start.6 = (bf16[2,64,512]{2,1,0:T(8,128)(2,1)S(1)}, bf16[2,64,512]{2,1,0:T(8,128)(2,1)S(1)}, u32[]{:S(2)}, u32[]{:S(2)}) collective-permute-start(bf16[2,64,512]{2,1,0:T(8,128)(2,1)S(1)} %get-tuple-element.162), channel_id=1, source_target_pairs={{0,2},{1,3},{2,0},{3,1},{4,6},{5,7},{6,4},{7,5},{8,10},{9,11},{10,... | collective-permute-start | bytes 393224 | tf_op jit(solution)/shard_map/ppermute | solution.py:526
  34.4 1.6 %collective-permute-start.7 = (bf16[2,64,512]{2,1,0:T(8,128)(2,1)S(1)}, bf16[2,64,512]{2,1,0:T(8,128)(2,1)S(1)}, u32[]{:S(2)}, u32[]{:S(2)}) collective-permute-start(bf16[2,64,512]{2,1,0:T(8,128)(2,1)S(1)} %get-tuple-element.163), channel_id=1, source_target_pairs={{0,6},{1,7},{2,4},{3,5},{4,2},{5,3},{6,0},{7,1},{8,14},{9,15},{10,... | collective-permute-start | bytes 393224 | tf_op jit(solution)/shard_map/ppermute | solution.py:526
  36.0 1.2 %back.4 = (bf16[16,128,512]{2,1,0:T(8,128)(2,1)S(1)}, bf16[16,128,64]{2,1,0:T(8,128)(2,1)S(1)}, f32[8,512]{1,0:T(8,128)S(1)}, f32[8,128]{1,0:T(8,128)S(1)}) custom-call(s32[1]{0:T(128)} %bitcast.me_ref, bf16[2,64,512]{2,1,0:T(8,128)(2,1)S(1)} %get-tuple-element.170.refs_0_, ...), custom_call_target="tpu_custom_call", output_to_operand_aliasing={{3}: (9, {})} | custom-call | flops 600000000 | bytes 3000000 | tf_op jit(solution)/shard_map/back/pallas_call | solution.py:471
  37.2 1.2 %back.5 = (bf16[16,128,512]{2,1,0:T(8,128)(2,1)S(1)}, bf16[16,128,64]{2,1,0:T(8,128)(2,1)S(1)}, f32[8,512]{1,0:T(8,128)S(1)}, f32[8,128]{1,0:T(8,128)S(1)}) custom-call(s32[1]{0:T(128)} %bitcast.me_ref, bf16[2,64,512]{2,1,0:T(8,128)(2,1)S(1)} %collective-permute-done.8.refs_0_, ...), custom_call_target="tpu_custom_call", output_to_operand_aliasing={{0}: (9, {}), {1}: (10, {}), {3}: (11, {})} | custom-call | flops 600000000 | bytes 3000000 | tf_op jit(solution)/shard_map/back/pallas_call | solution.py:471
  38.4 0.9 %early.1 = (f32[4,608,256]{2,1,0:T(8,128)S(1)}, f32[8,128]{1,0:T(8,128)S(1)}) custom-call(s32[1]{0:T(128)} %bitcast.me_ref, bf16[16,128,512]{2,1,0:T(8,128)(2,1)S(1)} %get-tuple-element.175.normed.refs_8_, bf16[16,128,1024]{2,1,0:T(8,128)(2,1)S(1)} %get-tuple-element.176.cot, ...), custom_call_target="tpu_custom_call", output_to_operand_aliasing={{1}: (5, {})} | custom-call | flops 600000000 | bytes 4000000 | tf_op jit(solution)/shard_map/early/pallas_call | solution.py:493
  39.3 2.5 %collective-permute-done.7.refs_2_ = bf16[2,64,512]{2,1,0:T(8,128)(2,1)S(1)} collective-permute-done((bf16[2,64,512]{2,1,0:T(8,128)(2,1)S(1)}, bf16[2,64,512]{2,1,0:T(8,128)(2,1)S(1)}, u32[]{:S(2)}, u32[]{:S(2)}) %collective-permute-start.7) | collective-permute-done | bytes 131104 | tf_op jit(solution)/shard_map/ppermute | solution.py:526
  41.8 0.2 land.1
  42.1 2.6 %back.6 = (bf16[16,128,512]{2,1,0:T(8,128)(2,1)S(1)}, bf16[16,128,64]{2,1,0:T(8,128)(2,1)S(1)}, f32[8,512]{1,0:T(8,128)S(1)}, f32[8,128]{1,0:T(8,128)S(1)}) custom-call(s32[1]{0:T(128)} %bitcast.me_ref, bf16[6,64,512]{2,1,0:T(8,128)(2,1)S(1)} %get-tuple-element.187.refs_0_, ...), custom_call_target="tpu_custom_call", output_to_operand_aliasing={{0}: (9, {}), {1}: (10, {}), {3}: (11, {})} | custom-call | flops 1800000000 | bytes 9000000 | tf_op jit(solution)/shard_map/back/pallas_call | solution.py:471
  44.7 2.6 %back.7 = (bf16[16,128,512]{2,1,0:T(8,128)(2,1)S(1)}, bf16[16,128,64]{2,1,0:T(8,128)(2,1)S(1)}, f32[8,512]{1,0:T(8,128)S(1)}, f32[8,128]{1,0:T(8,128)S(1)}) custom-call(s32[1]{0:T(128)} %bitcast.me_ref, bf16[6,64,512]{2,1,0:T(8,128)(2,1)S(1)} %collective-permute-done.9.refs_0_, ...), custom_call_target="tpu_custom_call", output_to_operand_aliasing={{0}: (9, {}), {1}: (10, {}), {3}: (11, {})} | custom-call | flops 1800000000 | bytes 9000000 | tf_op jit(solution)/shard_map/back/pallas_call | solution.py:471
  47.3 1.4 %late.3 = (f32[608,256]{1,0:T(8,128)S(1)}, bf16[608,256]{1,0:T(8,128)(2,1)S(1)}) custom-call(s32[1]{0:T(128)} %bitcast.me_ref, bf16[16,128,512]{2,1,0:T(8,128)(2,1)S(1)} %get-tuple-element.192.normed, bf16[16,128,1024]{2,1,0:T(8,128)(2,1)S(1)} %get-tuple-element.176.cot, bf16[16,128,64]{2,1,0:T(8,128)(2,1)S(1)} %get-tuple-element.193.read, ...), custom_call_target="tpu_custom_call" | custom-call | flops 800000000 | bytes 5000000 | tf_op jit(solution)/shard_map/late/pallas_call | solution.py:502
  48.7 0.6 collective-permute-start.17
  49.3 1.4 %late.2 = (f32[608,256]{1,0:T(8,128)S(1)}, bf16[608,256]{1,0:T(8,128)(2,1)S(1)}) custom-call(s32[1]{0:T(128)} %bitcast.me_ref, bf16[16,128,512]{2,1,0:T(8,128)(2,1)S(1)} %get-tuple-element.192.normed, bf16[16,128,1024]{2,1,0:T(8,128)(2,1)S(1)} %get-tuple-element.176.cot, bf16[16,128,64]{2,1,0:T(8,128)(2,1)S(1)} %get-tuple-element.193.read, ...), custom_call_target="tpu_custom_call" | custom-call | flops 800000000 | bytes 5000000 | tf_op jit(solution)/shard_map/late/pallas_call | solution.py:502
  50.9 1.0 %collective-permute-start.18 = (bf16[304,256]{1,0:T(8,128)(2,1)S(1)}, bf16[304,256]{1,0:T(8,128)(2,1)S(1)}, u32[]{:S(2)}, u32[]{:S(2)}) collective-permute-start(bf16[304,256]{1,0:T(8,128)(2,1)S(1)} %get-tuple-element.208), channel_id=1, source_target_pairs={{0,2},{1,3},{2,0},{3,1},{4,6},{5,7},{6,4},{7,5},{8,10},{9,11},{10,... | collective-permute-start | bytes 466952 | tf_op jit(solution)/shard_map/ppermute | solution.py:526
  52.0 0.4 collective-permute-done.10.came
  52.5 1.2 %collective-permute-start.11 = (bf16[304,256]{1,0:T(8,128)(2,1)S(1)}, bf16[304,256]{1,0:T(8,128)(2,1)S(1)}, u32[]{:S(2)}, u32[]{:S(2)}) collective-permute-start(bf16[304,256]{1,0:T(8,128)(2,1)S(1)} %get-tuple-element.202), channel_id=1, source_target_pairs={{0,4},{1,5},{2,6},{3,7},{4,0},{5,1},{6,2},{7,3},{8,12},{9,13},{10,... | collective-permute-start | bytes 466952 | tf_op jit(solution)/shard_map/ppermute | solution.py:526
  53.7 3.7 %collective-permute-done.18.came = bf16[304,256]{1,0:T(8,128)(2,1)S(1)} collective-permute-done((bf16[304,256]{1,0:T(8,128)(2,1)S(1)}, bf16[304,256]{1,0:T(8,128)(2,1)S(1)}, u32[]{:S(2)}, u32[]{:S(2)}) %collective-permute-start.18) | collective-permute-done | bytes 155680 | tf_op jit(solution)/shard_map/ppermute | solution.py:526
  57.5 1.2 %collective-permute-start.19 = (bf16[152,256]{1,0:T(8,128)(2,1)S(1)}, bf16[152,256]{1,0:T(8,128)(2,1)S(1)}, u32[]{:S(2)}, u32[]{:S(2)}) collective-permute-start(bf16[152,256]{1,0:T(8,128)(2,1)S(1)} %get-tuple-element.210), channel_id=1, source_target_pairs={{0,4},{1,5},{2,6},{3,7},{4,0},{5,1},{6,2},{7,3},{8,12},{9,13},{10,... | collective-permute-start | bytes 233480 | tf_op jit(solution)/shard_map/ppermute | solution.py:526
  58.7 1.3 %collective-permute-start.12 = (bf16[152,256]{1,0:T(8,128)(2,1)S(1)}, bf16[152,256]{1,0:T(8,128)(2,1)S(1)}, u32[]{:S(2)}, u32[]{:S(2)}) collective-permute-start(bf16[152,256]{1,0:T(8,128)(2,1)S(1)} %get-tuple-element.204), channel_id=1, source_target_pairs={{0,2},{1,3},{2,0},{3,1},{4,6},{5,7},{6,4},{7,5},{8,10},{9,11},{10,... | collective-permute-start | bytes 233480 | tf_op jit(solution)/shard_map/ppermute | solution.py:526
  59.9 2.0 %collective-permute-done.19 = bf16[152,256]{1,0:T(8,128)(2,1)S(1)} collective-permute-done((bf16[152,256]{1,0:T(8,128)(2,1)S(1)}, bf16[152,256]{1,0:T(8,128)(2,1)S(1)}, u32[]{:S(2)}, u32[]{:S(2)}) %collective-permute-start.19) | collective-permute-done | bytes 77856 | tf_op jit(solution)/shard_map/ppermute | solution.py:526
  61.9 3.1 %collective-permute-start.20 = (bf16[152,256]{1,0:T(8,128)(2,1)S(1)}, bf16[152,256]{1,0:T(8,128)(2,1)S(1)}, u32[]{:S(2)}, u32[]{:S(2)}) collective-permute-start(bf16[152,256]{1,0:T(8,128)(2,1)S(1)} %fusion.1), channel_id=1, source_target_pairs={{0,8},{1,9},{2,10},{3,11},{4,12},{5,13},{6,14},{7,15},{8,0},{9,1},... | collective-permute-start | bytes 233480 | tf_op jit(solution)/shard_map/ppermute | solution.py:526
  65.0 1.2 %collective-permute-start.13 = (bf16[152,256]{1,0:T(8,128)(2,1)S(1)}, bf16[152,256]{1,0:T(8,128)(2,1)S(1)}, u32[]{:S(2)}, u32[]{:S(2)}) collective-permute-start(bf16[152,256]{1,0:T(8,128)(2,1)S(1)} %fusion), channel_id=1, source_target_pairs={{0,8},{1,9},{2,10},{3,11},{4,12},{5,13},{6,14},{7,15},{8,0},{9,1},... | collective-permute-start | bytes 233480 | tf_op jit(solution)/shard_map/ppermute | solution.py:526
  66.2 3.5 %collective-permute-done.20 = bf16[152,256]{1,0:T(8,128)(2,1)S(1)} collective-permute-done((bf16[152,256]{1,0:T(8,128)(2,1)S(1)}, bf16[152,256]{1,0:T(8,128)(2,1)S(1)}, u32[]{:S(2)}, u32[]{:S(2)}) %collective-permute-start.20) | collective-permute-done | bytes 77856 | tf_op jit(solution)/shard_map/ppermute | solution.py:526
  69.7 1.0 %collective-permute-start.21 = (bf16[152,256]{1,0:T(8,128)(2,1)S(1)}, bf16[152,256]{1,0:T(8,128)(2,1)S(1)}, u32[]{:S(2)}, u32[]{:S(2)}) collective-permute-start(bf16[152,256]{1,0:T(8,128)(2,1)S(1)} %add_convert_fusion.part), channel_id=1, source_target_pairs={{0,4},{1,5},{2,6},{3,7},{4,0},{5,1},{6,2},{7,3},{8,12},{9,13},{10,... | collective-permute-start | bytes 233480 | tf_op jit(solution)/shard_map/ppermute | solution.py:526
  70.7 0.9 %collective-permute-done.13 = bf16[152,256]{1,0:T(8,128)(2,1)S(1)} collective-permute-done((bf16[152,256]{1,0:T(8,128)(2,1)S(1)}, bf16[152,256]{1,0:T(8,128)(2,1)S(1)}, u32[]{:S(2)}, u32[]{:S(2)}) %collective-permute-start.13) | collective-permute-done | bytes 77856 | tf_op jit(solution)/shard_map/ppermute | solution.py:526
  71.6 1.4 %collective-permute-start.14 = (bf16[152,256]{1,0:T(8,128)(2,1)S(1)}, bf16[152,256]{1,0:T(8,128)(2,1)S(1)}, u32[]{:S(2)}, u32[]{:S(2)}) collective-permute-start(bf16[152,256]{1,0:T(8,128)(2,1)S(1)} %add_convert_fusion.1.part), channel_id=1, source_target_pairs={{0,2},{1,3},{2,0},{3,1},{4,6},{5,7},{6,4},{7,5},{8,10},{9,11},{10,... | collective-permute-start | bytes 233480 | tf_op jit(solution)/shard_map/ppermute | solution.py:526
  73.0 1.2 %collective-permute-done.21.came = bf16[152,256]{1,0:T(8,128)(2,1)S(1)} collective-permute-done((bf16[152,256]{1,0:T(8,128)(2,1)S(1)}, bf16[152,256]{1,0:T(8,128)(2,1)S(1)}, u32[]{:S(2)}, u32[]{:S(2)}) %collective-permute-start.21) | collective-permute-done | bytes 77856 | tf_op jit(solution)/shard_map/ppermute | solution.py:526
  74.2 2.1 %collective-permute-start.22 = (bf16[304,256]{1,0:T(8,128)(2,1)S(1)}, bf16[304,256]{1,0:T(8,128)(2,1)S(1)}, u32[]{:S(2)}, u32[]{:S(2)}) collective-permute-start(bf16[304,256]{1,0:T(8,128)(2,1)S(1)} %join.6.part), channel_id=1, source_target_pairs={{0,2},{1,3},{2,0},{3,1},{4,6},{5,7},{6,4},{7,5},{8,10},{9,11},{10,... | collective-permute-start | bytes 466952 | tf_op jit(solution)/shard_map/ppermute | solution.py:526
  76.4 0.5 collective-permute-done.14.came
  77.0 2.6 %collective-permute-done.22.came = bf16[304,256]{1,0:T(8,128)(2,1)S(1)} collective-permute-done((bf16[304,256]{1,0:T(8,128)(2,1)S(1)}, bf16[304,256]{1,0:T(8,128)(2,1)S(1)}, u32[]{:S(2)}, u32[]{:S(2)}) %collective-permute-start.22) | collective-permute-done | bytes 155680 | tf_op jit(solution)/shard_map/ppermute | solution.py:526
  79.7 2.4 %collective-permute-done.15.came = bf16[304,256]{1,0:T(8,128)(2,1)S(1)} collective-permute-done((bf16[304,256]{1,0:T(8,128)(2,1)S(1)}, bf16[304,256]{1,0:T(8,128)(2,1)S(1)}, u32[]{:S(2)}, u32[]{:S(2)}) %collective-permute-start.15) | collective-permute-done | bytes 155680 | tf_op jit(solution)/shard_map/ppermute | solution.py:526
  82.3 1.1 %finish.2 = (f32[512,1024]{1,0:T(8,128)}, f32[64,1024]{1,0:T(8,128)}, f32[1,512]{1,0:T(1,128)}) custom-call(s32[1]{0:T(128)} %bitcast.me_ref, bf16[608,256]{1,0:T(8,128)(2,1)S(1)} %join.7.mine, bf16[608,256]{1,0:T(8,128)(2,1)S(1)} %collective-permute-done.23.came), custom_call_target="tpu_custom_call" | custom-call | flops 1000000 | bytes 2000000 | tf_op jit(solution)/shard_map/finish/pallas_call | solution.py:511
  83.4 0.5 collective-permute-done.16.came
  83.9 1.1 %finish.3 = (f32[512,1024]{1,0:T(8,128)}, f32[64,1024]{1,0:T(8,128)}, f32[1,512]{1,0:T(1,128)}) custom-call(s32[1]{0:T(128)} %bitcast.me_ref, bf16[608,256]{1,0:T(8,128)(2,1)S(1)} %join.5.mine, bf16[608,256]{1,0:T(8,128)(2,1)S(1)} %collective-permute-done.16.came, ...), custom_call_target="tpu_custom_call", output_to_operand_aliasing={{0}: (3, {}), {1}: (4, {}), {2}: (5, {})} | custom-call | flops 1000000 | bytes 2000000 | tf_op jit(solution)/shard_map/finish/pallas_call | solution.py:511
  (29 shorter events, 1.1 us)
Async XLA Ops:
  9.2 2.1 %collective-permute-start = (bf16[528,512]{1,0:T(8,128)(2,1)S(1)}, bf16[528,512]{1,0:T(8,128)(2,1)S(1)}, u32[]{:S(2)}, u32[]{:S(2)}) collective-permute-start(bf16[528,512]{1,0:T(8,128)(2,1)S(1)} %get-tuple-element.110), channel_id=1, source_target_pairs={{0,1},{1,0},{2,3},{3,2},{4,5},{5,4},{6,7},{7,6},{8,9},{9,8},{10,11... | collective-permute-start | bytes 1622024 | tf_op jit(solution)/shard_map/ppermute | solution.py:526
  11.6 10.5 %collective-permute-start.1 = (bf16[144,512]{1,0:T(8,128)(2,1)S(1)}, bf16[144,512]{1,0:T(8,128)(2,1)S(1)}, u32[]{:S(2)}, u32[]{:S(2)}) collective-permute-start(bf16[144,512]{1,0:T(8,128)(2,1)S(1)} %get-tuple-element.125), channel_id=1, source_target_pairs={{0,2},{1,3},{2,0},{3,1},{4,6},{5,7},{6,4},{7,5},{8,10},{9,11},{10,... | collective-permute-start | bytes 442376 | tf_op jit(solution)/shard_map/ppermute | solution.py:526
  14.6 7.6 %collective-permute-start.2 = (bf16[144,512]{1,0:T(8,128)(2,1)S(1)}, bf16[144,512]{1,0:T(8,128)(2,1)S(1)}, u32[]{:S(2)}, u32[]{:S(2)}) collective-permute-start(bf16[144,512]{1,0:T(8,128)(2,1)S(1)} %get-tuple-element.126), channel_id=1, source_target_pairs={{0,4},{1,5},{2,6},{3,7},{4,0},{5,1},{6,2},{7,3},{8,12},{9,13},{10,... | collective-permute-start | bytes 442376 | tf_op jit(solution)/shard_map/ppermute | solution.py:526
  16.1 7.0 %collective-permute-start.3 = (bf16[144,512]{1,0:T(8,128)(2,1)S(1)}, bf16[144,512]{1,0:T(8,128)(2,1)S(1)}, u32[]{:S(2)}, u32[]{:S(2)}) collective-permute-start(bf16[144,512]{1,0:T(8,128)(2,1)S(1)} %get-tuple-element.127), channel_id=1, source_target_pairs={{0,6},{1,7},{2,4},{3,5},{4,2},{5,3},{6,0},{7,1},{8,14},{9,15},{10,... | collective-permute-start | bytes 442376 | tf_op jit(solution)/shard_map/ppermute | solution.py:526
  23.5 8.6 %collective-permute-start.4 = (bf16[128,512]{1,0:T(8,128)(2,1)S(1)}, bf16[128,512]{1,0:T(8,128)(2,1)S(1)}, u32[]{:S(2)}, u32[]{:S(2)}) collective-permute-start(bf16[128,512]{1,0:T(8,128)(2,1)S(1)} %get-tuple-element.139), channel_id=1, source_target_pairs={{0,8},{1,9},{2,10},{3,11},{4,12},{5,13},{6,14},{7,15},{8,0},{9,1},... | collective-permute-start | bytes 393224 | tf_op jit(solution)/shard_map/ppermute | solution.py:526
  32.4 4.8 %collective-permute-start.8 = (bf16[2,64,512]{2,1,0:T(8,128)(2,1)S(1)}, bf16[2,64,512]{2,1,0:T(8,128)(2,1)S(1)}, u32[]{:S(2)}, u32[]{:S(2)}) collective-permute-start(bf16[2,64,512]{2,1,0:T(8,128)(2,1)S(1)} %get-tuple-element.164), channel_id=1, source_target_pairs={{0,1},{1,0},{2,3},{3,2},{4,5},{5,4},{6,7},{7,6},{8,9},{9,8},{10,11... | collective-permute-start | bytes 393224 | tf_op jit(solution)/shard_map/ppermute | solution.py:526
  32.4 6.8 %collective-permute-start.5 = (bf16[2,64,512]{2,1,0:T(8,128)(2,1)S(1)}, bf16[2,64,512]{2,1,0:T(8,128)(2,1)S(1)}, u32[]{:S(2)}, u32[]{:S(2)}) collective-permute-start(bf16[2,64,512]{2,1,0:T(8,128)(2,1)S(1)} %get-tuple-element.161), channel_id=1, source_target_pairs={{0,4},{1,5},{2,6},{3,7},{4,0},{5,1},{6,2},{7,3},{8,12},{9,13},{10,... | collective-permute-start | bytes 393224 | tf_op jit(solution)/shard_map/ppermute | solution.py:526
  33.0 6.2 %collective-permute-start.6 = (bf16[2,64,512]{2,1,0:T(8,128)(2,1)S(1)}, bf16[2,64,512]{2,1,0:T(8,128)(2,1)S(1)}, u32[]{:S(2)}, u32[]{:S(2)}) collective-permute-start(bf16[2,64,512]{2,1,0:T(8,128)(2,1)S(1)} %get-tuple-element.162), channel_id=1, source_target_pairs={{0,2},{1,3},{2,0},{3,1},{4,6},{5,7},{6,4},{7,5},{8,10},{9,11},{10,... | collective-permute-start | bytes 393224 | tf_op jit(solution)/shard_map/ppermute | solution.py:526
  34.4 7.4 %collective-permute-start.7 = (bf16[2,64,512]{2,1,0:T(8,128)(2,1)S(1)}, bf16[2,64,512]{2,1,0:T(8,128)(2,1)S(1)}, u32[]{:S(2)}, u32[]{:S(2)}) collective-permute-start(bf16[2,64,512]{2,1,0:T(8,128)(2,1)S(1)} %get-tuple-element.163), channel_id=1, source_target_pairs={{0,6},{1,7},{2,4},{3,5},{4,2},{5,3},{6,0},{7,1},{8,14},{9,15},{10,... | collective-permute-start | bytes 393224 | tf_op jit(solution)/shard_map/ppermute | solution.py:526
  42.0 2.7 %collective-permute-start.9 = (bf16[6,64,512]{2,1,0:T(8,128)(2,1)S(1)}, bf16[6,64,512]{2,1,0:T(8,128)(2,1)S(1)}, u32[]{:S(2)}, u32[]{:S(2)}) collective-permute-start(bf16[6,64,512]{2,1,0:T(8,128)(2,1)S(1)} %get-tuple-element.186), channel_id=1, source_target_pairs={{0,1},{1,0},{2,3},{3,2},{4,5},{5,4},{6,7},{7,6},{8,9},{9,8},{10,11... | collective-permute-start | bytes 1179656 | tf_op jit(solution)/shard_map/ppermute | solution.py:526
  48.7 2.1 %collective-permute-start.17 = (bf16[608,256]{1,0:T(8,128)(2,1)S(1)}, bf16[608,256]{1,0:T(8,128)(2,1)S(1)}, u32[]{:S(2)}, u32[]{:S(2)}) collective-permute-start(bf16[608,256]{1,0:T(8,128)(2,1)S(1)} %get-tuple-element.206), channel_id=1, source_target_pairs={{0,1},{1,0},{2,3},{3,2},{4,5},{5,4},{6,7},{7,6},{8,9},{9,8},{10,11... | collective-permute-start | bytes 933896 | tf_op jit(solution)/shard_map/ppermute | solution.py:526
  50.7 1.7 %collective-permute-start.10 = (bf16[608,256]{1,0:T(8,128)(2,1)S(1)}, bf16[608,256]{1,0:T(8,128)(2,1)S(1)}, u32[]{:S(2)}, u32[]{:S(2)}) collective-permute-start(bf16[608,256]{1,0:T(8,128)(2,1)S(1)} %get-tuple-element.200), channel_id=1, source_target_pairs={{0,1},{1,0},{2,3},{3,2},{4,5},{5,4},{6,7},{7,6},{8,9},{9,8},{10,11... | collective-permute-start | bytes 933896 | tf_op jit(solution)/shard_map/ppermute | solution.py:526
  50.9 6.5 %collective-permute-start.18 = (bf16[304,256]{1,0:T(8,128)(2,1)S(1)}, bf16[304,256]{1,0:T(8,128)(2,1)S(1)}, u32[]{:S(2)}, u32[]{:S(2)}) collective-permute-start(bf16[304,256]{1,0:T(8,128)(2,1)S(1)} %get-tuple-element.208), channel_id=1, source_target_pairs={{0,2},{1,3},{2,0},{3,1},{4,6},{5,7},{6,4},{7,5},{8,10},{9,11},{10,... | collective-permute-start | bytes 466952 | tf_op jit(solution)/shard_map/ppermute | solution.py:526
  52.5 6.1 %collective-permute-start.11 = (bf16[304,256]{1,0:T(8,128)(2,1)S(1)}, bf16[304,256]{1,0:T(8,128)(2,1)S(1)}, u32[]{:S(2)}, u32[]{:S(2)}) collective-permute-start(bf16[304,256]{1,0:T(8,128)(2,1)S(1)} %get-tuple-element.202), channel_id=1, source_target_pairs={{0,4},{1,5},{2,6},{3,7},{4,0},{5,1},{6,2},{7,3},{8,12},{9,13},{10,... | collective-permute-start | bytes 466952 | tf_op jit(solution)/shard_map/ppermute | solution.py:526
  57.5 4.5 %collective-permute-start.19 = (bf16[152,256]{1,0:T(8,128)(2,1)S(1)}, bf16[152,256]{1,0:T(8,128)(2,1)S(1)}, u32[]{:S(2)}, u32[]{:S(2)}) collective-permute-start(bf16[152,256]{1,0:T(8,128)(2,1)S(1)} %get-tuple-element.210), channel_id=1, source_target_pairs={{0,4},{1,5},{2,6},{3,7},{4,0},{5,1},{6,2},{7,3},{8,12},{9,13},{10,... | collective-permute-start | bytes 233480 | tf_op jit(solution)/shard_map/ppermute | solution.py:526
  58.7 6.3 %collective-permute-start.12 = (bf16[152,256]{1,0:T(8,128)(2,1)S(1)}, bf16[152,256]{1,0:T(8,128)(2,1)S(1)}, u32[]{:S(2)}, u32[]{:S(2)}) collective-permute-start(bf16[152,256]{1,0:T(8,128)(2,1)S(1)} %get-tuple-element.204), channel_id=1, source_target_pairs={{0,2},{1,3},{2,0},{3,1},{4,6},{5,7},{6,4},{7,5},{8,10},{9,11},{10,... | collective-permute-start | bytes 233480 | tf_op jit(solution)/shard_map/ppermute | solution.py:526
  61.9 7.8 %collective-permute-start.20 = (bf16[152,256]{1,0:T(8,128)(2,1)S(1)}, bf16[152,256]{1,0:T(8,128)(2,1)S(1)}, u32[]{:S(2)}, u32[]{:S(2)}) collective-permute-start(bf16[152,256]{1,0:T(8,128)(2,1)S(1)} %fusion.1), channel_id=1, source_target_pairs={{0,8},{1,9},{2,10},{3,11},{4,12},{5,13},{6,14},{7,15},{8,0},{9,1},... | collective-permute-start | bytes 233480 | tf_op jit(solution)/shard_map/ppermute | solution.py:526
  65.0 6.6 %collective-permute-start.13 = (bf16[152,256]{1,0:T(8,128)(2,1)S(1)}, bf16[152,256]{1,0:T(8,128)(2,1)S(1)}, u32[]{:S(2)}, u32[]{:S(2)}) collective-permute-start(bf16[152,256]{1,0:T(8,128)(2,1)S(1)} %fusion), channel_id=1, source_target_pairs={{0,8},{1,9},{2,10},{3,11},{4,12},{5,13},{6,14},{7,15},{8,0},{9,1},... | collective-permute-start | bytes 233480 | tf_op jit(solution)/shard_map/ppermute | solution.py:526
  69.7 4.5 %collective-permute-start.21 = (bf16[152,256]{1,0:T(8,128)(2,1)S(1)}, bf16[152,256]{1,0:T(8,128)(2,1)S(1)}, u32[]{:S(2)}, u32[]{:S(2)}) collective-permute-start(bf16[152,256]{1,0:T(8,128)(2,1)S(1)} %add_convert_fusion.part), channel_id=1, source_target_pairs={{0,4},{1,5},{2,6},{3,7},{4,0},{5,1},{6,2},{7,3},{8,12},{9,13},{10,... | collective-permute-start | bytes 233480 | tf_op jit(solution)/shard_map/ppermute | solution.py:526
  71.6 5.2 %collective-permute-start.14 = (bf16[152,256]{1,0:T(8,128)(2,1)S(1)}, bf16[152,256]{1,0:T(8,128)(2,1)S(1)}, u32[]{:S(2)}, u32[]{:S(2)}) collective-permute-start(bf16[152,256]{1,0:T(8,128)(2,1)S(1)} %add_convert_fusion.1.part), channel_id=1, source_target_pairs={{0,2},{1,3},{2,0},{3,1},{4,6},{5,7},{6,4},{7,5},{8,10},{9,11},{10,... | collective-permute-start | bytes 233480 | tf_op jit(solution)/shard_map/ppermute | solution.py:526
  74.2 5.3 %collective-permute-start.22 = (bf16[304,256]{1,0:T(8,128)(2,1)S(1)}, bf16[304,256]{1,0:T(8,128)(2,1)S(1)}, u32[]{:S(2)}, u32[]{:S(2)}) collective-permute-start(bf16[304,256]{1,0:T(8,128)(2,1)S(1)} %join.6.part), channel_id=1, source_target_pairs={{0,2},{1,3},{2,0},{3,1},{4,6},{5,7},{6,4},{7,5},{8,10},{9,11},{10,... | collective-permute-start | bytes 466952 | tf_op jit(solution)/shard_map/ppermute | solution.py:526
  76.9 5.3 %collective-permute-start.15 = (bf16[304,256]{1,0:T(8,128)(2,1)S(1)}, bf16[304,256]{1,0:T(8,128)(2,1)S(1)}, u32[]{:S(2)}, u32[]{:S(2)}) collective-permute-start(bf16[304,256]{1,0:T(8,128)(2,1)S(1)} %join.4.part), channel_id=1, source_target_pairs={{0,4},{1,5},{2,6},{3,7},{4,0},{5,1},{6,2},{7,3},{8,12},{9,13},{10,... | collective-permute-start | bytes 466952 | tf_op jit(solution)/shard_map/ppermute | solution.py:526
  79.6 2.7 %collective-permute-start.23 = (bf16[608,256]{1,0:T(8,128)(2,1)S(1)}, bf16[608,256]{1,0:T(8,128)(2,1)S(1)}, u32[]{:S(2)}, u32[]{:S(2)}) collective-permute-start(bf16[608,256]{1,0:T(8,128)(2,1)S(1)} %join.7.mine), channel_id=1, source_target_pairs={{0,1},{1,0},{2,3},{3,2},{4,5},{5,4},{6,7},{7,6},{8,9},{9,8},{10,11... | collective-permute-start | bytes 933896 | tf_op jit(solution)/shard_map/ppermute | solution.py:526
  82.3 1.7 %collective-permute-start.16 = (bf16[608,256]{1,0:T(8,128)(2,1)S(1)}, bf16[608,256]{1,0:T(8,128)(2,1)S(1)}, u32[]{:S(2)}, u32[]{:S(2)}) collective-permute-start(bf16[608,256]{1,0:T(8,128)(2,1)S(1)} %join.5.mine), channel_id=1, source_target_pairs={{0,1},{1,0},{2,3},{3,2},{4,5},{5,4},{6,7},{7,6},{8,9},{9,8},{10,11... | collective-permute-start | bytes 933896 | tf_op jit(solution)/shard_map/ppermute | solution.py:526

commit v8 on v7

--- a/solution.py
+++ b/solution.py
@@ -70,8 +70,9 @@
         copy.start()
     reading_copy(0).start()
     copies[-2].start()
+    reading_copy(1).start()
     copies[-1].start()
-    for k in range(1, chunks):
+    for k in range(2, chunks):
         reading_copy(k).start()
 
     token_ref[...] = jnp.zeros_like(token_ref)
@@ -104,13 +105,14 @@
     mix_chunk(0)
     copies[-2].wait()
     wms[:, 0:maps] = w_state[...]
-    copies[-1].wait()
     for i in range(chunks):
         here = slice(i * chunk, (i + 1) * chunk)
         if i + 1 < chunks:
             mix_chunk(i + 1)
         mixed = mixed_ref[:, here, :].reshape(rows, width)
         small = dot(mixed, wms[...])
+        if i == 0:
+            copies[-1].wait()
         channels_ref[:, here, :] = dot(mixed, w_channels[...]).astype(bf16).reshape(sensors, chunk, channels)
         maps_ref[:, here, :] = small[:, 0:maps].astype(bf16).reshape(sensors, chunk, maps)
         steps = small[:, maps:].reshape(sensors, chunk, lanes)
@@ -322,23 +324,29 @@
         total[piece, channels : channels + nstate, :] = into
 
 
-def late_kernel(me_ref, normed, cot, read, mixed, before, *refs, part):
-    *gains, keep_ref, send_ref, total = refs
+def late_kernel(me_ref, normed, cot, read, mixed, before, *refs, part, kept):
+    *gains, out_ref = refs
     channels, nstate = normed.shape[2], read.shape[2]
     pieces = before.shape[0]
     own = channels // pieces
     bit = me_ref[0] & 1
+    blocks = list(late_blocks(me_ref[0], normed.shape[0]))
     gain = sum(jnp.sum(ref[...], axis=0, keepdims=True) for ref in gains)
+    at = channels + nstate
+
+    def write(half):
+        piece = half * (pieces // 2) + part
+        out, into = grad_piece(normed, cot, read, mixed, blocks, piece)
+        out_ref[0:channels, :] = (out + before[piece, 0:channels, :]).astype(out_ref.dtype)
+        out_ref[channels:at, :] = (into + before[piece, channels:at, :]).astype(out_ref.dtype)
+        row_of = iota((out_ref.shape[0] - at, PIECE), 0)
+        lane = iota((out_ref.shape[0] - at, PIECE), 1)
+        values = jnp.concatenate([gain[:, piece * own : (piece + 1) * own]] * (PIECE // own), axis=1)
+        rest = jnp.where((row_of == 0) & (lane < own), values, 0.0)
+        out_ref[at:, :] = rest.astype(out_ref.dtype)
+
     for half in range(2):
-        piece = half * (pieces // 2) + part
-        out, into = grad_piece(normed, cot, read, mixed, list(late_blocks(me_ref[0], normed.shape[0])), piece)
-        total[half, 0:channels, :] = out + before[piece, 0:channels, :]
-        total[half, channels : channels + nstate, :] = into + before[piece, channels : channels + nstate, :]
-        rest = total.shape[1] - channels - nstate
-        total[half, channels + nstate :, :] = jnp.zeros((rest, PIECE), f32)
-        total[half, channels + nstate : channels + nstate + 1, 0:own] = gain[:, piece * own : (piece + 1) * own]
-    keep_ref[...] = total[bit]
-    send_ref[...] = total[1 - bit].astype(bf16)
+        pl.when(bit == (half if kept else 1 - half))(functools.partial(write, half))
 
 
 def finish_kernel(me_ref, mine, came, *refs, part, aliases):
@@ -497,13 +505,12 @@
     )(me, *[held(x) for x in (normed, cot, read, mixed)], token)
 
 
-def late_grads(me, normed, cot, read, mixed, before, gains, part):
+def late_grads(me, normed, cot, read, mixed, before, gains, part, kept):
     rows = before.shape[1]
     return call(
-        functools.partial(late_kernel, part=part), "late", 1, (), [HELD] * (5 + len(gains)), [HELD] * 2,
-        [pltpu.VMEM((rows, PIECE), f32), pltpu.VMEM((rows, PIECE), bf16)],
-        [pltpu.VMEM((2, rows, PIECE), f32)], 10, 8e8, 5e6,
-    )(me, *[held(x) for x in (normed, cot, read, mixed, before, *gains)])
+        functools.partial(late_kernel, part=part, kept=kept), "late", 1, (), [HELD] * (5 + len(gains)), [HELD],
+        [pltpu.VMEM((rows, PIECE), f32 if kept else bf16)], [], 10, 4e8, 3e6,
+    )(me, *[held(x) for x in (normed, cot, read, mixed, before, *gains)])[0]
 
 
 def finish(me, mine, came, part, channels, width, nstate, done):
@@ -776,9 +783,8 @@
     )(me, held(part), held(came))[0]
 
 
-def all_sum(keep, send, me, count, order):
+def all_sum(part, came, me, count, order):
     levels = count.bit_length() - 1
-    part, came = keep, swap(send, 1, count)
     for level in order:
         part, gone = halve(me, part, came, level)
         came = swap(gone, 1 << level, count)
@@ -861,12 +867,9 @@
     run_back((4, 2, 6), states)
     run_back((5, 3, 7), core)
     results = ()
-    sums = []
-    for part, order in ((0, (1, 2)), (1, (2, 1))):
-        keep_part, send_part = late_grads(
-            at, work["back"][0], cot, work["back"][1], mixed, early, work["gains"], part
-        )
-        sums.append(all_sum(keep_part, send_part, at, count, order))
+    late = functools.partial(late_grads, at, work["back"][0], cot, work["back"][1], mixed, early, work["gains"])
+    came = [swap(late(part, False), 1, count) for part in (0, 1)]
+    sums = [all_sum(late(part, True), came[part], at, count, order) for part, order in ((0, (1, 2)), (1, (2, 1)))]
     for part in (0, 1):
         results = finish(at, *sums[part], part, channels, width, nstate, tuple(results))
     grad_out, grad_read, grad_gain = results

time: 85.4 us -> 85 us (level)
  waiting for transfers between devices: 24 us -> 22.5 us
    ppermute x24, waiting for transfers between devices: 24 us -> 22.5 us  [swap(): return lax.ppermute(x, 'seq', [(i, i ^ distance) for i in range(count)])]
    pallas_call x2 -> x4, Pallas kernels: 2.86 us -> 3.32 us  [late_grads(): call(functools.partial(late_kernel, part=part, kept=kept), 'late', 1, (),...]
  transfers between devices with their start and end apart: 24 -> 24, of which waited for: 14 -> 14; matrix products, arithmetic and copies ran while one was open for 0% -> 0% of each run, Pallas kernels for 23% -> 24%
where the time goes in v8:
time: 85 us; the launch traced here: 84.8 us
  Pallas kernels  34.8 us (41%)
  starting transfers between devices  26.2 us (31%)
  waiting for transfers between devices  22.5 us (26%)
  between operations  1.11 us (1%)
    ppermute x24, starting transfers between devices, swap(): return lax.ppermute(x, 'seq', [(i, i ^ distance) for i in range(count)])  26.2 us
    ppermute x24, waiting for transfers between devices, swap(): return lax.ppermute(x, 'seq', [(i, i ^ distance) for i in range(count)])  22.5 us
    pallas_call x2, Pallas kernels, within(): call(functools.partial(within_kernel, heads=heads, first=first, count=cou...  9.8 us
    pallas_call x1, Pallas kernels, front(): call(functools.partial(front_kernel, heads=heads, chunk=chunk, n_small=le...  8.52 us
    pallas_call x4, Pallas kernels, back(): call(functools.partial(back_kernel, heads=heads, blocks=blocks, aliases=l...  7.55 us
    pallas_call x4, Pallas kernels, late_grads(): call(functools.partial(late_kernel, part=part, kept=kept), 'late', 1, (),...  3.32 us
    pallas_call x2, Pallas kernels, finish(): call(functools.partial(finish_kernel, part=part, aliases=len(done)), 'fin...  2.18 us
  transfers between devices with their start and end apart: 24, of which 14 were waited for; matrix products, arithmetic and copies ran while one was open for 0% of the time, Pallas kernels for 24%

profile of v8, /device:TPU:0, one launch (start us, length us, event | category | flops | bytes accessed | tf_op | source)
XLA Modules:
  0.0 84.8 jit_solution(179160695989114801)
XLA Ops:
  0.6 8.5 %front.1 = (bf16[16,128,1024]{2,1,0:T(8,128)(2,1)S(1)}, bf16[16,128,512]{2,1,0:T(8,128)(2,1)S(1)}, bf16[16,128,128]{2,1,0:T(8,128)(2,1)S(1)}, f32[128,128]{1,0:T...) custom-call(s32[1]{0:T(128)} %bitcast.me_ref, ...), custom_call_target="tpu_custom_call" | custom-call | flops 5000000000 | bytes 14000000 | tf_op jit(solution)/shard_map/front/pallas_call | solution.py:422
  9.2 0.5 collective-permute-start
  9.7 0.9 %own.1 = f32[8,64,512]{2,1,0:T(8,128)S(1)} custom-call(s32[1]{0:T(128)} %bitcast.me_ref, bf16[16,128,512]{2,1,0:T(8,128)(2,1)S(1)} %get-tuple-element.107.channels, bf16[16,128,128]{2,1,0:T(8,128)(2,1)S(1)} %get-tuple-element.108.maps.refs_1_, f32[128,128]{1,0:T(8,128)S(1)} %get-tuple-element.109.weight), custom_call_target="tpu_custom_call" | custom-call | flops 300000000 | bytes 2000000 | tf_op jit(solution)/shard_map/own/pallas_call | solution.py:440
  10.5 0.7 collective-permute-done.came
  11.2 0.3 cores.1
  11.6 2.9 %collective-permute-start.1 = (bf16[144,512]{1,0:T(8,128)(2,1)S(1)}, bf16[144,512]{1,0:T(8,128)(2,1)S(1)}, u32[]{:S(2)}, u32[]{:S(2)}) collective-permute-start(bf16[144,512]{1,0:T(8,128)(2,1)S(1)} %get-tuple-element.121), channel_id=1, source_target_pairs={{0,2},{1,3},{2,0},{3,1},{4,6},{5,7},{6,4},{7,5},{8,10},{9,11},{10,... | collective-permute-start | bytes 442376 | tf_op jit(solution)/shard_map/ppermute | solution.py:533
  14.5 1.6 %collective-permute-start.2 = (bf16[144,512]{1,0:T(8,128)(2,1)S(1)}, bf16[144,512]{1,0:T(8,128)(2,1)S(1)}, u32[]{:S(2)}, u32[]{:S(2)}) collective-permute-start(bf16[144,512]{1,0:T(8,128)(2,1)S(1)} %get-tuple-element.122), channel_id=1, source_target_pairs={{0,4},{1,5},{2,6},{3,7},{4,0},{5,1},{6,2},{7,3},{8,12},{9,13},{10,... | collective-permute-start | bytes 442376 | tf_op jit(solution)/shard_map/ppermute | solution.py:533
  16.1 6.1 %within.2 = (f32[16,128,512]{2,1,0:T(8,128)S(1)}, bf16[16,128,512]{2,1,0:T(8,128)(2,1)S(1)}, bf16[16,8,128,128]{3,2,1,0:T(8,128)(2,1)S(1)}, f32[16,128,512]{2,1,...) custom-call(bf16[16,128,512]{2,1,0:T(8,128)(2,1)S(1)} %get-tuple-ele, ...), custom_call_target="tpu_custom_call", output_to_operand_aliasing={{7}: (8, {})} | custom-call | flops 3000000000 | bytes 15000000 | tf_op jit(solution)/shard_map/within/pallas_call | solution.py:453
  22.3 0.8 collective-permute-done.3.refs_2_
  23.1 0.3 group.1
  23.4 2.8 %collective-permute-start.4 = (bf16[128,512]{1,0:T(8,128)(2,1)S(1)}, bf16[128,512]{1,0:T(8,128)(2,1)S(1)}, u32[]{:S(2)}, u32[]{:S(2)}) collective-permute-start(bf16[128,512]{1,0:T(8,128)(2,1)S(1)} %get-tuple-element.135), channel_id=1, source_target_pairs={{0,8},{1,9},{2,10},{3,11},{4,12},{5,13},{6,14},{7,15},{8,0},{9,1},... | collective-permute-start | bytes 393224 | tf_op jit(solution)/shard_map/ppermute | solution.py:533
  26.3 3.7 %within.3 = (f32[16,128,512]{2,1,0:T(8,128)S(1)}, bf16[16,128,512]{2,1,0:T(8,128)(2,1)S(1)}, bf16[16,8,128,128]{3,2,1,0:T(8,128)(2,1)S(1)}, f32[16,128,512]{2,1,...) custom-call(bf16[16,128,512]{2,1,0:T(8,128)(2,1)S(1)} %get-tuple-ele, ...), custom_call_target="tpu_custom_call", output_to_operand_aliasing={{0}: (8, {}), {1}: (9, {}), {2}: (10, {}), {3}: (11, {}), {... | custom-call | flops 1800000000 | bytes 9000000 | tf_op jit(solution)/shard_map/within/pallas_call | solution.py:453
  29.9 2.1 %collective-permute-done.4.came = bf16[128,512]{1,0:T(8,128)(2,1)S(1)} collective-permute-done((bf16[128,512]{1,0:T(8,128)(2,1)S(1)}, bf16[128,512]{1,0:T(8,128)(2,1)S(1)}, u32[]{:S(2)}, u32[]{:S(2)}) %collective-permute-start.4) | collective-permute-done | bytes 131104 | tf_op jit(solution)/shard_map/ppermute | solution.py:533
  32.0 0.3 fall.1
  32.4 0.6 collective-permute-start.5
  33.0 1.4 %collective-permute-start.6 = (bf16[2,64,512]{2,1,0:T(8,128)(2,1)S(1)}, bf16[2,64,512]{2,1,0:T(8,128)(2,1)S(1)}, u32[]{:S(2)}, u32[]{:S(2)}) collective-permute-start(bf16[2,64,512]{2,1,0:T(8,128)(2,1)S(1)} %get-tuple-element.158), channel_id=1, source_target_pairs={{0,2},{1,3},{2,0},{3,1},{4,6},{5,7},{6,4},{7,5},{8,10},{9,11},{10,... | collective-permute-start | bytes 393224 | tf_op jit(solution)/shard_map/ppermute | solution.py:533
  34.4 1.6 %collective-permute-start.7 = (bf16[2,64,512]{2,1,0:T(8,128)(2,1)S(1)}, bf16[2,64,512]{2,1,0:T(8,128)(2,1)S(1)}, u32[]{:S(2)}, u32[]{:S(2)}) collective-permute-start(bf16[2,64,512]{2,1,0:T(8,128)(2,1)S(1)} %get-tuple-element.159), channel_id=1, source_target_pairs={{0,6},{1,7},{2,4},{3,5},{4,2},{5,3},{6,0},{7,1},{8,14},{9,15},{10,... | collective-permute-start | bytes 393224 | tf_op jit(solution)/shard_map/ppermute | solution.py:533
  36.0 1.2 %back.4 = (bf16[16,128,512]{2,1,0:T(8,128)(2,1)S(1)}, bf16[16,128,64]{2,1,0:T(8,128)(2,1)S(1)}, f32[8,512]{1,0:T(8,128)S(1)}, f32[8,128]{1,0:T(8,128)S(1)}) custom-call(s32[1]{0:T(128)} %bitcast.me_ref, bf16[2,64,512]{2,1,0:T(8,128)(2,1)S(1)} %get-tuple-element.166.refs_0_, ...), custom_call_target="tpu_custom_call", output_to_operand_aliasing={{3}: (9, {})} | custom-call | flops 600000000 | bytes 3000000 | tf_op jit(solution)/shard_map/back/pallas_call | solution.py:479
  37.1 1.2 %back.5 = (bf16[16,128,512]{2,1,0:T(8,128)(2,1)S(1)}, bf16[16,128,64]{2,1,0:T(8,128)(2,1)S(1)}, f32[8,512]{1,0:T(8,128)S(1)}, f32[8,128]{1,0:T(8,128)S(1)}) custom-call(s32[1]{0:T(128)} %bitcast.me_ref, bf16[2,64,512]{2,1,0:T(8,128)(2,1)S(1)} %collective-permute-done.8.refs_0_, ...), custom_call_target="tpu_custom_call", output_to_operand_aliasing={{0}: (9, {}), {1}: (10, {}), {3}: (11, {})} | custom-call | flops 600000000 | bytes 3000000 | tf_op jit(solution)/shard_map/back/pallas_call | solution.py:479
  38.3 0.9 %early.1 = (f32[4,608,256]{2,1,0:T(8,128)S(1)}, f32[8,128]{1,0:T(8,128)S(1)}) custom-call(s32[1]{0:T(128)} %bitcast.me_ref, bf16[16,128,512]{2,1,0:T(8,128)(2,1)S(1)} %get-tuple-element.171.normed.refs_8_, bf16[16,128,1024]{2,1,0:T(8,128)(2,1)S(1)} %get-tuple-element.172.cot, ...), custom_call_target="tpu_custom_call", output_to_operand_aliasing={{1}: (5, {})} | custom-call | flops 600000000 | bytes 4000000 | tf_op jit(solution)/shard_map/early/pallas_call | solution.py:501
  39.3 2.5 %collective-permute-done.7.refs_2_ = bf16[2,64,512]{2,1,0:T(8,128)(2,1)S(1)} collective-permute-done((bf16[2,64,512]{2,1,0:T(8,128)(2,1)S(1)}, bf16[2,64,512]{2,1,0:T(8,128)(2,1)S(1)}, u32[]{:S(2)}, u32[]{:S(2)}) %collective-permute-start.7) | collective-permute-done | bytes 131104 | tf_op jit(solution)/shard_map/ppermute | solution.py:533
  42.0 2.6 %back.6 = (bf16[16,128,512]{2,1,0:T(8,128)(2,1)S(1)}, bf16[16,128,64]{2,1,0:T(8,128)(2,1)S(1)}, f32[8,512]{1,0:T(8,128)S(1)}, f32[8,128]{1,0:T(8,128)S(1)}) custom-call(s32[1]{0:T(128)} %bitcast.me_ref, bf16[6,64,512]{2,1,0:T(8,128)(2,1)S(1)} %get-tuple-element.183.refs_0_, ...), custom_call_target="tpu_custom_call", output_to_operand_aliasing={{0}: (9, {}), {1}: (10, {}), {3}: (11, {})} | custom-call | flops 1800000000 | bytes 9000000 | tf_op jit(solution)/shard_map/back/pallas_call | solution.py:479
  44.7 2.6 %back.7 = (bf16[16,128,512]{2,1,0:T(8,128)(2,1)S(1)}, bf16[16,128,64]{2,1,0:T(8,128)(2,1)S(1)}, f32[8,512]{1,0:T(8,128)S(1)}, f32[8,128]{1,0:T(8,128)S(1)}) custom-call(s32[1]{0:T(128)} %bitcast.me_ref, bf16[6,64,512]{2,1,0:T(8,128)(2,1)S(1)} %collective-permute-done.9.refs_0_, ...), custom_call_target="tpu_custom_call", output_to_operand_aliasing={{0}: (9, {}), {1}: (10, {}), {3}: (11, {})} | custom-call | flops 1800000000 | bytes 9000000 | tf_op jit(solution)/shard_map/back/pallas_call | solution.py:479
  47.3 1.0 %late.7 = bf16[608,256]{1,0:T(8,128)(2,1)S(1)} custom-call(s32[1]{0:T(128)} %bitcast.me_ref, bf16[16,128,512]{2,1,0:T(8,128)(2,1)S(1)} %get-tuple-element.188.normed, bf16[16,128,1024]{2,1,0:T(8,128)(2,1)S(1)} %get-tuple-element.172.cot, bf16[16,128,64]{2,1,0:T(8,128)(2,1)S(1)} %get-tuple-element.189.read, ...), custom_call_target="tpu_custom_call" | custom-call | flops 400000000 | bytes 3000000 | tf_op jit(solution)/shard_map/late/pallas_call | solution.py:510
  48.3 0.6 collective-permute-start.17
  48.8 0.8 late.5
  49.7 0.8 late.6.part
  50.6 1.0 %collective-permute-start.18 = (bf16[304,256]{1,0:T(8,128)(2,1)S(1)}, bf16[304,256]{1,0:T(8,128)(2,1)S(1)}, u32[]{:S(2)}, u32[]{:S(2)}) collective-permute-start(bf16[304,256]{1,0:T(8,128)(2,1)S(1)} %get-tuple-element.200), channel_id=1, source_target_pairs={{0,2},{1,3},{2,0},{3,1},{4,6},{5,7},{6,4},{7,5},{8,10},{9,11},{10,... | collective-permute-start | bytes 466952 | tf_op jit(solution)/shard_map/ppermute | solution.py:533
  51.7 0.8 late.4.part
  52.6 1.4 %collective-permute-start.11 = (bf16[304,256]{1,0:T(8,128)(2,1)S(1)}, bf16[304,256]{1,0:T(8,128)(2,1)S(1)}, u32[]{:S(2)}, u32[]{:S(2)}) collective-permute-start(bf16[304,256]{1,0:T(8,128)(2,1)S(1)} %get-tuple-element.196), channel_id=1, source_target_pairs={{0,4},{1,5},{2,6},{3,7},{4,0},{5,1},{6,2},{7,3},{8,12},{9,13},{10,... | collective-permute-start | bytes 466952 | tf_op jit(solution)/shard_map/ppermute | solution.py:533
  54.0 3.1 %collective-permute-done.18.came = bf16[304,256]{1,0:T(8,128)(2,1)S(1)} collective-permute-done((bf16[304,256]{1,0:T(8,128)(2,1)S(1)}, bf16[304,256]{1,0:T(8,128)(2,1)S(1)}, u32[]{:S(2)}, u32[]{:S(2)}) %collective-permute-start.18) | collective-permute-done | bytes 155680 | tf_op jit(solution)/shard_map/ppermute | solution.py:533
  57.1 1.2 %collective-permute-start.19 = (bf16[152,256]{1,0:T(8,128)(2,1)S(1)}, bf16[152,256]{1,0:T(8,128)(2,1)S(1)}, u32[]{:S(2)}, u32[]{:S(2)}) collective-permute-start(bf16[152,256]{1,0:T(8,128)(2,1)S(1)} %get-tuple-element.202), channel_id=1, source_target_pairs={{0,4},{1,5},{2,6},{3,7},{4,0},{5,1},{6,2},{7,3},{8,12},{9,13},{10,... | collective-permute-start | bytes 233480 | tf_op jit(solution)/shard_map/ppermute | solution.py:533
  58.3 0.4 collective-permute-done.11.came
  58.8 1.1 %collective-permute-start.12 = (bf16[152,256]{1,0:T(8,128)(2,1)S(1)}, bf16[152,256]{1,0:T(8,128)(2,1)S(1)}, u32[]{:S(2)}, u32[]{:S(2)}) collective-permute-start(bf16[152,256]{1,0:T(8,128)(2,1)S(1)} %get-tuple-element.198), channel_id=1, source_target_pairs={{0,2},{1,3},{2,0},{3,1},{4,6},{5,7},{6,4},{7,5},{8,10},{9,11},{10,... | collective-permute-start | bytes 233480 | tf_op jit(solution)/shard_map/ppermute | solution.py:533
  59.9 1.7 %collective-permute-done.19 = bf16[152,256]{1,0:T(8,128)(2,1)S(1)} collective-permute-done((bf16[152,256]{1,0:T(8,128)(2,1)S(1)}, bf16[152,256]{1,0:T(8,128)(2,1)S(1)}, u32[]{:S(2)}, u32[]{:S(2)}) %collective-permute-start.19) | collective-permute-done | bytes 77856 | tf_op jit(solution)/shard_map/ppermute | solution.py:533
  61.6 3.0 %collective-permute-start.20 = (bf16[152,256]{1,0:T(8,128)(2,1)S(1)}, bf16[152,256]{1,0:T(8,128)(2,1)S(1)}, u32[]{:S(2)}, u32[]{:S(2)}) collective-permute-start(bf16[152,256]{1,0:T(8,128)(2,1)S(1)} %fusion.1), channel_id=1, source_target_pairs={{0,8},{1,9},{2,10},{3,11},{4,12},{5,13},{6,14},{7,15},{8,0},{9,1},... | collective-permute-start | bytes 233480 | tf_op jit(solution)/shard_map/ppermute | solution.py:533
  64.7 2.1 %collective-permute-start.13 = (bf16[152,256]{1,0:T(8,128)(2,1)S(1)}, bf16[152,256]{1,0:T(8,128)(2,1)S(1)}, u32[]{:S(2)}, u32[]{:S(2)}) collective-permute-start(bf16[152,256]{1,0:T(8,128)(2,1)S(1)} %fusion), channel_id=1, source_target_pairs={{0,8},{1,9},{2,10},{3,11},{4,12},{5,13},{6,14},{7,15},{8,0},{9,1},... | collective-permute-start | bytes 233480 | tf_op jit(solution)/shard_map/ppermute | solution.py:533
  66.7 2.6 %collective-permute-done.20 = bf16[152,256]{1,0:T(8,128)(2,1)S(1)} collective-permute-done((bf16[152,256]{1,0:T(8,128)(2,1)S(1)}, bf16[152,256]{1,0:T(8,128)(2,1)S(1)}, u32[]{:S(2)}, u32[]{:S(2)}) %collective-permute-start.20) | collective-permute-done | bytes 77856 | tf_op jit(solution)/shard_map/ppermute | solution.py:533
  69.6 1.5 %collective-permute-done.13 = bf16[152,256]{1,0:T(8,128)(2,1)S(1)} collective-permute-done((bf16[152,256]{1,0:T(8,128)(2,1)S(1)}, bf16[152,256]{1,0:T(8,128)(2,1)S(1)}, u32[]{:S(2)}, u32[]{:S(2)}) %collective-permute-start.13) | collective-permute-done | bytes 77856 | tf_op jit(solution)/shard_map/ppermute | solution.py:533
  71.1 1.6 %collective-permute-start.14 = (bf16[152,256]{1,0:T(8,128)(2,1)S(1)}, bf16[152,256]{1,0:T(8,128)(2,1)S(1)}, u32[]{:S(2)}, u32[]{:S(2)}) collective-permute-start(bf16[152,256]{1,0:T(8,128)(2,1)S(1)} %add_convert_fusion.1.part), channel_id=1, source_target_pairs={{0,2},{1,3},{2,0},{3,1},{4,6},{5,7},{6,4},{7,5},{8,10},{9,11},{10,... | collective-permute-start | bytes 233480 | tf_op jit(solution)/shard_map/ppermute | solution.py:533
  72.7 1.2 %collective-permute-done.21.came = bf16[152,256]{1,0:T(8,128)(2,1)S(1)} collective-permute-done((bf16[152,256]{1,0:T(8,128)(2,1)S(1)}, bf16[152,256]{1,0:T(8,128)(2,1)S(1)}, u32[]{:S(2)}, u32[]{:S(2)}) %collective-permute-start.21) | collective-permute-done | bytes 77856 | tf_op jit(solution)/shard_map/ppermute | solution.py:533
  73.9 2.3 %collective-permute-start.22 = (bf16[304,256]{1,0:T(8,128)(2,1)S(1)}, bf16[304,256]{1,0:T(8,128)(2,1)S(1)}, u32[]{:S(2)}, u32[]{:S(2)}) collective-permute-start(bf16[304,256]{1,0:T(8,128)(2,1)S(1)} %join.6.part), channel_id=1, source_target_pairs={{0,2},{1,3},{2,0},{3,1},{4,6},{5,7},{6,4},{7,5},{8,10},{9,11},{10,... | collective-permute-start | bytes 466952 | tf_op jit(solution)/shard_map/ppermute | solution.py:533
  76.2 0.3 collective-permute-done.14.came
  76.5 2.8 %collective-permute-done.22.came = bf16[304,256]{1,0:T(8,128)(2,1)S(1)} collective-permute-done((bf16[304,256]{1,0:T(8,128)(2,1)S(1)}, bf16[304,256]{1,0:T(8,128)(2,1)S(1)}, u32[]{:S(2)}, u32[]{:S(2)}) %collective-permute-start.22) | collective-permute-done | bytes 155680 | tf_op jit(solution)/shard_map/ppermute | solution.py:533
  79.5 2.2 %collective-permute-done.15.came = bf16[304,256]{1,0:T(8,128)(2,1)S(1)} collective-permute-done((bf16[304,256]{1,0:T(8,128)(2,1)S(1)}, bf16[304,256]{1,0:T(8,128)(2,1)S(1)}, u32[]{:S(2)}, u32[]{:S(2)}) %collective-permute-start.15) | collective-permute-done | bytes 155680 | tf_op jit(solution)/shard_map/ppermute | solution.py:533
  81.9 1.1 %finish.2 = (f32[512,1024]{1,0:T(8,128)}, f32[64,1024]{1,0:T(8,128)}, f32[1,512]{1,0:T(1,128)}) custom-call(s32[1]{0:T(128)} %bitcast.me_ref, bf16[608,256]{1,0:T(8,128)(2,1)S(1)} %join.7.mine, bf16[608,256]{1,0:T(8,128)(2,1)S(1)} %collective-permute-done.23.came), custom_call_target="tpu_custom_call" | custom-call | flops 1000000 | bytes 2000000 | tf_op jit(solution)/shard_map/finish/pallas_call | solution.py:518
  83.0 0.5 collective-permute-done.16.came
  83.5 1.1 %finish.3 = (f32[512,1024]{1,0:T(8,128)}, f32[64,1024]{1,0:T(8,128)}, f32[1,512]{1,0:T(1,128)}) custom-call(s32[1]{0:T(128)} %bitcast.me_ref, bf16[608,256]{1,0:T(8,128)(2,1)S(1)} %join.5.mine, bf16[608,256]{1,0:T(8,128)(2,1)S(1)} %collective-permute-done.16.came, ...), custom_call_target="tpu_custom_call", output_to_operand_aliasing={{0}: (3, {}), {1}: (4, {}), {2}: (5, {})} | custom-call | flops 1000000 | bytes 2000000 | tf_op jit(solution)/shard_map/finish/pallas_call | solution.py:518
  (31 shorter events, 1.5 us)
Async XLA Ops:
  9.2 2.1 %collective-permute-start = (bf16[528,512]{1,0:T(8,128)(2,1)S(1)}, bf16[528,512]{1,0:T(8,128)(2,1)S(1)}, u32[]{:S(2)}, u32[]{:S(2)}) collective-permute-start(bf16[528,512]{1,0:T(8,128)(2,1)S(1)} %get-tuple-element.106), channel_id=1, source_target_pairs={{0,1},{1,0},{2,3},{3,2},{4,5},{5,4},{6,7},{7,6},{8,9},{9,8},{10,11... | collective-permute-start | bytes 1622024 | tf_op jit(solution)/shard_map/ppermute | solution.py:533
  11.6 10.7 %collective-permute-start.1 = (bf16[144,512]{1,0:T(8,128)(2,1)S(1)}, bf16[144,512]{1,0:T(8,128)(2,1)S(1)}, u32[]{:S(2)}, u32[]{:S(2)}) collective-permute-start(bf16[144,512]{1,0:T(8,128)(2,1)S(1)} %get-tuple-element.121), channel_id=1, source_target_pairs={{0,2},{1,3},{2,0},{3,1},{4,6},{5,7},{6,4},{7,5},{8,10},{9,11},{10,... | collective-permute-start | bytes 442376 | tf_op jit(solution)/shard_map/ppermute | solution.py:533
  14.5 7.7 %collective-permute-start.2 = (bf16[144,512]{1,0:T(8,128)(2,1)S(1)}, bf16[144,512]{1,0:T(8,128)(2,1)S(1)}, u32[]{:S(2)}, u32[]{:S(2)}) collective-permute-start(bf16[144,512]{1,0:T(8,128)(2,1)S(1)} %get-tuple-element.122), channel_id=1, source_target_pairs={{0,4},{1,5},{2,6},{3,7},{4,0},{5,1},{6,2},{7,3},{8,12},{9,13},{10,... | collective-permute-start | bytes 442376 | tf_op jit(solution)/shard_map/ppermute | solution.py:533
  16.1 7.0 %collective-permute-start.3 = (bf16[144,512]{1,0:T(8,128)(2,1)S(1)}, bf16[144,512]{1,0:T(8,128)(2,1)S(1)}, u32[]{:S(2)}, u32[]{:S(2)}) collective-permute-start(bf16[144,512]{1,0:T(8,128)(2,1)S(1)} %get-tuple-element.123), channel_id=1, source_target_pairs={{0,6},{1,7},{2,4},{3,5},{4,2},{5,3},{6,0},{7,1},{8,14},{9,15},{10,... | collective-permute-start | bytes 442376 | tf_op jit(solution)/shard_map/ppermute | solution.py:533
  23.4 8.6 %collective-permute-start.4 = (bf16[128,512]{1,0:T(8,128)(2,1)S(1)}, bf16[128,512]{1,0:T(8,128)(2,1)S(1)}, u32[]{:S(2)}, u32[]{:S(2)}) collective-permute-start(bf16[128,512]{1,0:T(8,128)(2,1)S(1)} %get-tuple-element.135), channel_id=1, source_target_pairs={{0,8},{1,9},{2,10},{3,11},{4,12},{5,13},{6,14},{7,15},{8,0},{9,1},... | collective-permute-start | bytes 393224 | tf_op jit(solution)/shard_map/ppermute | solution.py:533
  32.3 4.8 %collective-permute-start.8 = (bf16[2,64,512]{2,1,0:T(8,128)(2,1)S(1)}, bf16[2,64,512]{2,1,0:T(8,128)(2,1)S(1)}, u32[]{:S(2)}, u32[]{:S(2)}) collective-permute-start(bf16[2,64,512]{2,1,0:T(8,128)(2,1)S(1)} %get-tuple-element.160), channel_id=1, source_target_pairs={{0,1},{1,0},{2,3},{3,2},{4,5},{5,4},{6,7},{7,6},{8,9},{9,8},{10,11... | collective-permute-start | bytes 393224 | tf_op jit(solution)/shard_map/ppermute | solution.py:533
  32.4 6.8 %collective-permute-start.5 = (bf16[2,64,512]{2,1,0:T(8,128)(2,1)S(1)}, bf16[2,64,512]{2,1,0:T(8,128)(2,1)S(1)}, u32[]{:S(2)}, u32[]{:S(2)}) collective-permute-start(bf16[2,64,512]{2,1,0:T(8,128)(2,1)S(1)} %get-tuple-element.157), channel_id=1, source_target_pairs={{0,4},{1,5},{2,6},{3,7},{4,0},{5,1},{6,2},{7,3},{8,12},{9,13},{10,... | collective-permute-start | bytes 393224 | tf_op jit(solution)/shard_map/ppermute | solution.py:533
  33.0 6.3 %collective-permute-start.6 = (bf16[2,64,512]{2,1,0:T(8,128)(2,1)S(1)}, bf16[2,64,512]{2,1,0:T(8,128)(2,1)S(1)}, u32[]{:S(2)}, u32[]{:S(2)}) collective-permute-start(bf16[2,64,512]{2,1,0:T(8,128)(2,1)S(1)} %get-tuple-element.158), channel_id=1, source_target_pairs={{0,2},{1,3},{2,0},{3,1},{4,6},{5,7},{6,4},{7,5},{8,10},{9,11},{10,... | collective-permute-start | bytes 393224 | tf_op jit(solution)/shard_map/ppermute | solution.py:533
  34.4 7.4 %collective-permute-start.7 = (bf16[2,64,512]{2,1,0:T(8,128)(2,1)S(1)}, bf16[2,64,512]{2,1,0:T(8,128)(2,1)S(1)}, u32[]{:S(2)}, u32[]{:S(2)}) collective-permute-start(bf16[2,64,512]{2,1,0:T(8,128)(2,1)S(1)} %get-tuple-element.159), channel_id=1, source_target_pairs={{0,6},{1,7},{2,4},{3,5},{4,2},{5,3},{6,0},{7,1},{8,14},{9,15},{10,... | collective-permute-start | bytes 393224 | tf_op jit(solution)/shard_map/ppermute | solution.py:533
  42.0 2.7 %collective-permute-start.9 = (bf16[6,64,512]{2,1,0:T(8,128)(2,1)S(1)}, bf16[6,64,512]{2,1,0:T(8,128)(2,1)S(1)}, u32[]{:S(2)}, u32[]{:S(2)}) collective-permute-start(bf16[6,64,512]{2,1,0:T(8,128)(2,1)S(1)} %get-tuple-element.182), channel_id=1, source_target_pairs={{0,1},{1,0},{2,3},{3,2},{4,5},{5,4},{6,7},{7,6},{8,9},{9,8},{10,11... | collective-permute-start | bytes 1179656 | tf_op jit(solution)/shard_map/ppermute | solution.py:533
  48.3 2.2 %collective-permute-start.17 = (bf16[608,256]{1,0:T(8,128)(2,1)S(1)}, bf16[608,256]{1,0:T(8,128)(2,1)S(1)}, u32[]{:S(2)}, u32[]{:S(2)}) collective-permute-start(bf16[608,256]{1,0:T(8,128)(2,1)S(1)} %late.7), channel_id=1, source_target_pairs={{0,1},{1,0},{2,3},{3,2},{4,5},{5,4},{6,7},{7,6},{8,9},{9,8},{10,11... | collective-permute-start | bytes 933896 | tf_op jit(solution)/shard_map/ppermute | solution.py:533
  49.6 2.8 %collective-permute-start.10 = (bf16[608,256]{1,0:T(8,128)(2,1)S(1)}, bf16[608,256]{1,0:T(8,128)(2,1)S(1)}, u32[]{:S(2)}, u32[]{:S(2)}) collective-permute-start(bf16[608,256]{1,0:T(8,128)(2,1)S(1)} %late.5), channel_id=1, source_target_pairs={{0,1},{1,0},{2,3},{3,2},{4,5},{5,4},{6,7},{7,6},{8,9},{9,8},{10,11... | collective-permute-start | bytes 933896 | tf_op jit(solution)/shard_map/ppermute | solution.py:533
  50.6 6.5 %collective-permute-start.18 = (bf16[304,256]{1,0:T(8,128)(2,1)S(1)}, bf16[304,256]{1,0:T(8,128)(2,1)S(1)}, u32[]{:S(2)}, u32[]{:S(2)}) collective-permute-start(bf16[304,256]{1,0:T(8,128)(2,1)S(1)} %get-tuple-element.200), channel_id=1, source_target_pairs={{0,2},{1,3},{2,0},{3,1},{4,6},{5,7},{6,4},{7,5},{8,10},{9,11},{10,... | collective-permute-start | bytes 466952 | tf_op jit(solution)/shard_map/ppermute | solution.py:533
  52.6 6.2 %collective-permute-start.11 = (bf16[304,256]{1,0:T(8,128)(2,1)S(1)}, bf16[304,256]{1,0:T(8,128)(2,1)S(1)}, u32[]{:S(2)}, u32[]{:S(2)}) collective-permute-start(bf16[304,256]{1,0:T(8,128)(2,1)S(1)} %get-tuple-element.196), channel_id=1, source_target_pairs={{0,4},{1,5},{2,6},{3,7},{4,0},{5,1},{6,2},{7,3},{8,12},{9,13},{10,... | collective-permute-start | bytes 466952 | tf_op jit(solution)/shard_map/ppermute | solution.py:533
  57.1 4.5 %collective-permute-start.19 = (bf16[152,256]{1,0:T(8,128)(2,1)S(1)}, bf16[152,256]{1,0:T(8,128)(2,1)S(1)}, u32[]{:S(2)}, u32[]{:S(2)}) collective-permute-start(bf16[152,256]{1,0:T(8,128)(2,1)S(1)} %get-tuple-element.202), channel_id=1, source_target_pairs={{0,4},{1,5},{2,6},{3,7},{4,0},{5,1},{6,2},{7,3},{8,12},{9,13},{10,... | collective-permute-start | bytes 233480 | tf_op jit(solution)/shard_map/ppermute | solution.py:533
  58.8 5.9 %collective-permute-start.12 = (bf16[152,256]{1,0:T(8,128)(2,1)S(1)}, bf16[152,256]{1,0:T(8,128)(2,1)S(1)}, u32[]{:S(2)}, u32[]{:S(2)}) collective-permute-start(bf16[152,256]{1,0:T(8,128)(2,1)S(1)} %get-tuple-element.198), channel_id=1, source_target_pairs={{0,2},{1,3},{2,0},{3,1},{4,6},{5,7},{6,4},{7,5},{8,10},{9,11},{10,... | collective-permute-start | bytes 233480 | tf_op jit(solution)/shard_map/ppermute | solution.py:533
  61.6 7.7 %collective-permute-start.20 = (bf16[152,256]{1,0:T(8,128)(2,1)S(1)}, bf16[152,256]{1,0:T(8,128)(2,1)S(1)}, u32[]{:S(2)}, u32[]{:S(2)}) collective-permute-start(bf16[152,256]{1,0:T(8,128)(2,1)S(1)} %fusion.1), channel_id=1, source_target_pairs={{0,8},{1,9},{2,10},{3,11},{4,12},{5,13},{6,14},{7,15},{8,0},{9,1},... | collective-permute-start | bytes 233480 | tf_op jit(solution)/shard_map/ppermute | solution.py:533
  64.7 6.4 %collective-permute-start.13 = (bf16[152,256]{1,0:T(8,128)(2,1)S(1)}, bf16[152,256]{1,0:T(8,128)(2,1)S(1)}, u32[]{:S(2)}, u32[]{:S(2)}) collective-permute-start(bf16[152,256]{1,0:T(8,128)(2,1)S(1)} %fusion), channel_id=1, source_target_pairs={{0,8},{1,9},{2,10},{3,11},{4,12},{5,13},{6,14},{7,15},{8,0},{9,1},... | collective-permute-start | bytes 233480 | tf_op jit(solution)/shard_map/ppermute | solution.py:533
  69.4 4.5 %collective-permute-start.21 = (bf16[152,256]{1,0:T(8,128)(2,1)S(1)}, bf16[152,256]{1,0:T(8,128)(2,1)S(1)}, u32[]{:S(2)}, u32[]{:S(2)}) collective-permute-start(bf16[152,256]{1,0:T(8,128)(2,1)S(1)} %add_convert_fusion.part), channel_id=1, source_target_pairs={{0,4},{1,5},{2,6},{3,7},{4,0},{5,1},{6,2},{7,3},{8,12},{9,13},{10,... | collective-permute-start | bytes 233480 | tf_op jit(solution)/shard_map/ppermute | solution.py:533
  71.1 5.3 %collective-permute-start.14 = (bf16[152,256]{1,0:T(8,128)(2,1)S(1)}, bf16[152,256]{1,0:T(8,128)(2,1)S(1)}, u32[]{:S(2)}, u32[]{:S(2)}) collective-permute-start(bf16[152,256]{1,0:T(8,128)(2,1)S(1)} %add_convert_fusion.1.part), channel_id=1, source_target_pairs={{0,2},{1,3},{2,0},{3,1},{4,6},{5,7},{6,4},{7,5},{8,10},{9,11},{10,... | collective-permute-start | bytes 233480 | tf_op jit(solution)/shard_map/ppermute | solution.py:533
  73.9 5.5 %collective-permute-start.22 = (bf16[304,256]{1,0:T(8,128)(2,1)S(1)}, bf16[304,256]{1,0:T(8,128)(2,1)S(1)}, u32[]{:S(2)}, u32[]{:S(2)}) collective-permute-start(bf16[304,256]{1,0:T(8,128)(2,1)S(1)} %join.6.part), channel_id=1, source_target_pairs={{0,2},{1,3},{2,0},{3,1},{4,6},{5,7},{6,4},{7,5},{8,10},{9,11},{10,... | collective-permute-start | bytes 466952 | tf_op jit(solution)/shard_map/ppermute | solution.py:533
  76.4 5.3 %collective-permute-start.15 = (bf16[304,256]{1,0:T(8,128)(2,1)S(1)}, bf16[304,256]{1,0:T(8,128)(2,1)S(1)}, u32[]{:S(2)}, u32[]{:S(2)}) collective-permute-start(bf16[304,256]{1,0:T(8,128)(2,1)S(1)} %join.4.part), channel_id=1, source_target_pairs={{0,4},{1,5},{2,6},{3,7},{4,0},{5,1},{6,2},{7,3},{8,12},{9,13},{10,... | collective-permute-start | bytes 466952 | tf_op jit(solution)/shard_map/ppermute | solution.py:533
  79.4 2.5 %collective-permute-start.23 = (bf16[608,256]{1,0:T(8,128)(2,1)S(1)}, bf16[608,256]{1,0:T(8,128)(2,1)S(1)}, u32[]{:S(2)}, u32[]{:S(2)}) collective-permute-start(bf16[608,256]{1,0:T(8,128)(2,1)S(1)} %join.7.mine), channel_id=1, source_target_pairs={{0,1},{1,0},{2,3},{3,2},{4,5},{5,4},{6,7},{7,6},{8,9},{9,8},{10,11... | collective-permute-start | bytes 933896 | tf_op jit(solution)/shard_map/ppermute | solution.py:533
  81.8 1.7 %collective-permute-start.16 = (bf16[608,256]{1,0:T(8,128)(2,1)S(1)}, bf16[608,256]{1,0:T(8,128)(2,1)S(1)}, u32[]{:S(2)}, u32[]{:S(2)}) collective-permute-start(bf16[608,256]{1,0:T(8,128)(2,1)S(1)} %join.5.mine), channel_id=1, source_target_pairs={{0,1},{1,0},{2,3},{3,2},{4,5},{5,4},{6,7},{7,6},{8,9},{9,8},{10,11... | collective-permute-start | bytes 933896 | tf_op jit(solution)/shard_map/ppermute | solution.py:533

commit v9 on v8

--- a/solution.py
+++ b/solution.py
@@ -280,9 +280,10 @@
     gain_sum = jnp.zeros(gain_ref.shape, f32)
     for slot in range(len(todo)):
         carry_in(slot)
+    gain_sum = normalize(0, gain_sum)
     for slot in range(len(todo)):
-        gain_sum = normalize(slot, gain_sum)
-    for slot in range(len(todo)):
+        if slot + 1 < len(todo):
+            gain_sum = normalize(slot + 1, gain_sum)
         read_out(slot)
     gain_ref[...] = gain_sum
 

time: 85 us -> 85 us (level)
  no operation moved by 1% of the time
where the time goes in v9:
time: 85 us; the launch traced here: 84.8 us
  Pallas kernels  34.8 us (41%)
  starting transfers between devices  26.2 us (31%)
  waiting for transfers between devices  22.5 us (26%)
  between operations  1.11 us (1%)
    ppermute x24, starting transfers between devices, swap(): return lax.ppermute(x, 'seq', [(i, i ^ distance) for i in range(count)])  26.2 us
    ppermute x24, waiting for transfers between devices, swap(): return lax.ppermute(x, 'seq', [(i, i ^ distance) for i in range(count)])  22.5 us
    pallas_call x2, Pallas kernels, within(): call(functools.partial(within_kernel, heads=heads, first=first, count=cou...  9.8 us
    pallas_call x1, Pallas kernels, front(): call(functools.partial(front_kernel, heads=heads, chunk=chunk, n_small=le...  8.52 us
    pallas_call x4, Pallas kernels, back(): call(functools.partial(back_kernel, heads=heads, blocks=blocks, aliases=l...  7.55 us
    pallas_call x4, Pallas kernels, late_grads(): call(functools.partial(late_kernel, part=part, kept=kept), 'late', 1, (),...  3.32 us
    pallas_call x2, Pallas kernels, finish(): call(functools.partial(finish_kernel, part=part, aliases=len(done)), 'fin...  2.18 us
  transfers between devices with their start and end apart: 24, of which 14 were waited for; matrix products, arithmetic and copies ran while one was open for 0% of the time, Pallas kernels for 24%

profile of v9, /device:TPU:0, one launch (start us, length us, event | category | flops | bytes accessed | tf_op | source)
XLA Modules:
  0.0 84.8 jit_solution(179160695989114801)
XLA Ops:
  0.6 8.5 %front.1 = (bf16[16,128,1024]{2,1,0:T(8,128)(2,1)S(1)}, bf16[16,128,512]{2,1,0:T(8,128)(2,1)S(1)}, bf16[16,128,128]{2,1,0:T(8,128)(2,1)S(1)}, f32[128,128]{1,0:T...) custom-call(s32[1]{0:T(128)} %bitcast.me_ref, ...), custom_call_target="tpu_custom_call" | custom-call | flops 5000000000 | bytes 14000000 | tf_op jit(solution)/shard_map/front/pallas_call | solution.py:423
  9.2 0.5 collective-permute-start
  9.7 0.9 %own.1 = f32[8,64,512]{2,1,0:T(8,128)S(1)} custom-call(s32[1]{0:T(128)} %bitcast.me_ref, bf16[16,128,512]{2,1,0:T(8,128)(2,1)S(1)} %get-tuple-element.107.channels, bf16[16,128,128]{2,1,0:T(8,128)(2,1)S(1)} %get-tuple-element.108.maps.refs_1_, f32[128,128]{1,0:T(8,128)S(1)} %get-tuple-element.109.weight), custom_call_target="tpu_custom_call" | custom-call | flops 300000000 | bytes 2000000 | tf_op jit(solution)/shard_map/own/pallas_call | solution.py:441
  10.5 0.7 collective-permute-done.came
  11.2 0.3 cores.1
  11.6 2.9 %collective-permute-start.1 = (bf16[144,512]{1,0:T(8,128)(2,1)S(1)}, bf16[144,512]{1,0:T(8,128)(2,1)S(1)}, u32[]{:S(2)}, u32[]{:S(2)}) collective-permute-start(bf16[144,512]{1,0:T(8,128)(2,1)S(1)} %get-tuple-element.121), channel_id=1, source_target_pairs={{0,2},{1,3},{2,0},{3,1},{4,6},{5,7},{6,4},{7,5},{8,10},{9,11},{10,... | collective-permute-start | bytes 442376 | tf_op jit(solution)/shard_map/ppermute | solution.py:534
  14.5 1.6 %collective-permute-start.2 = (bf16[144,512]{1,0:T(8,128)(2,1)S(1)}, bf16[144,512]{1,0:T(8,128)(2,1)S(1)}, u32[]{:S(2)}, u32[]{:S(2)}) collective-permute-start(bf16[144,512]{1,0:T(8,128)(2,1)S(1)} %get-tuple-element.122), channel_id=1, source_target_pairs={{0,4},{1,5},{2,6},{3,7},{4,0},{5,1},{6,2},{7,3},{8,12},{9,13},{10,... | collective-permute-start | bytes 442376 | tf_op jit(solution)/shard_map/ppermute | solution.py:534
  16.1 6.1 %within.2 = (f32[16,128,512]{2,1,0:T(8,128)S(1)}, bf16[16,128,512]{2,1,0:T(8,128)(2,1)S(1)}, bf16[16,8,128,128]{3,2,1,0:T(8,128)(2,1)S(1)}, f32[16,128,512]{2,1,...) custom-call(bf16[16,128,512]{2,1,0:T(8,128)(2,1)S(1)} %get-tuple-ele, ...), custom_call_target="tpu_custom_call", output_to_operand_aliasing={{7}: (8, {})} | custom-call | flops 3000000000 | bytes 15000000 | tf_op jit(solution)/shard_map/within/pallas_call | solution.py:454
  22.3 0.8 collective-permute-done.3.refs_2_
  23.1 0.3 group.1
  23.4 2.8 %collective-permute-start.4 = (bf16[128,512]{1,0:T(8,128)(2,1)S(1)}, bf16[128,512]{1,0:T(8,128)(2,1)S(1)}, u32[]{:S(2)}, u32[]{:S(2)}) collective-permute-start(bf16[128,512]{1,0:T(8,128)(2,1)S(1)} %get-tuple-element.135), channel_id=1, source_target_pairs={{0,8},{1,9},{2,10},{3,11},{4,12},{5,13},{6,14},{7,15},{8,0},{9,1},... | collective-permute-start | bytes 393224 | tf_op jit(solution)/shard_map/ppermute | solution.py:534
  26.3 3.7 %within.3 = (f32[16,128,512]{2,1,0:T(8,128)S(1)}, bf16[16,128,512]{2,1,0:T(8,128)(2,1)S(1)}, bf16[16,8,128,128]{3,2,1,0:T(8,128)(2,1)S(1)}, f32[16,128,512]{2,1,...) custom-call(bf16[16,128,512]{2,1,0:T(8,128)(2,1)S(1)} %get-tuple-ele, ...), custom_call_target="tpu_custom_call", output_to_operand_aliasing={{0}: (8, {}), {1}: (9, {}), {2}: (10, {}), {3}: (11, {}), {... | custom-call | flops 1800000000 | bytes 9000000 | tf_op jit(solution)/shard_map/within/pallas_call | solution.py:454
  29.9 2.1 %collective-permute-done.4.came = bf16[128,512]{1,0:T(8,128)(2,1)S(1)} collective-permute-done((bf16[128,512]{1,0:T(8,128)(2,1)S(1)}, bf16[128,512]{1,0:T(8,128)(2,1)S(1)}, u32[]{:S(2)}, u32[]{:S(2)}) %collective-permute-start.4) | collective-permute-done | bytes 131104 | tf_op jit(solution)/shard_map/ppermute | solution.py:534
  32.0 0.3 fall.1
  32.4 0.6 collective-permute-start.5
  33.0 1.4 %collective-permute-start.6 = (bf16[2,64,512]{2,1,0:T(8,128)(2,1)S(1)}, bf16[2,64,512]{2,1,0:T(8,128)(2,1)S(1)}, u32[]{:S(2)}, u32[]{:S(2)}) collective-permute-start(bf16[2,64,512]{2,1,0:T(8,128)(2,1)S(1)} %get-tuple-element.158), channel_id=1, source_target_pairs={{0,2},{1,3},{2,0},{3,1},{4,6},{5,7},{6,4},{7,5},{8,10},{9,11},{10,... | collective-permute-start | bytes 393224 | tf_op jit(solution)/shard_map/ppermute | solution.py:534
  34.4 1.6 %collective-permute-start.7 = (bf16[2,64,512]{2,1,0:T(8,128)(2,1)S(1)}, bf16[2,64,512]{2,1,0:T(8,128)(2,1)S(1)}, u32[]{:S(2)}, u32[]{:S(2)}) collective-permute-start(bf16[2,64,512]{2,1,0:T(8,128)(2,1)S(1)} %get-tuple-element.159), channel_id=1, source_target_pairs={{0,6},{1,7},{2,4},{3,5},{4,2},{5,3},{6,0},{7,1},{8,14},{9,15},{10,... | collective-permute-start | bytes 393224 | tf_op jit(solution)/shard_map/ppermute | solution.py:534
  36.0 1.2 %back.4 = (bf16[16,128,512]{2,1,0:T(8,128)(2,1)S(1)}, bf16[16,128,64]{2,1,0:T(8,128)(2,1)S(1)}, f32[8,512]{1,0:T(8,128)S(1)}, f32[8,128]{1,0:T(8,128)S(1)}) custom-call(s32[1]{0:T(128)} %bitcast.me_ref, bf16[2,64,512]{2,1,0:T(8,128)(2,1)S(1)} %get-tuple-element.166.refs_0_, ...), custom_call_target="tpu_custom_call", output_to_operand_aliasing={{3}: (9, {})} | custom-call | flops 600000000 | bytes 3000000 | tf_op jit(solution)/shard_map/back/pallas_call | solution.py:480
  37.1 1.2 %back.5 = (bf16[16,128,512]{2,1,0:T(8,128)(2,1)S(1)}, bf16[16,128,64]{2,1,0:T(8,128)(2,1)S(1)}, f32[8,512]{1,0:T(8,128)S(1)}, f32[8,128]{1,0:T(8,128)S(1)}) custom-call(s32[1]{0:T(128)} %bitcast.me_ref, bf16[2,64,512]{2,1,0:T(8,128)(2,1)S(1)} %collective-permute-done.8.refs_0_, ...), custom_call_target="tpu_custom_call", output_to_operand_aliasing={{0}: (9, {}), {1}: (10, {}), {3}: (11, {})} | custom-call | flops 600000000 | bytes 3000000 | tf_op jit(solution)/shard_map/back/pallas_call | solution.py:480
  38.3 0.9 %early.1 = (f32[4,608,256]{2,1,0:T(8,128)S(1)}, f32[8,128]{1,0:T(8,128)S(1)}) custom-call(s32[1]{0:T(128)} %bitcast.me_ref, bf16[16,128,512]{2,1,0:T(8,128)(2,1)S(1)} %get-tuple-element.171.normed.refs_8_, bf16[16,128,1024]{2,1,0:T(8,128)(2,1)S(1)} %get-tuple-element.172.cot, ...), custom_call_target="tpu_custom_call", output_to_operand_aliasing={{1}: (5, {})} | custom-call | flops 600000000 | bytes 4000000 | tf_op jit(solution)/shard_map/early/pallas_call | solution.py:502
  39.3 2.5 %collective-permute-done.7.refs_2_ = bf16[2,64,512]{2,1,0:T(8,128)(2,1)S(1)} collective-permute-done((bf16[2,64,512]{2,1,0:T(8,128)(2,1)S(1)}, bf16[2,64,512]{2,1,0:T(8,128)(2,1)S(1)}, u32[]{:S(2)}, u32[]{:S(2)}) %collective-permute-start.7) | collective-permute-done | bytes 131104 | tf_op jit(solution)/shard_map/ppermute | solution.py:534
  42.0 2.6 %back.6 = (bf16[16,128,512]{2,1,0:T(8,128)(2,1)S(1)}, bf16[16,128,64]{2,1,0:T(8,128)(2,1)S(1)}, f32[8,512]{1,0:T(8,128)S(1)}, f32[8,128]{1,0:T(8,128)S(1)}) custom-call(s32[1]{0:T(128)} %bitcast.me_ref, bf16[6,64,512]{2,1,0:T(8,128)(2,1)S(1)} %get-tuple-element.183.refs_0_, ...), custom_call_target="tpu_custom_call", output_to_operand_aliasing={{0}: (9, {}), {1}: (10, {}), {3}: (11, {})} | custom-call | flops 1800000000 | bytes 9000000 | tf_op jit(solution)/shard_map/back/pallas_call | solution.py:480
  44.7 2.6 %back.7 = (bf16[16,128,512]{2,1,0:T(8,128)(2,1)S(1)}, bf16[16,128,64]{2,1,0:T(8,128)(2,1)S(1)}, f32[8,512]{1,0:T(8,128)S(1)}, f32[8,128]{1,0:T(8,128)S(1)}) custom-call(s32[1]{0:T(128)} %bitcast.me_ref, bf16[6,64,512]{2,1,0:T(8,128)(2,1)S(1)} %collective-permute-done.9.refs_0_, ...), custom_call_target="tpu_custom_call", output_to_operand_aliasing={{0}: (9, {}), {1}: (10, {}), {3}: (11, {})} | custom-call | flops 1800000000 | bytes 9000000 | tf_op jit(solution)/shard_map/back/pallas_call | solution.py:480
  47.3 1.0 %late.7 = bf16[608,256]{1,0:T(8,128)(2,1)S(1)} custom-call(s32[1]{0:T(128)} %bitcast.me_ref, bf16[16,128,512]{2,1,0:T(8,128)(2,1)S(1)} %get-tuple-element.188.normed, bf16[16,128,1024]{2,1,0:T(8,128)(2,1)S(1)} %get-tuple-element.172.cot, bf16[16,128,64]{2,1,0:T(8,128)(2,1)S(1)} %get-tuple-element.189.read, ...), custom_call_target="tpu_custom_call" | custom-call | flops 400000000 | bytes 3000000 | tf_op jit(solution)/shard_map/late/pallas_call | solution.py:511
  48.3 0.6 collective-permute-start.17
  48.8 0.8 late.5
  49.7 0.8 late.6.part
  50.6 1.0 %collective-permute-start.18 = (bf16[304,256]{1,0:T(8,128)(2,1)S(1)}, bf16[304,256]{1,0:T(8,128)(2,1)S(1)}, u32[]{:S(2)}, u32[]{:S(2)}) collective-permute-start(bf16[304,256]{1,0:T(8,128)(2,1)S(1)} %get-tuple-element.200), channel_id=1, source_target_pairs={{0,2},{1,3},{2,0},{3,1},{4,6},{5,7},{6,4},{7,5},{8,10},{9,11},{10,... | collective-permute-start | bytes 466952 | tf_op jit(solution)/shard_map/ppermute | solution.py:534
  51.7 0.8 late.4.part
  52.6 1.4 %collective-permute-start.11 = (bf16[304,256]{1,0:T(8,128)(2,1)S(1)}, bf16[304,256]{1,0:T(8,128)(2,1)S(1)}, u32[]{:S(2)}, u32[]{:S(2)}) collective-permute-start(bf16[304,256]{1,0:T(8,128)(2,1)S(1)} %get-tuple-element.196), channel_id=1, source_target_pairs={{0,4},{1,5},{2,6},{3,7},{4,0},{5,1},{6,2},{7,3},{8,12},{9,13},{10,... | collective-permute-start | bytes 466952 | tf_op jit(solution)/shard_map/ppermute | solution.py:534
  54.0 3.1 %collective-permute-done.18.came = bf16[304,256]{1,0:T(8,128)(2,1)S(1)} collective-permute-done((bf16[304,256]{1,0:T(8,128)(2,1)S(1)}, bf16[304,256]{1,0:T(8,128)(2,1)S(1)}, u32[]{:S(2)}, u32[]{:S(2)}) %collective-permute-start.18) | collective-permute-done | bytes 155680 | tf_op jit(solution)/shard_map/ppermute | solution.py:534
  57.1 1.2 %collective-permute-start.19 = (bf16[152,256]{1,0:T(8,128)(2,1)S(1)}, bf16[152,256]{1,0:T(8,128)(2,1)S(1)}, u32[]{:S(2)}, u32[]{:S(2)}) collective-permute-start(bf16[152,256]{1,0:T(8,128)(2,1)S(1)} %get-tuple-element.202), channel_id=1, source_target_pairs={{0,4},{1,5},{2,6},{3,7},{4,0},{5,1},{6,2},{7,3},{8,12},{9,13},{10,... | collective-permute-start | bytes 233480 | tf_op jit(solution)/shard_map/ppermute | solution.py:534
  58.3 0.4 collective-permute-done.11.came
  58.8 1.1 %collective-permute-start.12 = (bf16[152,256]{1,0:T(8,128)(2,1)S(1)}, bf16[152,256]{1,0:T(8,128)(2,1)S(1)}, u32[]{:S(2)}, u32[]{:S(2)}) collective-permute-start(bf16[152,256]{1,0:T(8,128)(2,1)S(1)} %get-tuple-element.198), channel_id=1, source_target_pairs={{0,2},{1,3},{2,0},{3,1},{4,6},{5,7},{6,4},{7,5},{8,10},{9,11},{10,... | collective-permute-start | bytes 233480 | tf_op jit(solution)/shard_map/ppermute | solution.py:534
  59.9 1.7 %collective-permute-done.19 = bf16[152,256]{1,0:T(8,128)(2,1)S(1)} collective-permute-done((bf16[152,256]{1,0:T(8,128)(2,1)S(1)}, bf16[152,256]{1,0:T(8,128)(2,1)S(1)}, u32[]{:S(2)}, u32[]{:S(2)}) %collective-permute-start.19) | collective-permute-done | bytes 77856 | tf_op jit(solution)/shard_map/ppermute | solution.py:534
  61.6 3.0 %collective-permute-start.20 = (bf16[152,256]{1,0:T(8,128)(2,1)S(1)}, bf16[152,256]{1,0:T(8,128)(2,1)S(1)}, u32[]{:S(2)}, u32[]{:S(2)}) collective-permute-start(bf16[152,256]{1,0:T(8,128)(2,1)S(1)} %fusion.1), channel_id=1, source_target_pairs={{0,8},{1,9},{2,10},{3,11},{4,12},{5,13},{6,14},{7,15},{8,0},{9,1},... | collective-permute-start | bytes 233480 | tf_op jit(solution)/shard_map/ppermute | solution.py:534
  64.7 2.1 %collective-permute-start.13 = (bf16[152,256]{1,0:T(8,128)(2,1)S(1)}, bf16[152,256]{1,0:T(8,128)(2,1)S(1)}, u32[]{:S(2)}, u32[]{:S(2)}) collective-permute-start(bf16[152,256]{1,0:T(8,128)(2,1)S(1)} %fusion), channel_id=1, source_target_pairs={{0,8},{1,9},{2,10},{3,11},{4,12},{5,13},{6,14},{7,15},{8,0},{9,1},... | collective-permute-start | bytes 233480 | tf_op jit(solution)/shard_map/ppermute | solution.py:534
  66.7 2.6 %collective-permute-done.20 = bf16[152,256]{1,0:T(8,128)(2,1)S(1)} collective-permute-done((bf16[152,256]{1,0:T(8,128)(2,1)S(1)}, bf16[152,256]{1,0:T(8,128)(2,1)S(1)}, u32[]{:S(2)}, u32[]{:S(2)}) %collective-permute-start.20) | collective-permute-done | bytes 77856 | tf_op jit(solution)/shard_map/ppermute | solution.py:534
  69.6 1.5 %collective-permute-done.13 = bf16[152,256]{1,0:T(8,128)(2,1)S(1)} collective-permute-done((bf16[152,256]{1,0:T(8,128)(2,1)S(1)}, bf16[152,256]{1,0:T(8,128)(2,1)S(1)}, u32[]{:S(2)}, u32[]{:S(2)}) %collective-permute-start.13) | collective-permute-done | bytes 77856 | tf_op jit(solution)/shard_map/ppermute | solution.py:534
  71.1 1.6 %collective-permute-start.14 = (bf16[152,256]{1,0:T(8,128)(2,1)S(1)}, bf16[152,256]{1,0:T(8,128)(2,1)S(1)}, u32[]{:S(2)}, u32[]{:S(2)}) collective-permute-start(bf16[152,256]{1,0:T(8,128)(2,1)S(1)} %add_convert_fusion.1.part), channel_id=1, source_target_pairs={{0,2},{1,3},{2,0},{3,1},{4,6},{5,7},{6,4},{7,5},{8,10},{9,11},{10,... | collective-permute-start | bytes 233480 | tf_op jit(solution)/shard_map/ppermute | solution.py:534
  72.7 1.2 %collective-permute-done.21.came = bf16[152,256]{1,0:T(8,128)(2,1)S(1)} collective-permute-done((bf16[152,256]{1,0:T(8,128)(2,1)S(1)}, bf16[152,256]{1,0:T(8,128)(2,1)S(1)}, u32[]{:S(2)}, u32[]{:S(2)}) %collective-permute-start.21) | collective-permute-done | bytes 77856 | tf_op jit(solution)/shard_map/ppermute | solution.py:534
  73.9 2.3 %collective-permute-start.22 = (bf16[304,256]{1,0:T(8,128)(2,1)S(1)}, bf16[304,256]{1,0:T(8,128)(2,1)S(1)}, u32[]{:S(2)}, u32[]{:S(2)}) collective-permute-start(bf16[304,256]{1,0:T(8,128)(2,1)S(1)} %join.6.part), channel_id=1, source_target_pairs={{0,2},{1,3},{2,0},{3,1},{4,6},{5,7},{6,4},{7,5},{8,10},{9,11},{10,... | collective-permute-start | bytes 466952 | tf_op jit(solution)/shard_map/ppermute | solution.py:534
  76.2 0.3 collective-permute-done.14.came
  76.5 2.8 %collective-permute-done.22.came = bf16[304,256]{1,0:T(8,128)(2,1)S(1)} collective-permute-done((bf16[304,256]{1,0:T(8,128)(2,1)S(1)}, bf16[304,256]{1,0:T(8,128)(2,1)S(1)}, u32[]{:S(2)}, u32[]{:S(2)}) %collective-permute-start.22) | collective-permute-done | bytes 155680 | tf_op jit(solution)/shard_map/ppermute | solution.py:534
  79.5 2.2 %collective-permute-done.15.came = bf16[304,256]{1,0:T(8,128)(2,1)S(1)} collective-permute-done((bf16[304,256]{1,0:T(8,128)(2,1)S(1)}, bf16[304,256]{1,0:T(8,128)(2,1)S(1)}, u32[]{:S(2)}, u32[]{:S(2)}) %collective-permute-start.15) | collective-permute-done | bytes 155680 | tf_op jit(solution)/shard_map/ppermute | solution.py:534
  81.9 1.1 %finish.2 = (f32[512,1024]{1,0:T(8,128)}, f32[64,1024]{1,0:T(8,128)}, f32[1,512]{1,0:T(1,128)}) custom-call(s32[1]{0:T(128)} %bitcast.me_ref, bf16[608,256]{1,0:T(8,128)(2,1)S(1)} %join.7.mine, bf16[608,256]{1,0:T(8,128)(2,1)S(1)} %collective-permute-done.23.came), custom_call_target="tpu_custom_call" | custom-call | flops 1000000 | bytes 2000000 | tf_op jit(solution)/shard_map/finish/pallas_call | solution.py:519
  83.0 0.5 collective-permute-done.16.came
  83.5 1.1 %finish.3 = (f32[512,1024]{1,0:T(8,128)}, f32[64,1024]{1,0:T(8,128)}, f32[1,512]{1,0:T(1,128)}) custom-call(s32[1]{0:T(128)} %bitcast.me_ref, bf16[608,256]{1,0:T(8,128)(2,1)S(1)} %join.5.mine, bf16[608,256]{1,0:T(8,128)(2,1)S(1)} %collective-permute-done.16.came, ...), custom_call_target="tpu_custom_call", output_to_operand_aliasing={{0}: (3, {}), {1}: (4, {}), {2}: (5, {})} | custom-call | flops 1000000 | bytes 2000000 | tf_op jit(solution)/shard_map/finish/pallas_call | solution.py:519
  (31 shorter events, 1.5 us)
Async XLA Ops:
  9.2 2.1 %collective-permute-start = (bf16[528,512]{1,0:T(8,128)(2,1)S(1)}, bf16[528,512]{1,0:T(8,128)(2,1)S(1)}, u32[]{:S(2)}, u32[]{:S(2)}) collective-permute-start(bf16[528,512]{1,0:T(8,128)(2,1)S(1)} %get-tuple-element.106), channel_id=1, source_target_pairs={{0,1},{1,0},{2,3},{3,2},{4,5},{5,4},{6,7},{7,6},{8,9},{9,8},{10,11... | collective-permute-start | bytes 1622024 | tf_op jit(solution)/shard_map/ppermute | solution.py:534
  11.6 10.7 %collective-permute-start.1 = (bf16[144,512]{1,0:T(8,128)(2,1)S(1)}, bf16[144,512]{1,0:T(8,128)(2,1)S(1)}, u32[]{:S(2)}, u32[]{:S(2)}) collective-permute-start(bf16[144,512]{1,0:T(8,128)(2,1)S(1)} %get-tuple-element.121), channel_id=1, source_target_pairs={{0,2},{1,3},{2,0},{3,1},{4,6},{5,7},{6,4},{7,5},{8,10},{9,11},{10,... | collective-permute-start | bytes 442376 | tf_op jit(solution)/shard_map/ppermute | solution.py:534
  14.5 7.7 %collective-permute-start.2 = (bf16[144,512]{1,0:T(8,128)(2,1)S(1)}, bf16[144,512]{1,0:T(8,128)(2,1)S(1)}, u32[]{:S(2)}, u32[]{:S(2)}) collective-permute-start(bf16[144,512]{1,0:T(8,128)(2,1)S(1)} %get-tuple-element.122), channel_id=1, source_target_pairs={{0,4},{1,5},{2,6},{3,7},{4,0},{5,1},{6,2},{7,3},{8,12},{9,13},{10,... | collective-permute-start | bytes 442376 | tf_op jit(solution)/shard_map/ppermute | solution.py:534
  16.1 7.0 %collective-permute-start.3 = (bf16[144,512]{1,0:T(8,128)(2,1)S(1)}, bf16[144,512]{1,0:T(8,128)(2,1)S(1)}, u32[]{:S(2)}, u32[]{:S(2)}) collective-permute-start(bf16[144,512]{1,0:T(8,128)(2,1)S(1)} %get-tuple-element.123), channel_id=1, source_target_pairs={{0,6},{1,7},{2,4},{3,5},{4,2},{5,3},{6,0},{7,1},{8,14},{9,15},{10,... | collective-permute-start | bytes 442376 | tf_op jit(solution)/shard_map/ppermute | solution.py:534
  23.4 8.6 %collective-permute-start.4 = (bf16[128,512]{1,0:T(8,128)(2,1)S(1)}, bf16[128,512]{1,0:T(8,128)(2,1)S(1)}, u32[]{:S(2)}, u32[]{:S(2)}) collective-permute-start(bf16[128,512]{1,0:T(8,128)(2,1)S(1)} %get-tuple-element.135), channel_id=1, source_target_pairs={{0,8},{1,9},{2,10},{3,11},{4,12},{5,13},{6,14},{7,15},{8,0},{9,1},... | collective-permute-start | bytes 393224 | tf_op jit(solution)/shard_map/ppermute | solution.py:534
  32.3 4.8 %collective-permute-start.8 = (bf16[2,64,512]{2,1,0:T(8,128)(2,1)S(1)}, bf16[2,64,512]{2,1,0:T(8,128)(2,1)S(1)}, u32[]{:S(2)}, u32[]{:S(2)}) collective-permute-start(bf16[2,64,512]{2,1,0:T(8,128)(2,1)S(1)} %get-tuple-element.160), channel_id=1, source_target_pairs={{0,1},{1,0},{2,3},{3,2},{4,5},{5,4},{6,7},{7,6},{8,9},{9,8},{10,11... | collective-permute-start | bytes 393224 | tf_op jit(solution)/shard_map/ppermute | solution.py:534
  32.4 6.8 %collective-permute-start.5 = (bf16[2,64,512]{2,1,0:T(8,128)(2,1)S(1)}, bf16[2,64,512]{2,1,0:T(8,128)(2,1)S(1)}, u32[]{:S(2)}, u32[]{:S(2)}) collective-permute-start(bf16[2,64,512]{2,1,0:T(8,128)(2,1)S(1)} %get-tuple-element.157), channel_id=1, source_target_pairs={{0,4},{1,5},{2,6},{3,7},{4,0},{5,1},{6,2},{7,3},{8,12},{9,13},{10,... | collective-permute-start | bytes 393224 | tf_op jit(solution)/shard_map/ppermute | solution.py:534
  33.0 6.3 %collective-permute-start.6 = (bf16[2,64,512]{2,1,0:T(8,128)(2,1)S(1)}, bf16[2,64,512]{2,1,0:T(8,128)(2,1)S(1)}, u32[]{:S(2)}, u32[]{:S(2)}) collective-permute-start(bf16[2,64,512]{2,1,0:T(8,128)(2,1)S(1)} %get-tuple-element.158), channel_id=1, source_target_pairs={{0,2},{1,3},{2,0},{3,1},{4,6},{5,7},{6,4},{7,5},{8,10},{9,11},{10,... | collective-permute-start | bytes 393224 | tf_op jit(solution)/shard_map/ppermute | solution.py:534
  34.4 7.4 %collective-permute-start.7 = (bf16[2,64,512]{2,1,0:T(8,128)(2,1)S(1)}, bf16[2,64,512]{2,1,0:T(8,128)(2,1)S(1)}, u32[]{:S(2)}, u32[]{:S(2)}) collective-permute-start(bf16[2,64,512]{2,1,0:T(8,128)(2,1)S(1)} %get-tuple-element.159), channel_id=1, source_target_pairs={{0,6},{1,7},{2,4},{3,5},{4,2},{5,3},{6,0},{7,1},{8,14},{9,15},{10,... | collective-permute-start | bytes 393224 | tf_op jit(solution)/shard_map/ppermute | solution.py:534
  42.0 2.7 %collective-permute-start.9 = (bf16[6,64,512]{2,1,0:T(8,128)(2,1)S(1)}, bf16[6,64,512]{2,1,0:T(8,128)(2,1)S(1)}, u32[]{:S(2)}, u32[]{:S(2)}) collective-permute-start(bf16[6,64,512]{2,1,0:T(8,128)(2,1)S(1)} %get-tuple-element.182), channel_id=1, source_target_pairs={{0,1},{1,0},{2,3},{3,2},{4,5},{5,4},{6,7},{7,6},{8,9},{9,8},{10,11... | collective-permute-start | bytes 1179656 | tf_op jit(solution)/shard_map/ppermute | solution.py:534
  48.3 2.2 %collective-permute-start.17 = (bf16[608,256]{1,0:T(8,128)(2,1)S(1)}, bf16[608,256]{1,0:T(8,128)(2,1)S(1)}, u32[]{:S(2)}, u32[]{:S(2)}) collective-permute-start(bf16[608,256]{1,0:T(8,128)(2,1)S(1)} %late.7), channel_id=1, source_target_pairs={{0,1},{1,0},{2,3},{3,2},{4,5},{5,4},{6,7},{7,6},{8,9},{9,8},{10,11... | collective-permute-start | bytes 933896 | tf_op jit(solution)/shard_map/ppermute | solution.py:534
  49.6 2.8 %collective-permute-start.10 = (bf16[608,256]{1,0:T(8,128)(2,1)S(1)}, bf16[608,256]{1,0:T(8,128)(2,1)S(1)}, u32[]{:S(2)}, u32[]{:S(2)}) collective-permute-start(bf16[608,256]{1,0:T(8,128)(2,1)S(1)} %late.5), channel_id=1, source_target_pairs={{0,1},{1,0},{2,3},{3,2},{4,5},{5,4},{6,7},{7,6},{8,9},{9,8},{10,11... | collective-permute-start | bytes 933896 | tf_op jit(solution)/shard_map/ppermute | solution.py:534
  50.6 6.5 %collective-permute-start.18 = (bf16[304,256]{1,0:T(8,128)(2,1)S(1)}, bf16[304,256]{1,0:T(8,128)(2,1)S(1)}, u32[]{:S(2)}, u32[]{:S(2)}) collective-permute-start(bf16[304,256]{1,0:T(8,128)(2,1)S(1)} %get-tuple-element.200), channel_id=1, source_target_pairs={{0,2},{1,3},{2,0},{3,1},{4,6},{5,7},{6,4},{7,5},{8,10},{9,11},{10,... | collective-permute-start | bytes 466952 | tf_op jit(solution)/shard_map/ppermute | solution.py:534
  52.6 6.2 %collective-permute-start.11 = (bf16[304,256]{1,0:T(8,128)(2,1)S(1)}, bf16[304,256]{1,0:T(8,128)(2,1)S(1)}, u32[]{:S(2)}, u32[]{:S(2)}) collective-permute-start(bf16[304,256]{1,0:T(8,128)(2,1)S(1)} %get-tuple-element.196), channel_id=1, source_target_pairs={{0,4},{1,5},{2,6},{3,7},{4,0},{5,1},{6,2},{7,3},{8,12},{9,13},{10,... | collective-permute-start | bytes 466952 | tf_op jit(solution)/shard_map/ppermute | solution.py:534
  57.1 4.5 %collective-permute-start.19 = (bf16[152,256]{1,0:T(8,128)(2,1)S(1)}, bf16[152,256]{1,0:T(8,128)(2,1)S(1)}, u32[]{:S(2)}, u32[]{:S(2)}) collective-permute-start(bf16[152,256]{1,0:T(8,128)(2,1)S(1)} %get-tuple-element.202), channel_id=1, source_target_pairs={{0,4},{1,5},{2,6},{3,7},{4,0},{5,1},{6,2},{7,3},{8,12},{9,13},{10,... | collective-permute-start | bytes 233480 | tf_op jit(solution)/shard_map/ppermute | solution.py:534
  58.8 5.9 %collective-permute-start.12 = (bf16[152,256]{1,0:T(8,128)(2,1)S(1)}, bf16[152,256]{1,0:T(8,128)(2,1)S(1)}, u32[]{:S(2)}, u32[]{:S(2)}) collective-permute-start(bf16[152,256]{1,0:T(8,128)(2,1)S(1)} %get-tuple-element.198), channel_id=1, source_target_pairs={{0,2},{1,3},{2,0},{3,1},{4,6},{5,7},{6,4},{7,5},{8,10},{9,11},{10,... | collective-permute-start | bytes 233480 | tf_op jit(solution)/shard_map/ppermute | solution.py:534
  61.6 7.7 %collective-permute-start.20 = (bf16[152,256]{1,0:T(8,128)(2,1)S(1)}, bf16[152,256]{1,0:T(8,128)(2,1)S(1)}, u32[]{:S(2)}, u32[]{:S(2)}) collective-permute-start(bf16[152,256]{1,0:T(8,128)(2,1)S(1)} %fusion.1), channel_id=1, source_target_pairs={{0,8},{1,9},{2,10},{3,11},{4,12},{5,13},{6,14},{7,15},{8,0},{9,1},... | collective-permute-start | bytes 233480 | tf_op jit(solution)/shard_map/ppermute | solution.py:534
  64.7 6.4 %collective-permute-start.13 = (bf16[152,256]{1,0:T(8,128)(2,1)S(1)}, bf16[152,256]{1,0:T(8,128)(2,1)S(1)}, u32[]{:S(2)}, u32[]{:S(2)}) collective-permute-start(bf16[152,256]{1,0:T(8,128)(2,1)S(1)} %fusion), channel_id=1, source_target_pairs={{0,8},{1,9},{2,10},{3,11},{4,12},{5,13},{6,14},{7,15},{8,0},{9,1},... | collective-permute-start | bytes 233480 | tf_op jit(solution)/shard_map/ppermute | solution.py:534
  69.4 4.5 %collective-permute-start.21 = (bf16[152,256]{1,0:T(8,128)(2,1)S(1)}, bf16[152,256]{1,0:T(8,128)(2,1)S(1)}, u32[]{:S(2)}, u32[]{:S(2)}) collective-permute-start(bf16[152,256]{1,0:T(8,128)(2,1)S(1)} %add_convert_fusion.part), channel_id=1, source_target_pairs={{0,4},{1,5},{2,6},{3,7},{4,0},{5,1},{6,2},{7,3},{8,12},{9,13},{10,... | collective-permute-start | bytes 233480 | tf_op jit(solution)/shard_map/ppermute | solution.py:534
  71.1 5.3 %collective-permute-start.14 = (bf16[152,256]{1,0:T(8,128)(2,1)S(1)}, bf16[152,256]{1,0:T(8,128)(2,1)S(1)}, u32[]{:S(2)}, u32[]{:S(2)}) collective-permute-start(bf16[152,256]{1,0:T(8,128)(2,1)S(1)} %add_convert_fusion.1.part), channel_id=1, source_target_pairs={{0,2},{1,3},{2,0},{3,1},{4,6},{5,7},{6,4},{7,5},{8,10},{9,11},{10,... | collective-permute-start | bytes 233480 | tf_op jit(solution)/shard_map/ppermute | solution.py:534
  73.9 5.5 %collective-permute-start.22 = (bf16[304,256]{1,0:T(8,128)(2,1)S(1)}, bf16[304,256]{1,0:T(8,128)(2,1)S(1)}, u32[]{:S(2)}, u32[]{:S(2)}) collective-permute-start(bf16[304,256]{1,0:T(8,128)(2,1)S(1)} %join.6.part), channel_id=1, source_target_pairs={{0,2},{1,3},{2,0},{3,1},{4,6},{5,7},{6,4},{7,5},{8,10},{9,11},{10,... | collective-permute-start | bytes 466952 | tf_op jit(solution)/shard_map/ppermute | solution.py:534
  76.4 5.3 %collective-permute-start.15 = (bf16[304,256]{1,0:T(8,128)(2,1)S(1)}, bf16[304,256]{1,0:T(8,128)(2,1)S(1)}, u32[]{:S(2)}, u32[]{:S(2)}) collective-permute-start(bf16[304,256]{1,0:T(8,128)(2,1)S(1)} %join.4.part), channel_id=1, source_target_pairs={{0,4},{1,5},{2,6},{3,7},{4,0},{5,1},{6,2},{7,3},{8,12},{9,13},{10,... | collective-permute-start | bytes 466952 | tf_op jit(solution)/shard_map/ppermute | solution.py:534
  79.4 2.5 %collective-permute-start.23 = (bf16[608,256]{1,0:T(8,128)(2,1)S(1)}, bf16[608,256]{1,0:T(8,128)(2,1)S(1)}, u32[]{:S(2)}, u32[]{:S(2)}) collective-permute-start(bf16[608,256]{1,0:T(8,128)(2,1)S(1)} %join.7.mine), channel_id=1, source_target_pairs={{0,1},{1,0},{2,3},{3,2},{4,5},{5,4},{6,7},{7,6},{8,9},{9,8},{10,11... | collective-permute-start | bytes 933896 | tf_op jit(solution)/shard_map/ppermute | solution.py:534
  81.8 1.7 %collective-permute-start.16 = (bf16[608,256]{1,0:T(8,128)(2,1)S(1)}, bf16[608,256]{1,0:T(8,128)(2,1)S(1)}, u32[]{:S(2)}, u32[]{:S(2)}) collective-permute-start(bf16[608,256]{1,0:T(8,128)(2,1)S(1)} %join.5.mine), channel_id=1, source_target_pairs={{0,1},{1,0},{2,3},{3,2},{4,5},{5,4},{6,7},{7,6},{8,9},{9,8},{10,11... | collective-permute-start | bytes 933896 | tf_op jit(solution)/shard_map/ppermute | solution.py:534
